TPU v7x, 256 devices: a whole 4x4x8 slice. The times are simulated.
256 devices in a mesh: aux: 2 (over core), row: 8 (over z), col: 16 (over x, y).
Axes of the slice: x: 4, y: 4, z: 8, core: 2. Of those that a mesh axis runs over, the one named last changes fastest.
Arguments:
- coulomb: bfloat16 [64, 2048, 2048], P('aux', 'row', 'col'), may hold values from -6 to 6
- occupied: bfloat16 [2048, 2048], P('row'), may hold values from -0.125 to 0.125
- virtual: bfloat16 [2048, 2048], P('row'), may hold values from -0.125 to 0.125
- tile_mask: int32 [16, 16], replicated, may hold values 0 or 1
Outputs:
- chi: float32 [64, 64], P('aux')
All inputs are finite; a program needn't handle non-finite values.
Results may differ from a plain program's by a relative error of at most 0.0042.
Values may be sent and summed in bfloat16 or wider, within the bound.
A program may use at most 128 MiB of HBM per device.

v0:
```python
import jax
import jax.numpy as jnp
from jax import lax
from jax.sharding import PartitionSpec as P

NAO = 2048
TILE = 128


def swapped(value, axis, apart):
    mask = 2**apart
    pairs = [(source, source ^ mask) for source in range(lax.axis_size(axis))]
    return lax.ppermute(value, axis, pairs)


def shards(coulomb, occupied, virtual, tile_mask):
    rows = lax.axis_size("row")
    cols = lax.axis_size("col")
    pdev, mrow, ncol = coulomb.shape
    nao = mrow * rows
    row_idx = lax.axis_index("row")
    col_idx = lax.axis_index("col")
    aux_idx = lax.axis_index("aux")
    tiles_r = mrow // TILE
    tiles_c = ncol // TILE
    local_tiles = lax.dynamic_slice(
        tile_mask, (row_idx * tiles_r, col_idx * tiles_c), (tiles_r, tiles_c)
    )
    local_mask = jnp.repeat(jnp.repeat(local_tiles, TILE, axis=0), TILE, axis=1).astype(
        jnp.bfloat16
    )
    screened = coulomb * local_mask[None]
    moved = lax.all_to_all(screened, "row", split_axis=0, concat_axis=1, tiled=True)
    pieces = moved.shape[0]
    occ_all, virt_all = (
        lax.all_gather(occupied, "row", axis=0, tiled=True),
        lax.all_gather(virtual, "row", axis=0, tiled=True),
    )
    half = jnp.einsum("ml,pmn->pln", occ_all, moved, preferred_element_type=jnp.float32).astype(
        jnp.bfloat16
    )
    jpart = mrow // cols
    shaped = half.reshape(pieces, rows, cols, jpart, ncol)
    spread = lax.all_to_all(shaped, "col", split_axis=2, concat_axis=4, tiled=True)
    spread = spread.reshape(pieces, rows * jpart, nao)
    dressed = jnp.einsum(
        "pln,ns->pls", spread, virt_all, preferred_element_type=jnp.float32
    ).astype(jnp.bfloat16)
    layered = dressed.reshape(pieces, rows, 1, jpart, cols, ncol)
    returned = lax.all_to_all(
        lax.all_to_all(layered, "row", split_axis=1, concat_axis=0, tiled=True),
        "col",
        split_axis=4,
        concat_axis=2,
        tiled=True,
    )
    aligned = returned.reshape(pdev, mrow, ncol)
    theirs = swapped(screened, "aux", 0)
    with_mine = jnp.einsum("pls,qls->pq", aligned, screened, preferred_element_type=jnp.float32)
    with_theirs = jnp.einsum("pls,qls->pq", aligned, theirs, preferred_element_type=jnp.float32)
    first_half = jnp.where(aux_idx == 0, with_mine, with_theirs)
    second_half = jnp.where(aux_idx == 0, with_theirs, with_mine)
    partial_chi = jnp.concatenate([first_half, second_half], axis=1)
    total_chi = lax.psum(partial_chi, ("row", "col"))
    return total_chi / NAO


def solution(mesh):
    placed = (P("aux", "row", "col"), P("row", None), P("row", None), P())
    return jax.shard_map(
        shards, mesh=mesh, in_specs=placed, out_specs=P("aux", None), check_vma=False
    )
```

profile of v0, /device:TPU:24, one launch (start us, length us, event | category | flops | bytes accessed | tf_op | source)
XLA Modules:
  0.0 1028.3 jit_solution(6755601709993652313)
XLA Ops:
  6.5 0.0 all-gather.3.cloned.1.call-start
  6.5 0.7 all-gather.3.cloned.1.call-update
  7.3 0.0 all-gather.5.cloned.1.call-start
  7.3 0.7 all-gather.5.cloned.1.call-update
  8.0 0.9 fusion.13
  8.9 0.1 broadcast_bitcast_fusion
  9.0 2.8 copy_multiply_fusion
  11.7 0.8 copy.15
  12.6 82.0 %all_to_all.66 = bf16[32,256,128]{2,1,0:T(8,128)(2,1)} all-to-all(bf16[32,256,128]{2,1,0:T(8,128)(2,1)S(1)} %copy.15), channel_id=1, replica_groups=mesh['aux'=2,'row'=8,'col'=16] {'row'}, dimensions={0} | all-to-all | bytes 4194304 | tf_op jit(solution)/shard_map/all_to_all | solution.py:33
  94.5 4.5 copy.16
  99.0 4.2 all_to_all.51
  103.2 45.4 %all-gather.3.cloned.1.call-done = bf16[2048,2048]{1,0:T(8,128)(2,1)} async-done(((bf16[256,2048]{1,0:T(8,128)(2,1)}), bf16[2048,2048]{1,0:T(8,128)(2,1)}) %all-gather.3.cloned.1.call-update) | async-done | bytes 8388624 | tf_op jit(solution)/shard_map/all_gather | solution.py:36
  148.6 9.8 fusion.10
  158.4 4.0 copy.17
  162.4 2.2 copy.18
  164.6 33.2 %all_to_all.67 = bf16[4,8,16,16,128]{4,3,1,0,2:T(8,128)(2,1)S(1)} all-to-all(bf16[4,8,16,16,128]{4,3,1,0,2:T(8,128)(2,1)S(1)} %copy.18), channel_id=1, replica_groups=mesh['aux'=2,'row'=8,'col'=16] {'col'}, dimensions={2} | all-to-all | bytes 4194304 | tf_op jit(solution)/shard_map/all_to_all | solution.py:44
  197.8 3.7 copy.19
  201.5 4.2 reshape.35
  205.7 37.6 %all-gather.5.cloned.1.call-done = bf16[2048,2048]{1,0:T(8,128)(2,1)} async-done(((bf16[256,2048]{1,0:T(8,128)(2,1)}), bf16[2048,2048]{1,0:T(8,128)(2,1)}) %all-gather.5.cloned.1.call-update) | async-done | bytes 8388624 | tf_op jit(solution)/shard_map/all_gather | solution.py:37
  243.3 8.5 fusion.7
  251.9 0.6 copy.23
  252.5 0.6 copy.20
  253.1 55.3 %all_to_all.68 = bf16[4,8,1,16,16,128]{5,4,3,0,2,1:T(8,128)(2,1)S(1)} all-to-all(bf16[4,8,1,16,16,128]{5,4,3,0,2,1:T(8,128)(2,1)S(1)} %copy.20), channel_id=1, replica_groups=mesh['aux'=2,'row'=8,'col'=16] {'row'}, dimensions={1} | all-to-all | bytes 4194304 | tf_op jit(solution)/shard_map/all_to_all | solution.py:51
  308.4 1.8 copy.21
  310.2 7.2 all-to-all-start.3
  317.4 0.0 collective-permute-start
  317.5 25.2 %all-to-all-done.3 = bf16[32,1,1,16,16,128]{5,3,0,2,1,4:T(8,128)(2,1)} async-done(((bf16[32,1,1,16,16,128]{5,3,0,2,1,4:T(8,128)(2,1)}), bf16[32,1,1,16,16,128]{5,3,0,2,1,4:T(8,128)(2,1)}, u32[]{:S(2)}, u32[]{:S(2)}) %all-to-all-start.3) | async-done | bytes 2097184 | tf_op jit(solution)/shard_map/all_to_all | solution.py:50
  342.7 2.1 copy.22
  344.8 0.7 convolution_bitcast_fusion.1
  345.5 0.0 collective-permute-done
  345.5 2.3 broadcast_select_fusion.1
  347.8 0.1 pad_maximum_fusion
  347.9 673.0 %psum.7 = f32[32,64]{1,0:T(8,128)S(1)} all-reduce(f32[32,64]{1,0:T(8,128)S(1)} %pad_maximum_fusion), channel_id=1, replica_groups=mesh['aux'=2,'row'=8,'col'=16] {'row','col'}, use_global_device_ids=true, to_apply=%region_0.1 | all-reduce | flops 2048 | bytes 16384 | tf_op jit(solution)/shard_map/psum | solution.py:64
  1020.9 0.6 broadcast_multiply_fusion
Async XLA Ops:
  6.5 142.1 %all-gather.3.cloned.1.call-start = ((), (), s32[]{:S(2)}) async-start(), calls=%async_computation.4 | async-start | bytes 9437184 | tf_op jit(solution)/shard_map/all_gather | solution.py:36
  7.3 236.1 %all-gather.5.cloned.1.call-start = ((), (), s32[]{:S(2)}) async-start(), calls=%async_computation.5 | async-start | bytes 9437184 | tf_op jit(solution)/shard_map/all_gather | solution.py:37
  310.2 32.4 %all-to-all-start.3 = ((bf16[32,1,1,16,16,128]{5,3,0,2,1,4:T(8,128)(2,1)}), bf16[32,1,1,16,16,128]{5,3,0,2,1,4:T(8,128)(2,1)}, u32[]{:S(2)}, u32[]{:S(2)}) async-start(bf16[32,1,1,16,16,128]{5,3,0,2,1,4:T(8,128)(2,1)} %copy.21), calls=%async_computation.3 | async-start | bytes 4194304 | tf_op jit(solution)/shard_map/all_to_all | solution.py:50
  317.4 28.0 %collective-permute-start = (bf16[32,256,128]{2,0,1:T(8,128)(2,1)S(1)}, bf16[32,256,128]{2,0,1:T(8,128)(2,1)}, u32[]{:S(2)}, u32[]{:S(2)}) collective-permute-start(bf16[32,256,128]{2,0,1:T(8,128)(2,1)S(1)} %copy_multiply_fusion), channel_id=1, source_target_pairs={{0,128},{128,0},{1,129},{129,1},{2,130},{130,2},{3,131},{131,3},{4... | collective-permute-start | bytes 6291464 | tf_op jit(solution)/shard_map/ppermute | solution.py:13
Sparse Core Ops, SparseCore 0:
  9.1 139.4 all-gather.2
  150.4 92.8 all-gather.4
where the time goes:
time: 1040 us; the launch traced here: 1030 us
  blocking collectives  843 us (81%)
  waiting for transfers between devices  110 us (11%)
  local copies, waits for them, and re-layouts  28.9 us (3%)
  matrix products  21.3 us (2%)
  between operations  13.5 us (1%)
    psum x1, blocking collectives, shards(): total_chi = lax.psum(partial_chi, ('row', 'col'))  673 us
    all_to_all x1, blocking collectives, shards(): lax.all_to_all(screened, 'row', split_axis=0, concat_axis=1, tiled=True)  82 us
    all_to_all x1, blocking collectives, shards(): lax.all_to_all(layered, 'row', split_axis=1, concat_axis=0, tiled=True)  55.3 us
    all_gather x1, waiting for transfers between devices, shards(): lax.all_gather(occupied, 'row', axis=0, tiled=True)  45.4 us
    all_gather x1, waiting for transfers between devices, shards(): lax.all_gather(virtual, 'row', axis=0, tiled=True)  37.6 us
    all_to_all x1, blocking collectives, shards(): lax.all_to_all(shaped, 'col', split_axis=2, concat_axis=4, tiled=True)  33.2 us
    all_to_all x1, waiting for transfers between devices, shards(): lax.all_to_all(lax.all_to_all(layered, 'row', split_axis=1, concat_axis=0...  25.2 us
  transfers between devices with their start and end apart: 4, of which 3 were waited for; matrix products, arithmetic and copies ran while one was open for 3% of the time, Pallas kernels for 0%

commit v1 on v0

--- a/solution.py
+++ b/solution.py
@@ -61,7 +61,11 @@
     first_half = jnp.where(aux_idx == 0, with_mine, with_theirs)
     second_half = jnp.where(aux_idx == 0, with_theirs, with_mine)
     partial_chi = jnp.concatenate([first_half, second_half], axis=1)
-    total_chi = lax.psum(partial_chi, ("row", "col"))
+    slots = lax.axis_size("aux")
+    placed = jnp.zeros((slots,) + partial_chi.shape, partial_chi.dtype)
+    placed = lax.dynamic_update_index_in_dim(placed, partial_chi, aux_idx, 0)
+    total = lax.psum(placed, ("aux", "row", "col"))
+    total_chi = lax.dynamic_index_in_dim(total, aux_idx, 0, keepdims=False)
     return total_chi / NAO
 
 

time: 1040 us -> 431 us (0.41)
  blocking collectives: 843 us -> 244 us
    psum x1, blocking collectives: 673 us -> 73.8 us  [shards(): total = lax.psum(placed, ('aux', 'row', 'col'))]
  transfers between devices with their start and end apart: 4 -> 4, of which waited for: 3 -> 3; matrix products, arithmetic and copies ran while one was open for 3% -> 8% of each run, Pallas kernels for 0% -> 0%
where the time goes in v1:
time: 431 us; the launch traced here: 429 us
  blocking collectives  244 us (57%)
  waiting for transfers between devices  110 us (26%)
  local copies, waits for them, and re-layouts  28.9 us (7%)
  matrix products  21.3 us (5%)
  between operations  13.5 us (3%)
  starting transfers between devices  7.25 us (2%)
  other arithmetic  4.33 us (1%)
    all_to_all x1, blocking collectives, shards(): lax.all_to_all(screened, 'row', split_axis=0, concat_axis=1, tiled=True)  82 us
    psum x1, blocking collectives, shards(): total = lax.psum(placed, ('aux', 'row', 'col'))  73.8 us
    all_to_all x1, blocking collectives, shards(): lax.all_to_all(layered, 'row', split_axis=1, concat_axis=0, tiled=True)  55.3 us
    all_gather x1, waiting for transfers between devices, shards(): lax.all_gather(occupied, 'row', axis=0, tiled=True)  45.4 us
    all_gather x1, waiting for transfers between devices, shards(): lax.all_gather(virtual, 'row', axis=0, tiled=True)  37.6 us
    all_to_all x1, blocking collectives, shards(): lax.all_to_all(shaped, 'col', split_axis=2, concat_axis=4, tiled=True)  33.2 us
    all_to_all x1, waiting for transfers between devices, shards(): lax.all_to_all(lax.all_to_all(layered, 'row', split_axis=1, concat_axis=0...  25.2 us
    dot_general x1, matrix products, shards(): jnp.einsum('ml,pmn->pln', occ_all, moved, preferred_element_type=jnp.floa...  9.81 us
  transfers between devices with their start and end apart: 4, of which 3 were waited for; matrix products, arithmetic and copies ran while one was open for 8% of the time, Pallas kernels for 0%

profile of v1, /device:TPU:24, one launch (start us, length us, event | category | flops | bytes accessed | tf_op | source)
XLA Modules:
  0.0 429.1 jit_solution(17136864265026919637)
XLA Ops:
  6.5 0.0 all-gather.3.cloned.1.call-start
  6.5 0.7 all-gather.3.cloned.1.call-update
  7.3 0.0 all-gather.5.cloned.1.call-start
  7.3 0.7 all-gather.5.cloned.1.call-update
  8.0 0.9 fusion.14
  8.9 0.1 broadcast_bitcast_fusion
  9.0 2.8 copy_multiply_fusion
  11.7 0.8 copy.15
  12.6 82.0 %all_to_all.66 = bf16[32,256,128]{2,1,0:T(8,128)(2,1)} all-to-all(bf16[32,256,128]{2,1,0:T(8,128)(2,1)S(1)} %copy.15), channel_id=1, replica_groups=mesh['aux'=2,'row'=8,'col'=16] {'row'}, dimensions={0} | all-to-all | bytes 4194304 | tf_op jit(solution)/shard_map/all_to_all | solution.py:33
  94.5 4.5 %copy.16 = bf16[8,4,256,128]{2,0,3,1:T(8,128)(2,1)} copy(bf16[8,4,256,128]{3,2,1,0:T(8,128)(2,1)} %bitcast.62) | data formatting | bytes 4194304 | tf_op jit(solution)/shard_map/all_to_all | solution.py:33
  99.0 4.2 all_to_all.51
  103.2 45.4 %all-gather.3.cloned.1.call-done = bf16[2048,2048]{1,0:T(8,128)(2,1)} async-done(((bf16[256,2048]{1,0:T(8,128)(2,1)}), bf16[2048,2048]{1,0:T(8,128)(2,1)}) %all-gather.3.cloned.1.call-update) | async-done | bytes 8388624 | tf_op jit(solution)/shard_map/all_gather | solution.py:36
  148.6 9.8 %fusion.10 = bf16[4,2048,128]{1,2,0:T(8,128)(2,1)} fusion(bf16[4,2048,128]{1,2,0:T(8,128)(2,1)} %all_to_all.51, bf16[2048,2048]{1,0:T(8,128)(2,1)} %all-gather.3.cloned.1.call-done), kind=kOutput, calls=%fused_computation.6 | convolution fusion | flops 4296015872 | bytes 12582912 | tf_op jit(solution)/shard_map/ml,pmn->pln/dot_general | solution.py:39
  158.4 4.0 copy.17
  162.4 2.2 copy.18
  164.6 33.2 %all_to_all.67 = bf16[4,8,16,16,128]{4,3,1,0,2:T(8,128)(2,1)S(1)} all-to-all(bf16[4,8,16,16,128]{4,3,1,0,2:T(8,128)(2,1)S(1)} %copy.18), channel_id=1, replica_groups=mesh['aux'=2,'row'=8,'col'=16] {'col'}, dimensions={2} | all-to-all | bytes 4194304 | tf_op jit(solution)/shard_map/all_to_all | solution.py:44
  197.8 3.7 copy.19
  201.5 4.2 reshape.37
  205.7 37.6 %all-gather.5.cloned.1.call-done = bf16[2048,2048]{1,0:T(8,128)(2,1)} async-done(((bf16[256,2048]{1,0:T(8,128)(2,1)}), bf16[2048,2048]{1,0:T(8,128)(2,1)}) %all-gather.5.cloned.1.call-update) | async-done | bytes 8388624 | tf_op jit(solution)/shard_map/all_gather | solution.py:37
  243.3 8.5 %fusion.7 = bf16[4,128,2048]{2,1,0:T(8,128)(2,1)S(1)} fusion(bf16[4,128,2048]{2,1,0:T(8,128)(2,1)} %reshape.37, bf16[2048,2048]{1,0:T(8,128)(2,1)} %all-gather.5.cloned.1.call-done), kind=kOutput, calls=%fused_computation.5 | convolution fusion | flops 4296015872 | bytes 12582912 | tf_op jit(solution)/shard_map/pln,ns->pls/dot_general | solution.py:46
  251.9 0.6 copy.23
  252.5 0.6 copy.20
  253.1 55.3 %all_to_all.68 = bf16[4,8,1,16,16,128]{5,4,3,0,2,1:T(8,128)(2,1)S(1)} all-to-all(bf16[4,8,1,16,16,128]{5,4,3,0,2,1:T(8,128)(2,1)S(1)} %copy.20), channel_id=1, replica_groups=mesh['aux'=2,'row'=8,'col'=16] {'row'}, dimensions={1} | all-to-all | bytes 4194304 | tf_op jit(solution)/shard_map/all_to_all | solution.py:51
  308.4 1.8 copy.21
  310.2 7.2 %all-to-all-start.3 = ((bf16[32,1,1,16,16,128]{5,3,0,2,1,4:T(8,128)(2,1)}), bf16[32,1,1,16,16,128]{5,3,0,2,1,4:T(8,128)(2,1)}, u32[]{:S(2)}, u32[]{:S(2)}) async-start(bf16[32,1,1,16,16,128]{5,3,0,2,1,4:T(8,128)(2,1)} %copy.21), calls=%async_computation.3 | async-start | bytes 4194304 | tf_op jit(solution)/shard_map/all_to_all | solution.py:50
  317.4 0.0 collective-permute-start
  317.5 25.2 %all-to-all-done.3 = bf16[32,1,1,16,16,128]{5,3,0,2,1,4:T(8,128)(2,1)} async-done(((bf16[32,1,1,16,16,128]{5,3,0,2,1,4:T(8,128)(2,1)}), bf16[32,1,1,16,16,128]{5,3,0,2,1,4:T(8,128)(2,1)}, u32[]{:S(2)}, u32[]{:S(2)}) %all-to-all-start.3) | async-done | bytes 2097184 | tf_op jit(solution)/shard_map/all_to_all | solution.py:50
  342.7 2.1 copy.22
  344.8 0.7 convolution_bitcast_fusion.1
  345.5 0.0 collective-permute-done
  345.5 2.3 broadcast_select_fusion.1
  347.8 0.1 fusion.13
  347.9 73.8 %psum.7 = f32[2,32,64]{2,1,0:T(8,128)S(1)} all-reduce(f32[2,32,64]{2,1,0:T(8,128)S(1)} %fusion.13), channel_id=1, replica_groups=mesh['aux'=2,'row'=8,'col'=16] {'aux','row','col'}, use_global_device_ids=true, to_apply=%region_0.1 | all-reduce | flops 4096 | bytes 32768 | tf_op jit(solution)/shard_map/psum | solution.py:67
  421.7 0.6 multiply_bitcast_fusion
  (1 shorter events, 0.0 us)
Async XLA Ops:
  6.5 142.1 %all-gather.3.cloned.1.call-start = ((), (), s32[]{:S(2)}) async-start(), calls=%async_computation.4 | async-start | bytes 9437184 | tf_op jit(solution)/shard_map/all_gather | solution.py:36
  7.3 236.1 %all-gather.5.cloned.1.call-start = ((), (), s32[]{:S(2)}) async-start(), calls=%async_computation.5 | async-start | bytes 9437184 | tf_op jit(solution)/shard_map/all_gather | solution.py:37
  310.2 32.4 %all-to-all-start.3 = ((bf16[32,1,1,16,16,128]{5,3,0,2,1,4:T(8,128)(2,1)}), bf16[32,1,1,16,16,128]{5,3,0,2,1,4:T(8,128)(2,1)}, u32[]{:S(2)}, u32[]{:S(2)}) async-start(bf16[32,1,1,16,16,128]{5,3,0,2,1,4:T(8,128)(2,1)} %copy.21), calls=%async_computation.3 | async-start | bytes 4194304 | tf_op jit(solution)/shard_map/all_to_all | solution.py:50
  317.4 28.0 %collective-permute-start = (bf16[32,256,128]{2,0,1:T(8,128)(2,1)S(1)}, bf16[32,256,128]{2,0,1:T(8,128)(2,1)}, u32[]{:S(2)}, u32[]{:S(2)}) collective-permute-start(bf16[32,256,128]{2,0,1:T(8,128)(2,1)S(1)} %copy_multiply_fusion), channel_id=1, source_target_pairs={{0,128},{128,0},{1,129},{129,1},{2,130},{130,2},{3,131},{131,3},{4... | collective-permute-start | bytes 6291464 | tf_op jit(solution)/shard_map/ppermute | solution.py:13
Sparse Core Ops, SparseCore 0:
  9.1 139.4 all-gather.2
  150.4 92.8 all-gather.4

commit v2 on v1

--- a/solution.py
+++ b/solution.py
@@ -11,6 +11,18 @@
     mask = 2**apart
     pairs = [(source, source ^ mask) for source in range(lax.axis_size(axis))]
     return lax.ppermute(value, axis, pairs)
+
+
+def spread_density(local):
+    cols = lax.axis_size("col")
+    cores = lax.axis_size("aux")
+    width = local.shape[1] // cols
+    piece = lax.dynamic_slice_in_dim(local, lax.axis_index("col") * width, width, axis=1)
+    column = lax.all_gather(piece, "row", axis=0, tiled=True)
+    height = column.shape[0] // cores
+    part = lax.dynamic_slice_in_dim(column, lax.axis_index("aux") * height, height, axis=0)
+    rows = lax.all_gather(part, "col", axis=1, tiled=True)
+    return lax.all_gather(rows, "aux", axis=0, tiled=True)
 
 
 def shards(coulomb, occupied, virtual, tile_mask):
@@ -32,10 +44,7 @@
     screened = coulomb * local_mask[None]
     moved = lax.all_to_all(screened, "row", split_axis=0, concat_axis=1, tiled=True)
     pieces = moved.shape[0]
-    occ_all, virt_all = (
-        lax.all_gather(occupied, "row", axis=0, tiled=True),
-        lax.all_gather(virtual, "row", axis=0, tiled=True),
-    )
+    occ_all, virt_all = spread_density(occupied), spread_density(virtual)
     half = jnp.einsum("ml,pmn->pln", occ_all, moved, preferred_element_type=jnp.float32).astype(
         jnp.bfloat16
     )

time: 431 us -> 469 us (1.088)
  blocking collectives: 244 us -> 266 us
  waiting for transfers between devices: 110 us -> 122 us
    all_gather x0 -> x2, blocking collectives: none -> 54.7 us  [spread_density(): column = lax.all_gather(piece, 'row', axis=0, tiled=True)]
    all_to_all x1, blocking collectives: 82 us -> 57.2 us  [shards(): lax.all_to_all(screened, 'row', split_axis=0, concat_axis=1, tiled=True)]
    all_gather x2 -> x4, waiting for transfers between devices: 83 us -> 98.4 us  [the longest x2 98.4 us: spread_density(): rows = lax.all_gather(part, 'col', axis=1, tiled=True)]
    all_to_all x1, blocking collectives: 33.2 us -> 28.3 us  [shards(): lax.all_to_all(shaped, 'col', split_axis=2, concat_axis=4, tiled=True)]
  transfers between devices with their start and end apart: 4 -> 6, of which waited for: 3 -> 3; matrix products, arithmetic and copies ran while one was open for 8% -> 8% of each run, Pallas kernels for 0% -> 0%
where the time goes in v2:
time: 469 us; the launch traced here: 467 us
  blocking collectives  266 us (57%)
  waiting for transfers between devices  122 us (26%)
  local copies, waits for them, and re-layouts  32.5 us (7%)
  matrix products  21.3 us (5%)
  between operations  13.2 us (3%)
  starting transfers between devices  6.77 us (1%)
    all_gather x2, waiting for transfers between devices, spread_density(): rows = lax.all_gather(part, 'col', axis=1, tiled=True)  98.4 us
    psum x1, blocking collectives, shards(): total = lax.psum(placed, ('aux', 'row', 'col'))  73.4 us
    all_to_all x1, blocking collectives, shards(): lax.all_to_all(screened, 'row', split_axis=0, concat_axis=1, tiled=True)  57.2 us
    all_gather x2, blocking collectives, spread_density(): column = lax.all_gather(piece, 'row', axis=0, tiled=True)  54.7 us
    all_to_all x1, blocking collectives, shards(): lax.all_to_all(layered, 'row', split_axis=1, concat_axis=0, tiled=True)  52.4 us
    all_to_all x1, blocking collectives, shards(): lax.all_to_all(shaped, 'col', split_axis=2, concat_axis=4, tiled=True)  28.3 us
    all_to_all x1, waiting for transfers between devices, shards(): lax.all_to_all(lax.all_to_all(layered, 'row', split_axis=1, concat_axis=0...  24 us
    dot_general x1, matrix products, shards(): jnp.einsum('ml,pmn->pln', occ_all, moved, preferred_element_type=jnp.floa...  9.83 us
  transfers between devices with their start and end apart: 6, of which 3 were waited for; matrix products, arithmetic and copies ran while one was open for 8% of the time, Pallas kernels for 0%

profile of v2, /device:TPU:24, one launch (start us, length us, event | category | flops | bytes accessed | tf_op | source)
XLA Modules:
  0.0 466.7 jit_solution(12967270680666020211)
XLA Ops:
  6.5 0.0 copy-start
  6.5 0.0 all-gather.5.cloned.1.call-start
  6.5 1.2 copy-done
  7.8 29.3 %all_gather.18 = bf16[2048,128]{1,0:T(8,128)(2,1)S(1)} all-gather(bf16[256,128]{1,0:T(8,128)(2,1)S(1)} %constant_dynamic-slice_fusion.3), channel_id=1, replica_groups=mesh['aux'=2,'row'=8,'col'=16] {'row'}, dimensions={0}, use_global_device_ids=true | all-gather | bytes 589824 | tf_op jit(solution)/shard_map/all_gather | solution.py:21
  37.1 0.7 constant_dynamic-slice_fusion.2
  37.8 0.0 all-gather.5.cloned.1.call-update
  37.8 0.0 all-gather.9.cloned.1.call-start
  37.9 0.9 constant_dynamic-slice_fusion.1
  38.7 25.4 %all_gather.21 = bf16[2048,128]{1,0:T(8,128)(2,1)S(1)} all-gather(bf16[256,128]{1,0:T(8,128)(2,1)S(1)} %constant_dynamic-slice_fusion.1), channel_id=1, replica_groups=mesh['aux'=2,'row'=8,'col'=16] {'row'}, dimensions={0}, use_global_device_ids=true | all-gather | bytes 589824 | tf_op jit(solution)/shard_map/all_gather | solution.py:21
  64.1 0.7 constant_dynamic-slice_fusion
  64.9 0.0 all-gather.9.cloned.1.call-update
  64.9 0.0 all-gather.7.cloned.1.call-start
  64.9 34.0 %all-gather.5.cloned.1.call-done = bf16[1024,2048]{1,0:T(8,128)(2,1)} async-done(((bf16[1024,128]{1,0:T(8,128)(2,1)}), bf16[1024,2048]{1,0:T(8,128)(2,1)}) %all-gather.5.cloned.1.call-update) | async-done | bytes 4194320 | tf_op jit(solution)/shard_map/all_gather | solution.py:24
  98.9 0.0 all-gather.7.cloned.1.call-update
  99.0 0.0 all-gather.11.cloned.1.call-start
  99.0 64.4 %all-gather.9.cloned.1.call-done = bf16[1024,2048]{1,0:T(8,128)(2,1)} async-done(((bf16[1024,128]{1,0:T(8,128)(2,1)}), bf16[1024,2048]{1,0:T(8,128)(2,1)}) %all-gather.9.cloned.1.call-update) | async-done | bytes 4194320 | tf_op jit(solution)/shard_map/all_gather | solution.py:24
  163.4 0.0 all-gather.11.cloned.1.call-update
  163.4 0.9 fusion.14
  164.3 0.1 broadcast_bitcast_fusion
  164.4 2.8 copy_multiply_fusion
  167.2 0.8 copy.15
  168.0 57.2 %all_to_all.66 = bf16[32,256,128]{2,1,0:T(8,128)(2,1)} all-to-all(bf16[32,256,128]{2,1,0:T(8,128)(2,1)S(1)} %copy.15), channel_id=1, replica_groups=mesh['aux'=2,'row'=8,'col'=16] {'row'}, dimensions={0} | all-to-all | bytes 4194304 | tf_op jit(solution)/shard_map/all_to_all | solution.py:45
  225.2 4.5 copy.16
  229.8 4.2 all_to_all.51
  234.0 0.0 all-gather.7.cloned.1.call-done
  234.0 9.8 %fusion.10 = bf16[4,2048,128]{1,2,0:T(8,128)(2,1)} fusion(bf16[4,2048,128]{1,2,0:T(8,128)(2,1)} %all_to_all.51, bf16[2048,2048]{1,0:T(8,128)(2,1)} %all-gather.7.cloned.1.call-done), kind=kOutput, calls=%fused_computation.6 | convolution fusion | flops 4296015872 | bytes 12582912 | tf_op jit(solution)/shard_map/ml,pmn->pln/dot_general | solution.py:48
  243.8 3.9 copy.17
  247.7 2.2 copy.18
  249.9 28.3 %all_to_all.67 = bf16[4,8,16,16,128]{4,3,1,0,2:T(8,128)(2,1)S(1)} all-to-all(bf16[4,8,16,16,128]{4,3,1,0,2:T(8,128)(2,1)S(1)} %copy.18), channel_id=1, replica_groups=mesh['aux'=2,'row'=8,'col'=16] {'col'}, dimensions={2} | all-to-all | bytes 4194304 | tf_op jit(solution)/shard_map/all_to_all | solution.py:53
  278.2 3.8 copy.19
  282.0 4.2 reshape.37
  286.2 0.0 all-gather.11.cloned.1.call-done
  286.2 8.5 %fusion.7 = bf16[4,128,2048]{2,1,0:T(8,128)(2,1)S(1)} fusion(bf16[4,128,2048]{2,1,0:T(8,128)(2,1)} %reshape.37, bf16[2048,2048]{1,0:T(8,128)(2,1)} %all-gather.11.cloned.1.call-done), kind=kOutput, calls=%fused_computation.5 | convolution fusion | flops 4296015872 | bytes 12582912 | tf_op jit(solution)/shard_map/pln,ns->pls/dot_general | solution.py:55
  294.7 0.6 copy.23
  295.3 0.6 copy.20
  295.9 52.4 %all_to_all.68 = bf16[4,8,1,16,16,128]{5,4,3,0,2,1:T(8,128)(2,1)S(1)} all-to-all(bf16[4,8,1,16,16,128]{5,4,3,0,2,1:T(8,128)(2,1)S(1)} %copy.20), channel_id=1, replica_groups=mesh['aux'=2,'row'=8,'col'=16] {'row'}, dimensions={1} | all-to-all | bytes 4194304 | tf_op jit(solution)/shard_map/all_to_all | solution.py:60
  348.3 1.9 copy.21
  350.2 6.6 %all-to-all-start.3 = ((bf16[32,1,1,16,16,128]{5,3,0,2,1,4:T(8,128)(2,1)}), bf16[32,1,1,16,16,128]{5,3,0,2,1,4:T(8,128)(2,1)}, u32[]{:S(2)}, u32[]{:S(2)}) async-start(bf16[32,1,1,16,16,128]{5,3,0,2,1,4:T(8,128)(2,1)} %copy.21), calls=%async_computation.3 | async-start | bytes 4194304 | tf_op jit(solution)/shard_map/all_to_all | solution.py:59
  356.8 0.0 collective-permute-start
  356.8 24.0 %all-to-all-done.3 = bf16[32,1,1,16,16,128]{5,3,0,2,1,4:T(8,128)(2,1)} async-done(((bf16[32,1,1,16,16,128]{5,3,0,2,1,4:T(8,128)(2,1)}), bf16[32,1,1,16,16,128]{5,3,0,2,1,4:T(8,128)(2,1)}, u32[]{:S(2)}, u32[]{:S(2)}) %all-to-all-start.3) | async-done | bytes 2097184 | tf_op jit(solution)/shard_map/all_to_all | solution.py:59
  380.9 2.1 copy.22
  383.0 0.0 copy-start.1
  383.0 0.7 convolution_bitcast_fusion.1
  383.7 0.0 collective-permute-done
  383.7 2.3 broadcast_select_fusion.1
  386.0 0.1 fusion.13
  386.1 73.4 %psum.7 = f32[2,32,64]{2,1,0:T(8,128)S(1)} all-reduce(f32[2,32,64]{2,1,0:T(8,128)S(1)} %fusion.13), channel_id=1, replica_groups=mesh['aux'=2,'row'=8,'col'=16] {'aux','row','col'}, use_global_device_ids=true, to_apply=%region_0.1 | all-reduce | flops 4096 | bytes 32768 | tf_op jit(solution)/shard_map/psum | solution.py:76
  459.5 0.6 multiply_bitcast_fusion
  460.1 0.0 copy-done.1
  (2 shorter events, 0.0 us)
Async XLA Ops:
  6.5 1.2 copy-start
  6.5 92.4 %all-gather.5.cloned.1.call-start = ((), (), s32[]{:S(2)}) async-start(), calls=%async_computation.4 | async-start | bytes 4456448 | tf_op jit(solution)/shard_map/all_gather | solution.py:24
  37.8 125.6 %all-gather.9.cloned.1.call-start = ((), (), s32[]{:S(2)}) async-start(), calls=%async_computation.6 | async-start | bytes 4456448 | tf_op jit(solution)/shard_map/all_gather | solution.py:24
  64.9 169.1 %all-gather.7.cloned.1.call-start = ((), (), s32[]{:S(2)}) async-start(), calls=%async_computation.5 | async-start | bytes 12582912 | tf_op jit(solution)/shard_map/all_gather | solution.py:25
  99.0 187.2 %all-gather.11.cloned.1.call-start = ((), (), s32[]{:S(2)}) async-start(), calls=%async_computation.7 | async-start | bytes 12582912 | tf_op jit(solution)/shard_map/all_gather | solution.py:25
  350.2 30.7 %all-to-all-start.3 = ((bf16[32,1,1,16,16,128]{5,3,0,2,1,4:T(8,128)(2,1)}), bf16[32,1,1,16,16,128]{5,3,0,2,1,4:T(8,128)(2,1)}, u32[]{:S(2)}, u32[]{:S(2)}) async-start(bf16[32,1,1,16,16,128]{5,3,0,2,1,4:T(8,128)(2,1)} %copy.21), calls=%async_computation.3 | async-start | bytes 4194304 | tf_op jit(solution)/shard_map/all_to_all | solution.py:59
  356.8 26.9 %collective-permute-start = (bf16[32,256,128]{2,0,1:T(8,128)(2,1)S(1)}, bf16[32,256,128]{2,0,1:T(8,128)(2,1)}, u32[]{:S(2)}, u32[]{:S(2)}) collective-permute-start(bf16[32,256,128]{2,0,1:T(8,128)(2,1)S(1)} %copy_multiply_fusion), channel_id=1, source_target_pairs={{0,128},{128,0},{1,129},{129,1},{2,130},{130,2},{3,131},{131,3},{4... | collective-permute-start | bytes 6291464 | tf_op jit(solution)/shard_map/ppermute | solution.py:13
  383.0 77.1 %copy-start.1 = (bf16[256,2048]{1,0:T(8,128)(2,1)S(1)}, bf16[256,2048]{1,0:T(8,128)(2,1)}, u32[]{:S(2)}) copy-start(bf16[256,2048]{1,0:T(8,128)(2,1)} %param.5) | copy-start | bytes 3145732
Sparse Core Ops, SparseCore 0:
  37.9 60.9 all-gather.4
  101.3 62.0 all-gather.8
  165.2 24.9 all-gather.6
  191.9 26.4 all-gather.10

commit v3 on v0

--- a/solution.py
+++ b/solution.py
@@ -1,7 +1,11 @@
+import functools
+
 import jax
 import jax.numpy as jnp
 from jax import lax
 from jax.sharding import PartitionSpec as P
+from jax.experimental import pallas as pl
+from jax.experimental.pallas import tpu as pltpu
 
 NAO = 2048
 TILE = 128
@@ -11,6 +15,62 @@
     mask = 2**apart
     pairs = [(source, source ^ mask) for source in range(lax.axis_size(axis))]
     return lax.ppermute(value, axis, pairs)
+
+
+def partner_rounds():
+    rounds = []
+    for axis in ("col", "row"):
+        bit = 1
+        while bit < lax.axis_size(axis):
+            rounds.append((axis, bit))
+            bit *= 2
+    return rounds
+
+
+def doubling_kernel(rounds, x_ref, o_ref, recv, send_sem, recv_sem):
+    here = {name: lax.axis_index(name) for name in ("aux", "row", "col")}
+
+    def partner(axis, bit):
+        place = dict(here)
+        place[axis] = here[axis] ^ bit
+        return (place["aux"], place["row"], place["col"])
+
+    barrier = pltpu.get_barrier_semaphore()
+    for axis, bit in rounds:
+        pl.semaphore_signal(
+            barrier, inc=1, device_id=partner(axis, bit), device_id_type=pl.DeviceIdType.MESH
+        )
+    pl.semaphore_wait(barrier, len(rounds))
+
+    o_ref[...] = x_ref[...]
+    for step, (axis, bit) in enumerate(rounds):
+        copy = pltpu.make_async_remote_copy(
+            src_ref=o_ref,
+            dst_ref=recv.at[step],
+            send_sem=send_sem.at[step],
+            recv_sem=recv_sem.at[step],
+            device_id=partner(axis, bit),
+            device_id_type=pl.DeviceIdType.MESH,
+        )
+        copy.start()
+        copy.wait()
+        o_ref[...] = o_ref[...] + recv[step]
+
+
+def doubling_sum(partial):
+    rounds = partner_rounds()
+    return pl.pallas_call(
+        functools.partial(doubling_kernel, rounds),
+        out_shape=jax.ShapeDtypeStruct(partial.shape, partial.dtype),
+        in_specs=[pl.BlockSpec(memory_space=pltpu.VMEM)],
+        out_specs=pl.BlockSpec(memory_space=pltpu.VMEM),
+        scratch_shapes=[
+            pltpu.VMEM((len(rounds),) + partial.shape, partial.dtype),
+            pltpu.SemaphoreType.DMA((len(rounds),)),
+            pltpu.SemaphoreType.DMA((len(rounds),)),
+        ],
+        compiler_params=pltpu.CompilerParams(collective_id=0, has_side_effects=True),
+    )(partial)
 
 
 def shards(coulomb, occupied, virtual, tile_mask):
@@ -61,7 +121,7 @@
     first_half = jnp.where(aux_idx == 0, with_mine, with_theirs)
     second_half = jnp.where(aux_idx == 0, with_theirs, with_mine)
     partial_chi = jnp.concatenate([first_half, second_half], axis=1)
-    total_chi = lax.psum(partial_chi, ("row", "col"))
+    total_chi = doubling_sum(partial_chi)
     return total_chi / NAO
 
 

time: 1040 us -> 385 us (0.37); the launches traced: 1030 us -> 384 us
  blocking collectives: 843 us -> 170 us
  Pallas kernels: 0 us -> 27.8 us
    psum x1 -> x0, blocking collectives: 673 us -> none  [shards(): total_chi = lax.psum(partial_chi, ('row', 'col'))]
    pallas_call x0 -> x1, Pallas kernels: none -> 27.8 us  [doubling_sum(): pl.pallas_call(functools.partial(doubling_kernel, rounds), out_shape=jax....]
  transfers between devices with their start and end apart: 4 -> 4, of which waited for: 3 -> 3; matrix products, arithmetic and copies ran while one was open for 3% -> 9% of each run, Pallas kernels for 0% -> 0%
where the time goes in v3:
time: 385 us; the launch traced here: 384 us
  blocking collectives  170 us (44%)
  waiting for transfers between devices  110 us (29%)
  local copies, waits for them, and re-layouts  28.9 us (8%)
  Pallas kernels  27.8 us (7%)
  matrix products  21.3 us (6%)
  between operations  13.5 us (4%)
  starting transfers between devices  7.25 us (2%)
  other arithmetic  5.67 us (1%)
    all_to_all x1, blocking collectives, shards(): lax.all_to_all(screened, 'row', split_axis=0, concat_axis=1, tiled=True)  82 us
    all_to_all x1, blocking collectives, shards(): lax.all_to_all(layered, 'row', split_axis=1, concat_axis=0, tiled=True)  55.3 us
    all_gather x1, waiting for transfers between devices, shards(): lax.all_gather(occupied, 'row', axis=0, tiled=True)  45.4 us
    all_gather x1, waiting for transfers between devices, shards(): lax.all_gather(virtual, 'row', axis=0, tiled=True)  37.8 us
    all_to_all x1, blocking collectives, shards(): lax.all_to_all(shaped, 'col', split_axis=2, concat_axis=4, tiled=True)  32.9 us
    pallas_call x1, Pallas kernels, doubling_sum(): pl.pallas_call(functools.partial(doubling_kernel, rounds), out_shape=jax....  27.8 us
    all_to_all x1, waiting for transfers between devices, shards(): lax.all_to_all(lax.all_to_all(layered, 'row', split_axis=1, concat_axis=0...  25.2 us
    dot_general x1, matrix products, shards(): jnp.einsum('ml,pmn->pln', occ_all, moved, preferred_element_type=jnp.floa...  9.82 us
  transfers between devices with their start and end apart: 4, of which 3 were waited for; matrix products, arithmetic and copies ran while one was open for 9% of the time, Pallas kernels for 0%

profile of v3, /device:TPU:24, one launch (start us, length us, event | category | flops | bytes accessed | tf_op | source)
XLA Modules:
  0.0 384.5 jit_solution(3911334805613075366)
XLA Ops:
  6.5 0.0 all-gather.3.cloned.1.call-start
  6.5 0.7 all-gather.3.cloned.1.call-update
  7.3 0.0 all-gather.5.cloned.1.call-start
  7.3 0.7 all-gather.5.cloned.1.call-update
  8.0 0.9 fusion.13
  8.9 0.1 broadcast_bitcast_fusion
  9.0 2.8 copy_multiply_fusion
  11.7 0.8 copy.15
  12.6 82.0 %all_to_all.66 = bf16[32,256,128]{2,1,0:T(8,128)(2,1)} all-to-all(bf16[32,256,128]{2,1,0:T(8,128)(2,1)S(1)} %copy.15), channel_id=1, replica_groups=mesh['aux'=2,'row'=8,'col'=16] {'row'}, dimensions={0} | all-to-all | bytes 4194304 | tf_op jit(solution)/shard_map/all_to_all | solution.py:93
  94.5 4.5 %copy.16 = bf16[8,4,256,128]{2,0,3,1:T(8,128)(2,1)} copy(bf16[8,4,256,128]{3,2,1,0:T(8,128)(2,1)} %bitcast.56) | data formatting | bytes 4194304 | tf_op jit(solution)/shard_map/all_to_all | solution.py:93
  99.0 4.2 %all_to_all.51 = bf16[4,2048,128]{1,2,0:T(8,128)(2,1)} reshape(bf16[4,8,256,128]{2,1,3,0:T(8,128)(2,1)} %bitcast.57) | data formatting | bytes 4194304 | tf_op jit(solution)/shard_map/all_to_all | solution.py:93
  103.2 45.4 %all-gather.3.cloned.1.call-done = bf16[2048,2048]{1,0:T(8,128)(2,1)} async-done(((bf16[256,2048]{1,0:T(8,128)(2,1)}), bf16[2048,2048]{1,0:T(8,128)(2,1)}) %all-gather.3.cloned.1.call-update) | async-done | bytes 8388624 | tf_op jit(solution)/shard_map/all_gather | solution.py:96
  148.6 9.8 %fusion.10 = bf16[4,2048,128]{1,2,0:T(8,128)(2,1)} fusion(bf16[4,2048,128]{1,2,0:T(8,128)(2,1)} %all_to_all.51, bf16[2048,2048]{1,0:T(8,128)(2,1)} %all-gather.3.cloned.1.call-done), kind=kOutput, calls=%fused_computation.6 | convolution fusion | flops 4296015872 | bytes 12582912 | tf_op jit(solution)/shard_map/ml,pmn->pln/dot_general | solution.py:99
  158.4 4.0 %copy.17 = bf16[4,2048,128]{2,1,0:T(8,128)(2,1)} copy(bf16[4,2048,128]{1,2,0:T(8,128)(2,1)} %fusion.10) | data formatting | bytes 4194304 | tf_op jit(solution)/shard_map/convert_element_type | solution.py:99
  162.4 2.2 copy.18
  164.6 32.9 %all_to_all.67 = bf16[4,8,16,16,128]{4,3,1,0,2:T(8,128)(2,1)S(1)} all-to-all(bf16[4,8,16,16,128]{4,3,1,0,2:T(8,128)(2,1)S(1)} %copy.18), channel_id=1, replica_groups=mesh['aux'=2,'row'=8,'col'=16] {'col'}, dimensions={2} | all-to-all | bytes 4194304 | tf_op jit(solution)/shard_map/all_to_all | solution.py:104
  197.5 3.8 copy.19
  201.3 4.2 %reshape.35 = bf16[4,128,2048]{2,1,0:T(8,128)(2,1)} reshape(bf16[4,8,1,16,16,128]{5,4,3,1,0,2:T(8,128)(2,1)} %copy.19) | data formatting | bytes 4194304 | tf_op jit(solution)/shard_map/reshape | solution.py:105
  205.5 37.8 %all-gather.5.cloned.1.call-done = bf16[2048,2048]{1,0:T(8,128)(2,1)} async-done(((bf16[256,2048]{1,0:T(8,128)(2,1)}), bf16[2048,2048]{1,0:T(8,128)(2,1)}) %all-gather.5.cloned.1.call-update) | async-done | bytes 8388624 | tf_op jit(solution)/shard_map/all_gather | solution.py:97
  243.3 8.5 %fusion.7 = bf16[4,128,2048]{2,1,0:T(8,128)(2,1)S(1)} fusion(bf16[4,128,2048]{2,1,0:T(8,128)(2,1)} %reshape.35, bf16[2048,2048]{1,0:T(8,128)(2,1)} %all-gather.5.cloned.1.call-done), kind=kOutput, calls=%fused_computation.5 | convolution fusion | flops 4296015872 | bytes 12582912 | tf_op jit(solution)/shard_map/pln,ns->pls/dot_general | solution.py:106
  251.9 0.6 copy.23
  252.5 0.6 copy.20
  253.1 55.3 %all_to_all.68 = bf16[4,8,1,16,16,128]{5,4,3,0,2,1:T(8,128)(2,1)S(1)} all-to-all(bf16[4,8,1,16,16,128]{5,4,3,0,2,1:T(8,128)(2,1)S(1)} %copy.20), channel_id=1, replica_groups=mesh['aux'=2,'row'=8,'col'=16] {'row'}, dimensions={1} | all-to-all | bytes 4194304 | tf_op jit(solution)/shard_map/all_to_all | solution.py:111
  308.4 1.9 copy.21
  310.2 7.2 %all-to-all-start.3 = ((bf16[32,1,1,16,16,128]{5,3,0,2,1,4:T(8,128)(2,1)}), bf16[32,1,1,16,16,128]{5,3,0,2,1,4:T(8,128)(2,1)}, u32[]{:S(2)}, u32[]{:S(2)}) async-start(bf16[32,1,1,16,16,128]{5,3,0,2,1,4:T(8,128)(2,1)} %copy.21), calls=%async_computation.3 | async-start | bytes 4194304 | tf_op jit(solution)/shard_map/all_to_all | solution.py:110
  317.5 0.0 collective-permute-start
  317.5 25.2 %all-to-all-done.3 = bf16[32,1,1,16,16,128]{5,3,0,2,1,4:T(8,128)(2,1)} async-done(((bf16[32,1,1,16,16,128]{5,3,0,2,1,4:T(8,128)(2,1)}), bf16[32,1,1,16,16,128]{5,3,0,2,1,4:T(8,128)(2,1)}, u32[]{:S(2)}, u32[]{:S(2)}) %all-to-all-start.3) | async-done | bytes 2097184 | tf_op jit(solution)/shard_map/all_to_all | solution.py:110
  342.7 2.1 copy.22
  344.8 0.7 convolution_bitcast_fusion.1
  345.5 0.0 collective-permute-done
  345.5 2.3 broadcast_select_fusion.1
  347.8 0.7 pad_maximum_fusion.x_ref
  348.5 27.8 %shard_map.46 = f32[32,64]{1,0:T(8,128)} custom-call(f32[32,64]{1,0:T(8,128)} %pad_maximum_fusion.x_ref), custom_call_target="tpu_custom_call" | custom-call | tf_op jit(solution)/shard_map/pallas_call | solution.py:62
  376.3 1.3 broadcast_multiply_fusion
Async XLA Ops:
  6.5 142.1 %all-gather.3.cloned.1.call-start = ((), (), s32[]{:S(2)}) async-start(), calls=%async_computation.4 | async-start | bytes 9437184 | tf_op jit(solution)/shard_map/all_gather | solution.py:96
  7.3 236.1 %all-gather.5.cloned.1.call-start = ((), (), s32[]{:S(2)}) async-start(), calls=%async_computation.5 | async-start | bytes 9437184 | tf_op jit(solution)/shard_map/all_gather | solution.py:97
  310.2 32.4 %all-to-all-start.3 = ((bf16[32,1,1,16,16,128]{5,3,0,2,1,4:T(8,128)(2,1)}), bf16[32,1,1,16,16,128]{5,3,0,2,1,4:T(8,128)(2,1)}, u32[]{:S(2)}, u32[]{:S(2)}) async-start(bf16[32,1,1,16,16,128]{5,3,0,2,1,4:T(8,128)(2,1)} %copy.21), calls=%async_computation.3 | async-start | bytes 4194304 | tf_op jit(solution)/shard_map/all_to_all | solution.py:110
  317.5 28.0 %collective-permute-start = (bf16[32,256,128]{2,0,1:T(8,128)(2,1)S(1)}, bf16[32,256,128]{2,0,1:T(8,128)(2,1)}, u32[]{:S(2)}, u32[]{:S(2)}) collective-permute-start(bf16[32,256,128]{2,0,1:T(8,128)(2,1)S(1)} %copy_multiply_fusion), channel_id=1, source_target_pairs={{0,128},{128,0},{1,129},{129,1},{2,130},{130,2},{3,131},{131,3},{4... | collective-permute-start | bytes 6291464 | tf_op jit(solution)/shard_map/ppermute | solution.py:17
Sparse Core Ops, SparseCore 0:
  9.1 139.4 all-gather.2
  150.4 92.8 all-gather.4

commit v4 on v3

--- a/solution.py
+++ b/solution.py
@@ -73,6 +73,25 @@
     )(partial)
 
 
+def gather_half(local):
+    width = local.shape[1] // 2
+    part = lax.dynamic_slice_in_dim(local, lax.axis_index("aux") * width, width, axis=1)
+    return lax.all_gather(part, "row", axis=0, tiled=True)
+
+
+def join_halves(own, other, axis):
+    first = lax.axis_index("aux") == 0
+    return jnp.where(
+        first,
+        jnp.concatenate([own, other], axis=axis),
+        jnp.concatenate([other, own], axis=axis),
+    )
+
+
+def swapped_core(value):
+    return lax.ppermute(value, "aux", [(0, 1), (1, 0)])
+
+
 def shards(coulomb, occupied, virtual, tile_mask):
     rows = lax.axis_size("row")
     cols = lax.axis_size("col")
@@ -90,15 +109,15 @@
         jnp.bfloat16
     )
     screened = coulomb * local_mask[None]
+    occ_own, virt_own = gather_half(occupied), gather_half(virtual)
     moved = lax.all_to_all(screened, "row", split_axis=0, concat_axis=1, tiled=True)
+    occ_own, virt_own, moved = lax.optimization_barrier((occ_own, virt_own, moved))
     pieces = moved.shape[0]
-    occ_all, virt_all = (
-        lax.all_gather(occupied, "row", axis=0, tiled=True),
-        lax.all_gather(virtual, "row", axis=0, tiled=True),
-    )
-    half = jnp.einsum("ml,pmn->pln", occ_all, moved, preferred_element_type=jnp.float32).astype(
-        jnp.bfloat16
-    )
+    occ_other = swapped_core(occ_own)
+    virt_all = join_halves(virt_own, swapped_core(virt_own), axis=1)
+    half_own = jnp.einsum("ml,pmn->pln", occ_own, moved, preferred_element_type=jnp.float32)
+    half_other = jnp.einsum("ml,pmn->pln", occ_other, moved, preferred_element_type=jnp.float32)
+    half = join_halves(half_own.astype(jnp.bfloat16), half_other.astype(jnp.bfloat16), axis=1)
     jpart = mrow // cols
     shaped = half.reshape(pieces, rows, cols, jpart, ncol)
     spread = lax.all_to_all(shaped, "col", split_axis=2, concat_axis=4, tiled=True)

time: 385 us -> 371 us (0.964)
  waiting for transfers between devices: 110 us -> 87.1 us
  local copies, waits for them, and re-layouts: 28.9 us -> 32.9 us
    all_gather x2, waiting for transfers between devices: 83.2 us -> 60.6 us  [gather_half(): return lax.all_gather(part, 'row', axis=0, tiled=True)]
    select_n x0 -> x2, local copies, waits for them, and re-layouts: none -> 6.15 us  [join_halves(): jnp.where(first, jnp.concatenate([own, other], axis=axis), jnp.concatenat...]
    convert_element_type x1 -> x0, local copies, waits for them, and re-layouts: 3.97 us -> none  [shards(): jnp.einsum('ml,pmn->pln', occ_all, moved, preferred_element_type=jnp.floa...]
    dot_general x1 -> x2, matrix products: 9.82 us -> 9.83 us  [the longest x1 5.29 us: shards(): jnp.einsum('ml,pmn->pln', occ_own, moved, preferred_element_type=jnp.floa...]
  transfers between devices with their start and end apart: 4 -> 6, of which waited for: 3 -> 4; matrix products, arithmetic and copies ran while one was open for 9% -> 11% of each run, Pallas kernels for 0% -> 0%
where the time goes in v4:
time: 371 us; the launch traced here: 370 us
  blocking collectives  170 us (46%)
  waiting for transfers between devices  87.1 us (23%)
  local copies, waits for them, and re-layouts  32.9 us (9%)
  Pallas kernels  27.9 us (8%)
  matrix products  23.8 us (6%)
  between operations  13.5 us (4%)
  other arithmetic  7.81 us (2%)
  starting transfers between devices  6.78 us (2%)
    all_to_all x1, blocking collectives, shards(): lax.all_to_all(screened, 'row', split_axis=0, concat_axis=1, tiled=True)  82.4 us
    all_gather x2, waiting for transfers between devices, gather_half(): return lax.all_gather(part, 'row', axis=0, tiled=True)  60.6 us
    all_to_all x1, blocking collectives, shards(): lax.all_to_all(layered, 'row', split_axis=1, concat_axis=0, tiled=True)  54.5 us
    all_to_all x1, blocking collectives, shards(): lax.all_to_all(shaped, 'col', split_axis=2, concat_axis=4, tiled=True)  33.1 us
    pallas_call x1, Pallas kernels, doubling_sum(): pl.pallas_call(functools.partial(doubling_kernel, rounds), out_shape=jax....  27.9 us
    all_to_all x1, waiting for transfers between devices, shards(): lax.all_to_all(lax.all_to_all(layered, 'row', split_axis=1, concat_axis=0...  24.7 us
    dot_general x1, matrix products, shards(): jnp.einsum('pln,ns->pls', spread, virt_all, preferred_element_type=jnp.fl...  11 us
    all_to_all x2, local copies, waits for them, and re-layouts, shards(): lax.all_to_all(screened, 'row', split_axis=0, concat_axis=1, tiled=True)  8.73 us
  transfers between devices with their start and end apart: 6, of which 4 were waited for; matrix products, arithmetic and copies ran while one was open for 11% of the time, Pallas kernels for 0%

profile of v4, /device:TPU:24, one launch (start us, length us, event | category | flops | bytes accessed | tf_op | source)
XLA Modules:
  0.0 369.6 jit_solution(8817944757537477054)
XLA Ops:
  6.5 0.0 copy-start
  6.5 0.0 all-gather.3.cloned.1.call-start
  6.5 1.2 copy-done
  7.8 0.9 constant_dynamic-slice_fusion.1
  8.6 0.0 all-gather.3.cloned.1.call-update
  8.6 0.0 all-gather.5.cloned.1.call-start
  8.7 1.9 constant_dynamic-slice_fusion
  10.6 0.0 all-gather.5.cloned.1.call-update
  10.6 0.9 fusion.23
  11.5 0.1 broadcast_bitcast_fusion
  11.6 2.8 copy_multiply_fusion
  14.3 0.8 copy.15
  15.2 82.4 %all_to_all.66 = bf16[32,256,128]{2,1,0:T(8,128)(2,1)} all-to-all(bf16[32,256,128]{2,1,0:T(8,128)(2,1)S(1)} %copy.15), channel_id=1, replica_groups=mesh['aux'=2,'row'=8,'col'=16] {'row'}, dimensions={0} | all-to-all | bytes 4194304 | tf_op jit(solution)/shard_map/all_to_all | solution.py:113
  97.5 4.5 %copy.16 = bf16[4,8,256,128]{2,1,3,0:T(8,128)(2,1)} copy(bf16[4,8,256,128]{3,2,0,1:T(8,128)(2,1)} %bitcast.67) | data formatting | bytes 4194304 | tf_op jit(solution)/shard_map/all_to_all | solution.py:113
  102.1 4.2 %all_to_all.51 = bf16[4,2048,128]{1,2,0:T(8,128)(2,1)} reshape(bf16[4,8,256,128]{2,1,3,0:T(8,128)(2,1)} %copy.16) | data formatting | bytes 4194304 | tf_op jit(solution)/shard_map/all_to_all | solution.py:113
  106.3 5.4 %all-gather.3.cloned.1.call-done = bf16[2048,1024]{1,0:T(8,128)(2,1)} async-done(((bf16[256,1024]{1,0:T(8,128)(2,1)}), bf16[2048,1024]{1,0:T(8,128)(2,1)}) %all-gather.3.cloned.1.call-update) | async-done | bytes 4194320 | tf_op jit(solution)/shard_map/all_gather | solution.py:79
  111.6 55.2 %all-gather.5.cloned.1.call-done = bf16[2048,1024]{1,0:T(8,128)(2,1)} async-done(((bf16[256,1024]{1,0:T(8,128)(2,1)}), bf16[2048,1024]{1,0:T(8,128)(2,1)}) %all-gather.5.cloned.1.call-update) | async-done | bytes 4194320 | tf_op jit(solution)/shard_map/all_gather | solution.py:79
  166.9 0.0 collective-permute-start
  166.9 0.5 collective-permute-start.1
  167.4 0.0 copy-start.1
  167.4 5.3 %fusion.20 = bf16[4,1024,128]{1,2,0:T(8,128)(2,1)S(1)} fusion(bf16[4,2048,128]{1,2,0:T(8,128)(2,1)} %all_to_all.51, bf16[2048,1024]{1,0:T(8,128)(2,1)} %all-gather.3.cloned.1.call-done), kind=kOutput, calls=%fused_computation.14 | convolution fusion | flops 2148007936 | bytes 7340032 | tf_op jit(solution)/shard_map/ml,pmn->pln/dot_general | solution.py:118
  172.7 1.7 collective-permute-done
  174.4 0.0 copy-done.1
  174.4 4.5 %fusion.17 = bf16[4,1024,128]{1,2,0:T(8,128)(2,1)S(1)} fusion(bf16[4,2048,128]{1,2,0:T(8,128)(2,1)S(1)} %copy-done.1, bf16[2048,1024]{1,0:T(8,128)(2,1)} %collective-permute-done), kind=kOutput, calls=%fused_computation.13 | convolution fusion | flops 2148007936 | bytes 7340032 | tf_op jit(solution)/shard_map/ml,pmn->pln/dot_general | solution.py:119
  178.9 2.1 maximum_select_fusion.1
  181.1 4.0 %copy.17 = bf16[4,2048,128]{2,1,0:T(8,128)(2,1)} copy(bf16[4,2048,128]{1,2,0:T(8,128)(2,1)} %maximum_select_fusion.1) | data formatting | bytes 4194304 | tf_op jit(solution)/shard_map/jit(_where)/select_n | solution.py:84
  185.0 2.2 copy.18
  187.2 33.1 %all_to_all.67 = bf16[4,8,16,16,128]{4,3,1,0,2:T(8,128)(2,1)S(1)} all-to-all(bf16[4,8,16,16,128]{4,3,1,0,2:T(8,128)(2,1)S(1)} %copy.18), channel_id=1, replica_groups=mesh['aux'=2,'row'=8,'col'=16] {'col'}, dimensions={2} | all-to-all | bytes 4194304 | tf_op jit(solution)/shard_map/all_to_all | solution.py:123
  220.3 3.8 %copy.19 = bf16[4,8,1,16,16,128]{5,4,3,1,0,2:T(8,128)(2,1)} copy(bf16[4,8,1,16,16,128]{5,3,1,0,4,2:T(8,128)(2,1)S(1)} %bitcast.69) | data formatting | bytes 4194304 | tf_op jit(solution)/shard_map/all_to_all | solution.py:123
  224.1 4.1 %reshape.36 = bf16[4,128,2048]{2,1,0:T(8,128)(2,1)} reshape(bf16[4,8,1,16,16,128]{5,4,3,1,0,2:T(8,128)(2,1)} %copy.19) | data formatting | bytes 4194304 | tf_op jit(solution)/shard_map/reshape | solution.py:124
  228.2 0.0 collective-permute-done.1
  228.2 11.0 %fusion.8 = bf16[4,128,2048]{2,1,0:T(8,128)(2,1)S(1)} fusion(bf16[4,128,2048]{2,1,0:T(8,128)(2,1)} %reshape.36, bf16[2048,1024]{1,0:T(8,128)(2,1)} %collective-permute-done.1, bf16[2048,1024]{1,0:T(8,128)(2,1)} %all-gather.5.cloned.1.call-done, pred[]{:T(512)S(6)} %eq.2), kind=kOutput, calls=%fused_computation.8 | convolution fusion | flops 4333764608 | bytes 12582913 | tf_op jit(solution)/shard_map/pln,ns->pls/dot_general | solution.py:125
  239.2 0.6 copy.23
  239.8 0.6 copy.20
  240.4 54.5 %all_to_all.68 = bf16[4,8,1,16,16,128]{5,4,3,0,2,1:T(8,128)(2,1)S(1)} all-to-all(bf16[4,8,1,16,16,128]{5,4,3,0,2,1:T(8,128)(2,1)S(1)} %copy.20), channel_id=1, replica_groups=mesh['aux'=2,'row'=8,'col'=16] {'row'}, dimensions={1} | all-to-all | bytes 4194304 | tf_op jit(solution)/shard_map/all_to_all | solution.py:130
  294.9 1.9 copy.21
  296.8 6.2 %all-to-all-start.3 = ((bf16[32,1,1,16,16,128]{5,3,0,2,1,4:T(8,128)(2,1)}), bf16[32,1,1,16,16,128]{5,3,0,2,1,4:T(8,128)(2,1)}, u32[]{:S(2)}, u32[]{:S(2)}) async-start(bf16[32,1,1,16,16,128]{5,3,0,2,1,4:T(8,128)(2,1)} %copy.21), calls=%async_computation.3 | async-start | bytes 4194304 | tf_op jit(solution)/shard_map/all_to_all | solution.py:129
  303.0 0.0 collective-permute-start.2
  303.0 24.7 %all-to-all-done.3 = bf16[32,1,1,16,16,128]{5,3,0,2,1,4:T(8,128)(2,1)} async-done(((bf16[32,1,1,16,16,128]{5,3,0,2,1,4:T(8,128)(2,1)}), bf16[32,1,1,16,16,128]{5,3,0,2,1,4:T(8,128)(2,1)}, u32[]{:S(2)}, u32[]{:S(2)}) %all-to-all-start.3) | async-done | bytes 2097184 | tf_op jit(solution)/shard_map/all_to_all | solution.py:129
  327.7 2.1 copy.22
  329.9 0.7 convolution_bitcast_fusion.1
  330.5 0.0 collective-permute-done.2
  330.6 2.3 broadcast_select_fusion.1
  332.9 0.7 pad_maximum_fusion.x_ref
  333.6 27.9 %shard_map.46 = f32[32,64]{1,0:T(8,128)} custom-call(f32[32,64]{1,0:T(8,128)} %pad_maximum_fusion.x_ref), custom_call_target="tpu_custom_call" | custom-call | tf_op jit(solution)/shard_map/pallas_call | solution.py:62
  361.5 1.3 broadcast_multiply_fusion
Async XLA Ops:
  6.5 1.2 copy-start
  6.5 105.1 %all-gather.3.cloned.1.call-start = ((), (), s32[]{:S(2)}) async-start(), calls=%async_computation.4 | async-start | bytes 4718592 | tf_op jit(solution)/shard_map/all_gather | solution.py:79
  8.6 158.2 %all-gather.5.cloned.1.call-start = ((), (), s32[]{:S(2)}) async-start(), calls=%async_computation.5 | async-start | bytes 4718592 | tf_op jit(solution)/shard_map/all_gather | solution.py:79
  166.9 7.5 %collective-permute-start = (bf16[2048,1024]{1,0:T(8,128)(2,1)}, bf16[2048,1024]{1,0:T(8,128)(2,1)}, u32[]{:S(2)}, u32[]{:S(2)}) collective-permute-start(bf16[2048,1024]{1,0:T(8,128)(2,1)} %all-gather.3.cloned.1.call-done), channel_id=1, source_target_pairs={{0,128},{128,0},{1,129},{129,1},{2,130},{130,2},{3,131},{131,3},{4... | collective-permute-start | bytes 12582920 | tf_op jit(solution)/shard_map/ppermute | solution.py:92
  166.9 61.3 %collective-permute-start.1 = (bf16[2048,1024]{1,0:T(8,128)(2,1)}, bf16[2048,1024]{1,0:T(8,128)(2,1)}, u32[]{:S(2)}, u32[]{:S(2)}) collective-permute-start(bf16[2048,1024]{1,0:T(8,128)(2,1)} %all-gather.5.cloned.1.call-done), channel_id=1, source_target_pairs={{0,128},{128,0},{1,129},{129,1},{2,130},{130,2},{3,131},{131,3},{4... | collective-permute-start | bytes 12582920 | tf_op jit(solution)/shard_map/ppermute | solution.py:92
  167.4 7.0 %copy-start.1 = (bf16[4,2048,128]{1,2,0:T(8,128)(2,1)S(1)}, bf16[4,2048,128]{1,2,0:T(8,128)(2,1)}, u32[]{:S(2)}) copy-start(bf16[4,2048,128]{1,2,0:T(8,128)(2,1)} %all_to_all.51) | copy-start | bytes 6291460
  296.8 31.0 %all-to-all-start.3 = ((bf16[32,1,1,16,16,128]{5,3,0,2,1,4:T(8,128)(2,1)}), bf16[32,1,1,16,16,128]{5,3,0,2,1,4:T(8,128)(2,1)}, u32[]{:S(2)}, u32[]{:S(2)}) async-start(bf16[32,1,1,16,16,128]{5,3,0,2,1,4:T(8,128)(2,1)} %copy.21), calls=%async_computation.3 | async-start | bytes 4194304 | tf_op jit(solution)/shard_map/all_to_all | solution.py:129
  303.0 27.5 %collective-permute-start.2 = (bf16[32,256,128]{2,0,1:T(8,128)(2,1)S(1)}, bf16[32,256,128]{2,0,1:T(8,128)(2,1)}, u32[]{:S(2)}, u32[]{:S(2)}) collective-permute-start(bf16[32,256,128]{2,0,1:T(8,128)(2,1)S(1)} %copy_multiply_fusion), channel_id=1, source_target_pairs={{0,128},{128,0},{1,129},{129,1},{2,130},{130,2},{3,131},{131,3},{4... | collective-permute-start | bytes 6291464 | tf_op jit(solution)/shard_map/ppermute | solution.py:17
Sparse Core Ops, SparseCore 0:
  9.1 102.4 all-gather.2
  113.4 53.4 all-gather.4

commit v5 on v4

--- a/solution.py
+++ b/solution.py
@@ -111,10 +111,9 @@
     screened = coulomb * local_mask[None]
     occ_own, virt_own = gather_half(occupied), gather_half(virtual)
     moved = lax.all_to_all(screened, "row", split_axis=0, concat_axis=1, tiled=True)
-    occ_own, virt_own, moved = lax.optimization_barrier((occ_own, virt_own, moved))
+    occ_own, moved = lax.optimization_barrier((occ_own, moved))
     pieces = moved.shape[0]
     occ_other = swapped_core(occ_own)
-    virt_all = join_halves(virt_own, swapped_core(virt_own), axis=1)
     half_own = jnp.einsum("ml,pmn->pln", occ_own, moved, preferred_element_type=jnp.float32)
     half_other = jnp.einsum("ml,pmn->pln", occ_other, moved, preferred_element_type=jnp.float32)
     half = join_halves(half_own.astype(jnp.bfloat16), half_other.astype(jnp.bfloat16), axis=1)
@@ -122,6 +121,8 @@
     shaped = half.reshape(pieces, rows, cols, jpart, ncol)
     spread = lax.all_to_all(shaped, "col", split_axis=2, concat_axis=4, tiled=True)
     spread = spread.reshape(pieces, rows * jpart, nao)
+    virt_own, spread = lax.optimization_barrier((virt_own, spread))
+    virt_all = join_halves(virt_own, swapped_core(virt_own), axis=1)
     dressed = jnp.einsum(
         "pln,ns->pls", spread, virt_all, preferred_element_type=jnp.float32
     ).astype(jnp.bfloat16)

time: 371 us -> 325 us (0.88)
  blocking collectives: 170 us -> 88.9 us
  waiting for transfers between devices: 87.1 us -> 113 us
  starting transfers between devices: 6.78 us -> 15.4 us
    all_to_all x1 -> x0, blocking collectives: 82.4 us -> none  [shards(): lax.all_to_all(screened, 'row', split_axis=0, concat_axis=1, tiled=True)]
    all_to_all x0 -> x1, waiting for transfers between devices: none -> 72.2 us  [shards(): lax.all_to_all(screened, 'row', split_axis=0, concat_axis=1, tiled=True)]
    all_gather x2, waiting for transfers between devices: 60.6 us -> 5.59 us  [gather_half(): return lax.all_gather(part, 'row', axis=0, tiled=True)]
    all_to_all x0 -> x1, starting transfers between devices: none -> 8.47 us  [shards(): lax.all_to_all(screened, 'row', split_axis=0, concat_axis=1, tiled=True)]
    ppermute x2, waiting for transfers between devices: 1.69 us -> 9.52 us  [swapped_core(): return lax.ppermute(value, 'aux', [(0, 1), (1, 0)])]
  transfers between devices with their start and end apart: 6 -> 7, of which waited for: 4 -> 5; matrix products, arithmetic and copies ran while one was open for 11% -> 13% of each run, Pallas kernels for 0% -> 0%
where the time goes in v5:
time: 325 us; the launch traced here: 324 us
  waiting for transfers between devices  113 us (35%)
  blocking collectives  88.9 us (27%)
  local copies, waits for them, and re-layouts  34.2 us (11%)
  Pallas kernels  27.9 us (9%)
  matrix products  23.1 us (7%)
  starting transfers between devices  15.4 us (5%)
  between operations  13.5 us (4%)
  other arithmetic  7.82 us (2%)
    all_to_all x1, waiting for transfers between devices, shards(): lax.all_to_all(screened, 'row', split_axis=0, concat_axis=1, tiled=True)  72.2 us
    all_to_all x1, blocking collectives, shards(): lax.all_to_all(layered, 'row', split_axis=1, concat_axis=0, tiled=True)  55.9 us
    all_to_all x1, blocking collectives, shards(): lax.all_to_all(shaped, 'col', split_axis=2, concat_axis=4, tiled=True)  33 us
    pallas_call x1, Pallas kernels, doubling_sum(): pl.pallas_call(functools.partial(doubling_kernel, rounds), out_shape=jax....  27.9 us
    all_to_all x1, waiting for transfers between devices, shards(): lax.all_to_all(lax.all_to_all(layered, 'row', split_axis=1, concat_axis=0...  25.7 us
    dot_general x1, matrix products, shards(): jnp.einsum('pln,ns->pls', spread, virt_all, preferred_element_type=jnp.fl...  10.3 us
    ppermute x2, waiting for transfers between devices, swapped_core(): return lax.ppermute(value, 'aux', [(0, 1), (1, 0)])  9.52 us
    all_to_all x2, local copies, waits for them, and re-layouts, shards(): lax.all_to_all(screened, 'row', split_axis=0, concat_axis=1, tiled=True)  8.73 us
  transfers between devices with their start and end apart: 7, of which 5 were waited for; matrix products, arithmetic and copies ran while one was open for 13% of the time, Pallas kernels for 0%

profile of v5, /device:TPU:24, one launch (start us, length us, event | category | flops | bytes accessed | tf_op | source)
XLA Modules:
  0.0 323.8 jit_solution(6041889960570835012)
XLA Ops:
  6.5 0.0 copy-start
  6.5 0.0 all-gather.5.cloned.1.call-start
  6.5 1.2 copy-done
  7.8 0.9 constant_dynamic-slice_fusion
  8.6 0.0 all-gather.5.cloned.1.call-update
  8.7 0.9 fusion.23
  9.5 0.1 broadcast_bitcast_fusion
  9.6 2.8 copy_multiply_fusion
  12.4 2.1 copy.20
  14.5 8.5 %all-to-all-start = ((bf16[32,256,128]{2,1,0:T(8,128)(2,1)}), bf16[32,256,128]{2,1,0:T(8,128)(2,1)}, u32[]{:S(2)}, u32[]{:S(2)}) async-start(bf16[32,256,128]{2,1,0:T(8,128)(2,1)} %copy.20), calls=%async_computation | async-start | bytes 4194304 | tf_op jit(solution)/shard_map/all_to_all | solution.py:113
  23.0 0.0 all-gather.3.cloned.1.call-start
  23.0 1.9 constant_dynamic-slice_fusion.1
  24.9 0.0 all-gather.3.cloned.1.call-update
  25.0 72.2 %all-to-all-done = bf16[32,256,128]{2,1,0:T(8,128)(2,1)} async-done(((bf16[32,256,128]{2,1,0:T(8,128)(2,1)}), bf16[32,256,128]{2,1,0:T(8,128)(2,1)}, u32[]{:S(2)}, u32[]{:S(2)}) %all-to-all-start) | async-done | bytes 2097184 | tf_op jit(solution)/shard_map/all_to_all | solution.py:113
  97.1 4.5 %copy.21 = bf16[4,8,256,128]{2,1,3,0:T(8,128)(2,1)} copy(bf16[4,8,256,128]{3,2,0,1:T(8,128)(2,1)} %bitcast.2) | data formatting | bytes 4194304 | tf_op jit(solution)/shard_map/all_to_all | solution.py:113
  101.6 4.2 %all_to_all.51 = bf16[4,2048,128]{1,2,0:T(8,128)(2,1)} reshape(bf16[4,8,256,128]{2,1,3,0:T(8,128)(2,1)} %copy.21) | data formatting | bytes 4194304 | tf_op jit(solution)/shard_map/all_to_all | solution.py:113
  105.9 5.6 %all-gather.5.cloned.1.call-done = bf16[2048,1024]{1,0:T(8,128)(2,1)} async-done(((bf16[256,1024]{1,0:T(8,128)(2,1)}), bf16[2048,1024]{1,0:T(8,128)(2,1)}) %all-gather.5.cloned.1.call-update) | async-done | bytes 4194320 | tf_op jit(solution)/shard_map/all_gather | solution.py:79
  111.4 0.0 collective-permute-start
  111.5 0.0 copy-start.1
  111.5 5.3 %fusion.20 = bf16[4,1024,128]{1,2,0:T(8,128)(2,1)S(1)} fusion(bf16[4,2048,128]{1,2,0:T(8,128)(2,1)} %all_to_all.51, bf16[2048,1024]{1,0:T(8,128)(2,1)} %all-gather.5.cloned.1.call-done), kind=kOutput, calls=%fused_computation.14 | convolution fusion | flops 2148007936 | bytes 7340032 | tf_op jit(solution)/shard_map/ml,pmn->pln/dot_general | solution.py:117
  116.8 2.2 collective-permute-done
  119.0 0.0 copy-done.1
  119.0 4.5 %fusion.17 = bf16[4,1024,128]{1,2,0:T(8,128)(2,1)S(1)} fusion(bf16[4,2048,128]{1,2,0:T(8,128)(2,1)S(1)} %copy-done.1, bf16[2048,1024]{1,0:T(8,128)(2,1)} %collective-permute-done), kind=kOutput, calls=%fused_computation.13 | convolution fusion | flops 2148007936 | bytes 7340032 | tf_op jit(solution)/shard_map/ml,pmn->pln/dot_general | solution.py:118
  123.5 2.1 maximum_select_fusion.1
  125.6 4.0 %copy.22 = bf16[4,2048,128]{2,1,0:T(8,128)(2,1)} copy(bf16[4,2048,128]{1,2,0:T(8,128)(2,1)} %maximum_select_fusion.1) | data formatting | bytes 4194304 | tf_op jit(solution)/shard_map/jit(_where)/select_n | solution.py:84
  129.6 2.2 copy.23
  131.8 33.0 %all_to_all.66 = bf16[4,8,16,16,128]{4,3,1,0,2:T(8,128)(2,1)S(1)} all-to-all(bf16[4,8,16,16,128]{4,3,1,0,2:T(8,128)(2,1)S(1)} %copy.23), channel_id=1, replica_groups=mesh['aux'=2,'row'=8,'col'=16] {'col'}, dimensions={2} | all-to-all | bytes 4194304 | tf_op jit(solution)/shard_map/all_to_all | solution.py:122
  164.9 3.8 %copy.24 = bf16[4,8,1,16,16,128]{5,4,3,1,0,2:T(8,128)(2,1)} copy(bf16[4,8,1,16,16,128]{5,3,1,0,4,2:T(8,128)(2,1)S(1)} %bitcast.68) | data formatting | bytes 4194304 | tf_op jit(solution)/shard_map/all_to_all | solution.py:122
  168.6 4.2 %reshape.36 = bf16[4,128,2048]{2,1,0:T(8,128)(2,1)} reshape(bf16[4,8,1,16,16,128]{5,4,3,1,0,2:T(8,128)(2,1)} %copy.24) | data formatting | bytes 4194304 | tf_op jit(solution)/shard_map/reshape | solution.py:123
  172.8 0.0 all-gather.3.cloned.1.call-done
  172.8 0.0 collective-permute-start.1
  172.8 7.4 %collective-permute-done.1 = bf16[2048,1024]{1,0:T(8,128)(2,1)S(1)} collective-permute-done((bf16[2048,1024]{1,0:T(8,128)(2,1)}, bf16[2048,1024]{1,0:T(8,128)(2,1)S(1)}, u32[]{:S(2)}, u32[]{:S(2)}) %collective-permute-start.1) | collective-permute-done | bytes 4194336 | tf_op jit(solution)/shard_map/ppermute | solution.py:92
  180.2 10.3 %fusion.8 = bf16[4,128,2048]{2,1,0:T(8,128)(2,1)S(1)} fusion(bf16[4,128,2048]{2,1,0:T(8,128)(2,1)} %reshape.36, bf16[2048,1024]{1,0:T(8,128)(2,1)S(1)} %collective-permute-done.1, bf16[2048,1024]{1,0:T(8,128)(2,1)} %all-gather.3.cloned.1.call-done, pred[]{:T(512)S(6)} %eq.2), kind=kOutput, calls=%fused_computation.8 | convolution fusion | flops 4333764608 | bytes 12582913 | tf_op jit(solution)/shard_map/pln,ns->pls/dot_general | solution.py:126
  190.4 0.6 copy.28
  191.0 0.6 copy.25
  191.6 55.9 %all_to_all.67 = bf16[4,8,1,16,16,128]{5,4,3,0,2,1:T(8,128)(2,1)S(1)} all-to-all(bf16[4,8,1,16,16,128]{5,4,3,0,2,1:T(8,128)(2,1)S(1)} %copy.25), channel_id=1, replica_groups=mesh['aux'=2,'row'=8,'col'=16] {'row'}, dimensions={1} | all-to-all | bytes 4194304 | tf_op jit(solution)/shard_map/all_to_all | solution.py:131
  247.5 1.9 copy.26
  249.4 6.8 %all-to-all-start.3 = ((bf16[32,1,1,16,16,128]{5,3,0,2,1,4:T(8,128)(2,1)}), bf16[32,1,1,16,16,128]{5,3,0,2,1,4:T(8,128)(2,1)}, u32[]{:S(2)}, u32[]{:S(2)}) async-start(bf16[32,1,1,16,16,128]{5,3,0,2,1,4:T(8,128)(2,1)} %copy.26), calls=%async_computation.3 | async-start | bytes 4194304 | tf_op jit(solution)/shard_map/all_to_all | solution.py:130
  256.2 0.0 collective-permute-start.2
  256.2 25.7 %all-to-all-done.3 = bf16[32,1,1,16,16,128]{5,3,0,2,1,4:T(8,128)(2,1)} async-done(((bf16[32,1,1,16,16,128]{5,3,0,2,1,4:T(8,128)(2,1)}), bf16[32,1,1,16,16,128]{5,3,0,2,1,4:T(8,128)(2,1)}, u32[]{:S(2)}, u32[]{:S(2)}) %all-to-all-start.3) | async-done | bytes 2097184 | tf_op jit(solution)/shard_map/all_to_all | solution.py:130
  281.9 2.1 copy.27
  284.1 0.7 convolution_bitcast_fusion.1
  284.7 0.0 collective-permute-done.2
  284.7 2.3 broadcast_select_fusion.1
  287.0 0.7 pad_maximum_fusion.x_ref
  287.7 27.9 %shard_map.46 = f32[32,64]{1,0:T(8,128)} custom-call(f32[32,64]{1,0:T(8,128)} %pad_maximum_fusion.x_ref), custom_call_target="tpu_custom_call" | custom-call | tf_op jit(solution)/shard_map/pallas_call | solution.py:62
  315.6 1.3 broadcast_multiply_fusion
Async XLA Ops:
  6.5 1.2 copy-start
  6.5 104.9 %all-gather.5.cloned.1.call-start = ((), (), s32[]{:S(2)}) async-start(), calls=%async_computation.5 | async-start | bytes 4718592 | tf_op jit(solution)/shard_map/all_gather | solution.py:79
  14.5 82.6 %all-to-all-start = ((bf16[32,256,128]{2,1,0:T(8,128)(2,1)}), bf16[32,256,128]{2,1,0:T(8,128)(2,1)}, u32[]{:S(2)}, u32[]{:S(2)}) async-start(bf16[32,256,128]{2,1,0:T(8,128)(2,1)} %copy.20), calls=%async_computation | async-start | bytes 4194304 | tf_op jit(solution)/shard_map/all_to_all | solution.py:113
  23.0 149.8 %all-gather.3.cloned.1.call-start = ((), (), s32[]{:S(2)}) async-start(), calls=%async_computation.4 | async-start | bytes 4718592 | tf_op jit(solution)/shard_map/all_gather | solution.py:79
  111.4 7.5 %collective-permute-start = (bf16[2048,1024]{1,0:T(8,128)(2,1)}, bf16[2048,1024]{1,0:T(8,128)(2,1)}, u32[]{:S(2)}, u32[]{:S(2)}) collective-permute-start(bf16[2048,1024]{1,0:T(8,128)(2,1)} %all-gather.5.cloned.1.call-done), channel_id=1, source_target_pairs={{0,128},{128,0},{1,129},{129,1},{2,130},{130,2},{3,131},{131,3},{4... | collective-permute-start | bytes 12582920 | tf_op jit(solution)/shard_map/ppermute | solution.py:92
  111.5 7.5 %copy-start.1 = (bf16[4,2048,128]{1,2,0:T(8,128)(2,1)S(1)}, bf16[4,2048,128]{1,2,0:T(8,128)(2,1)}, u32[]{:S(2)}) copy-start(bf16[4,2048,128]{1,2,0:T(8,128)(2,1)} %all_to_all.51) | copy-start | bytes 6291460
  172.8 7.4 %collective-permute-start.1 = (bf16[2048,1024]{1,0:T(8,128)(2,1)}, bf16[2048,1024]{1,0:T(8,128)(2,1)S(1)}, u32[]{:S(2)}, u32[]{:S(2)}) collective-permute-start(bf16[2048,1024]{1,0:T(8,128)(2,1)} %all-gather.3.cloned.1.call-done), channel_id=1, source_target_pairs={{0,128},{128,0},{1,129},{129,1},{2,130},{130,2},{3,131},{131,3},{4... | collective-permute-start | bytes 12582920 | tf_op jit(solution)/shard_map/ppermute | solution.py:92
  249.4 32.6 %all-to-all-start.3 = ((bf16[32,1,1,16,16,128]{5,3,0,2,1,4:T(8,128)(2,1)}), bf16[32,1,1,16,16,128]{5,3,0,2,1,4:T(8,128)(2,1)}, u32[]{:S(2)}, u32[]{:S(2)}) async-start(bf16[32,1,1,16,16,128]{5,3,0,2,1,4:T(8,128)(2,1)} %copy.26), calls=%async_computation.3 | async-start | bytes 4194304 | tf_op jit(solution)/shard_map/all_to_all | solution.py:130
  256.2 28.5 %collective-permute-start.2 = (bf16[32,256,128]{2,0,1:T(8,128)(2,1)S(1)}, bf16[32,256,128]{2,0,1:T(8,128)(2,1)}, u32[]{:S(2)}, u32[]{:S(2)}) collective-permute-start(bf16[32,256,128]{2,0,1:T(8,128)(2,1)S(1)} %copy_multiply_fusion), channel_id=1, source_target_pairs={{0,128},{128,0},{1,129},{129,1},{2,130},{130,2},{3,131},{131,3},{4... | collective-permute-start | bytes 6291464 | tf_op jit(solution)/shard_map/ppermute | solution.py:17
Sparse Core Ops, SparseCore 0:
  9.1 102.2 all-gather.4
  113.2 53.5 all-gather.2

commit v6 on v5

--- a/solution.py
+++ b/solution.py
@@ -92,6 +92,78 @@
     return lax.ppermute(value, "aux", [(0, 1), (1, 0)])
 
 
+def exchange_kernel(x_ref, o_ref, send_sem, recv_sem, local_sem):
+    here = {name: lax.axis_index(name) for name in ("aux", "row", "col")}
+    me, n = here["row"], lax.axis_size("row")
+    depth = x_ref.shape[0] // n
+    height = x_ref.shape[1]
+
+    def device(index):
+        return (here["aux"], index, here["col"])
+
+    def piece(index):
+        return x_ref.at[pl.ds(index * depth, depth)]
+
+    def slot(index):
+        return o_ref.at[:, pl.ds(index * height, height)]
+
+    barrier = pltpu.get_barrier_semaphore()
+    for step in range(1, n):
+        pl.semaphore_signal(
+            barrier, inc=1, device_id=device(lax.rem(me + step, n)),
+            device_id_type=pl.DeviceIdType.MESH,
+        )
+    pl.semaphore_wait(barrier, n - 1)
+
+    local = pltpu.make_async_copy(piece(me), slot(me), local_sem)
+    local.start()
+    sends = []
+    for step in range(1, n):
+        dest = lax.rem(me + step, n)
+        copy = pltpu.make_async_remote_copy(
+            src_ref=piece(dest),
+            dst_ref=slot(me),
+            send_sem=send_sem.at[step],
+            recv_sem=recv_sem.at[step],
+            device_id=device(dest),
+            device_id_type=pl.DeviceIdType.MESH,
+        )
+        copy.start()
+        sends.append(copy)
+    for step in range(1, n):
+        source = lax.rem(me + n - step, n)
+        incoming = pltpu.make_async_remote_copy(
+            src_ref=piece(me),
+            dst_ref=slot(source),
+            send_sem=send_sem.at[step],
+            recv_sem=recv_sem.at[step],
+            device_id=device(source),
+            device_id_type=pl.DeviceIdType.MESH,
+        )
+        incoming.wait_recv()
+        sends[step - 1].wait_send()
+    local.wait()
+
+
+def exchange_rows(x):
+    n = lax.axis_size("row")
+    shape = (x.shape[0] // n, x.shape[1] * n) + x.shape[2:]
+    nbytes = x.size * x.dtype.itemsize
+    return pl.pallas_call(
+        exchange_kernel,
+        out_shape=jax.ShapeDtypeStruct(shape, x.dtype),
+        in_specs=[pl.BlockSpec(memory_space=pl.ANY)],
+        out_specs=pl.BlockSpec(memory_space=pl.ANY),
+        scratch_shapes=[
+            pltpu.SemaphoreType.DMA((n,)),
+            pltpu.SemaphoreType.DMA((n,)),
+            pltpu.SemaphoreType.DMA(()),
+        ],
+        compiler_params=pltpu.CompilerParams(collective_id=1, has_side_effects=True),
+        cost_estimate=pl.CostEstimate(flops=0, bytes_accessed=2 * nbytes, transcendentals=0),
+    )(x)
+
+
 def shards(coulomb, occupied, virtual, tile_mask):
     rows = lax.axis_size("row")
     cols = lax.axis_size("col")
@@ -110,7 +182,7 @@
     )
     screened = coulomb * local_mask[None]
     occ_own, virt_own = gather_half(occupied), gather_half(virtual)
-    moved = lax.all_to_all(screened, "row", split_axis=0, concat_axis=1, tiled=True)
+    moved = exchange_rows(screened)
     occ_own, moved = lax.optimization_barrier((occ_own, moved))
     pieces = moved.shape[0]
     occ_other = swapped_core(occ_own)

time: 325 us -> 316 us (0.972)
  Pallas kernels: 27.9 us -> 104 us
  waiting for transfers between devices: 113 us -> 53.1 us
  local copies, waits for them, and re-layouts: 34.2 us -> 18.7 us
  starting transfers between devices: 15.4 us -> 7.36 us
    pallas_call x0 -> x1, Pallas kernels: none -> 76 us  [exchange_rows(): pl.pallas_call(exchange_kernel, out_shape=jax.ShapeDtypeStruct(shape, x.d...]
    all_to_all x1 -> x0, waiting for transfers between devices: 72.2 us -> none  [shards(): lax.all_to_all(screened, 'row', split_axis=0, concat_axis=1, tiled=True)]
    all_gather x2, waiting for transfers between devices: 5.59 us -> 18.1 us  [gather_half(): return lax.all_gather(part, 'row', axis=0, tiled=True)]
    all_to_all x2 -> x0, local copies, waits for them, and re-layouts: 8.73 us -> none  [shards(): lax.all_to_all(screened, 'row', split_axis=0, concat_axis=1, tiled=True)]
    all_to_all x1 -> x0, starting transfers between devices: 8.47 us -> none  [shards(): lax.all_to_all(screened, 'row', split_axis=0, concat_axis=1, tiled=True)]
  transfers between devices with their start and end apart: 7 -> 6, of which waited for: 5 -> 5; matrix products, arithmetic and copies ran while one was open for 13% -> 9% of each run, Pallas kernels for 0% -> 24%
where the time goes in v6:
time: 316 us; the launch traced here: 315 us
  Pallas kernels  104 us (33%)
  blocking collectives  88.8 us (28%)
  waiting for transfers between devices  53.1 us (17%)
  matrix products  24.8 us (8%)
  local copies, waits for them, and re-layouts  18.7 us (6%)
  between operations  13.5 us (4%)
  starting transfers between devices  7.36 us (2%)
  other arithmetic  5.26 us (2%)
    pallas_call x1, Pallas kernels, exchange_rows(): pl.pallas_call(exchange_kernel, out_shape=jax.ShapeDtypeStruct(shape, x.d...  76 us
    all_to_all x1, blocking collectives, shards(): lax.all_to_all(layered, 'row', split_axis=1, concat_axis=0, tiled=True)  55.8 us
    all_to_all x1, blocking collectives, shards(): lax.all_to_all(shaped, 'col', split_axis=2, concat_axis=4, tiled=True)  33 us
    pallas_call x1, Pallas kernels, doubling_sum(): pl.pallas_call(functools.partial(doubling_kernel, rounds), out_shape=jax....  27.8 us
    all_to_all x1, waiting for transfers between devices, shards(): lax.all_to_all(lax.all_to_all(layered, 'row', split_axis=1, concat_axis=0...  25.5 us
    all_gather x2, waiting for transfers between devices, gather_half(): return lax.all_gather(part, 'row', axis=0, tiled=True)  18.1 us
    dot_general x1, matrix products, shards(): jnp.einsum('pln,ns->pls', spread, virt_all, preferred_element_type=jnp.fl...  10.3 us
    ppermute x2, waiting for transfers between devices, swapped_core(): return lax.ppermute(value, 'aux', [(0, 1), (1, 0)])  9.48 us
  transfers between devices with their start and end apart: 6, of which 5 were waited for; matrix products, arithmetic and copies ran while one was open for 9% of the time, Pallas kernels for 24%

profile of v6, /device:TPU:24, one launch (start us, length us, event | category | flops | bytes accessed | tf_op | source)
XLA Modules:
  0.0 315.4 jit_solution(7326071632307918790)
XLA Ops:
  6.5 0.0 copy-start
  6.5 0.0 copy-start.2
  6.5 0.0 all-gather.5.cloned.1.call-start
  6.5 1.2 copy-done
  7.8 0.9 constant_dynamic-slice_fusion
  8.6 0.0 all-gather.5.cloned.1.call-update
  8.7 0.0 all-gather.3.cloned.1.call-start
  8.7 1.9 constant_dynamic-slice_fusion.1
  10.6 0.0 all-gather.3.cloned.1.call-update
  10.6 0.9 fusion.33
  11.5 0.1 broadcast_bitcast_fusion
  11.6 0.0 copy-done.2
  11.6 1.6 broadcast_multiply_fusion.x_ref
  13.2 76.0 %shard_map.46 = bf16[4,2048,128]{2,1,0:T(8,128)(2,1)} custom-call(bf16[32,256,128]{2,1,0:T(8,128)(2,1)} %broadcast_multiply_fusion.x_ref), custom_call_target="tpu_custom_call" | custom-call | bytes 4194304 | tf_op jit(solution)/shard_map/pallas_call | solution.py:152
  89.2 17.7 %all-gather.5.cloned.1.call-done = bf16[2048,1024]{1,0:T(8,128)(2,1)} async-done(((bf16[256,1024]{1,0:T(8,128)(2,1)}), bf16[2048,1024]{1,0:T(8,128)(2,1)}) %all-gather.5.cloned.1.call-update) | async-done | bytes 4194320 | tf_op jit(solution)/shard_map/all_gather | solution.py:79
  106.9 0.1 collective-permute-start
  106.9 0.0 copy-start.3
  106.9 5.3 %fusion.24 = bf16[4,1024,128]{1,2,0:T(8,128)(2,1)S(1)} fusion(bf16[4,2048,128]{2,1,0:T(8,128)(2,1)} %shard_map.46, bf16[2048,1024]{1,0:T(8,128)(2,1)} %all-gather.5.cloned.1.call-done), kind=kOutput, calls=%fused_computation.17 | convolution fusion | flops 2148007936 | bytes 7340032 | tf_op jit(solution)/shard_map/ml,pmn->pln/dot_general | solution.py:189
  112.3 2.1 collective-permute-done
  114.4 0.0 copy-done.3
  114.4 4.6 %fusion.21 = bf16[4,1024,128]{1,2,0:T(8,128)(2,1)S(1)} fusion(bf16[4,2048,128]{2,1,0:T(8,128)(2,1)S(1)} %copy-done.3, bf16[2048,1024]{1,0:T(8,128)(2,1)} %collective-permute-done), kind=kOutput, calls=%fused_computation.16 | convolution fusion | flops 2148007936 | bytes 7340032 | tf_op jit(solution)/shard_map/ml,pmn->pln/dot_general | solution.py:190
  119.0 0.8 maximum_select_fusion.1
  119.8 2.5 copy.27
  122.3 2.2 copy.28
  124.5 33.0 %all_to_all.48 = bf16[4,8,16,16,128]{4,3,1,0,2:T(8,128)(2,1)S(1)} all-to-all(bf16[4,8,16,16,128]{4,3,1,0,2:T(8,128)(2,1)S(1)} %copy.28), channel_id=1, replica_groups=mesh['aux'=2,'row'=8,'col'=16] {'col'}, dimensions={2} | all-to-all | bytes 4194304 | tf_op jit(solution)/shard_map/all_to_all | solution.py:194
  157.5 2.4 copy.29
  159.9 2.3 reshape.36
  162.2 0.4 all-gather.3.cloned.1.call-done
  162.6 0.0 collective-permute-start.1
  162.6 7.4 %collective-permute-done.1 = bf16[2048,1024]{1,0:T(8,128)(2,1)S(1)} collective-permute-done((bf16[2048,1024]{1,0:T(8,128)(2,1)}, bf16[2048,1024]{1,0:T(8,128)(2,1)S(1)}, u32[]{:S(2)}, u32[]{:S(2)}) %collective-permute-start.1) | collective-permute-done | bytes 4194336 | tf_op jit(solution)/shard_map/ppermute | solution.py:92
  170.0 10.3 %fusion.8 = bf16[4,128,2048]{2,1,0:T(8,128)(2,1)S(1)} fusion(bf16[4,128,2048]{2,1,0:T(8,128)(2,1)} %reshape.36, bf16[2048,1024]{1,0:T(8,128)(2,1)S(1)} %collective-permute-done.1, bf16[2048,1024]{1,0:T(8,128)(2,1)} %all-gather.3.cloned.1.call-done, pred[]{:T(512)S(6)} %eq.2), kind=kOutput, calls=%fused_computation.8 | convolution fusion | flops 4333764608 | bytes 12582913 | tf_op jit(solution)/shard_map/pln,ns->pls/dot_general | solution.py:198
  180.2 0.6 copy.37
  180.9 0.6 copy.30
  181.5 55.8 %all_to_all.49 = bf16[4,8,1,16,16,128]{5,4,3,0,2,1:T(8,128)(2,1)S(1)} all-to-all(bf16[4,8,1,16,16,128]{5,4,3,0,2,1:T(8,128)(2,1)S(1)} %copy.30), channel_id=1, replica_groups=mesh['aux'=2,'row'=8,'col'=16] {'row'}, dimensions={1} | all-to-all | bytes 4194304 | tf_op jit(solution)/shard_map/all_to_all | solution.py:203
  237.3 1.9 copy.31
  239.1 0.0 copy-start.1
  239.1 7.2 %all-to-all-start.2 = ((bf16[32,1,1,16,16,128]{5,3,0,2,1,4:T(8,128)(2,1)}), bf16[32,1,1,16,16,128]{5,3,0,2,1,4:T(8,128)(2,1)}, u32[]{:S(2)}, u32[]{:S(2)}) async-start(bf16[32,1,1,16,16,128]{5,3,0,2,1,4:T(8,128)(2,1)} %copy.31), calls=%async_computation.2 | async-start | bytes 4194304 | tf_op jit(solution)/shard_map/all_to_all | solution.py:202
  246.3 0.0 copy-done.1
  246.3 0.1 collective-permute-start.2
  246.4 25.5 %all-to-all-done.2 = bf16[32,1,1,16,16,128]{5,3,0,2,1,4:T(8,128)(2,1)} async-done(((bf16[32,1,1,16,16,128]{5,3,0,2,1,4:T(8,128)(2,1)}), bf16[32,1,1,16,16,128]{5,3,0,2,1,4:T(8,128)(2,1)}, u32[]{:S(2)}, u32[]{:S(2)}) %all-to-all-start.2) | async-done | bytes 2097184 | tf_op jit(solution)/shard_map/all_to_all | solution.py:202
  271.9 2.1 copy.32
  274.0 1.5 fusion.27
  275.6 0.0 collective-permute-done.2
  275.6 3.2 %broadcast_select_fusion.1 = (f32[32,32]{1,0:T(8,128)S(1)}, f32[32,32]{1,0:T(8,128)S(1)}) fusion(f32[32,32]{1,0:T(8,128)S(1)} %fusion.27, pred[]{:T(512)S(6)} %eq.2, bf16[32,256,128]{2,0,1:T(8,128)(2,1)S(1)} %bitcast.61, bf16[32,256,128]{2,1,0:T(8,128)(2,1)} %collective-permute-done.2), kind=kOutput, calls=%fused_computation.24 | convolution fusion | flops 67110912 | bytes 4206593 | tf_op jit(solution)/shard_map/pls,qls->pq/dot_general | solution.py:212
  278.8 0.7 pad_maximum_fusion.x_ref
  279.5 27.8 %shard_map.47 = f32[32,64]{1,0:T(8,128)} custom-call(f32[32,64]{1,0:T(8,128)} %pad_maximum_fusion.x_ref), custom_call_target="tpu_custom_call" | custom-call | tf_op jit(solution)/shard_map/pallas_call | solution.py:62
  307.3 1.3 broadcast_multiply_fusion.1
Async XLA Ops:
  6.5 1.2 copy-start
  6.5 5.0 %copy-start.2 = (bf16[32,256,128]{2,1,0:T(8,128)(2,1)S(1)}, bf16[32,256,128]{2,1,0:T(8,128)(2,1)}, u32[]{:S(2)}) copy-start(bf16[32,256,128]{2,1,0:T(8,128)(2,1)} %param.4) | copy-start | bytes 6291460
  6.5 100.3 %all-gather.5.cloned.1.call-start = ((), (), s32[]{:S(2)}) async-start(), calls=%async_computation.4 | async-start | bytes 4718592 | tf_op jit(solution)/shard_map/all_gather | solution.py:79
  8.7 153.9 %all-gather.3.cloned.1.call-start = ((), (), s32[]{:S(2)}) async-start(), calls=%async_computation.3 | async-start | bytes 4718592 | tf_op jit(solution)/shard_map/all_gather | solution.py:79
  106.9 7.5 %collective-permute-start = (bf16[2048,1024]{1,0:T(8,128)(2,1)}, bf16[2048,1024]{1,0:T(8,128)(2,1)}, u32[]{:S(2)}, u32[]{:S(2)}) collective-permute-start(bf16[2048,1024]{1,0:T(8,128)(2,1)} %all-gather.5.cloned.1.call-done), channel_id=1, source_target_pairs={{0,128},{128,0},{1,129},{129,1},{2,130},{130,2},{3,131},{131,3},{4... | collective-permute-start | bytes 12582920 | tf_op jit(solution)/shard_map/ppermute | solution.py:92
  106.9 7.4 %copy-start.3 = (bf16[4,2048,128]{2,1,0:T(8,128)(2,1)S(1)}, bf16[4,2048,128]{2,1,0:T(8,128)(2,1)}, u32[]{:S(2)}) copy-start(bf16[4,2048,128]{2,1,0:T(8,128)(2,1)} %shard_map.46) | copy-start | bytes 6291460
  162.6 7.4 %collective-permute-start.1 = (bf16[2048,1024]{1,0:T(8,128)(2,1)}, bf16[2048,1024]{1,0:T(8,128)(2,1)S(1)}, u32[]{:S(2)}, u32[]{:S(2)}) collective-permute-start(bf16[2048,1024]{1,0:T(8,128)(2,1)} %all-gather.3.cloned.1.call-done), channel_id=1, source_target_pairs={{0,128},{128,0},{1,129},{129,1},{2,130},{130,2},{3,131},{131,3},{4... | collective-permute-start | bytes 12582920 | tf_op jit(solution)/shard_map/ppermute | solution.py:92
  239.1 7.2 %copy-start.1 = (bf16[32,256,128]{2,1,0:T(8,128)(2,1)S(1)}, bf16[32,256,128]{2,1,0:T(8,128)(2,1)}, u32[]{:S(2)}) copy-start(bf16[32,256,128]{2,1,0:T(8,128)(2,1)} %broadcast_multiply_fusion.x_ref) | copy-start | bytes 6291460
  239.1 32.8 %all-to-all-start.2 = ((bf16[32,1,1,16,16,128]{5,3,0,2,1,4:T(8,128)(2,1)}), bf16[32,1,1,16,16,128]{5,3,0,2,1,4:T(8,128)(2,1)}, u32[]{:S(2)}, u32[]{:S(2)}) async-start(bf16[32,1,1,16,16,128]{5,3,0,2,1,4:T(8,128)(2,1)} %copy.31), calls=%async_computation.2 | async-start | bytes 4194304 | tf_op jit(solution)/shard_map/all_to_all | solution.py:202
  246.3 29.3 %collective-permute-start.2 = (bf16[32,256,128]{2,1,0:T(8,128)(2,1)S(1)}, bf16[32,256,128]{2,1,0:T(8,128)(2,1)}, u32[]{:S(2)}, u32[]{:S(2)}) collective-permute-start(bf16[32,256,128]{2,1,0:T(8,128)(2,1)S(1)} %copy-done.1), channel_id=1, source_target_pairs={{0,128},{128,0},{1,129},{129,1},{2,130},{130,2},{3,131},{131,3},{4... | collective-permute-start | bytes 6291464 | tf_op jit(solution)/shard_map/ppermute | solution.py:17
Sparse Core Ops, SparseCore 0:
  9.1 97.6 all-gather.4
  108.7 53.9 all-gather.2

commit v7 on v6

--- a/solution.py
+++ b/solution.py
@@ -92,20 +92,26 @@
     return lax.ppermute(value, "aux", [(0, 1), (1, 0)])
 
 
-def exchange_kernel(x_ref, o_ref, send_sem, recv_sem, local_sem):
+def sliced(ref, axis, start, size):
+    index = [slice(None)] * len(ref.shape)
+    index[axis] = pl.ds(start, size)
+    return ref.at[tuple(index)]
+
+
+def exchange_kernel(split_axis, concat_axis, x_ref, o_ref, send_sem, recv_sem, local_sem):
     here = {name: lax.axis_index(name) for name in ("aux", "row", "col")}
     me, n = here["row"], lax.axis_size("row")
-    depth = x_ref.shape[0] // n
-    height = x_ref.shape[1]
+    depth = x_ref.shape[split_axis] // n
+    height = o_ref.shape[concat_axis] // n
 
     def device(index):
         return (here["aux"], index, here["col"])
 
     def piece(index):
-        return x_ref.at[pl.ds(index * depth, depth)]
+        return sliced(x_ref, split_axis, index * depth, depth)
 
     def slot(index):
-        return o_ref.at[:, pl.ds(index * height, height)]
+        return sliced(o_ref, concat_axis, index * height, height)
 
     barrier = pltpu.get_barrier_semaphore()
     for step in range(1, n):
@@ -145,13 +151,15 @@
     local.wait()
 
 
-def exchange_rows(x):
+def exchange_rows(x, split_axis, concat_axis, collective_id):
     n = lax.axis_size("row")
-    shape = (x.shape[0] // n, x.shape[1] * n) + x.shape[2:]
+    shape = list(x.shape)
+    shape[split_axis] //= n
+    shape[concat_axis] *= n
     nbytes = x.size * x.dtype.itemsize
     return pl.pallas_call(
-        exchange_kernel,
-        out_shape=jax.ShapeDtypeStruct(shape, x.dtype),
+        functools.partial(exchange_kernel, split_axis, concat_axis),
+        out_shape=jax.ShapeDtypeStruct(tuple(shape), x.dtype),
         in_specs=[pl.BlockSpec(memory_space=pl.ANY)],
         out_specs=pl.BlockSpec(memory_space=pl.ANY),
         scratch_shapes=[
@@ -159,7 +167,9 @@
             pltpu.SemaphoreType.DMA((n,)),
             pltpu.SemaphoreType.DMA(()),
         ],
-        compiler_params=pltpu.CompilerParams(collective_id=1, has_side_effects=True),
+        compiler_params=pltpu.CompilerParams(
+            collective_id=collective_id, has_side_effects=True
+        ),
         cost_estimate=pl.CostEstimate(flops=0, bytes_accessed=2 * nbytes, transcendentals=0),
     )(x)
 
@@ -182,7 +192,7 @@
     )
     screened = coulomb * local_mask[None]
     occ_own, virt_own = gather_half(occupied), gather_half(virtual)
-    moved = exchange_rows(screened)
+    moved = exchange_rows(screened, 0, 1, 1)
     occ_own, moved = lax.optimization_barrier((occ_own, moved))
     pieces = moved.shape[0]
     occ_other = swapped_core(occ_own)
@@ -198,9 +208,9 @@
     dressed = jnp.einsum(
         "pln,ns->pls", spread, virt_all, preferred_element_type=jnp.float32
     ).astype(jnp.bfloat16)
-    layered = dressed.reshape(pieces, rows, 1, jpart, cols, ncol)
+    by_row = exchange_rows(dressed, 1, 0, 2).reshape(pdev, 1, 1, jpart, cols, ncol)
     returned = lax.all_to_all(
-        lax.all_to_all(layered, "row", split_axis=1, concat_axis=0, tiled=True),
+        by_row,
         "col",
         split_axis=4,
         concat_axis=2,

time: 316 us -> 316 us (level)
  blocking collectives: 88.8 us -> 33 us
  Pallas kernels: 104 us -> 155 us
    all_to_all x1 -> x0, blocking collectives: 55.8 us -> none  [shards(): lax.all_to_all(layered, 'row', split_axis=1, concat_axis=0, tiled=True)]
    pallas_call x1 -> x2, Pallas kernels: 76 us -> 127 us  [exchange_rows(): pl.pallas_call(functools.partial(exchange_kernel, split_axis, concat_axis...]
where the time goes in v7:
time: 316 us; the launch traced here: 315 us
  Pallas kernels  155 us (49%)
  waiting for transfers between devices  55 us (17%)
  blocking collectives  33 us (10%)
  matrix products  25.8 us (8%)
  local copies, waits for them, and re-layouts  19.7 us (6%)
  between operations  13.5 us (4%)
  starting transfers between devices  7.55 us (2%)
  other arithmetic  5.26 us (2%)
    pallas_call x2, Pallas kernels, exchange_rows(): pl.pallas_call(functools.partial(exchange_kernel, split_axis, concat_axis...  127 us
    all_to_all x1, blocking collectives, shards(): lax.all_to_all(shaped, 'col', split_axis=2, concat_axis=4, tiled=True)  33 us
    pallas_call x1, Pallas kernels, doubling_sum(): pl.pallas_call(functools.partial(doubling_kernel, rounds), out_shape=jax....  28.5 us
    all_to_all x1, waiting for transfers between devices, shards(): lax.all_to_all(by_row, 'col', split_axis=4, concat_axis=2, tiled=True)  27.4 us
    all_gather x2, waiting for transfers between devices, gather_half(): return lax.all_gather(part, 'row', axis=0, tiled=True)  18.1 us
    dot_general x1, matrix products, shards(): jnp.einsum('pln,ns->pls', spread, virt_all, preferred_element_type=jnp.fl...  11.2 us
    ppermute x2, waiting for transfers between devices, swapped_core(): return lax.ppermute(value, 'aux', [(0, 1), (1, 0)])  9.48 us
    all_to_all x1, starting transfers between devices, shards(): lax.all_to_all(by_row, 'col', split_axis=4, concat_axis=2, tiled=True)  7.34 us
  transfers between devices with their start and end apart: 6, of which 5 were waited for; matrix products, arithmetic and copies ran while one was open for 9% of the time, Pallas kernels for 24%

profile of v7, /device:TPU:24, one launch (start us, length us, event | category | flops | bytes accessed | tf_op | source)
XLA Modules:
  0.0 315.0 jit_solution(8854946365186814449)
XLA Ops:
  6.5 0.0 copy-start
  6.5 0.0 copy-start.2
  6.5 0.0 all-gather.5.cloned.1.call-start
  6.5 1.2 copy-done
  7.8 0.9 constant_dynamic-slice_fusion
  8.6 0.0 all-gather.5.cloned.1.call-update
  8.7 0.0 all-gather.3.cloned.1.call-start
  8.7 1.9 constant_dynamic-slice_fusion.1
  10.6 0.0 all-gather.3.cloned.1.call-update
  10.6 0.9 fusion.33
  11.5 0.1 broadcast_bitcast_fusion
  11.6 0.0 copy-done.2
  11.6 1.6 broadcast_multiply_fusion.x_ref
  13.2 76.0 %shard_map.46 = bf16[4,2048,128]{2,1,0:T(8,128)(2,1)} custom-call(bf16[32,256,128]{2,1,0:T(8,128)(2,1)} %broadcast_multiply_fusion.x_ref), custom_call_target="tpu_custom_call" | custom-call | bytes 4194304 | tf_op jit(solution)/shard_map/pallas_call | solution.py:160
  89.2 17.7 %all-gather.5.cloned.1.call-done = bf16[2048,1024]{1,0:T(8,128)(2,1)} async-done(((bf16[256,1024]{1,0:T(8,128)(2,1)}), bf16[2048,1024]{1,0:T(8,128)(2,1)}) %all-gather.5.cloned.1.call-update) | async-done | bytes 4194320 | tf_op jit(solution)/shard_map/all_gather | solution.py:79
  106.9 0.1 collective-permute-start
  106.9 0.0 copy-start.3
  106.9 5.3 %fusion.24 = bf16[4,1024,128]{1,2,0:T(8,128)(2,1)S(1)} fusion(bf16[4,2048,128]{2,1,0:T(8,128)(2,1)} %shard_map.46, bf16[2048,1024]{1,0:T(8,128)(2,1)} %all-gather.5.cloned.1.call-done), kind=kOutput, calls=%fused_computation.17 | convolution fusion | flops 2148007936 | bytes 7340032 | tf_op jit(solution)/shard_map/ml,pmn->pln/dot_general | solution.py:199
  112.3 2.1 collective-permute-done
  114.4 0.0 copy-done.3
  114.4 4.6 %fusion.21 = bf16[4,1024,128]{1,2,0:T(8,128)(2,1)S(1)} fusion(bf16[4,2048,128]{2,1,0:T(8,128)(2,1)S(1)} %copy-done.3, bf16[2048,1024]{1,0:T(8,128)(2,1)} %collective-permute-done), kind=kOutput, calls=%fused_computation.16 | convolution fusion | flops 2148007936 | bytes 7340032 | tf_op jit(solution)/shard_map/ml,pmn->pln/dot_general | solution.py:200
  119.0 0.8 maximum_select_fusion.1
  119.8 2.5 copy.26
  122.3 2.2 copy.27
  124.5 33.0 %all_to_all.30 = bf16[4,8,16,16,128]{4,3,1,0,2:T(8,128)(2,1)S(1)} all-to-all(bf16[4,8,16,16,128]{4,3,1,0,2:T(8,128)(2,1)S(1)} %copy.27), channel_id=1, replica_groups=mesh['aux'=2,'row'=8,'col'=16] {'col'}, dimensions={2} | all-to-all | bytes 4194304 | tf_op jit(solution)/shard_map/all_to_all | solution.py:204
  157.5 2.4 copy.28
  159.9 2.3 reshape.36
  162.2 0.4 all-gather.3.cloned.1.call-done
  162.6 0.0 collective-permute-start.1
  162.6 7.4 %collective-permute-done.1 = bf16[2048,1024]{1,0:T(8,128)(2,1)S(1)} collective-permute-done((bf16[2048,1024]{1,0:T(8,128)(2,1)}, bf16[2048,1024]{1,0:T(8,128)(2,1)S(1)}, u32[]{:S(2)}, u32[]{:S(2)}) %collective-permute-start.1) | collective-permute-done | bytes 4194336 | tf_op jit(solution)/shard_map/ppermute | solution.py:92
  170.0 11.2 %fusion.8.x_ref = bf16[4,128,2048]{2,1,0:T(8,128)(2,1)} fusion(bf16[4,128,2048]{2,1,0:T(8,128)(2,1)} %reshape.36, bf16[2048,1024]{1,0:T(8,128)(2,1)S(1)} %collective-permute-done.1, bf16[2048,1024]{1,0:T(8,128)(2,1)} %all-gather.3.cloned.1.call-done, pred[]{:T(512)S(6)} %eq.2), kind=kOutput, calls=%fused_computation.8 | convolution fusion | flops 4333764608 | bytes 12582913 | tf_op jit(solution)/shard_map/pln,ns->pls/dot_general | solution.py:208
  181.2 50.6 %shard_map.47 = bf16[32,16,2048]{2,1,0:T(8,128)(2,1)} custom-call(bf16[4,128,2048]{2,1,0:T(8,128)(2,1)} %fusion.8.x_ref), custom_call_target="tpu_custom_call" | custom-call | bytes 4194304 | tf_op jit(solution)/shard_map/pallas_call | solution.py:160
  231.8 2.2 copy.35
  234.1 1.9 copy.29
  235.9 0.0 copy-start.1
  235.9 7.3 %all-to-all-start.1 = ((bf16[32,1,1,16,16,128]{5,3,0,2,1,4:T(8,128)(2,1)}), bf16[32,1,1,16,16,128]{5,3,0,2,1,4:T(8,128)(2,1)}, u32[]{:S(2)}, u32[]{:S(2)}) async-start(bf16[32,1,1,16,16,128]{5,3,0,2,1,4:T(8,128)(2,1)} %copy.29), calls=%async_computation.1 | async-start | bytes 4194304 | tf_op jit(solution)/shard_map/all_to_all | solution.py:212
  243.3 0.0 copy-done.1
  243.3 0.1 collective-permute-start.2
  243.4 27.4 %all-to-all-done.1 = bf16[32,1,1,16,16,128]{5,3,0,2,1,4:T(8,128)(2,1)} async-done(((bf16[32,1,1,16,16,128]{5,3,0,2,1,4:T(8,128)(2,1)}), bf16[32,1,1,16,16,128]{5,3,0,2,1,4:T(8,128)(2,1)}, u32[]{:S(2)}, u32[]{:S(2)}) %all-to-all-start.1) | async-done | bytes 2097184 | tf_op jit(solution)/shard_map/all_to_all | solution.py:212
  270.8 2.1 copy.30
  272.9 1.5 fusion.27
  274.5 0.0 collective-permute-done.2
  274.5 3.2 %broadcast_select_fusion.1 = (f32[32,32]{1,0:T(8,128)S(1)}, f32[32,32]{1,0:T(8,128)S(1)}) fusion(f32[32,32]{1,0:T(8,128)S(1)} %fusion.27, pred[]{:T(512)S(6)} %eq.2, bf16[32,256,128]{2,0,1:T(8,128)(2,1)S(1)} %bitcast.56, bf16[32,256,128]{2,1,0:T(8,128)(2,1)} %collective-permute-done.2), kind=kOutput, calls=%fused_computation.24 | convolution fusion | flops 67110912 | bytes 4206593 | tf_op jit(solution)/shard_map/pls,qls->pq/dot_general | solution.py:222
  277.7 0.7 pad_maximum_fusion.x_ref
  278.3 28.5 %shard_map.48 = f32[32,64]{1,0:T(8,128)} custom-call(f32[32,64]{1,0:T(8,128)} %pad_maximum_fusion.x_ref), custom_call_target="tpu_custom_call" | custom-call | tf_op jit(solution)/shard_map/pallas_call | solution.py:62
  306.8 1.3 broadcast_multiply_fusion.1
Async XLA Ops:
  6.5 1.2 copy-start
  6.5 5.0 %copy-start.2 = (bf16[32,256,128]{2,1,0:T(8,128)(2,1)S(1)}, bf16[32,256,128]{2,1,0:T(8,128)(2,1)}, u32[]{:S(2)}) copy-start(bf16[32,256,128]{2,1,0:T(8,128)(2,1)} %param.4) | copy-start | bytes 6291460
  6.5 100.3 %all-gather.5.cloned.1.call-start = ((), (), s32[]{:S(2)}) async-start(), calls=%async_computation.3 | async-start | bytes 4718592 | tf_op jit(solution)/shard_map/all_gather | solution.py:79
  8.7 153.9 %all-gather.3.cloned.1.call-start = ((), (), s32[]{:S(2)}) async-start(), calls=%async_computation.2 | async-start | bytes 4718592 | tf_op jit(solution)/shard_map/all_gather | solution.py:79
  106.9 7.5 %collective-permute-start = (bf16[2048,1024]{1,0:T(8,128)(2,1)}, bf16[2048,1024]{1,0:T(8,128)(2,1)}, u32[]{:S(2)}, u32[]{:S(2)}) collective-permute-start(bf16[2048,1024]{1,0:T(8,128)(2,1)} %all-gather.5.cloned.1.call-done), channel_id=1, source_target_pairs={{0,128},{128,0},{1,129},{129,1},{2,130},{130,2},{3,131},{131,3},{4... | collective-permute-start | bytes 12582920 | tf_op jit(solution)/shard_map/ppermute | solution.py:92
  106.9 7.4 %copy-start.3 = (bf16[4,2048,128]{2,1,0:T(8,128)(2,1)S(1)}, bf16[4,2048,128]{2,1,0:T(8,128)(2,1)}, u32[]{:S(2)}) copy-start(bf16[4,2048,128]{2,1,0:T(8,128)(2,1)} %shard_map.46) | copy-start | bytes 6291460
  162.6 7.4 %collective-permute-start.1 = (bf16[2048,1024]{1,0:T(8,128)(2,1)}, bf16[2048,1024]{1,0:T(8,128)(2,1)S(1)}, u32[]{:S(2)}, u32[]{:S(2)}) collective-permute-start(bf16[2048,1024]{1,0:T(8,128)(2,1)} %all-gather.3.cloned.1.call-done), channel_id=1, source_target_pairs={{0,128},{128,0},{1,129},{129,1},{2,130},{130,2},{3,131},{131,3},{4... | collective-permute-start | bytes 12582920 | tf_op jit(solution)/shard_map/ppermute | solution.py:92
  235.9 7.3 %copy-start.1 = (bf16[32,256,128]{2,1,0:T(8,128)(2,1)S(1)}, bf16[32,256,128]{2,1,0:T(8,128)(2,1)}, u32[]{:S(2)}) copy-start(bf16[32,256,128]{2,1,0:T(8,128)(2,1)} %broadcast_multiply_fusion.x_ref) | copy-start | bytes 6291460
  235.9 34.9 %all-to-all-start.1 = ((bf16[32,1,1,16,16,128]{5,3,0,2,1,4:T(8,128)(2,1)}), bf16[32,1,1,16,16,128]{5,3,0,2,1,4:T(8,128)(2,1)}, u32[]{:S(2)}, u32[]{:S(2)}) async-start(bf16[32,1,1,16,16,128]{5,3,0,2,1,4:T(8,128)(2,1)} %copy.29), calls=%async_computation.1 | async-start | bytes 4194304 | tf_op jit(solution)/shard_map/all_to_all | solution.py:212
  243.3 31.2 %collective-permute-start.2 = (bf16[32,256,128]{2,1,0:T(8,128)(2,1)S(1)}, bf16[32,256,128]{2,1,0:T(8,128)(2,1)}, u32[]{:S(2)}, u32[]{:S(2)}) collective-permute-start(bf16[32,256,128]{2,1,0:T(8,128)(2,1)S(1)} %copy-done.1), channel_id=1, source_target_pairs={{0,128},{128,0},{1,129},{129,1},{2,130},{130,2},{3,131},{131,3},{4... | collective-permute-start | bytes 6291464 | tf_op jit(solution)/shard_map/ppermute | solution.py:17
Sparse Core Ops, SparseCore 0:
  9.1 97.6 all-gather.4
  108.7 53.9 all-gather.2

commit v8 on v6

--- a/solution.py
+++ b/solution.py
@@ -17,57 +17,77 @@
     return lax.ppermute(value, axis, pairs)
 
 
-def partner_rounds():
-    rounds = []
+def gather_round(axis, here, own, slots, send_sem, recv_sem):
+    me, n = here[axis], lax.axis_size(axis)
+
+    def device(index):
+        place = dict(here)
+        place[axis] = index
+        return (place["aux"], place["row"], place["col"])
+
+    slots[me] = own
+    sends = []
+    for step in range(1, n):
+        dest = lax.rem(me + step, n)
+        copy = pltpu.make_async_remote_copy(
+            src_ref=slots.at[me],
+            dst_ref=slots.at[me],
+            send_sem=send_sem.at[step],
+            recv_sem=recv_sem.at[step],
+            device_id=device(dest),
+            device_id_type=pl.DeviceIdType.MESH,
+        )
+        copy.start()
+        sends.append(copy)
+    for step in range(1, n):
+        source = lax.rem(me + n - step, n)
+        incoming = pltpu.make_async_remote_copy(
+            src_ref=slots.at[me],
+            dst_ref=slots.at[source],
+            send_sem=send_sem.at[step],
+            recv_sem=recv_sem.at[step],
+            device_id=device(source),
+            device_id_type=pl.DeviceIdType.MESH,
+        )
+        incoming.wait_recv()
+        sends[step - 1].wait_send()
+    total = slots[0]
+    for index in range(1, n):
+        total = total + slots[index]
+    return total
+
+
+def two_round_kernel(x_ref, o_ref, col_slots, row_slots, send_a, recv_a, send_b, recv_b):
+    here = {name: lax.axis_index(name) for name in ("aux", "row", "col")}
+    peers = []
     for axis in ("col", "row"):
-        bit = 1
-        while bit < lax.axis_size(axis):
-            rounds.append((axis, bit))
-            bit *= 2
-    return rounds
-
-
-def doubling_kernel(rounds, x_ref, o_ref, recv, send_sem, recv_sem):
-    here = {name: lax.axis_index(name) for name in ("aux", "row", "col")}
-
-    def partner(axis, bit):
-        place = dict(here)
-        place[axis] = here[axis] ^ bit
-        return (place["aux"], place["row"], place["col"])
-
+        n = lax.axis_size(axis)
+        for step in range(1, n):
+            place = dict(here)
+            place[axis] = lax.rem(here[axis] + step, n)
+            peers.append((place["aux"], place["row"], place["col"]))
     barrier = pltpu.get_barrier_semaphore()
-    for axis, bit in rounds:
-        pl.semaphore_signal(
-            barrier, inc=1, device_id=partner(axis, bit), device_id_type=pl.DeviceIdType.MESH
-        )
-    pl.semaphore_wait(barrier, len(rounds))
-
-    o_ref[...] = x_ref[...]
-    for step, (axis, bit) in enumerate(rounds):
-        copy = pltpu.make_async_remote_copy(
-            src_ref=o_ref,
-            dst_ref=recv.at[step],
-            send_sem=send_sem.at[step],
-            recv_sem=recv_sem.at[step],
-            device_id=partner(axis, bit),
-            device_id_type=pl.DeviceIdType.MESH,
-        )
-        copy.start()
-        copy.wait()
-        o_ref[...] = o_ref[...] + recv[step]
+    for peer in peers:
+        pl.semaphore_signal(barrier, inc=1, device_id=peer, device_id_type=pl.DeviceIdType.MESH)
+    pl.semaphore_wait(barrier, len(peers))
+    by_col = gather_round("col", here, x_ref[...], col_slots, send_a, recv_a)
+    o_ref[...] = gather_round("row", here, by_col, row_slots, send_b, recv_b)
 
 
 def doubling_sum(partial):
-    rounds = partner_rounds()
+    cols, rows = lax.axis_size("col"), lax.axis_size("row")
     return pl.pallas_call(
-        functools.partial(doubling_kernel, rounds),
+        two_round_kernel,
         out_shape=jax.ShapeDtypeStruct(partial.shape, partial.dtype),
         in_specs=[pl.BlockSpec(memory_space=pltpu.VMEM)],
         out_specs=pl.BlockSpec(memory_space=pltpu.VMEM),
         scratch_shapes=[
-            pltpu.VMEM((len(rounds),) + partial.shape, partial.dtype),
-            pltpu.SemaphoreType.DMA((len(rounds),)),
-            pltpu.SemaphoreType.DMA((len(rounds),)),
+            pltpu.VMEM((cols,) + partial.shape, partial.dtype),
+            pltpu.VMEM((rows,) + partial.shape, partial.dtype),
+            pltpu.SemaphoreType.DMA((cols,)),
+            pltpu.SemaphoreType.DMA((cols,)),
+            pltpu.SemaphoreType.DMA((rows,)),
+            pltpu.SemaphoreType.DMA((rows,)),
         ],
         compiler_params=pltpu.CompilerParams(collective_id=0, has_side_effects=True),
     )(partial)

time: 316 us -> 306 us (0.968)
  Pallas kernels: 104 us -> 93.7 us
    pallas_call x1, Pallas kernels: 27.8 us -> 17.7 us  [doubling_sum(): pl.pallas_call(two_round_kernel, out_shape=jax.ShapeDtypeStruct(partial.s...]
  transfers between devices with their start and end apart: 6 -> 6, of which waited for: 5 -> 5; matrix products, arithmetic and copies ran while one was open for 9% -> 9% of each run, Pallas kernels for 24% -> 25%
where the time goes in v8:
time: 306 us; the launch traced here: 305 us
  Pallas kernels  93.7 us (31%)
  blocking collectives  88.8 us (29%)
  waiting for transfers between devices  53.1 us (17%)
  matrix products  24.8 us (8%)
  local copies, waits for them, and re-layouts  18.7 us (6%)
  between operations  13.5 us (4%)
  starting transfers between devices  7.36 us (2%)
  other arithmetic  5.26 us (2%)
    pallas_call x1, Pallas kernels, exchange_rows(): pl.pallas_call(exchange_kernel, out_shape=jax.ShapeDtypeStruct(shape, x.d...  76 us
    all_to_all x1, blocking collectives, shards(): lax.all_to_all(layered, 'row', split_axis=1, concat_axis=0, tiled=True)  55.8 us
    all_to_all x1, blocking collectives, shards(): lax.all_to_all(shaped, 'col', split_axis=2, concat_axis=4, tiled=True)  33 us
    all_to_all x1, waiting for transfers between devices, shards(): lax.all_to_all(lax.all_to_all(layered, 'row', split_axis=1, concat_axis=0...  25.5 us
    all_gather x2, waiting for transfers between devices, gather_half(): return lax.all_gather(part, 'row', axis=0, tiled=True)  18.1 us
    pallas_call x1, Pallas kernels, doubling_sum(): pl.pallas_call(two_round_kernel, out_shape=jax.ShapeDtypeStruct(partial.s...  17.7 us
    dot_general x1, matrix products, shards(): jnp.einsum('pln,ns->pls', spread, virt_all, preferred_element_type=jnp.fl...  10.3 us
    ppermute x2, waiting for transfers between devices, swapped_core(): return lax.ppermute(value, 'aux', [(0, 1), (1, 0)])  9.48 us
  transfers between devices with their start and end apart: 6, of which 5 were waited for; matrix products, arithmetic and copies ran while one was open for 9% of the time, Pallas kernels for 25%

profile of v8, /device:TPU:24, one launch (start us, length us, event | category | flops | bytes accessed | tf_op | source)
XLA Modules:
  0.0 305.3 jit_solution(9265743866168738236)
XLA Ops:
  6.5 0.0 copy-start
  6.5 0.0 copy-start.2
  6.5 0.0 all-gather.5.cloned.1.call-start
  6.5 1.2 copy-done
  7.8 0.9 constant_dynamic-slice_fusion
  8.6 0.0 all-gather.5.cloned.1.call-update
  8.7 0.0 all-gather.3.cloned.1.call-start
  8.7 1.9 constant_dynamic-slice_fusion.1
  10.6 0.0 all-gather.3.cloned.1.call-update
  10.6 0.9 fusion.33
  11.5 0.1 broadcast_bitcast_fusion
  11.6 0.0 copy-done.2
  11.6 1.6 broadcast_multiply_fusion.x_ref
  13.2 76.0 %shard_map.46 = bf16[4,2048,128]{2,1,0:T(8,128)(2,1)} custom-call(bf16[32,256,128]{2,1,0:T(8,128)(2,1)} %broadcast_multiply_fusion.x_ref), custom_call_target="tpu_custom_call" | custom-call | bytes 4194304 | tf_op jit(solution)/shard_map/pallas_call | solution.py:172
  89.2 17.7 %all-gather.5.cloned.1.call-done = bf16[2048,1024]{1,0:T(8,128)(2,1)} async-done(((bf16[256,1024]{1,0:T(8,128)(2,1)}), bf16[2048,1024]{1,0:T(8,128)(2,1)}) %all-gather.5.cloned.1.call-update) | async-done | bytes 4194320 | tf_op jit(solution)/shard_map/all_gather | solution.py:99
  106.9 0.1 collective-permute-start
  106.9 0.0 copy-start.3
  106.9 5.3 %fusion.24 = bf16[4,1024,128]{1,2,0:T(8,128)(2,1)S(1)} fusion(bf16[4,2048,128]{2,1,0:T(8,128)(2,1)} %shard_map.46, bf16[2048,1024]{1,0:T(8,128)(2,1)} %all-gather.5.cloned.1.call-done), kind=kOutput, calls=%fused_computation.17 | convolution fusion | flops 2148007936 | bytes 7340032 | tf_op jit(solution)/shard_map/ml,pmn->pln/dot_general | solution.py:209
  112.3 2.1 collective-permute-done
  114.4 0.0 copy-done.3
  114.4 4.6 %fusion.21 = bf16[4,1024,128]{1,2,0:T(8,128)(2,1)S(1)} fusion(bf16[4,2048,128]{2,1,0:T(8,128)(2,1)S(1)} %copy-done.3, bf16[2048,1024]{1,0:T(8,128)(2,1)} %collective-permute-done), kind=kOutput, calls=%fused_computation.16 | convolution fusion | flops 2148007936 | bytes 7340032 | tf_op jit(solution)/shard_map/ml,pmn->pln/dot_general | solution.py:210
  119.0 0.8 maximum_select_fusion.1
  119.8 2.5 copy.27
  122.3 2.2 copy.28
  124.5 33.0 %all_to_all.48 = bf16[4,8,16,16,128]{4,3,1,0,2:T(8,128)(2,1)S(1)} all-to-all(bf16[4,8,16,16,128]{4,3,1,0,2:T(8,128)(2,1)S(1)} %copy.28), channel_id=1, replica_groups=mesh['aux'=2,'row'=8,'col'=16] {'col'}, dimensions={2} | all-to-all | bytes 4194304 | tf_op jit(solution)/shard_map/all_to_all | solution.py:214
  157.5 2.4 copy.29
  159.9 2.3 reshape.36
  162.2 0.4 all-gather.3.cloned.1.call-done
  162.6 0.0 collective-permute-start.1
  162.6 7.4 %collective-permute-done.1 = bf16[2048,1024]{1,0:T(8,128)(2,1)S(1)} collective-permute-done((bf16[2048,1024]{1,0:T(8,128)(2,1)}, bf16[2048,1024]{1,0:T(8,128)(2,1)S(1)}, u32[]{:S(2)}, u32[]{:S(2)}) %collective-permute-start.1) | collective-permute-done | bytes 4194336 | tf_op jit(solution)/shard_map/ppermute | solution.py:112
  170.0 10.3 %fusion.8 = bf16[4,128,2048]{2,1,0:T(8,128)(2,1)S(1)} fusion(bf16[4,128,2048]{2,1,0:T(8,128)(2,1)} %reshape.36, bf16[2048,1024]{1,0:T(8,128)(2,1)S(1)} %collective-permute-done.1, bf16[2048,1024]{1,0:T(8,128)(2,1)} %all-gather.3.cloned.1.call-done, pred[]{:T(512)S(6)} %eq.2), kind=kOutput, calls=%fused_computation.8 | convolution fusion | flops 4333764608 | bytes 12582913 | tf_op jit(solution)/shard_map/pln,ns->pls/dot_general | solution.py:218
  180.2 0.6 copy.37
  180.9 0.6 copy.30
  181.5 55.8 %all_to_all.49 = bf16[4,8,1,16,16,128]{5,4,3,0,2,1:T(8,128)(2,1)S(1)} all-to-all(bf16[4,8,1,16,16,128]{5,4,3,0,2,1:T(8,128)(2,1)S(1)} %copy.30), channel_id=1, replica_groups=mesh['aux'=2,'row'=8,'col'=16] {'row'}, dimensions={1} | all-to-all | bytes 4194304 | tf_op jit(solution)/shard_map/all_to_all | solution.py:223
  237.3 1.9 copy.31
  239.1 0.0 copy-start.1
  239.1 7.2 %all-to-all-start.2 = ((bf16[32,1,1,16,16,128]{5,3,0,2,1,4:T(8,128)(2,1)}), bf16[32,1,1,16,16,128]{5,3,0,2,1,4:T(8,128)(2,1)}, u32[]{:S(2)}, u32[]{:S(2)}) async-start(bf16[32,1,1,16,16,128]{5,3,0,2,1,4:T(8,128)(2,1)} %copy.31), calls=%async_computation.2 | async-start | bytes 4194304 | tf_op jit(solution)/shard_map/all_to_all | solution.py:222
  246.3 0.0 copy-done.1
  246.3 0.1 collective-permute-start.2
  246.4 25.5 %all-to-all-done.2 = bf16[32,1,1,16,16,128]{5,3,0,2,1,4:T(8,128)(2,1)} async-done(((bf16[32,1,1,16,16,128]{5,3,0,2,1,4:T(8,128)(2,1)}), bf16[32,1,1,16,16,128]{5,3,0,2,1,4:T(8,128)(2,1)}, u32[]{:S(2)}, u32[]{:S(2)}) %all-to-all-start.2) | async-done | bytes 2097184 | tf_op jit(solution)/shard_map/all_to_all | solution.py:222
  271.9 2.1 copy.32
  274.0 1.5 fusion.27
  275.6 0.0 collective-permute-done.2
  275.6 3.2 %broadcast_select_fusion.1 = (f32[32,32]{1,0:T(8,128)S(1)}, f32[32,32]{1,0:T(8,128)S(1)}) fusion(f32[32,32]{1,0:T(8,128)S(1)} %fusion.27, pred[]{:T(512)S(6)} %eq.2, bf16[32,256,128]{2,0,1:T(8,128)(2,1)S(1)} %bitcast.61, bf16[32,256,128]{2,1,0:T(8,128)(2,1)} %collective-permute-done.2), kind=kOutput, calls=%fused_computation.24 | convolution fusion | flops 67110912 | bytes 4206593 | tf_op jit(solution)/shard_map/pls,qls->pq/dot_general | solution.py:232
  278.8 0.7 pad_maximum_fusion.x_ref
  279.5 17.7 %shard_map.47 = f32[32,64]{1,0:T(8,128)} custom-call(f32[32,64]{1,0:T(8,128)} %pad_maximum_fusion.x_ref), custom_call_target="tpu_custom_call" | custom-call | tf_op jit(solution)/shard_map/pallas_call | solution.py:79
  297.1 1.3 broadcast_multiply_fusion.1
Async XLA Ops:
  6.5 1.2 copy-start
  6.5 5.0 %copy-start.2 = (bf16[32,256,128]{2,1,0:T(8,128)(2,1)S(1)}, bf16[32,256,128]{2,1,0:T(8,128)(2,1)}, u32[]{:S(2)}) copy-start(bf16[32,256,128]{2,1,0:T(8,128)(2,1)} %param.4) | copy-start | bytes 6291460
  6.5 100.3 %all-gather.5.cloned.1.call-start = ((), (), s32[]{:S(2)}) async-start(), calls=%async_computation.4 | async-start | bytes 4718592 | tf_op jit(solution)/shard_map/all_gather | solution.py:99
  8.7 153.9 %all-gather.3.cloned.1.call-start = ((), (), s32[]{:S(2)}) async-start(), calls=%async_computation.3 | async-start | bytes 4718592 | tf_op jit(solution)/shard_map/all_gather | solution.py:99
  106.9 7.5 %collective-permute-start = (bf16[2048,1024]{1,0:T(8,128)(2,1)}, bf16[2048,1024]{1,0:T(8,128)(2,1)}, u32[]{:S(2)}, u32[]{:S(2)}) collective-permute-start(bf16[2048,1024]{1,0:T(8,128)(2,1)} %all-gather.5.cloned.1.call-done), channel_id=1, source_target_pairs={{0,128},{128,0},{1,129},{129,1},{2,130},{130,2},{3,131},{131,3},{4... | collective-permute-start | bytes 12582920 | tf_op jit(solution)/shard_map/ppermute | solution.py:112
  106.9 7.4 %copy-start.3 = (bf16[4,2048,128]{2,1,0:T(8,128)(2,1)S(1)}, bf16[4,2048,128]{2,1,0:T(8,128)(2,1)}, u32[]{:S(2)}) copy-start(bf16[4,2048,128]{2,1,0:T(8,128)(2,1)} %shard_map.46) | copy-start | bytes 6291460
  162.6 7.4 %collective-permute-start.1 = (bf16[2048,1024]{1,0:T(8,128)(2,1)}, bf16[2048,1024]{1,0:T(8,128)(2,1)S(1)}, u32[]{:S(2)}, u32[]{:S(2)}) collective-permute-start(bf16[2048,1024]{1,0:T(8,128)(2,1)} %all-gather.3.cloned.1.call-done), channel_id=1, source_target_pairs={{0,128},{128,0},{1,129},{129,1},{2,130},{130,2},{3,131},{131,3},{4... | collective-permute-start | bytes 12582920 | tf_op jit(solution)/shard_map/ppermute | solution.py:112
  239.1 7.2 %copy-start.1 = (bf16[32,256,128]{2,1,0:T(8,128)(2,1)S(1)}, bf16[32,256,128]{2,1,0:T(8,128)(2,1)}, u32[]{:S(2)}) copy-start(bf16[32,256,128]{2,1,0:T(8,128)(2,1)} %broadcast_multiply_fusion.x_ref) | copy-start | bytes 6291460
  239.1 32.8 %all-to-all-start.2 = ((bf16[32,1,1,16,16,128]{5,3,0,2,1,4:T(8,128)(2,1)}), bf16[32,1,1,16,16,128]{5,3,0,2,1,4:T(8,128)(2,1)}, u32[]{:S(2)}, u32[]{:S(2)}) async-start(bf16[32,1,1,16,16,128]{5,3,0,2,1,4:T(8,128)(2,1)} %copy.31), calls=%async_computation.2 | async-start | bytes 4194304 | tf_op jit(solution)/shard_map/all_to_all | solution.py:222
  246.3 29.3 %collective-permute-start.2 = (bf16[32,256,128]{2,1,0:T(8,128)(2,1)S(1)}, bf16[32,256,128]{2,1,0:T(8,128)(2,1)}, u32[]{:S(2)}, u32[]{:S(2)}) collective-permute-start(bf16[32,256,128]{2,1,0:T(8,128)(2,1)S(1)} %copy-done.1), channel_id=1, source_target_pairs={{0,128},{128,0},{1,129},{129,1},{2,130},{130,2},{3,131},{131,3},{4... | collective-permute-start | bytes 6291464 | tf_op jit(solution)/shard_map/ppermute | solution.py:17
Sparse Core Ops, SparseCore 0:
  9.1 97.6 all-gather.4
  108.7 53.9 all-gather.2

commit v9 on v8

--- a/solution.py
+++ b/solution.py
@@ -112,20 +112,28 @@
     return lax.ppermute(value, "aux", [(0, 1), (1, 0)])
 
 
-def exchange_kernel(x_ref, o_ref, send_sem, recv_sem, local_sem):
+def sliced(ref, axis, start, size):
+    index = [slice(None)] * len(ref.shape)
+    index[axis] = pl.ds(start, size)
+    return ref.at[tuple(index)]
+
+
+def exchange_kernel(mesh_axis, split_axis, concat_axis, x_ref, o_ref, send_sem, recv_sem, local_sem):
     here = {name: lax.axis_index(name) for name in ("aux", "row", "col")}
-    me, n = here["row"], lax.axis_size("row")
-    depth = x_ref.shape[0] // n
-    height = x_ref.shape[1]
+    me, n = here[mesh_axis], lax.axis_size(mesh_axis)
+    depth = x_ref.shape[split_axis] // n
+    height = o_ref.shape[concat_axis] // n
 
     def device(index):
-        return (here["aux"], index, here["col"])
+        place = dict(here)
+        place[mesh_axis] = index
+        return (place["aux"], place["row"], place["col"])
 
     def piece(index):
-        return x_ref.at[pl.ds(index * depth, depth)]
+        return sliced(x_ref, split_axis, index * depth, depth)
 
     def slot(index):
-        return o_ref.at[:, pl.ds(index * height, height)]
+        return sliced(o_ref, concat_axis, index * height, height)
 
     barrier = pltpu.get_barrier_semaphore()
     for step in range(1, n):
@@ -165,13 +173,15 @@
     local.wait()
 
 
-def exchange_rows(x):
-    n = lax.axis_size("row")
-    shape = (x.shape[0] // n, x.shape[1] * n) + x.shape[2:]
+def exchange(x, mesh_axis, split_axis, concat_axis, collective_id):
+    n = lax.axis_size(mesh_axis)
+    shape = list(x.shape)
+    shape[split_axis] //= n
+    shape[concat_axis] *= n
     nbytes = x.size * x.dtype.itemsize
     return pl.pallas_call(
-        exchange_kernel,
-        out_shape=jax.ShapeDtypeStruct(shape, x.dtype),
+        functools.partial(exchange_kernel, mesh_axis, split_axis, concat_axis),
+        out_shape=jax.ShapeDtypeStruct(tuple(shape), x.dtype),
         in_specs=[pl.BlockSpec(memory_space=pl.ANY)],
         out_specs=pl.BlockSpec(memory_space=pl.ANY),
         scratch_shapes=[
@@ -179,7 +189,9 @@
             pltpu.SemaphoreType.DMA((n,)),
             pltpu.SemaphoreType.DMA(()),
         ],
-        compiler_params=pltpu.CompilerParams(collective_id=1, has_side_effects=True),
+        compiler_params=pltpu.CompilerParams(
+            collective_id=collective_id, has_side_effects=True
+        ),
         cost_estimate=pl.CostEstimate(flops=0, bytes_accessed=2 * nbytes, transcendentals=0),
     )(x)
 
@@ -202,7 +214,7 @@
     )
     screened = coulomb * local_mask[None]
     occ_own, virt_own = gather_half(occupied), gather_half(virtual)
-    moved = exchange_rows(screened)
+    moved = exchange(screened, "row", 0, 1, 1)
     occ_own, moved = lax.optimization_barrier((occ_own, moved))
     pieces = moved.shape[0]
     occ_other = swapped_core(occ_own)
@@ -210,23 +222,15 @@
     half_other = jnp.einsum("ml,pmn->pln", occ_other, moved, preferred_element_type=jnp.float32)
     half = join_halves(half_own.astype(jnp.bfloat16), half_other.astype(jnp.bfloat16), axis=1)
     jpart = mrow // cols
-    shaped = half.reshape(pieces, rows, cols, jpart, ncol)
-    spread = lax.all_to_all(shaped, "col", split_axis=2, concat_axis=4, tiled=True)
-    spread = spread.reshape(pieces, rows * jpart, nao)
+    shaped = half.reshape(pieces, rows, mrow, ncol)
+    spread = exchange(shaped, "col", 2, 3, 3).reshape(pieces, rows * jpart, nao)
     virt_own, spread = lax.optimization_barrier((virt_own, spread))
     virt_all = join_halves(virt_own, swapped_core(virt_own), axis=1)
     dressed = jnp.einsum(
         "pln,ns->pls", spread, virt_all, preferred_element_type=jnp.float32
     ).astype(jnp.bfloat16)
-    layered = dressed.reshape(pieces, rows, 1, jpart, cols, ncol)
-    returned = lax.all_to_all(
-        lax.all_to_all(layered, "row", split_axis=1, concat_axis=0, tiled=True),
-        "col",
-        split_axis=4,
-        concat_axis=2,
-        tiled=True,
-    )
-    aligned = returned.reshape(pdev, mrow, ncol)
+    by_row = exchange(dressed, "row", 1, 0, 2)
+    aligned = exchange(by_row, "col", 2, 1, 4)
     theirs = swapped(screened, "aux", 0)
     with_mine = jnp.einsum("pls,qls->pq", aligned, screened, preferred_element_type=jnp.float32)
     with_theirs = jnp.einsum("pls,qls->pq", aligned, theirs, preferred_element_type=jnp.float32)

time: 306 us -> 316 us (1.033)
  Pallas kernels: 93.7 us -> 229 us
  blocking collectives: 88.8 us -> 0 us
  waiting for transfers between devices: 53.1 us -> 29.7 us
  local copies, waits for them, and re-layouts: 18.7 us -> 6.61 us
  starting transfers between devices: 7.36 us -> 0.69 us
  matrix products: 24.8 us -> 29.3 us
    pallas_call x1 -> x4, Pallas kernels: 76 us -> 207 us  [exchange(): pl.pallas_call(functools.partial(exchange_kernel, mesh_axis, split_axis,...]
    all_to_all x2 -> x0, blocking collectives: 88.8 us -> none  [the longest x1 55.8 us: shards(): lax.all_to_all(layered, 'row', split_axis=1, concat_axis=0, tiled=True)]
    all_to_all x1 -> x0, waiting for transfers between devices: 25.5 us -> none  [shards(): lax.all_to_all(lax.all_to_all(layered, 'row', split_axis=1, concat_axis=0...]
    all_to_all x1 -> x0, starting transfers between devices: 7.16 us -> none  [shards(): lax.all_to_all(lax.all_to_all(layered, 'row', split_axis=1, concat_axis=0...]
    all_to_all x3 -> x0, local copies, waits for them, and re-layouts: 6.42 us -> none  [the longest x1 2.43 us: shards(): lax.all_to_all(shaped, 'col', split_axis=2, concat_axis=4, tiled=True)]
    pallas_call x1, Pallas kernels: 17.7 us -> 21.7 us  [doubling_sum(): pl.pallas_call(two_round_kernel, out_shape=jax.ShapeDtypeStruct(partial.s...]
  transfers between devices with their start and end apart: 6 -> 5, of which waited for: 5 -> 3; matrix products, arithmetic and copies ran while one was open for 9% -> 11% of each run, Pallas kernels for 25% -> 66%
where the time goes in v9:
time: 316 us; the launch traced here: 314 us
  Pallas kernels  229 us (72%)
  waiting for transfers between devices  29.7 us (9%)
  matrix products  29.3 us (9%)
  between operations  13.5 us (4%)
  local copies, waits for them, and re-layouts  6.61 us (2%)
  other arithmetic  5.24 us (2%)
    pallas_call x4, Pallas kernels, exchange(): pl.pallas_call(functools.partial(exchange_kernel, mesh_axis, split_axis,...  207 us
    pallas_call x1, Pallas kernels, doubling_sum(): pl.pallas_call(two_round_kernel, out_shape=jax.ShapeDtypeStruct(partial.s...  21.7 us
    all_gather x2, waiting for transfers between devices, gather_half(): return lax.all_gather(part, 'row', axis=0, tiled=True)  17.7 us
    ppermute x2, waiting for transfers between devices, swapped_core(): return lax.ppermute(value, 'aux', [(0, 1), (1, 0)])  12 us
    dot_general x1, matrix products, shards(): jnp.einsum('pln,ns->pls', spread, virt_all, preferred_element_type=jnp.fl...  11.2 us
  transfers between devices with their start and end apart: 5, of which 3 were waited for; matrix products, arithmetic and copies ran while one was open for 11% of the time, Pallas kernels for 66%

profile of v9, /device:TPU:24, one launch (start us, length us, event | category | flops | bytes accessed | tf_op | source)
XLA Modules:
  0.0 314.1 jit_solution(242356756011151730)
XLA Ops:
  6.5 0.0 copy-start
  6.5 0.0 copy-start.2
  6.5 0.0 all-gather.5.cloned.1.call-start
  6.5 1.2 copy-done
  7.8 0.9 constant_dynamic-slice_fusion
  8.6 0.0 all-gather.5.cloned.1.call-update
  8.7 0.0 all-gather.3.cloned.1.call-start
  8.7 1.9 constant_dynamic-slice_fusion.1
  10.6 0.0 all-gather.3.cloned.1.call-update
  10.6 0.9 fusion.39
  11.5 0.1 broadcast_bitcast_fusion
  11.6 0.0 copy-done.2
  11.6 1.5 broadcast_multiply_fusion.x_ref
  13.1 76.0 %shard_map.46 = bf16[4,2048,128]{2,1,0:T(8,128)(2,1)} custom-call(bf16[32,256,128]{2,1,0:T(8,128)(2,1)} %broadcast_multiply_fusion.x_ref), custom_call_target="tpu_custom_call" | custom-call | bytes 4194304 | tf_op jit(solution)/shard_map/pallas_call | solution.py:182
  89.1 17.7 %all-gather.5.cloned.1.call-done = bf16[2048,1024]{1,0:T(8,128)(2,1)} async-done(((bf16[256,1024]{1,0:T(8,128)(2,1)}), bf16[2048,1024]{1,0:T(8,128)(2,1)}) %all-gather.5.cloned.1.call-update) | async-done | bytes 4194320 | tf_op jit(solution)/shard_map/all_gather | solution.py:99
  106.8 0.1 collective-permute-start
  106.9 0.0 copy-start.3
  106.9 5.3 %fusion.26 = bf16[4,1024,128]{1,2,0:T(8,128)(2,1)S(1)} fusion(bf16[4,2048,128]{2,1,0:T(8,128)(2,1)} %shard_map.46, bf16[2048,1024]{1,0:T(8,128)(2,1)} %all-gather.5.cloned.1.call-done), kind=kOutput, calls=%fused_computation.19 | convolution fusion | flops 2148007936 | bytes 7340032 | tf_op jit(solution)/shard_map/ml,pmn->pln/dot_general | solution.py:221
  112.2 2.1 collective-permute-done
  114.3 0.0 copy-done.3
  114.3 4.5 %fusion.23 = bf16[4,1024,128]{1,2,0:T(8,128)(2,1)S(1)} fusion(bf16[4,2048,128]{2,1,0:T(8,128)(2,1)S(1)} %copy-done.3, bf16[2048,1024]{1,0:T(8,128)(2,1)} %collective-permute-done), kind=kOutput, calls=%fused_computation.18 | convolution fusion | flops 2148007936 | bytes 7340032 | tf_op jit(solution)/shard_map/ml,pmn->pln/dot_general | solution.py:222
  118.9 0.8 maximum_select_fusion.1
  119.7 2.5 copy.7
  122.2 0.0 copy-start.1
  122.2 43.4 %shard_map.47 = bf16[4,8,16,2048]{3,2,1,0:T(8,128)(2,1)} custom-call(bf16[4,8,256,128]{3,2,1,0:T(8,128)(2,1)} %bitcast.34), custom_call_target="tpu_custom_call" | custom-call | bytes 4194304 | tf_op jit(solution)/shard_map/pallas_call | solution.py:182
  165.7 0.0 all-gather.3.cloned.1.call-done
  165.7 0.1 collective-permute-start.1
  165.8 0.0 copy-done.1
  165.8 0.5 collective-permute-start.2
  166.3 9.9 %collective-permute-done.1 = bf16[2048,1024]{1,0:T(8,128)(2,1)S(1)} collective-permute-done((bf16[2048,1024]{1,0:T(8,128)(2,1)}, bf16[2048,1024]{1,0:T(8,128)(2,1)S(1)}, u32[]{:S(2)}, u32[]{:S(2)}) %collective-permute-start.1) | collective-permute-done | bytes 4194336 | tf_op jit(solution)/shard_map/ppermute | solution.py:112
  176.2 11.2 %fusion.8.x_ref = bf16[4,128,2048]{2,1,0:T(8,128)(2,1)} fusion(bf16[4,128,2048]{2,1,0:T(8,128)(2,1)} %bitcast.35, bf16[2048,1024]{1,0:T(8,128)(2,1)S(1)} %collective-permute-done.1, bf16[2048,1024]{1,0:T(8,128)(2,1)} %all-gather.3.cloned.1.call-done, pred[]{:T(512)S(6)} %eq.2), kind=kOutput, calls=%fused_computation.8 | convolution fusion | flops 4333764608 | bytes 12582913 | tf_op jit(solution)/shard_map/pln,ns->pls/dot_general | solution.py:229
  187.4 50.4 %shard_map.48.x_ref = bf16[32,16,2048]{2,1,0:T(8,128)(2,1)} custom-call(bf16[4,128,2048]{2,1,0:T(8,128)(2,1)} %fusion.8.x_ref), custom_call_target="tpu_custom_call" | custom-call | bytes 4194304 | tf_op jit(solution)/shard_map/pallas_call | solution.py:182
  237.8 37.4 %shard_map.49 = bf16[32,256,128]{2,1,0:T(8,128)(2,1)} custom-call(bf16[32,16,2048]{2,1,0:T(8,128)(2,1)} %shard_map.48.x_ref), custom_call_target="tpu_custom_call" | custom-call | bytes 4194304 | tf_op jit(solution)/shard_map/pallas_call | solution.py:182
  275.3 0.0 copy-start.4
  275.3 4.2 %fusion.29 = f32[32,32]{1,0:T(8,128)S(1)} fusion(bf16[32,256,128]{2,1,0:T(8,128)(2,1)S(1)} %copy-done.1, bf16[32,256,128]{2,1,0:T(8,128)(2,1)} %shard_map.49), kind=kOutput, calls=%fused_computation.20 | convolution fusion | flops 67108864 | bytes 4198400 | tf_op jit(solution)/shard_map/pls,qls->pq/dot_general | solution.py:235
  279.5 0.0 collective-permute-done.2
  279.5 0.0 copy-done.4
  279.5 4.0 %broadcast_select_fusion.1 = (f32[32,32]{1,0:T(8,128)S(1)}, f32[32,32]{1,0:T(8,128)S(1)}) fusion(f32[32,32]{1,0:T(8,128)S(1)} %fusion.29, pred[]{:T(512)S(6)} %eq.2, bf16[32,256,128]{2,1,0:T(8,128)(2,1)} %collective-permute-done.2, bf16[32,256,128]{2,1,0:T(8,128)(2,1)S(1)} %copy-done.4), kind=kOutput, calls=%fused_computation.26 | convolution fusion | flops 67110912 | bytes 4206593 | tf_op jit(solution)/shard_map/pls,qls->pq/dot_general | solution.py:236
  283.5 0.7 pad_maximum_fusion.x_ref
  284.2 21.7 %shard_map.50 = f32[32,64]{1,0:T(8,128)} custom-call(f32[32,64]{1,0:T(8,128)} %pad_maximum_fusion.x_ref), custom_call_target="tpu_custom_call" | custom-call | tf_op jit(solution)/shard_map/pallas_call | solution.py:79
  305.9 1.3 broadcast_multiply_fusion.1
Async XLA Ops:
  6.5 1.2 copy-start
  6.5 5.0 %copy-start.2 = (bf16[32,256,128]{2,1,0:T(8,128)(2,1)S(1)}, bf16[32,256,128]{2,1,0:T(8,128)(2,1)}, u32[]{:S(2)}) copy-start(bf16[32,256,128]{2,1,0:T(8,128)(2,1)} %param.4) | copy-start | bytes 6291460
  6.5 100.3 %all-gather.5.cloned.1.call-start = ((), (), s32[]{:S(2)}) async-start(), calls=%async_computation.1 | async-start | bytes 4718592 | tf_op jit(solution)/shard_map/all_gather | solution.py:99
  8.7 157.0 %all-gather.3.cloned.1.call-start = ((), (), s32[]{:S(2)}) async-start(), calls=%async_computation | async-start | bytes 4718592 | tf_op jit(solution)/shard_map/all_gather | solution.py:99
  106.8 7.5 %collective-permute-start = (bf16[2048,1024]{1,0:T(8,128)(2,1)}, bf16[2048,1024]{1,0:T(8,128)(2,1)}, u32[]{:S(2)}, u32[]{:S(2)}) collective-permute-start(bf16[2048,1024]{1,0:T(8,128)(2,1)} %all-gather.5.cloned.1.call-done), channel_id=1, source_target_pairs={{0,128},{128,0},{1,129},{129,1},{2,130},{130,2},{3,131},{131,3},{4... | collective-permute-start | bytes 12582920 | tf_op jit(solution)/shard_map/ppermute | solution.py:112
  106.9 7.4 %copy-start.3 = (bf16[4,2048,128]{2,1,0:T(8,128)(2,1)S(1)}, bf16[4,2048,128]{2,1,0:T(8,128)(2,1)}, u32[]{:S(2)}) copy-start(bf16[4,2048,128]{2,1,0:T(8,128)(2,1)} %shard_map.46) | copy-start | bytes 6291460
  122.2 43.6 %copy-start.1 = (bf16[32,256,128]{2,1,0:T(8,128)(2,1)S(1)}, bf16[32,256,128]{2,1,0:T(8,128)(2,1)}, u32[]{:S(2)}) copy-start(bf16[32,256,128]{2,1,0:T(8,128)(2,1)} %broadcast_multiply_fusion.x_ref) | copy-start | bytes 6291460
  165.7 10.5 %collective-permute-start.1 = (bf16[2048,1024]{1,0:T(8,128)(2,1)}, bf16[2048,1024]{1,0:T(8,128)(2,1)S(1)}, u32[]{:S(2)}, u32[]{:S(2)}) collective-permute-start(bf16[2048,1024]{1,0:T(8,128)(2,1)} %all-gather.3.cloned.1.call-done), channel_id=1, source_target_pairs={{0,128},{128,0},{1,129},{129,1},{2,130},{130,2},{3,131},{131,3},{4... | collective-permute-start | bytes 12582920 | tf_op jit(solution)/shard_map/ppermute | solution.py:112
  165.8 113.7 %collective-permute-start.2 = (bf16[32,256,128]{2,1,0:T(8,128)(2,1)S(1)}, bf16[32,256,128]{2,1,0:T(8,128)(2,1)}, u32[]{:S(2)}, u32[]{:S(2)}) collective-permute-start(bf16[32,256,128]{2,1,0:T(8,128)(2,1)S(1)} %copy-done.1), channel_id=1, source_target_pairs={{0,128},{128,0},{1,129},{129,1},{2,130},{130,2},{3,131},{131,3},{4... | collective-permute-start | bytes 6291464 | tf_op jit(solution)/shard_map/ppermute | solution.py:17
  275.3 4.2 %copy-start.4 = (bf16[32,256,128]{2,1,0:T(8,128)(2,1)S(1)}, bf16[32,256,128]{2,1,0:T(8,128)(2,1)}, u32[]{:S(2)}) copy-start(bf16[32,256,128]{2,1,0:T(8,128)(2,1)} %shard_map.49) | copy-start | bytes 6291460
Sparse Core Ops, SparseCore 0:
  9.1 97.6 all-gather.4
  108.6 53.8 all-gather.2

commit v10 on v8

--- a/solution.py
+++ b/solution.py
@@ -214,10 +214,14 @@
     spread = lax.all_to_all(shaped, "col", split_axis=2, concat_axis=4, tiled=True)
     spread = spread.reshape(pieces, rows * jpart, nao)
     virt_own, spread = lax.optimization_barrier((virt_own, spread))
-    virt_all = join_halves(virt_own, swapped_core(virt_own), axis=1)
-    dressed = jnp.einsum(
-        "pln,ns->pls", spread, virt_all, preferred_element_type=jnp.float32
-    ).astype(jnp.bfloat16)
+    virt_other = swapped_core(virt_own)
+    dressed_own = jnp.einsum("pln,ns->pls", spread, virt_own, preferred_element_type=jnp.float32)
+    dressed_other = jnp.einsum(
+        "pln,ns->pls", spread, virt_other, preferred_element_type=jnp.float32
+    )
+    dressed = join_halves(
+        dressed_own.astype(jnp.bfloat16), dressed_other.astype(jnp.bfloat16), axis=2
+    )
     layered = dressed.reshape(pieces, rows, 1, jpart, cols, ncol)
     returned = lax.all_to_all(
         lax.all_to_all(layered, "row", split_axis=1, concat_axis=0, tiled=True),

time: 306 us -> 299 us (0.977)
  waiting for transfers between devices: 53.1 us -> 47.8 us
    ppermute x2, waiting for transfers between devices: 9.48 us -> 4.17 us  [swapped_core(): return lax.ppermute(value, 'aux', [(0, 1), (1, 0)])]
    dot_general x1 -> x2, matrix products: 10.3 us -> 7.68 us  [the longest x1 5.31 us: shards(): jnp.einsum('pln,ns->pls', spread, virt_own, preferred_element_type=jnp.fl...]
  transfers between devices with their start and end apart: 6 -> 6, of which waited for: 5 -> 5; matrix products, arithmetic and copies ran while one was open for 9% -> 11% of each run, Pallas kernels for 25% -> 25%
where the time goes in v10:
time: 299 us; the launch traced here: 298 us
  Pallas kernels  93.6 us (31%)
  blocking collectives  88.9 us (30%)
  waiting for transfers between devices  47.8 us (16%)
  matrix products  22.3 us (7%)
  local copies, waits for them, and re-layouts  18.7 us (6%)
  between operations  13.5 us (5%)
  starting transfers between devices  7.34 us (2%)
  other arithmetic  6.06 us (2%)
    pallas_call x1, Pallas kernels, exchange_rows(): pl.pallas_call(exchange_kernel, out_shape=jax.ShapeDtypeStruct(shape, x.d...  76 us
    all_to_all x1, blocking collectives, shards(): lax.all_to_all(layered, 'row', split_axis=1, concat_axis=0, tiled=True)  55.8 us
    all_to_all x1, blocking collectives, shards(): lax.all_to_all(shaped, 'col', split_axis=2, concat_axis=4, tiled=True)  33 us
    all_to_all x1, waiting for transfers between devices, shards(): lax.all_to_all(lax.all_to_all(layered, 'row', split_axis=1, concat_axis=0...  25.5 us
    all_gather x2, waiting for transfers between devices, gather_half(): return lax.all_gather(part, 'row', axis=0, tiled=True)  18 us
    pallas_call x1, Pallas kernels, doubling_sum(): pl.pallas_call(two_round_kernel, out_shape=jax.ShapeDtypeStruct(partial.s...  17.6 us
    all_to_all x1, starting transfers between devices, shards(): lax.all_to_all(lax.all_to_all(layered, 'row', split_axis=1, concat_axis=0...  7.13 us
  transfers between devices with their start and end apart: 6, of which 5 were waited for; matrix products, arithmetic and copies ran while one was open for 11% of the time, Pallas kernels for 25%

profile of v10, /device:TPU:24, one launch (start us, length us, event | category | flops | bytes accessed | tf_op | source)
XLA Modules:
  0.0 298.1 jit_solution(18046981941382287623)
XLA Ops:
  6.5 0.0 copy-start
  6.5 0.0 copy-start.2
  6.5 0.0 all-gather.5.cloned.1.call-start
  6.5 1.2 copy-done
  7.8 0.9 constant_dynamic-slice_fusion
  8.6 0.0 all-gather.5.cloned.1.call-update
  8.7 0.0 all-gather.3.cloned.1.call-start
  8.7 1.9 constant_dynamic-slice_fusion.1
  10.6 0.0 all-gather.3.cloned.1.call-update
  10.6 0.9 fusion.36
  11.5 0.1 broadcast_bitcast_fusion
  11.6 0.0 copy-done.2
  11.6 1.6 broadcast_multiply_fusion.x_ref
  13.1 76.0 %shard_map.46 = bf16[4,2048,128]{2,1,0:T(8,128)(2,1)} custom-call(bf16[32,256,128]{2,1,0:T(8,128)(2,1)} %broadcast_multiply_fusion.x_ref), custom_call_target="tpu_custom_call" | custom-call | bytes 4194304 | tf_op jit(solution)/shard_map/pallas_call | solution.py:172
  89.1 17.7 %all-gather.5.cloned.1.call-done = bf16[2048,1024]{1,0:T(8,128)(2,1)} async-done(((bf16[256,1024]{1,0:T(8,128)(2,1)}), bf16[2048,1024]{1,0:T(8,128)(2,1)}) %all-gather.5.cloned.1.call-update) | async-done | bytes 4194320 | tf_op jit(solution)/shard_map/all_gather | solution.py:99
  106.8 0.1 collective-permute-start
  106.9 0.0 copy-start.3
  106.9 5.3 %fusion.27 = bf16[4,1024,128]{1,2,0:T(8,128)(2,1)S(1)} fusion(bf16[4,2048,128]{2,1,0:T(8,128)(2,1)} %shard_map.46, bf16[2048,1024]{1,0:T(8,128)(2,1)} %all-gather.5.cloned.1.call-done), kind=kOutput, calls=%fused_computation.19 | convolution fusion | flops 2148007936 | bytes 7340032 | tf_op jit(solution)/shard_map/ml,pmn->pln/dot_general | solution.py:209
  112.2 2.1 collective-permute-done
  114.3 0.0 copy-done.3
  114.3 4.6 %fusion.24 = bf16[4,1024,128]{1,2,0:T(8,128)(2,1)S(1)} fusion(bf16[4,2048,128]{2,1,0:T(8,128)(2,1)S(1)} %copy-done.3, bf16[2048,1024]{1,0:T(8,128)(2,1)} %collective-permute-done), kind=kOutput, calls=%fused_computation.18 | convolution fusion | flops 2148007936 | bytes 7340032 | tf_op jit(solution)/shard_map/ml,pmn->pln/dot_general | solution.py:210
  118.9 0.8 maximum_select_fusion
  119.7 2.5 copy.27
  122.3 2.2 copy.28
  124.5 33.0 %all_to_all.48 = bf16[4,8,16,16,128]{4,3,1,0,2:T(8,128)(2,1)S(1)} all-to-all(bf16[4,8,16,16,128]{4,3,1,0,2:T(8,128)(2,1)S(1)} %copy.28), channel_id=1, replica_groups=mesh['aux'=2,'row'=8,'col'=16] {'col'}, dimensions={2} | all-to-all | bytes 4194304 | tf_op jit(solution)/shard_map/all_to_all | solution.py:214
  157.5 2.4 copy.29
  159.9 2.3 reshape.53
  162.2 0.0 copy-start.4
  162.2 0.3 all-gather.3.cloned.1.call-done
  162.6 0.0 collective-permute-start.1
  162.6 5.3 %fusion.18 = bf16[4,128,1024]{2,1,0:T(8,128)(2,1)S(1)} fusion(bf16[4,128,2048]{2,1,0:T(8,128)(2,1)} %reshape.53, bf16[2048,1024]{1,0:T(8,128)(2,1)} %all-gather.3.cloned.1.call-done), kind=kOutput, calls=%fused_computation.16 | convolution fusion | flops 2148007936 | bytes 7340032 | tf_op jit(solution)/shard_map/pln,ns->pls/dot_general | solution.py:218
  167.9 2.0 collective-permute-done.1
  169.9 0.0 copy-done.4
  169.9 2.4 fusion.21
  172.3 0.8 maximum_select_fusion.1
  173.1 0.6 copy.37
  173.8 0.6 copy.30
  174.4 55.8 %all_to_all.49 = bf16[4,8,1,16,16,128]{5,4,3,0,2,1:T(8,128)(2,1)S(1)} all-to-all(bf16[4,8,1,16,16,128]{5,4,3,0,2,1:T(8,128)(2,1)S(1)} %copy.30), channel_id=1, replica_groups=mesh['aux'=2,'row'=8,'col'=16] {'row'}, dimensions={1} | all-to-all | bytes 4194304 | tf_op jit(solution)/shard_map/all_to_all | solution.py:227
  230.2 1.9 copy.31
  232.1 0.0 copy-start.1
  232.1 7.1 %all-to-all-start.2 = ((bf16[32,1,1,16,16,128]{5,3,0,2,1,4:T(8,128)(2,1)}), bf16[32,1,1,16,16,128]{5,3,0,2,1,4:T(8,128)(2,1)}, u32[]{:S(2)}, u32[]{:S(2)}) async-start(bf16[32,1,1,16,16,128]{5,3,0,2,1,4:T(8,128)(2,1)} %copy.31), calls=%async_computation.2 | async-start | bytes 4194304 | tf_op jit(solution)/shard_map/all_to_all | solution.py:226
  239.2 0.0 copy-done.1
  239.2 0.1 collective-permute-start.2
  239.3 25.5 %all-to-all-done.2 = bf16[32,1,1,16,16,128]{5,3,0,2,1,4:T(8,128)(2,1)} async-done(((bf16[32,1,1,16,16,128]{5,3,0,2,1,4:T(8,128)(2,1)}), bf16[32,1,1,16,16,128]{5,3,0,2,1,4:T(8,128)(2,1)}, u32[]{:S(2)}, u32[]{:S(2)}) %all-to-all-start.2) | async-done | bytes 2097184 | tf_op jit(solution)/shard_map/all_to_all | solution.py:226
  264.8 2.1 copy.32
  267.0 1.5 fusion.30
  268.5 0.0 collective-permute-done.2
  268.5 3.2 %broadcast_select_fusion.1 = (f32[32,32]{1,0:T(8,128)S(1)}, f32[32,32]{1,0:T(8,128)S(1)}) fusion(f32[32,32]{1,0:T(8,128)S(1)} %fusion.30, pred[]{:T(512)S(6)} %eq.2, bf16[32,256,128]{2,0,1:T(8,128)(2,1)S(1)} %bitcast.68, bf16[32,256,128]{2,1,0:T(8,128)(2,1)} %collective-permute-done.2), kind=kOutput, calls=%fused_computation.26 | convolution fusion | flops 67110912 | bytes 4206593 | tf_op jit(solution)/shard_map/pls,qls->pq/dot_general | solution.py:236
  271.7 0.7 pad_maximum_fusion.x_ref
  272.4 17.6 %shard_map.47 = f32[32,64]{1,0:T(8,128)} custom-call(f32[32,64]{1,0:T(8,128)} %pad_maximum_fusion.x_ref), custom_call_target="tpu_custom_call" | custom-call | tf_op jit(solution)/shard_map/pallas_call | solution.py:79
  290.0 1.3 broadcast_multiply_fusion.1
Async XLA Ops:
  6.5 1.2 copy-start
  6.5 5.0 %copy-start.2 = (bf16[32,256,128]{2,1,0:T(8,128)(2,1)S(1)}, bf16[32,256,128]{2,1,0:T(8,128)(2,1)}, u32[]{:S(2)}) copy-start(bf16[32,256,128]{2,1,0:T(8,128)(2,1)} %param.4) | copy-start | bytes 6291460
  6.5 100.3 %all-gather.5.cloned.1.call-start = ((), (), s32[]{:S(2)}) async-start(), calls=%async_computation.4 | async-start | bytes 4718592 | tf_op jit(solution)/shard_map/all_gather | solution.py:99
  8.7 153.9 %all-gather.3.cloned.1.call-start = ((), (), s32[]{:S(2)}) async-start(), calls=%async_computation.3 | async-start | bytes 4718592 | tf_op jit(solution)/shard_map/all_gather | solution.py:99
  106.8 7.5 %collective-permute-start = (bf16[2048,1024]{1,0:T(8,128)(2,1)}, bf16[2048,1024]{1,0:T(8,128)(2,1)}, u32[]{:S(2)}, u32[]{:S(2)}) collective-permute-start(bf16[2048,1024]{1,0:T(8,128)(2,1)} %all-gather.5.cloned.1.call-done), channel_id=1, source_target_pairs={{0,128},{128,0},{1,129},{129,1},{2,130},{130,2},{3,131},{131,3},{4... | collective-permute-start | bytes 12582920 | tf_op jit(solution)/shard_map/ppermute | solution.py:112
  106.9 7.4 %copy-start.3 = (bf16[4,2048,128]{2,1,0:T(8,128)(2,1)S(1)}, bf16[4,2048,128]{2,1,0:T(8,128)(2,1)}, u32[]{:S(2)}) copy-start(bf16[4,2048,128]{2,1,0:T(8,128)(2,1)} %shard_map.46) | copy-start | bytes 6291460
  162.2 7.7 %copy-start.4 = (bf16[4,128,2048]{2,1,0:T(8,128)(2,1)S(1)}, bf16[4,128,2048]{2,1,0:T(8,128)(2,1)}, u32[]{:S(2)}) copy-start(bf16[4,128,2048]{2,1,0:T(8,128)(2,1)} %reshape.53) | copy-start | bytes 6291460
  162.6 7.4 %collective-permute-start.1 = (bf16[2048,1024]{1,0:T(8,128)(2,1)}, bf16[2048,1024]{1,0:T(8,128)(2,1)S(1)}, u32[]{:S(2)}, u32[]{:S(2)}) collective-permute-start(bf16[2048,1024]{1,0:T(8,128)(2,1)} %all-gather.3.cloned.1.call-done), channel_id=1, source_target_pairs={{0,128},{128,0},{1,129},{129,1},{2,130},{130,2},{3,131},{131,3},{4... | collective-permute-start | bytes 12582920 | tf_op jit(solution)/shard_map/ppermute | solution.py:112
  232.1 7.1 %copy-start.1 = (bf16[32,256,128]{2,1,0:T(8,128)(2,1)S(1)}, bf16[32,256,128]{2,1,0:T(8,128)(2,1)}, u32[]{:S(2)}) copy-start(bf16[32,256,128]{2,1,0:T(8,128)(2,1)} %broadcast_multiply_fusion.x_ref) | copy-start | bytes 6291460
  232.1 32.8 %all-to-all-start.2 = ((bf16[32,1,1,16,16,128]{5,3,0,2,1,4:T(8,128)(2,1)}), bf16[32,1,1,16,16,128]{5,3,0,2,1,4:T(8,128)(2,1)}, u32[]{:S(2)}, u32[]{:S(2)}) async-start(bf16[32,1,1,16,16,128]{5,3,0,2,1,4:T(8,128)(2,1)} %copy.31), calls=%async_computation.2 | async-start | bytes 4194304 | tf_op jit(solution)/shard_map/all_to_all | solution.py:226
  239.2 29.3 %collective-permute-start.2 = (bf16[32,256,128]{2,1,0:T(8,128)(2,1)S(1)}, bf16[32,256,128]{2,1,0:T(8,128)(2,1)}, u32[]{:S(2)}, u32[]{:S(2)}) collective-permute-start(bf16[32,256,128]{2,1,0:T(8,128)(2,1)S(1)} %copy-done.1), channel_id=1, source_target_pairs={{0,128},{128,0},{1,129},{129,1},{2,130},{130,2},{3,131},{131,3},{4... | collective-permute-start | bytes 6291464 | tf_op jit(solution)/shard_map/ppermute | solution.py:17
Sparse Core Ops, SparseCore 0:
  9.1 97.6 all-gather.4
  108.6 53.9 all-gather.2

commit v11 on v9

--- a/solution.py
+++ b/solution.py
@@ -222,18 +222,39 @@
     half_other = jnp.einsum("ml,pmn->pln", occ_other, moved, preferred_element_type=jnp.float32)
     half = join_halves(half_own.astype(jnp.bfloat16), half_other.astype(jnp.bfloat16), axis=1)
     jpart = mrow // cols
-    shaped = half.reshape(pieces, rows, mrow, ncol)
-    spread = exchange(shaped, "col", 2, 3, 3).reshape(pieces, rows * jpart, nao)
+    shaped = half.reshape(pieces, rows, cols, jpart, ncol)
+    spread = lax.all_to_all(shaped, "col", split_axis=2, concat_axis=4, tiled=True)
+    spread = spread.reshape(pieces, rows * jpart, nao)
     virt_own, spread = lax.optimization_barrier((virt_own, spread))
-    virt_all = join_halves(virt_own, swapped_core(virt_own), axis=1)
-    dressed = jnp.einsum(
-        "pln,ns->pls", spread, virt_all, preferred_element_type=jnp.float32
-    ).astype(jnp.bfloat16)
-    by_row = exchange(dressed, "row", 1, 0, 2)
-    aligned = exchange(by_row, "col", 2, 1, 4)
+    virt_other = swapped_core(virt_own)
     theirs = swapped(screened, "aux", 0)
-    with_mine = jnp.einsum("pls,qls->pq", aligned, screened, preferred_element_type=jnp.float32)
-    with_theirs = jnp.einsum("pls,qls->pq", aligned, theirs, preferred_element_type=jnp.float32)
+    chunks = 2
+    per = pieces // chunks
+    mine_parts, theirs_parts = [], []
+    for chunk in range(chunks):
+        part = spread[chunk * per:(chunk + 1) * per]
+        dressed_own = jnp.einsum("pln,ns->pls", part, virt_own, preferred_element_type=jnp.float32)
+        dressed_other = jnp.einsum(
+            "pln,ns->pls", part, virt_other, preferred_element_type=jnp.float32
+        )
+        dressed = join_halves(
+            dressed_own.astype(jnp.bfloat16), dressed_other.astype(jnp.bfloat16), axis=2
+        )
+        by_row = exchange(dressed, "row", 1, 0, 2).reshape(rows * per, 1, 1, jpart, cols, ncol)
+        returned = lax.all_to_all(by_row, "col", split_axis=4, concat_axis=2, tiled=True)
+        aligned = returned.reshape(rows * per, mrow, ncol)
+        mine_parts.append(
+            jnp.einsum("pls,qls->pq", aligned, screened, preferred_element_type=jnp.float32)
+        )
+        theirs_parts.append(
+            jnp.einsum("pls,qls->pq", aligned, theirs, preferred_element_type=jnp.float32)
+        )
+
+    def in_order(parts):
+        stacked = jnp.stack(parts).reshape(chunks, rows, per, pdev)
+        return stacked.transpose(1, 0, 2, 3).reshape(pdev, pdev)
+
+    with_mine, with_theirs = in_order(mine_parts), in_order(theirs_parts)
     first_half = jnp.where(aux_idx == 0, with_mine, with_theirs)
     second_half = jnp.where(aux_idx == 0, with_theirs, with_mine)
     partial_chi = jnp.concatenate([first_half, second_half], axis=1)

time: 316 us -> 308 us (0.975)
  Pallas kernels: 229 us -> 152 us
  blocking collectives: 0 us -> 33 us
  local copies, waits for them, and re-layouts: 6.61 us -> 23.3 us
  starting transfers between devices: 0.69 us -> 14.6 us
  waiting for transfers between devices: 29.7 us -> 34 us
    pallas_call x4 -> x3, Pallas kernels: 207 us -> 133 us  [exchange(): pl.pallas_call(functools.partial(exchange_kernel, mesh_axis, split_axis,...]
    all_to_all x0 -> x1, blocking collectives: none -> 33 us  [shards(): lax.all_to_all(shaped, 'col', split_axis=2, concat_axis=4, tiled=True)]
    all_to_all x0 -> x2, starting transfers between devices: none -> 14.4 us  [shards(): lax.all_to_all(by_row, 'col', split_axis=4, concat_axis=2, tiled=True)]
    all_to_all x0 -> x2, waiting for transfers between devices: none -> 11.9 us  [shards(): lax.all_to_all(by_row, 'col', split_axis=4, concat_axis=2, tiled=True)]
    ppermute x2, waiting for transfers between devices: 12 us -> 4.04 us  [swapped_core(): return lax.ppermute(value, 'aux', [(0, 1), (1, 0)])]
    all_to_all x0 -> x3, local copies, waits for them, and re-layouts: none -> 6.52 us  [the longest x2 4.08 us: shards(): lax.all_to_all(by_row, 'col', split_axis=4, concat_axis=2, tiled=True)]
    reshape x0 -> x3, local copies, waits for them, and re-layouts: none -> 4.82 us  [the longest x2 2.51 us: shards(): exchange(dressed, 'row', 1, 0, 2)]
    dot_general x1 -> x4, matrix products: 11.2 us -> 7.77 us  [the longest x2 5.19 us: shards(): jnp.einsum('pln,ns->pls', part, virt_own, preferred_element_type=jnp.floa...]
  transfers between devices with their start and end apart: 5 -> 7, of which waited for: 3 -> 5; matrix products, arithmetic and copies ran while one was open for 11% -> 13% of each run, Pallas kernels for 66% -> 34%
where the time goes in v11:
time: 308 us; the launch traced here: 306 us
  Pallas kernels  152 us (49%)
  waiting for transfers between devices  34 us (11%)
  blocking collectives  33 us (11%)
  matrix products  28.1 us (9%)
  local copies, waits for them, and re-layouts  23.3 us (8%)
  starting transfers between devices  14.6 us (5%)
  between operations  13.6 us (4%)
  other arithmetic  7.41 us (2%)
    pallas_call x3, Pallas kernels, exchange(): pl.pallas_call(functools.partial(exchange_kernel, mesh_axis, split_axis,...  133 us
    all_to_all x1, blocking collectives, shards(): lax.all_to_all(shaped, 'col', split_axis=2, concat_axis=4, tiled=True)  33 us
    pallas_call x1, Pallas kernels, doubling_sum(): pl.pallas_call(two_round_kernel, out_shape=jax.ShapeDtypeStruct(partial.s...  18.7 us
    all_gather x2, waiting for transfers between devices, gather_half(): return lax.all_gather(part, 'row', axis=0, tiled=True)  18 us
    all_to_all x2, starting transfers between devices, shards(): lax.all_to_all(by_row, 'col', split_axis=4, concat_axis=2, tiled=True)  14.4 us
    all_to_all x2, waiting for transfers between devices, shards(): lax.all_to_all(by_row, 'col', split_axis=4, concat_axis=2, tiled=True)  11.9 us
    dot_general x2, matrix products, shards(): jnp.einsum('pls,qls->pq', aligned, theirs, preferred_element_type=jnp.flo...  6.83 us
  transfers between devices with their start and end apart: 7, of which 5 were waited for; matrix products, arithmetic and copies ran while one was open for 13% of the time, Pallas kernels for 34%

profile of v11, /device:TPU:24, one launch (start us, length us, event | category | flops | bytes accessed | tf_op | source)
XLA Modules:
  0.0 306.1 jit_solution(1175475772130774863)
XLA Ops:
  6.5 0.0 copy-start
  6.5 0.0 copy-start.2
  6.5 0.0 all-gather.5.cloned.1.call-start
  6.5 1.2 copy-done
  7.8 0.9 constant_dynamic-slice_fusion
  8.6 0.0 all-gather.5.cloned.1.call-update
  8.7 0.0 all-gather.3.cloned.1.call-start
  8.7 1.9 constant_dynamic-slice_fusion.1
  10.6 0.0 all-gather.3.cloned.1.call-update
  10.6 0.9 fusion.64
  11.5 0.1 broadcast_bitcast_fusion
  11.6 0.0 copy-done.2
  11.6 1.6 broadcast_multiply_fusion.x_ref
  13.2 76.0 %shard_map.46 = bf16[4,2048,128]{2,1,0:T(8,128)(2,1)} custom-call(bf16[32,256,128]{2,1,0:T(8,128)(2,1)} %broadcast_multiply_fusion.x_ref), custom_call_target="tpu_custom_call" | custom-call | bytes 4194304 | tf_op jit(solution)/shard_map/pallas_call | solution.py:182
  89.2 17.7 %all-gather.5.cloned.1.call-done = bf16[2048,1024]{1,0:T(8,128)(2,1)} async-done(((bf16[256,1024]{1,0:T(8,128)(2,1)}), bf16[2048,1024]{1,0:T(8,128)(2,1)}) %all-gather.5.cloned.1.call-update) | async-done | bytes 4194320 | tf_op jit(solution)/shard_map/all_gather | solution.py:99
  106.9 0.1 collective-permute-start
  107.0 0.0 copy-start.3
  107.0 5.3 %fusion.33 = bf16[4,1024,128]{1,2,0:T(8,128)(2,1)S(1)} fusion(bf16[4,2048,128]{2,1,0:T(8,128)(2,1)} %shard_map.46, bf16[2048,1024]{1,0:T(8,128)(2,1)} %all-gather.5.cloned.1.call-done), kind=kOutput, calls=%fused_computation.28 | convolution fusion | flops 2148007936 | bytes 7340032 | tf_op jit(solution)/shard_map/ml,pmn->pln/dot_general | solution.py:221
  112.3 2.1 collective-permute-done
  114.4 0.0 copy-done.3
  114.4 4.6 %fusion.30 = bf16[4,1024,128]{1,2,0:T(8,128)(2,1)S(1)} fusion(bf16[4,2048,128]{2,1,0:T(8,128)(2,1)S(1)} %copy-done.3, bf16[2048,1024]{1,0:T(8,128)(2,1)} %collective-permute-done), kind=kOutput, calls=%fused_computation.27 | convolution fusion | flops 2148007936 | bytes 7340032 | tf_op jit(solution)/shard_map/ml,pmn->pln/dot_general | solution.py:222
  119.0 0.8 maximum_select_fusion
  119.8 2.6 copy.32
  122.4 2.2 copy.33
  124.6 33.0 %all_to_all.45 = bf16[4,8,16,16,128]{4,3,1,0,2:T(8,128)(2,1)S(1)} all-to-all(bf16[4,8,16,16,128]{4,3,1,0,2:T(8,128)(2,1)S(1)} %copy.33), channel_id=1, replica_groups=mesh['aux'=2,'row'=8,'col'=16] {'col'}, dimensions={2} | all-to-all | bytes 4194304 | tf_op jit(solution)/shard_map/all_to_all | solution.py:226
  157.6 2.4 copy.34
  160.0 2.3 reshape.79
  162.3 0.0 copy-start.4
  162.3 0.3 all-gather.3.cloned.1.call-done
  162.6 0.0 copy-start.6
  162.6 0.0 collective-permute-start.1
  162.6 3.9 %fusion.39 = bf16[2,128,1024]{2,1,0:T(8,128)(2,1)S(1)} fusion(bf16[4,128,2048]{2,1,0:T(8,128)(2,1)} %reshape.79, bf16[2048,1024]{1,0:T(8,128)(2,1)} %all-gather.3.cloned.1.call-done), kind=kOutput, calls=%fused_computation.30 | convolution fusion | flops 1074003968 | bytes 6815744 | tf_op jit(solution)/shard_map/pln,ns->pls/dot_general | solution.py:236
  166.6 0.0 copy-done.4
  166.6 0.2 copy-done.6
  166.8 1.3 fusion.36
  168.1 1.9 collective-permute-done.1
  170.0 1.3 fusion.45
  171.3 1.3 fusion.42
  172.6 2.1 maximum_select_fusion.1
  174.7 28.1 %shard_map.47 = bf16[16,16,2048]{2,1,0:T(8,128)(2,1)} custom-call(bf16[2,128,2048]{2,1,0:T(8,128)(2,1)} %get-tuple-element.15.x_ref), custom_call_target="tpu_custom_call" | custom-call | bytes 2097152 | tf_op jit(solution)/shard_map/pallas_call | solution.py:182
  202.9 1.4 copy.55
  204.3 0.0 copy-start.1
  204.3 1.2 copy.35
  205.6 7.2 %all-to-all-start.1 = ((bf16[16,1,1,16,16,128]{5,3,0,2,1,4:T(8,128)(2,1)}), bf16[16,1,1,16,16,128]{5,3,0,2,1,4:T(8,128)(2,1)}, u32[]{:S(2)}, u32[]{:S(2)}) async-start(bf16[16,1,1,16,16,128]{5,3,0,2,1,4:T(8,128)(2,1)} %copy.35), calls=%async_computation.1 | async-start | bytes 2097152 | tf_op jit(solution)/shard_map/all_to_all | solution.py:244
  212.8 0.0 copy-done.1
  212.8 0.1 collective-permute-start.2
  212.9 29.1 %shard_map.48 = bf16[16,16,2048]{2,1,0:T(8,128)(2,1)} custom-call(bf16[2,128,2048]{2,1,0:T(8,128)(2,1)} %get-tuple-element.16.x_ref), custom_call_target="tpu_custom_call" | custom-call | bytes 2097152 | tf_op jit(solution)/shard_map/pallas_call | solution.py:182
  242.1 1.4 copy.56
  243.5 1.3 copy.39
  244.8 0.0 all-to-all-done.1
  244.8 7.2 %all-to-all-start.2 = ((bf16[16,1,1,16,16,128]{5,3,0,2,1,4:T(8,128)(2,1)}), bf16[16,1,1,16,16,128]{5,3,0,2,1,4:T(8,128)(2,1)}, u32[]{:S(2)}, u32[]{:S(2)}) async-start(bf16[16,1,1,16,16,128]{5,3,0,2,1,4:T(8,128)(2,1)} %copy.39), calls=%async_computation.2 | async-start | bytes 2097152 | tf_op jit(solution)/shard_map/all_to_all | solution.py:244
  252.0 2.5 copy.36
  254.5 11.9 %all-to-all-done.2 = bf16[16,1,1,16,16,128]{5,3,0,2,1,4:T(8,128)(2,1)} async-done(((bf16[16,1,1,16,16,128]{5,3,0,2,1,4:T(8,128)(2,1)}), bf16[16,1,1,16,16,128]{5,3,0,2,1,4:T(8,128)(2,1)}, u32[]{:S(2)}, u32[]{:S(2)}) %all-to-all-start.2) | async-done | bytes 1048608 | tf_op jit(solution)/shard_map/all_to_all | solution.py:244
  266.4 0.0 copy-start.5
  266.4 1.6 copy.40
  268.0 0.0 copy-done.5
  268.0 1.8 fusion.48
  269.8 1.8 fusion.51
  271.6 0.0 collective-permute-done.2
  271.6 3.4 %fusion.54 = f32[1,8,2,32]{3,1,2,0:T(8,128)S(1)} fusion(bf16[32,256,128]{2,1,0:T(8,128)(2,1)} %collective-permute-done.2, bf16[8,2,256,128]{3,2,1,0:T(8,128)(2,1)S(1)} %bitcast.121), kind=kOutput, calls=%fused_computation.35 | convolution fusion | flops 33554432 | bytes 3147776 | tf_op jit(solution)/shard_map/pls,qls->pq/dot_general | solution.py:250
  275.1 3.4 %fusion.57 = f32[1,8,2,32]{3,1,2,0:T(8,128)S(1)} fusion(bf16[32,256,128]{2,1,0:T(8,128)(2,1)} %collective-permute-done.2, bf16[8,2,256,128]{3,2,1,0:T(8,128)(2,1)S(1)} %bitcast.123), kind=kOutput, calls=%fused_computation.36 | convolution fusion | flops 33554432 | bytes 3147776 | tf_op jit(solution)/shard_map/pls,qls->pq/dot_general | solution.py:250
  278.5 0.7 pad_maximum_fusion.2.x_ref
  279.2 18.7 %shard_map.49 = f32[32,64]{1,0:T(8,128)} custom-call(f32[32,64]{1,0:T(8,128)} %pad_maximum_fusion.2.x_ref), custom_call_target="tpu_custom_call" | custom-call | tf_op jit(solution)/shard_map/pallas_call | solution.py:79
  297.9 1.3 broadcast_multiply_fusion.1
  (3 shorter events, 0.0 us)
Async XLA Ops:
  6.5 1.2 copy-start
  6.5 5.1 %copy-start.2 = (bf16[32,256,128]{2,1,0:T(8,128)(2,1)S(1)}, bf16[32,256,128]{2,1,0:T(8,128)(2,1)}, u32[]{:S(2)}) copy-start(bf16[32,256,128]{2,1,0:T(8,128)(2,1)} %param.4) | copy-start | bytes 6291460
  6.5 100.4 %all-gather.5.cloned.1.call-start = ((), (), s32[]{:S(2)}) async-start(), calls=%async_computation.4 | async-start | bytes 4718592 | tf_op jit(solution)/shard_map/all_gather | solution.py:99
  8.7 154.0 %all-gather.3.cloned.1.call-start = ((), (), s32[]{:S(2)}) async-start(), calls=%async_computation.3 | async-start | bytes 4718592 | tf_op jit(solution)/shard_map/all_gather | solution.py:99
  106.9 7.5 %collective-permute-start = (bf16[2048,1024]{1,0:T(8,128)(2,1)}, bf16[2048,1024]{1,0:T(8,128)(2,1)}, u32[]{:S(2)}, u32[]{:S(2)}) collective-permute-start(bf16[2048,1024]{1,0:T(8,128)(2,1)} %all-gather.5.cloned.1.call-done), channel_id=1, source_target_pairs={{0,128},{128,0},{1,129},{129,1},{2,130},{130,2},{3,131},{131,3},{4... | collective-permute-start | bytes 12582920 | tf_op jit(solution)/shard_map/ppermute | solution.py:112
  107.0 7.4 %copy-start.3 = (bf16[4,2048,128]{2,1,0:T(8,128)(2,1)S(1)}, bf16[4,2048,128]{2,1,0:T(8,128)(2,1)}, u32[]{:S(2)}) copy-start(bf16[4,2048,128]{2,1,0:T(8,128)(2,1)} %shard_map.46) | copy-start | bytes 6291460
  162.3 4.2 %copy-start.4 = (bf16[4,128,2048]{2,1,0:T(8,128)(2,1)S(1)}, bf16[4,128,2048]{2,1,0:T(8,128)(2,1)}, u32[]{:S(2)}) copy-start(bf16[4,128,2048]{2,1,0:T(8,128)(2,1)} %reshape.79) | copy-start | bytes 6291460
  162.6 4.2 %copy-start.6 = (bf16[2048,1024]{1,0:T(8,128)(2,1)S(1)}, bf16[2048,1024]{1,0:T(8,128)(2,1)}, u32[]{:S(2)}) copy-start(bf16[2048,1024]{1,0:T(8,128)(2,1)} %all-gather.3.cloned.1.call-done) | copy-start | bytes 12582916
  162.6 7.4 %collective-permute-start.1 = (bf16[2048,1024]{1,0:T(8,128)(2,1)}, bf16[2048,1024]{1,0:T(8,128)(2,1)S(1)}, u32[]{:S(2)}, u32[]{:S(2)}) collective-permute-start(bf16[2048,1024]{1,0:T(8,128)(2,1)} %all-gather.3.cloned.1.call-done), channel_id=1, source_target_pairs={{0,128},{128,0},{1,129},{129,1},{2,130},{130,2},{3,131},{131,3},{4... | collective-permute-start | bytes 12582920 | tf_op jit(solution)/shard_map/ppermute | solution.py:112
  204.3 8.5 %copy-start.1 = (bf16[32,256,128]{2,1,0:T(8,128)(2,1)S(1)}, bf16[32,256,128]{2,1,0:T(8,128)(2,1)}, u32[]{:S(2)}) copy-start(bf16[32,256,128]{2,1,0:T(8,128)(2,1)} %broadcast_multiply_fusion.x_ref) | copy-start | bytes 6291460
  205.6 39.2 %all-to-all-start.1 = ((bf16[16,1,1,16,16,128]{5,3,0,2,1,4:T(8,128)(2,1)}), bf16[16,1,1,16,16,128]{5,3,0,2,1,4:T(8,128)(2,1)}, u32[]{:S(2)}, u32[]{:S(2)}) async-start(bf16[16,1,1,16,16,128]{5,3,0,2,1,4:T(8,128)(2,1)} %copy.35), calls=%async_computation.1 | async-start | bytes 2097152 | tf_op jit(solution)/shard_map/all_to_all | solution.py:244
  212.8 58.8 %collective-permute-start.2 = (bf16[32,256,128]{2,1,0:T(8,128)(2,1)S(1)}, bf16[32,256,128]{2,1,0:T(8,128)(2,1)}, u32[]{:S(2)}, u32[]{:S(2)}) collective-permute-start(bf16[32,256,128]{2,1,0:T(8,128)(2,1)S(1)} %copy-done.1), channel_id=1, source_target_pairs={{0,128},{128,0},{1,129},{129,1},{2,130},{130,2},{3,131},{131,3},{4... | collective-permute-start | bytes 6291464 | tf_op jit(solution)/shard_map/ppermute | solution.py:17
  244.8 21.6 %all-to-all-start.2 = ((bf16[16,1,1,16,16,128]{5,3,0,2,1,4:T(8,128)(2,1)}), bf16[16,1,1,16,16,128]{5,3,0,2,1,4:T(8,128)(2,1)}, u32[]{:S(2)}, u32[]{:S(2)}) async-start(bf16[16,1,1,16,16,128]{5,3,0,2,1,4:T(8,128)(2,1)} %copy.39), calls=%async_computation.2 | async-start | bytes 2097152 | tf_op jit(solution)/shard_map/all_to_all | solution.py:244
  266.4 1.6 copy-start.5
Sparse Core Ops, SparseCore 0:
  9.1 97.7 all-gather.4
  108.7 53.9 all-gather.2

commit v12 on v9

--- a/solution.py
+++ b/solution.py
@@ -196,6 +196,16 @@
     )(x)
 
 
+def gather_occ_rows(local):
+    rows, cols = lax.axis_size("row"), lax.axis_size("col")
+    width = local.shape[1] // cols
+    piece = lax.dynamic_slice_in_dim(local, lax.axis_index("col") * width, width, axis=1)
+    column = exchange(jnp.tile(piece, (rows, 1)), "row", 0, 0, 5)
+    height = column.shape[0] // 2
+    part = lax.dynamic_slice_in_dim(column, lax.axis_index("aux") * height, height, axis=0)
+    return lax.all_gather(part, "col", axis=1, tiled=True)
+
+
 def shards(coulomb, occupied, virtual, tile_mask):
     rows = lax.axis_size("row")
     cols = lax.axis_size("col")
@@ -213,24 +223,41 @@
         jnp.bfloat16
     )
     screened = coulomb * local_mask[None]
-    occ_own, virt_own = gather_half(occupied), gather_half(virtual)
+    occ_rows = gather_occ_rows(occupied)
+    virt_own = gather_half(virtual)
     moved = exchange(screened, "row", 0, 1, 1)
-    occ_own, moved = lax.optimization_barrier((occ_own, moved))
+    occ_rows, moved = lax.optimization_barrier((occ_rows, moved))
     pieces = moved.shape[0]
-    occ_other = swapped_core(occ_own)
-    half_own = jnp.einsum("ml,pmn->pln", occ_own, moved, preferred_element_type=jnp.float32)
-    half_other = jnp.einsum("ml,pmn->pln", occ_other, moved, preferred_element_type=jnp.float32)
-    half = join_halves(half_own.astype(jnp.bfloat16), half_other.astype(jnp.bfloat16), axis=1)
+    occ_other = swapped_core(occ_rows)
+    depth = occ_rows.shape[0]
+    mine = lax.dynamic_slice_in_dim(moved, aux_idx * depth, depth, axis=1)
+    other = lax.dynamic_slice_in_dim(moved, (1 - aux_idx) * depth, depth, axis=1)
+    half = (
+        jnp.einsum("ml,pmn->pln", occ_rows, mine, preferred_element_type=jnp.float32)
+        + jnp.einsum("ml,pmn->pln", occ_other, other, preferred_element_type=jnp.float32)
+    ).astype(jnp.bfloat16)
     jpart = mrow // cols
-    shaped = half.reshape(pieces, rows, mrow, ncol)
-    spread = exchange(shaped, "col", 2, 3, 3).reshape(pieces, rows * jpart, nao)
+    shaped = half.reshape(pieces, rows, cols, jpart, ncol)
+    spread = lax.all_to_all(shaped, "col", split_axis=2, concat_axis=4, tiled=True)
+    spread = spread.reshape(pieces, rows * jpart, nao)
     virt_own, spread = lax.optimization_barrier((virt_own, spread))
-    virt_all = join_halves(virt_own, swapped_core(virt_own), axis=1)
-    dressed = jnp.einsum(
-        "pln,ns->pls", spread, virt_all, preferred_element_type=jnp.float32
-    ).astype(jnp.bfloat16)
-    by_row = exchange(dressed, "row", 1, 0, 2)
-    aligned = exchange(by_row, "col", 2, 1, 4)
+    virt_other = swapped_core(virt_own)
+    dressed_own = jnp.einsum("pln,ns->pls", spread, virt_own, preferred_element_type=jnp.float32)
+    dressed_other = jnp.einsum(
+        "pln,ns->pls", spread, virt_other, preferred_element_type=jnp.float32
+    )
+    dressed = join_halves(
+        dressed_own.astype(jnp.bfloat16), dressed_other.astype(jnp.bfloat16), axis=2
+    )
+    layered = dressed.reshape(pieces, rows, 1, jpart, cols, ncol)
+    returned = lax.all_to_all(
+        lax.all_to_all(layered, "row", split_axis=1, concat_axis=0, tiled=True),
+        "col",
+        split_axis=4,
+        concat_axis=2,
+        tiled=True,
+    )
+    aligned = returned.reshape(pdev, mrow, ncol)
     theirs = swapped(screened, "aux", 0)
     with_mine = jnp.einsum("pls,qls->pq", aligned, screened, preferred_element_type=jnp.float32)
     with_theirs = jnp.einsum("pls,qls->pq", aligned, theirs, preferred_element_type=jnp.float32)

time: 316 us -> 287 us (0.908)
  Pallas kernels: 229 us -> 86.6 us
  blocking collectives: 0 us -> 87.2 us
  waiting for transfers between devices: 29.7 us -> 42.8 us
  local copies, waits for them, and re-layouts: 6.61 us -> 18.1 us
  starting transfers between devices: 0.69 us -> 7.49 us
  matrix products: 29.3 us -> 25.5 us
    pallas_call x4 -> x2, Pallas kernels: 207 us -> 69.5 us  [exchange(): pl.pallas_call(functools.partial(exchange_kernel, mesh_axis, split_axis,...]
    all_to_all x0 -> x2, blocking collectives: none -> 87.2 us  [the longest x1 55.6 us: shards(): lax.all_to_all(layered, 'row', split_axis=1, concat_axis=0, tiled=True)]
    all_to_all x0 -> x1, waiting for transfers between devices: none -> 25.7 us  [shards(): lax.all_to_all(lax.all_to_all(layered, 'row', split_axis=1, concat_axis=0...]
    all_gather x2 -> x1, waiting for transfers between devices: 17.7 us -> 3.03 us  [gather_half(): return lax.all_gather(part, 'row', axis=0, tiled=True)]
    all_gather x0 -> x1, waiting for transfers between devices: none -> 9.39 us  [gather_occ_rows(): return lax.all_gather(part, 'col', axis=1, tiled=True)]
    all_to_all x0 -> x1, starting transfers between devices: none -> 7.34 us  [shards(): lax.all_to_all(lax.all_to_all(layered, 'row', split_axis=1, concat_axis=0...]
    ppermute x2, waiting for transfers between devices: 12 us -> 4.65 us  [swapped_core(): return lax.ppermute(value, 'aux', [(0, 1), (1, 0)])]
    all_to_all x0 -> x3, local copies, waits for them, and re-layouts: none -> 6.43 us  [the longest x1 2.43 us: shards(): lax.all_to_all(shaped, 'col', split_axis=2, concat_axis=4, tiled=True)]
  transfers between devices with their start and end apart: 5 -> 6, of which waited for: 3 -> 5; matrix products, arithmetic and copies ran while one was open for 11% -> 11% of each run, Pallas kernels for 66% -> 17%
where the time goes in v12:
time: 287 us; the launch traced here: 286 us
  blocking collectives  87.2 us (30%)
  Pallas kernels  86.6 us (30%)
  waiting for transfers between devices  42.8 us (15%)
  matrix products  25.5 us (9%)
  local copies, waits for them, and re-layouts  18.1 us (6%)
  between operations  13.5 us (5%)
  starting transfers between devices  7.49 us (3%)
  other arithmetic  5.25 us (2%)
    pallas_call x2, Pallas kernels, exchange(): pl.pallas_call(functools.partial(exchange_kernel, mesh_axis, split_axis,...  69.5 us
    all_to_all x1, blocking collectives, shards(): lax.all_to_all(layered, 'row', split_axis=1, concat_axis=0, tiled=True)  55.6 us
    all_to_all x1, blocking collectives, shards(): lax.all_to_all(shaped, 'col', split_axis=2, concat_axis=4, tiled=True)  31.6 us
    all_to_all x1, waiting for transfers between devices, shards(): lax.all_to_all(lax.all_to_all(layered, 'row', split_axis=1, concat_axis=0...  25.7 us
    pallas_call x1, Pallas kernels, doubling_sum(): pl.pallas_call(two_round_kernel, out_shape=jax.ShapeDtypeStruct(partial.s...  17.1 us
    all_gather x1, waiting for transfers between devices, gather_occ_rows(): return lax.all_gather(part, 'col', axis=1, tiled=True)  9.39 us
    all_to_all x1, starting transfers between devices, shards(): lax.all_to_all(lax.all_to_all(layered, 'row', split_axis=1, concat_axis=0...  7.34 us
    dot_general x1, matrix products, shards(): jnp.einsum('ml,pmn->pln', occ_other, other, preferred_element_type=jnp.fl...  5.91 us
  transfers between devices with their start and end apart: 6, of which 5 were waited for; matrix products, arithmetic and copies ran while one was open for 11% of the time, Pallas kernels for 17%

profile of v12, /device:TPU:24, one launch (start us, length us, event | category | flops | bytes accessed | tf_op | source)
XLA Modules:
  0.0 286.4 jit_solution(10902471369126023673)
XLA Ops:
  6.5 0.0 copy-start
  6.5 0.0 copy-start.3
  6.5 0.0 all-gather.5.cloned.1.call-start
  6.5 1.0 constant_dynamic-slice_fusion.1
  7.5 0.9 tile.4
  8.4 20.4 %shard_map.46 = bf16[2048,128]{1,0:T(8,128)(2,1)} custom-call(bf16[2048,128]{1,0:T(8,128)(2,1)} %bitcast.62), custom_call_target="tpu_custom_call" | custom-call | bytes 1048576 | tf_op jit(solution)/shard_map/pallas_call | solution.py:182
  28.8 1.7 constant_dynamic-slice_fusion
  30.5 0.0 all-gather.5.cloned.1.call-update
  30.5 0.0 all-gather.3.cloned.1.call-start
  30.5 0.0 copy-done
  30.6 0.8 constant_dynamic-slice_fusion.2
  31.4 0.0 all-gather.3.cloned.1.call-update
  31.4 0.9 fusion.33
  32.3 0.1 broadcast_bitcast_fusion
  32.4 0.0 copy-done.3
  32.4 1.6 broadcast_multiply_fusion.x_ref
  34.0 49.1 %shard_map.47 = bf16[4,2048,128]{2,1,0:T(8,128)(2,1)} custom-call(bf16[32,256,128]{2,1,0:T(8,128)(2,1)} %broadcast_multiply_fusion.x_ref), custom_call_target="tpu_custom_call" | custom-call | bytes 4194304 | tf_op jit(solution)/shard_map/pallas_call | solution.py:182
  83.1 9.4 %all-gather.5.cloned.1.call-done = bf16[1024,2048]{1,0:T(8,128)(2,1)} async-done(((bf16[1024,128]{1,0:T(8,128)(2,1)}), bf16[1024,2048]{1,0:T(8,128)(2,1)}) %all-gather.5.cloned.1.call-update) | async-done | bytes 4194320 | tf_op jit(solution)/shard_map/all_gather | solution.py:206
  92.5 0.0 collective-permute-start
  92.5 0.0 copy-start.1
  92.5 5.0 %fusion.6 = f32[4,128,2048]{2,1,0:T(8,128)S(1)} fusion(bf16[1024,2048]{1,0:T(8,128)(2,1)} %all-gather.5.cloned.1.call-done, bf16[4,2048,128]{2,1,0:T(8,128)(2,1)} %shard_map.47, s32[]{:T(128)S(6)} %select_n.49), kind=kOutput, calls=%fused_computation.6 | convolution fusion | flops 2147483648 | bytes 9437188 | tf_op jit(solution)/shard_map/ml,pmn->pln/dot_general | solution.py:236
  97.5 2.5 collective-permute-done
  100.0 0.0 copy-done.1
  100.0 5.9 %fusion.10 = bf16[4,2048,128]{1,2,0:T(8,128)(2,1)} fusion(f32[4,128,2048]{2,1,0:T(8,128)S(1)} %fusion.6, bf16[1024,2048]{1,0:T(8,128)(2,1)} %collective-permute-done, bf16[4,2048,128]{2,1,0:T(8,128)(2,1)S(1)} %copy-done.1, s32[]{:T(128)S(6)} %select_n.53), kind=kOutput, calls=%fused_computation.9 | convolution fusion | flops 2149580800 | bytes 11534340 | tf_op jit(solution)/shard_map/ml,pmn->pln/dot_general | solution.py:237
  105.9 3.0 %copy.27 = bf16[4,2048,128]{2,1,0:T(8,128)(2,1)S(1)} copy(bf16[4,2048,128]{1,2,0:T(8,128)(2,1)} %fusion.10) | data formatting | bytes 4194304 | tf_op jit(solution)/shard_map/convert_element_type | solution.py:238
  108.9 0.6 copy.28
  109.5 31.6 %all_to_all.48 = bf16[4,8,16,16,128]{4,3,1,0,2:T(8,128)(2,1)S(1)} all-to-all(bf16[4,8,16,16,128]{4,3,1,0,2:T(8,128)(2,1)S(1)} %copy.28), channel_id=1, replica_groups=mesh['aux'=2,'row'=8,'col'=16] {'col'}, dimensions={2} | all-to-all | bytes 4194304 | tf_op jit(solution)/shard_map/all_to_all | solution.py:241
  141.1 2.4 copy.29
  143.6 2.3 reshape.56
  145.9 3.0 %all-gather.3.cloned.1.call-done = bf16[2048,1024]{1,0:T(8,128)(2,1)} async-done(((bf16[256,1024]{1,0:T(8,128)(2,1)}), bf16[2048,1024]{1,0:T(8,128)(2,1)}) %all-gather.3.cloned.1.call-update) | async-done | bytes 4194320 | tf_op jit(solution)/shard_map/all_gather | solution.py:99
  148.9 0.0 collective-permute-start.1
  148.9 0.0 copy-start.4
  148.9 5.3 %fusion.17 = bf16[4,128,1024]{2,1,0:T(8,128)(2,1)S(1)} fusion(bf16[4,128,2048]{2,1,0:T(8,128)(2,1)} %reshape.56, bf16[2048,1024]{1,0:T(8,128)(2,1)} %all-gather.3.cloned.1.call-done), kind=kOutput, calls=%fused_computation.15 | convolution fusion | flops 2148007936 | bytes 7340032 | tf_op jit(solution)/shard_map/pln,ns->pls/dot_general | solution.py:245
  154.2 2.2 collective-permute-done.1
  156.4 0.0 copy-done.4
  156.4 4.5 %fusion.20 = bf16[4,128,1024]{2,1,0:T(8,128)(2,1)S(1)} fusion(bf16[4,128,2048]{2,1,0:T(8,128)(2,1)S(1)} %copy-done.4, bf16[2048,1024]{1,0:T(8,128)(2,1)} %collective-permute-done.1), kind=kOutput, calls=%fused_computation.16 | convolution fusion | flops 2148007936 | bytes 7340032 | tf_op jit(solution)/shard_map/pln,ns->pls/dot_general | solution.py:246
  161.0 0.8 maximum_select_fusion
  161.8 0.6 copy.37
  162.4 0.6 copy.30
  163.0 55.6 %all_to_all.49 = bf16[4,8,1,16,16,128]{5,4,3,0,2,1:T(8,128)(2,1)S(1)} all-to-all(bf16[4,8,1,16,16,128]{5,4,3,0,2,1:T(8,128)(2,1)S(1)} %copy.30), channel_id=1, replica_groups=mesh['aux'=2,'row'=8,'col'=16] {'row'}, dimensions={1} | all-to-all | bytes 4194304 | tf_op jit(solution)/shard_map/all_to_all | solution.py:254
  218.6 1.9 copy.31
  220.5 0.0 copy-start.2
  220.5 7.3 %all-to-all-start.2 = ((bf16[32,1,1,16,16,128]{5,3,0,2,1,4:T(8,128)(2,1)}), bf16[32,1,1,16,16,128]{5,3,0,2,1,4:T(8,128)(2,1)}, u32[]{:S(2)}, u32[]{:S(2)}) async-start(bf16[32,1,1,16,16,128]{5,3,0,2,1,4:T(8,128)(2,1)} %copy.31), calls=%async_computation.2 | async-start | bytes 4194304 | tf_op jit(solution)/shard_map/all_to_all | solution.py:253
  227.8 0.0 copy-done.2
  227.8 0.1 collective-permute-start.2
  227.9 25.7 %all-to-all-done.2 = bf16[32,1,1,16,16,128]{5,3,0,2,1,4:T(8,128)(2,1)} async-done(((bf16[32,1,1,16,16,128]{5,3,0,2,1,4:T(8,128)(2,1)}), bf16[32,1,1,16,16,128]{5,3,0,2,1,4:T(8,128)(2,1)}, u32[]{:S(2)}, u32[]{:S(2)}) %all-to-all-start.2) | async-done | bytes 2097184 | tf_op jit(solution)/shard_map/all_to_all | solution.py:253
  253.6 2.1 copy.32
  255.7 1.5 fusion.23
  257.3 0.0 collective-permute-done.2
  257.3 3.2 %broadcast_select_fusion.1 = (f32[32,32]{1,0:T(8,128)S(1)}, f32[32,32]{1,0:T(8,128)S(1)}) fusion(f32[32,32]{1,0:T(8,128)S(1)} %fusion.23, pred[]{:T(512)S(6)} %eq.2, bf16[32,256,128]{2,0,1:T(8,128)(2,1)S(1)} %bitcast.61, bf16[32,256,128]{2,1,0:T(8,128)(2,1)} %collective-permute-done.2), kind=kOutput, calls=%fused_computation.25 | convolution fusion | flops 67110912 | bytes 4206593 | tf_op jit(solution)/shard_map/pls,qls->pq/dot_general | solution.py:263
  260.5 0.7 pad_maximum_fusion.x_ref
  261.2 17.1 %shard_map.48 = f32[32,64]{1,0:T(8,128)} custom-call(f32[32,64]{1,0:T(8,128)} %pad_maximum_fusion.x_ref), custom_call_target="tpu_custom_call" | custom-call | tf_op jit(solution)/shard_map/pallas_call | solution.py:79
  278.2 1.3 broadcast_multiply_fusion.1
Async XLA Ops:
  6.5 24.0 %copy-start = (bf16[256,2048]{1,0:T(8,128)(2,1)S(1)}, bf16[256,2048]{1,0:T(8,128)(2,1)}, u32[]{:S(2)}) copy-start(bf16[256,2048]{1,0:T(8,128)(2,1)} %param.6) | copy-start | bytes 3145732
  6.5 25.9 %copy-start.3 = (bf16[32,256,128]{2,1,0:T(8,128)(2,1)S(1)}, bf16[32,256,128]{2,1,0:T(8,128)(2,1)}, u32[]{:S(2)}) copy-start(bf16[32,256,128]{2,1,0:T(8,128)(2,1)} %param.4) | copy-start | bytes 6291460
  6.5 85.9 %all-gather.5.cloned.1.call-start = ((), (), s32[]{:S(2)}) async-start(), calls=%async_computation.4 | async-start | bytes 4456448 | tf_op jit(solution)/shard_map/all_gather | solution.py:206
  30.5 118.4 %all-gather.3.cloned.1.call-start = ((), (), s32[]{:S(2)}) async-start(), calls=%async_computation.3 | async-start | bytes 4718592 | tf_op jit(solution)/shard_map/all_gather | solution.py:99
  92.5 7.5 %collective-permute-start = (bf16[1024,2048]{1,0:T(8,128)(2,1)}, bf16[1024,2048]{1,0:T(8,128)(2,1)}, u32[]{:S(2)}, u32[]{:S(2)}) collective-permute-start(bf16[1024,2048]{1,0:T(8,128)(2,1)} %all-gather.5.cloned.1.call-done), channel_id=1, source_target_pairs={{0,128},{128,0},{1,129},{129,1},{2,130},{130,2},{3,131},{131,3},{4... | collective-permute-start | bytes 12582920 | tf_op jit(solution)/shard_map/ppermute | solution.py:112
  92.5 7.5 %copy-start.1 = (bf16[4,2048,128]{2,1,0:T(8,128)(2,1)S(1)}, bf16[4,2048,128]{2,1,0:T(8,128)(2,1)}, u32[]{:S(2)}) copy-start(bf16[4,2048,128]{2,1,0:T(8,128)(2,1)} %shard_map.47) | copy-start | bytes 6291460
  148.9 7.5 %collective-permute-start.1 = (bf16[2048,1024]{1,0:T(8,128)(2,1)}, bf16[2048,1024]{1,0:T(8,128)(2,1)}, u32[]{:S(2)}, u32[]{:S(2)}) collective-permute-start(bf16[2048,1024]{1,0:T(8,128)(2,1)} %all-gather.3.cloned.1.call-done), channel_id=1, source_target_pairs={{0,128},{128,0},{1,129},{129,1},{2,130},{130,2},{3,131},{131,3},{4... | collective-permute-start | bytes 12582920 | tf_op jit(solution)/shard_map/ppermute | solution.py:112
  148.9 7.5 %copy-start.4 = (bf16[4,128,2048]{2,1,0:T(8,128)(2,1)S(1)}, bf16[4,128,2048]{2,1,0:T(8,128)(2,1)}, u32[]{:S(2)}) copy-start(bf16[4,128,2048]{2,1,0:T(8,128)(2,1)} %reshape.56) | copy-start | bytes 6291460
  220.5 7.3 %copy-start.2 = (bf16[32,256,128]{2,1,0:T(8,128)(2,1)S(1)}, bf16[32,256,128]{2,1,0:T(8,128)(2,1)}, u32[]{:S(2)}) copy-start(bf16[32,256,128]{2,1,0:T(8,128)(2,1)} %broadcast_multiply_fusion.x_ref) | copy-start | bytes 6291460
  220.5 33.1 %all-to-all-start.2 = ((bf16[32,1,1,16,16,128]{5,3,0,2,1,4:T(8,128)(2,1)}), bf16[32,1,1,16,16,128]{5,3,0,2,1,4:T(8,128)(2,1)}, u32[]{:S(2)}, u32[]{:S(2)}) async-start(bf16[32,1,1,16,16,128]{5,3,0,2,1,4:T(8,128)(2,1)} %copy.31), calls=%async_computation.2 | async-start | bytes 4194304 | tf_op jit(solution)/shard_map/all_to_all | solution.py:253
  227.8 29.4 %collective-permute-start.2 = (bf16[32,256,128]{2,1,0:T(8,128)(2,1)S(1)}, bf16[32,256,128]{2,1,0:T(8,128)(2,1)}, u32[]{:S(2)}, u32[]{:S(2)}) collective-permute-start(bf16[32,256,128]{2,1,0:T(8,128)(2,1)S(1)} %copy-done.2), channel_id=1, source_target_pairs={{0,128},{128,0},{1,129},{129,1},{2,130},{130,2},{3,131},{131,3},{4... | collective-permute-start | bytes 6291464 | tf_op jit(solution)/shard_map/ppermute | solution.py:17
Sparse Core Ops, SparseCore 0:
  30.6 61.8 all-gather.4
  94.3 54.6 all-gather.2

commit v13 on v12

--- a/solution.py
+++ b/solution.py
@@ -199,11 +199,20 @@
 def gather_occ_rows(local):
     rows, cols = lax.axis_size("row"), lax.axis_size("col")
     width = local.shape[1] // cols
-    piece = lax.dynamic_slice_in_dim(local, lax.axis_index("col") * width, width, axis=1)
+    height = local.shape[0] // 2
+    piece = lax.dynamic_slice(
+        local, (lax.axis_index("aux") * height, lax.axis_index("col") * width), (height, width)
+    )
     column = exchange(jnp.tile(piece, (rows, 1)), "row", 0, 0, 5)
-    height = column.shape[0] // 2
-    part = lax.dynamic_slice_in_dim(column, lax.axis_index("aux") * height, height, axis=0)
-    return lax.all_gather(part, "col", axis=1, tiled=True)
+    return lax.all_gather(column, "col", axis=1, tiled=True)
+
+
+def core_rows(moved, core):
+    pieces, nao, ncol = moved.shape
+    rows = lax.axis_size("row")
+    split = moved.reshape(pieces, rows, 2, nao // (2 * rows), ncol)
+    picked = lax.dynamic_index_in_dim(split, core, axis=2, keepdims=False)
+    return picked.reshape(pieces, nao // 2, ncol)
 
 
 def shards(coulomb, occupied, virtual, tile_mask):
@@ -229,9 +238,8 @@
     occ_rows, moved = lax.optimization_barrier((occ_rows, moved))
     pieces = moved.shape[0]
     occ_other = swapped_core(occ_rows)
-    depth = occ_rows.shape[0]
-    mine = lax.dynamic_slice_in_dim(moved, aux_idx * depth, depth, axis=1)
-    other = lax.dynamic_slice_in_dim(moved, (1 - aux_idx) * depth, depth, axis=1)
+    mine = core_rows(moved, aux_idx)
+    other = core_rows(moved, 1 - aux_idx)
     half = (
         jnp.einsum("ml,pmn->pln", occ_rows, mine, preferred_element_type=jnp.float32)
         + jnp.einsum("ml,pmn->pln", occ_other, other, preferred_element_type=jnp.float32)

time: 287 us -> 280 us (0.976)
  Pallas kernels: 86.6 us -> 81.7 us
    pallas_call x2, Pallas kernels: 69.5 us -> 64.6 us  [exchange(): pl.pallas_call(functools.partial(exchange_kernel, mesh_axis, split_axis,...]
  transfers between devices with their start and end apart: 6 -> 6, of which waited for: 5 -> 5; matrix products, arithmetic and copies ran while one was open for 11% -> 11% of each run, Pallas kernels for 17% -> 18%
where the time goes in v13:
time: 280 us; the launch traced here: 279 us
  blocking collectives  87.2 us (31%)
  Pallas kernels  81.7 us (29%)
  waiting for transfers between devices  42 us (15%)
  matrix products  22.9 us (8%)
  local copies, waits for them, and re-layouts  19 us (7%)
  between operations  13.6 us (5%)
  starting transfers between devices  7.49 us (3%)
  other arithmetic  5.27 us (2%)
    pallas_call x2, Pallas kernels, exchange(): pl.pallas_call(functools.partial(exchange_kernel, mesh_axis, split_axis,...  64.6 us
    all_to_all x1, blocking collectives, shards(): lax.all_to_all(layered, 'row', split_axis=1, concat_axis=0, tiled=True)  55.6 us
    all_to_all x1, blocking collectives, shards(): lax.all_to_all(shaped, 'col', split_axis=2, concat_axis=4, tiled=True)  31.6 us
    all_to_all x1, waiting for transfers between devices, shards(): lax.all_to_all(lax.all_to_all(layered, 'row', split_axis=1, concat_axis=0...  25.7 us
    pallas_call x1, Pallas kernels, doubling_sum(): pl.pallas_call(two_round_kernel, out_shape=jax.ShapeDtypeStruct(partial.s...  17.1 us
    all_gather x1, waiting for transfers between devices, gather_occ_rows(): return lax.all_gather(column, 'col', axis=1, tiled=True)  8.8 us
    all_to_all x1, starting transfers between devices, shards(): lax.all_to_all(lax.all_to_all(layered, 'row', split_axis=1, concat_axis=0...  7.34 us
    dot_general x1, matrix products, shards(): jnp.einsum('ml,pmn->pln', occ_other, other, preferred_element_type=jnp.fl...  5.91 us
  transfers between devices with their start and end apart: 6, of which 5 were waited for; matrix products, arithmetic and copies ran while one was open for 11% of the time, Pallas kernels for 18%

profile of v13, /device:TPU:24, one launch (start us, length us, event | category | flops | bytes accessed | tf_op | source)
XLA Modules:
  0.0 279.1 jit_solution(3119818605905825542)
XLA Ops:
  6.5 0.0 copy-start
  6.5 0.0 copy-start.3
  6.5 0.0 all-gather.5.cloned.1.call-start
  6.5 0.9 dynamic_slice.17
  7.5 0.7 tile.4
  8.2 14.7 %shard_map.46 = bf16[1024,128]{1,0:T(8,128)(2,1)} custom-call(bf16[1024,128]{1,0:T(8,128)(2,1)} %bitcast.70), custom_call_target="tpu_custom_call" | custom-call | bytes 524288 | tf_op jit(solution)/shard_map/pallas_call | solution.py:182
  22.9 0.0 all-gather.5.cloned.1.call-update
  22.9 0.0 all-gather.3.cloned.1.call-start
  23.0 0.0 copy-done
  23.0 0.8 constant_dynamic-slice_fusion.2
  23.8 0.0 all-gather.3.cloned.1.call-update
  23.9 0.9 fusion.29
  24.7 0.1 broadcast_bitcast_fusion
  24.8 0.0 copy-done.3
  24.8 1.6 broadcast_multiply_fusion.x_ref
  26.4 49.9 %shard_map.47 = bf16[4,2048,128]{2,1,0:T(8,128)(2,1)} custom-call(bf16[32,256,128]{2,1,0:T(8,128)(2,1)} %broadcast_multiply_fusion.x_ref), custom_call_target="tpu_custom_call" | custom-call | bytes 4194304 | tf_op jit(solution)/shard_map/pallas_call | solution.py:182
  76.3 8.8 %all-gather.5.cloned.1.call-done = bf16[1024,2048]{1,0:T(8,128)(2,1)} async-done(((bf16[1024,128]{1,0:T(8,128)(2,1)}), bf16[1024,2048]{1,0:T(8,128)(2,1)}) %all-gather.5.cloned.1.call-update) | async-done | bytes 4194320 | tf_op jit(solution)/shard_map/all_gather | solution.py:207
  85.1 0.0 collective-permute-start
  85.1 0.0 copy-start.2
  85.1 1.8 constant_dynamic-slice_fusion
  87.0 1.0 copy-done.2
  87.9 2.4 fusion.6
  90.4 2.2 collective-permute-done
  92.6 5.9 %fusion.10 = bf16[4,2048,128]{1,2,0:T(8,128)(2,1)} fusion(f32[4,128,2048]{2,1,0:T(8,128)S(1)} %fusion.6, bf16[4,1024,128]{2,1,0:T(8,128)(2,1)S(1)} %bitcast.67, bf16[1024,2048]{1,0:T(8,128)(2,1)} %collective-permute-done), kind=kOutput, calls=%fused_computation.9 | convolution fusion | flops 2149580800 | bytes 11534336 | tf_op jit(solution)/shard_map/ml,pmn->pln/dot_general | solution.py:245
  98.5 3.0 %copy.27 = bf16[4,2048,128]{2,1,0:T(8,128)(2,1)S(1)} copy(bf16[4,2048,128]{1,2,0:T(8,128)(2,1)} %fusion.10) | data formatting | bytes 4194304 | tf_op jit(solution)/shard_map/convert_element_type | solution.py:246
  101.6 0.6 copy.28
  102.2 31.6 %all_to_all.48 = bf16[4,8,16,16,128]{4,3,1,0,2:T(8,128)(2,1)S(1)} all-to-all(bf16[4,8,16,16,128]{4,3,1,0,2:T(8,128)(2,1)S(1)} %copy.28), channel_id=1, replica_groups=mesh['aux'=2,'row'=8,'col'=16] {'col'}, dimensions={2} | all-to-all | bytes 4194304 | tf_op jit(solution)/shard_map/all_to_all | solution.py:249
  133.8 2.4 copy.29
  136.2 2.3 reshape.71
  138.5 3.0 %all-gather.3.cloned.1.call-done = bf16[2048,1024]{1,0:T(8,128)(2,1)} async-done(((bf16[256,1024]{1,0:T(8,128)(2,1)}), bf16[2048,1024]{1,0:T(8,128)(2,1)}) %all-gather.3.cloned.1.call-update) | async-done | bytes 4194320 | tf_op jit(solution)/shard_map/all_gather | solution.py:99
  141.6 0.0 collective-permute-start.1
  141.6 0.0 copy-start.4
  141.6 5.3 %fusion.17 = bf16[4,128,1024]{2,1,0:T(8,128)(2,1)S(1)} fusion(bf16[4,128,2048]{2,1,0:T(8,128)(2,1)} %reshape.71, bf16[2048,1024]{1,0:T(8,128)(2,1)} %all-gather.3.cloned.1.call-done), kind=kOutput, calls=%fused_computation.15 | convolution fusion | flops 2148007936 | bytes 7340032 | tf_op jit(solution)/shard_map/pln,ns->pls/dot_general | solution.py:253
  146.9 2.2 collective-permute-done.1
  149.1 0.0 copy-done.4
  149.1 4.5 %fusion.20 = bf16[4,128,1024]{2,1,0:T(8,128)(2,1)S(1)} fusion(bf16[4,128,2048]{2,1,0:T(8,128)(2,1)S(1)} %copy-done.4, bf16[2048,1024]{1,0:T(8,128)(2,1)} %collective-permute-done.1), kind=kOutput, calls=%fused_computation.16 | convolution fusion | flops 2148007936 | bytes 7340032 | tf_op jit(solution)/shard_map/pln,ns->pls/dot_general | solution.py:254
  153.6 0.8 maximum_select_fusion
  154.4 0.6 copy.37
  155.0 0.6 copy.30
  155.6 55.6 %all_to_all.49 = bf16[4,8,1,16,16,128]{5,4,3,0,2,1:T(8,128)(2,1)S(1)} all-to-all(bf16[4,8,1,16,16,128]{5,4,3,0,2,1:T(8,128)(2,1)S(1)} %copy.30), channel_id=1, replica_groups=mesh['aux'=2,'row'=8,'col'=16] {'row'}, dimensions={1} | all-to-all | bytes 4194304 | tf_op jit(solution)/shard_map/all_to_all | solution.py:262
  211.3 1.9 copy.31
  213.1 0.0 copy-start.1
  213.1 7.3 %all-to-all-start.2 = ((bf16[32,1,1,16,16,128]{5,3,0,2,1,4:T(8,128)(2,1)}), bf16[32,1,1,16,16,128]{5,3,0,2,1,4:T(8,128)(2,1)}, u32[]{:S(2)}, u32[]{:S(2)}) async-start(bf16[32,1,1,16,16,128]{5,3,0,2,1,4:T(8,128)(2,1)} %copy.31), calls=%async_computation.2 | async-start | bytes 4194304 | tf_op jit(solution)/shard_map/all_to_all | solution.py:261
  220.5 0.0 copy-done.1
  220.5 0.1 collective-permute-start.2
  220.6 25.7 %all-to-all-done.2 = bf16[32,1,1,16,16,128]{5,3,0,2,1,4:T(8,128)(2,1)} async-done(((bf16[32,1,1,16,16,128]{5,3,0,2,1,4:T(8,128)(2,1)}), bf16[32,1,1,16,16,128]{5,3,0,2,1,4:T(8,128)(2,1)}, u32[]{:S(2)}, u32[]{:S(2)}) %all-to-all-start.2) | async-done | bytes 2097184 | tf_op jit(solution)/shard_map/all_to_all | solution.py:261
  246.3 2.1 copy.32
  248.4 1.5 fusion.23
  249.9 0.0 collective-permute-done.2
  249.9 3.2 %broadcast_select_fusion.1 = (f32[32,32]{1,0:T(8,128)S(1)}, f32[32,32]{1,0:T(8,128)S(1)}) fusion(f32[32,32]{1,0:T(8,128)S(1)} %fusion.23, pred[]{:T(512)S(6)} %eq.2, bf16[32,256,128]{2,0,1:T(8,128)(2,1)S(1)} %bitcast.69, bf16[32,256,128]{2,1,0:T(8,128)(2,1)} %collective-permute-done.2), kind=kOutput, calls=%fused_computation.23 | convolution fusion | flops 67110912 | bytes 4206593 | tf_op jit(solution)/shard_map/pls,qls->pq/dot_general | solution.py:271
  253.1 0.7 pad_maximum_fusion.x_ref
  253.8 17.1 %shard_map.48 = f32[32,64]{1,0:T(8,128)} custom-call(f32[32,64]{1,0:T(8,128)} %pad_maximum_fusion.x_ref), custom_call_target="tpu_custom_call" | custom-call | tf_op jit(solution)/shard_map/pallas_call | solution.py:79
  270.9 1.3 broadcast_multiply_fusion.1
Async XLA Ops:
  6.5 16.4 %copy-start = (bf16[256,2048]{1,0:T(8,128)(2,1)S(1)}, bf16[256,2048]{1,0:T(8,128)(2,1)}, u32[]{:S(2)}) copy-start(bf16[256,2048]{1,0:T(8,128)(2,1)} %param.6) | copy-start | bytes 3145732
  6.5 18.3 %copy-start.3 = (bf16[32,256,128]{2,1,0:T(8,128)(2,1)S(1)}, bf16[32,256,128]{2,1,0:T(8,128)(2,1)}, u32[]{:S(2)}) copy-start(bf16[32,256,128]{2,1,0:T(8,128)(2,1)} %param.4) | copy-start | bytes 6291460
  6.5 78.6 %all-gather.5.cloned.1.call-start = ((), (), s32[]{:S(2)}) async-start(), calls=%async_computation.4 | async-start | bytes 4456448 | tf_op jit(solution)/shard_map/all_gather | solution.py:207
  22.9 118.6 %all-gather.3.cloned.1.call-start = ((), (), s32[]{:S(2)}) async-start(), calls=%async_computation.3 | async-start | bytes 4718592 | tf_op jit(solution)/shard_map/all_gather | solution.py:99
  85.1 7.5 %collective-permute-start = (bf16[1024,2048]{1,0:T(8,128)(2,1)}, bf16[1024,2048]{1,0:T(8,128)(2,1)}, u32[]{:S(2)}, u32[]{:S(2)}) collective-permute-start(bf16[1024,2048]{1,0:T(8,128)(2,1)} %all-gather.5.cloned.1.call-done), channel_id=1, source_target_pairs={{0,128},{128,0},{1,129},{129,1},{2,130},{130,2},{3,131},{131,3},{4... | collective-permute-start | bytes 12582920 | tf_op jit(solution)/shard_map/ppermute | solution.py:112
  85.1 2.8 %copy-start.2 = (bf16[1024,2048]{1,0:T(8,128)(2,1)S(1)}, bf16[1024,2048]{1,0:T(8,128)(2,1)}, u32[]{:S(2)}) copy-start(bf16[1024,2048]{1,0:T(8,128)(2,1)} %all-gather.5.cloned.1.call-done) | copy-start | bytes 12582916
  141.6 7.5 %collective-permute-start.1 = (bf16[2048,1024]{1,0:T(8,128)(2,1)}, bf16[2048,1024]{1,0:T(8,128)(2,1)}, u32[]{:S(2)}, u32[]{:S(2)}) collective-permute-start(bf16[2048,1024]{1,0:T(8,128)(2,1)} %all-gather.3.cloned.1.call-done), channel_id=1, source_target_pairs={{0,128},{128,0},{1,129},{129,1},{2,130},{130,2},{3,131},{131,3},{4... | collective-permute-start | bytes 12582920 | tf_op jit(solution)/shard_map/ppermute | solution.py:112
  141.6 7.5 %copy-start.4 = (bf16[4,128,2048]{2,1,0:T(8,128)(2,1)S(1)}, bf16[4,128,2048]{2,1,0:T(8,128)(2,1)}, u32[]{:S(2)}) copy-start(bf16[4,128,2048]{2,1,0:T(8,128)(2,1)} %reshape.71) | copy-start | bytes 6291460
  213.1 7.3 %copy-start.1 = (bf16[32,256,128]{2,1,0:T(8,128)(2,1)S(1)}, bf16[32,256,128]{2,1,0:T(8,128)(2,1)}, u32[]{:S(2)}) copy-start(bf16[32,256,128]{2,1,0:T(8,128)(2,1)} %broadcast_multiply_fusion.x_ref) | copy-start | bytes 6291460
  213.1 33.1 %all-to-all-start.2 = ((bf16[32,1,1,16,16,128]{5,3,0,2,1,4:T(8,128)(2,1)}), bf16[32,1,1,16,16,128]{5,3,0,2,1,4:T(8,128)(2,1)}, u32[]{:S(2)}, u32[]{:S(2)}) async-start(bf16[32,1,1,16,16,128]{5,3,0,2,1,4:T(8,128)(2,1)} %copy.31), calls=%async_computation.2 | async-start | bytes 4194304 | tf_op jit(solution)/shard_map/all_to_all | solution.py:261
  220.5 29.5 %collective-permute-start.2 = (bf16[32,256,128]{2,1,0:T(8,128)(2,1)S(1)}, bf16[32,256,128]{2,1,0:T(8,128)(2,1)}, u32[]{:S(2)}, u32[]{:S(2)}) collective-permute-start(bf16[32,256,128]{2,1,0:T(8,128)(2,1)S(1)} %copy-done.1), channel_id=1, source_target_pairs={{0,128},{128,0},{1,129},{129,1},{2,130},{130,2},{3,131},{131,3},{4... | collective-permute-start | bytes 6291464 | tf_op jit(solution)/shard_map/ppermute | solution.py:17
Sparse Core Ops, SparseCore 0:
  23.0 62.0 all-gather.4
  86.9 54.6 all-gather.2

commit v14 on v13

--- a/solution.py
+++ b/solution.py
@@ -257,14 +257,13 @@
     dressed = join_halves(
         dressed_own.astype(jnp.bfloat16), dressed_other.astype(jnp.bfloat16), axis=2
     )
-    layered = dressed.reshape(pieces, rows, 1, jpart, cols, ncol)
-    returned = lax.all_to_all(
-        lax.all_to_all(layered, "row", split_axis=1, concat_axis=0, tiled=True),
-        "col",
-        split_axis=4,
-        concat_axis=2,
-        tiled=True,
-    )
+    by_dest = (
+        dressed.reshape(pieces, rows, jpart, cols, ncol)
+        .transpose(1, 3, 0, 2, 4)
+        .reshape(rows * cols, pieces, jpart, ncol)
+    )
+    got = lax.all_to_all(by_dest, ("row", "col"), split_axis=0, concat_axis=0, tiled=True)
+    returned = got.reshape(rows, cols, pieces, jpart, ncol).transpose(0, 2, 1, 3, 4)
     aligned = returned.reshape(pdev, mrow, ncol)
     theirs = swapped(screened, "aux", 0)
     with_mine = jnp.einsum("pls,qls->pq", aligned, screened, preferred_element_type=jnp.float32)

time: 280 us -> 253 us (0.904)
  blocking collectives: 87.2 us -> 31.6 us
  waiting for transfers between devices: 42 us -> 67.9 us
  starting transfers between devices: 7.49 us -> 11.8 us
    all_to_all x1 -> x0, blocking collectives: 55.6 us -> none  [shards(): lax.all_to_all(layered, 'row', split_axis=1, concat_axis=0, tiled=True)]
    all_to_all x1, waiting for transfers between devices: 25.7 us -> 51.6 us  [shards(): lax.all_to_all(by_dest, ('row', 'col'), split_axis=0, concat_axis=0, tile...]
    all_to_all x1, starting transfers between devices: 7.34 us -> 11.6 us  [shards(): lax.all_to_all(by_dest, ('row', 'col'), split_axis=0, concat_axis=0, tile...]
    all_to_all x2 -> x0, local copies, waits for them, and re-layouts: 3.99 us -> none  [the longest x1 2.13 us: shards(): lax.all_to_all(lax.all_to_all(layered, 'row', split_axis=1, concat_axis=0...]
  transfers between devices with their start and end apart: 6 -> 6, of which waited for: 5 -> 5; matrix products, arithmetic and copies ran while one was open for 11% -> 12% of each run, Pallas kernels for 18% -> 20%
where the time goes in v14:
time: 253 us; the launch traced here: 252 us
  Pallas kernels  80.5 us (32%)
  waiting for transfers between devices  67.9 us (27%)
  blocking collectives  31.6 us (12%)
  matrix products  22.8 us (9%)
  local copies, waits for them, and re-layouts  18.9 us (7%)
  between operations  13.6 us (5%)
  starting transfers between devices  11.8 us (5%)
  other arithmetic  5.27 us (2%)
    pallas_call x2, Pallas kernels, exchange(): pl.pallas_call(functools.partial(exchange_kernel, mesh_axis, split_axis,...  64.6 us
    all_to_all x1, waiting for transfers between devices, shards(): lax.all_to_all(by_dest, ('row', 'col'), split_axis=0, concat_axis=0, tile...  51.6 us
    all_to_all x1, blocking collectives, shards(): lax.all_to_all(shaped, 'col', split_axis=2, concat_axis=4, tiled=True)  31.6 us
    pallas_call x1, Pallas kernels, doubling_sum(): pl.pallas_call(two_round_kernel, out_shape=jax.ShapeDtypeStruct(partial.s...  15.8 us
    all_to_all x1, starting transfers between devices, shards(): lax.all_to_all(by_dest, ('row', 'col'), split_axis=0, concat_axis=0, tile...  11.6 us
    all_gather x1, waiting for transfers between devices, gather_occ_rows(): return lax.all_gather(column, 'col', axis=1, tiled=True)  8.8 us
    dot_general x1, matrix products, shards(): jnp.einsum('ml,pmn->pln', occ_other, other, preferred_element_type=jnp.fl...  5.91 us
    dot_general x1, matrix products, shards(): jnp.einsum('pln,ns->pls', spread, virt_own, preferred_element_type=jnp.fl...  5.3 us
  transfers between devices with their start and end apart: 6, of which 5 were waited for; matrix products, arithmetic and copies ran while one was open for 12% of the time, Pallas kernels for 20%

profile of v14, /device:TPU:24, one launch (start us, length us, event | category | flops | bytes accessed | tf_op | source)
XLA Modules:
  0.0 252.2 jit_solution(14139809310476102207)
XLA Ops:
  6.5 0.0 copy-start
  6.5 0.0 copy-start.3
  6.5 0.0 all-gather.5.cloned.1.call-start
  6.5 0.9 dynamic_slice.17
  7.5 0.7 tile.4
  8.2 14.7 %shard_map.46 = bf16[1024,128]{1,0:T(8,128)(2,1)} custom-call(bf16[1024,128]{1,0:T(8,128)(2,1)} %bitcast.67), custom_call_target="tpu_custom_call" | custom-call | bytes 524288 | tf_op jit(solution)/shard_map/pallas_call | solution.py:182
  22.9 0.0 all-gather.5.cloned.1.call-update
  22.9 0.0 all-gather.3.cloned.1.call-start
  23.0 0.0 copy-done
  23.0 0.8 constant_dynamic-slice_fusion.2
  23.8 0.0 all-gather.3.cloned.1.call-update
  23.9 0.9 fusion.29
  24.7 0.1 broadcast_bitcast_fusion
  24.8 0.0 copy-done.3
  24.8 1.6 broadcast_multiply_fusion.x_ref
  26.4 49.9 %shard_map.47 = bf16[4,2048,128]{2,1,0:T(8,128)(2,1)} custom-call(bf16[32,256,128]{2,1,0:T(8,128)(2,1)} %broadcast_multiply_fusion.x_ref), custom_call_target="tpu_custom_call" | custom-call | bytes 4194304 | tf_op jit(solution)/shard_map/pallas_call | solution.py:182
  76.3 8.8 %all-gather.5.cloned.1.call-done = bf16[1024,2048]{1,0:T(8,128)(2,1)} async-done(((bf16[1024,128]{1,0:T(8,128)(2,1)}), bf16[1024,2048]{1,0:T(8,128)(2,1)}) %all-gather.5.cloned.1.call-update) | async-done | bytes 4194320 | tf_op jit(solution)/shard_map/all_gather | solution.py:207
  85.1 0.0 collective-permute-start
  85.1 0.0 copy-start.2
  85.1 1.8 constant_dynamic-slice_fusion
  87.0 1.0 copy-done.2
  87.9 2.4 fusion.6
  90.4 2.2 collective-permute-done
  92.6 5.9 %fusion.10 = bf16[4,2048,128]{1,2,0:T(8,128)(2,1)} fusion(f32[4,128,2048]{2,1,0:T(8,128)S(1)} %fusion.6, bf16[4,1024,128]{2,1,0:T(8,128)(2,1)S(1)} %bitcast.64, bf16[1024,2048]{1,0:T(8,128)(2,1)} %collective-permute-done), kind=kOutput, calls=%fused_computation.9 | convolution fusion | flops 2149580800 | bytes 11534336 | tf_op jit(solution)/shard_map/ml,pmn->pln/dot_general | solution.py:245
  98.5 3.0 %copy.27 = bf16[4,2048,128]{2,1,0:T(8,128)(2,1)S(1)} copy(bf16[4,2048,128]{1,2,0:T(8,128)(2,1)} %fusion.10) | data formatting | bytes 4194304 | tf_op jit(solution)/shard_map/convert_element_type | solution.py:246
  101.6 0.6 copy.28
  102.2 31.6 %all_to_all.20 = bf16[4,8,16,16,128]{4,3,1,0,2:T(8,128)(2,1)S(1)} all-to-all(bf16[4,8,16,16,128]{4,3,1,0,2:T(8,128)(2,1)S(1)} %copy.28), channel_id=1, replica_groups=mesh['aux'=2,'row'=8,'col'=16] {'col'}, dimensions={2} | all-to-all | bytes 4194304 | tf_op jit(solution)/shard_map/all_to_all | solution.py:249
  133.8 2.4 copy.29
  136.2 2.3 reshape.61
  138.5 3.0 %all-gather.3.cloned.1.call-done = bf16[2048,1024]{1,0:T(8,128)(2,1)} async-done(((bf16[256,1024]{1,0:T(8,128)(2,1)}), bf16[2048,1024]{1,0:T(8,128)(2,1)}) %all-gather.3.cloned.1.call-update) | async-done | bytes 4194320 | tf_op jit(solution)/shard_map/all_gather | solution.py:99
  141.6 0.0 collective-permute-start.1
  141.6 0.0 copy-start.4
  141.6 5.3 %fusion.17 = bf16[4,128,1024]{2,1,0:T(8,128)(2,1)S(1)} fusion(bf16[4,128,2048]{2,1,0:T(8,128)(2,1)} %reshape.61, bf16[2048,1024]{1,0:T(8,128)(2,1)} %all-gather.3.cloned.1.call-done), kind=kOutput, calls=%fused_computation.15 | convolution fusion | flops 2148007936 | bytes 7340032 | tf_op jit(solution)/shard_map/pln,ns->pls/dot_general | solution.py:253
  146.9 2.2 collective-permute-done.1
  149.1 0.0 copy-done.4
  149.1 4.5 %fusion.20 = bf16[4,128,1024]{2,1,0:T(8,128)(2,1)S(1)} fusion(bf16[4,128,2048]{2,1,0:T(8,128)(2,1)S(1)} %copy-done.4, bf16[2048,1024]{1,0:T(8,128)(2,1)} %collective-permute-done.1), kind=kOutput, calls=%fused_computation.16 | convolution fusion | flops 2148007936 | bytes 7340032 | tf_op jit(solution)/shard_map/pln,ns->pls/dot_general | solution.py:254
  153.6 0.8 maximum_select_fusion
  154.4 0.6 copy.36
  155.0 1.9 copy.30
  156.9 0.0 copy-start.1
  156.9 11.6 %all-to-all-start.1 = ((bf16[128,4,16,128]{3,2,1,0:T(8,128)(2,1)}), bf16[128,4,16,128]{3,2,1,0:T(8,128)(2,1)}, u32[]{:S(2)}, u32[]{:S(2)}) async-start(bf16[128,4,16,128]{3,2,1,0:T(8,128)(2,1)} %bitcast.58), calls=%async_computation.1 | async-start | bytes 4194304 | tf_op jit(solution)/shard_map/all_to_all | solution.py:265
  168.5 0.0 copy-done.1
  168.5 0.1 collective-permute-start.2
  168.6 51.6 %all-to-all-done.1 = bf16[128,4,16,128]{3,2,1,0:T(8,128)(2,1)} async-done(((bf16[128,4,16,128]{3,2,1,0:T(8,128)(2,1)}), bf16[128,4,16,128]{3,2,1,0:T(8,128)(2,1)}, u32[]{:S(2)}, u32[]{:S(2)}) %all-to-all-start.1) | async-done | bytes 2097184 | tf_op jit(solution)/shard_map/all_to_all | solution.py:265
  220.3 2.6 %copy.31 = bf16[8,4,16,16,128]{4,1,0,3,2:T(4,128)(2,1)S(1)} copy(bf16[8,4,16,16,128]{4,3,1,2,0:T(8,128)(2,1)} %bitcast.16) | data formatting | bytes 4194304 | tf_op jit(solution)/shard_map/transpose | solution.py:266
  222.9 1.5 fusion.23
  224.4 0.0 collective-permute-done.2
  224.4 3.1 %broadcast_select_fusion.1 = (f32[32,32]{1,0:T(8,128)S(1)}, f32[32,32]{1,0:T(8,128)S(1)}) fusion(f32[32,32]{1,0:T(8,128)S(1)} %fusion.23, pred[]{:T(512)S(6)} %eq.2, bf16[32,256,128]{2,0,1:T(8,128)(2,1)S(1)} %bitcast.66, bf16[32,256,128]{2,1,0:T(8,128)(2,1)} %collective-permute-done.2), kind=kOutput, calls=%fused_computation.23 | convolution fusion | flops 67110912 | bytes 4206593 | tf_op jit(solution)/shard_map/pls,qls->pq/dot_general | solution.py:270
  227.5 0.7 pad_maximum_fusion.x_ref
  228.2 15.8 %shard_map.48 = f32[32,64]{1,0:T(8,128)} custom-call(f32[32,64]{1,0:T(8,128)} %pad_maximum_fusion.x_ref), custom_call_target="tpu_custom_call" | custom-call | tf_op jit(solution)/shard_map/pallas_call | solution.py:79
  244.1 1.3 broadcast_multiply_fusion.1
Async XLA Ops:
  6.5 16.4 %copy-start = (bf16[256,2048]{1,0:T(8,128)(2,1)S(1)}, bf16[256,2048]{1,0:T(8,128)(2,1)}, u32[]{:S(2)}) copy-start(bf16[256,2048]{1,0:T(8,128)(2,1)} %param.6) | copy-start | bytes 3145732
  6.5 18.3 %copy-start.3 = (bf16[32,256,128]{2,1,0:T(8,128)(2,1)S(1)}, bf16[32,256,128]{2,1,0:T(8,128)(2,1)}, u32[]{:S(2)}) copy-start(bf16[32,256,128]{2,1,0:T(8,128)(2,1)} %param.4) | copy-start | bytes 6291460
  6.5 78.6 %all-gather.5.cloned.1.call-start = ((), (), s32[]{:S(2)}) async-start(), calls=%async_computation.3 | async-start | bytes 4456448 | tf_op jit(solution)/shard_map/all_gather | solution.py:207
  22.9 118.6 %all-gather.3.cloned.1.call-start = ((), (), s32[]{:S(2)}) async-start(), calls=%async_computation.2 | async-start | bytes 4718592 | tf_op jit(solution)/shard_map/all_gather | solution.py:99
  85.1 7.5 %collective-permute-start = (bf16[1024,2048]{1,0:T(8,128)(2,1)}, bf16[1024,2048]{1,0:T(8,128)(2,1)}, u32[]{:S(2)}, u32[]{:S(2)}) collective-permute-start(bf16[1024,2048]{1,0:T(8,128)(2,1)} %all-gather.5.cloned.1.call-done), channel_id=1, source_target_pairs={{0,128},{128,0},{1,129},{129,1},{2,130},{130,2},{3,131},{131,3},{4... | collective-permute-start | bytes 12582920 | tf_op jit(solution)/shard_map/ppermute | solution.py:112
  85.1 2.8 %copy-start.2 = (bf16[1024,2048]{1,0:T(8,128)(2,1)S(1)}, bf16[1024,2048]{1,0:T(8,128)(2,1)}, u32[]{:S(2)}) copy-start(bf16[1024,2048]{1,0:T(8,128)(2,1)} %all-gather.5.cloned.1.call-done) | copy-start | bytes 12582916
  141.6 7.5 %collective-permute-start.1 = (bf16[2048,1024]{1,0:T(8,128)(2,1)}, bf16[2048,1024]{1,0:T(8,128)(2,1)}, u32[]{:S(2)}, u32[]{:S(2)}) collective-permute-start(bf16[2048,1024]{1,0:T(8,128)(2,1)} %all-gather.3.cloned.1.call-done), channel_id=1, source_target_pairs={{0,128},{128,0},{1,129},{129,1},{2,130},{130,2},{3,131},{131,3},{4... | collective-permute-start | bytes 12582920 | tf_op jit(solution)/shard_map/ppermute | solution.py:112
  141.6 7.5 %copy-start.4 = (bf16[4,128,2048]{2,1,0:T(8,128)(2,1)S(1)}, bf16[4,128,2048]{2,1,0:T(8,128)(2,1)}, u32[]{:S(2)}) copy-start(bf16[4,128,2048]{2,1,0:T(8,128)(2,1)} %reshape.61) | copy-start | bytes 6291460
  156.9 11.6 %copy-start.1 = (bf16[32,256,128]{2,1,0:T(8,128)(2,1)S(1)}, bf16[32,256,128]{2,1,0:T(8,128)(2,1)}, u32[]{:S(2)}) copy-start(bf16[32,256,128]{2,1,0:T(8,128)(2,1)} %broadcast_multiply_fusion.x_ref) | copy-start | bytes 6291460
  156.9 63.4 %all-to-all-start.1 = ((bf16[128,4,16,128]{3,2,1,0:T(8,128)(2,1)}), bf16[128,4,16,128]{3,2,1,0:T(8,128)(2,1)}, u32[]{:S(2)}, u32[]{:S(2)}) async-start(bf16[128,4,16,128]{3,2,1,0:T(8,128)(2,1)} %bitcast.58), calls=%async_computation.1 | async-start | bytes 4194304 | tf_op jit(solution)/shard_map/all_to_all | solution.py:265
  168.5 55.8 %collective-permute-start.2 = (bf16[32,256,128]{2,1,0:T(8,128)(2,1)S(1)}, bf16[32,256,128]{2,1,0:T(8,128)(2,1)}, u32[]{:S(2)}, u32[]{:S(2)}) collective-permute-start(bf16[32,256,128]{2,1,0:T(8,128)(2,1)S(1)} %copy-done.1), channel_id=1, source_target_pairs={{0,128},{128,0},{1,129},{129,1},{2,130},{130,2},{3,131},{131,3},{4... | collective-permute-start | bytes 6291464 | tf_op jit(solution)/shard_map/ppermute | solution.py:17
Sparse Core Ops, SparseCore 0:
  23.0 62.0 all-gather.4
  86.9 54.6 all-gather.2

commit v15 on v14

--- a/solution.py
+++ b/solution.py
@@ -203,8 +203,9 @@
     piece = lax.dynamic_slice(
         local, (lax.axis_index("aux") * height, lax.axis_index("col") * width), (height, width)
     )
-    column = exchange(jnp.tile(piece, (rows, 1)), "row", 0, 0, 5)
-    return lax.all_gather(column, "col", axis=1, tiled=True)
+    blocks = lax.all_gather(piece, ("row", "col"), axis=0, tiled=False)
+    blocks = blocks.reshape(rows, cols, height, width).transpose(0, 2, 1, 3)
+    return blocks.reshape(rows * height, cols * width)
 
 
 def core_rows(moved, core):

time: 253 us -> 315 us (1.25)
  waiting for transfers between devices: 67.9 us -> 131 us
  Pallas kernels: 80.5 us -> 70.7 us
  local copies, waits for them, and re-layouts: 18.9 us -> 25.1 us
    all_gather x1, waiting for transfers between devices: 8.8 us -> 75 us  [gather_occ_rows(): blocks = lax.all_gather(piece, ('row', 'col'), axis=0, tiled=False)]
    pallas_call x2 -> x1, Pallas kernels: 64.6 us -> 54.8 us  [exchange(): pl.pallas_call(functools.partial(exchange_kernel, mesh_axis, split_axis,...]
    reshape x0 -> x1, local copies, waits for them, and re-layouts: none -> 4.9 us  [gather_occ_rows(): blocks = blocks.reshape(rows, cols, height, width).transpose(0, 2, 1, 3)]
  transfers between devices with their start and end apart: 6 -> 6, of which waited for: 5 -> 4; matrix products, arithmetic and copies ran while one was open for 12% -> 14% of each run, Pallas kernels for 20% -> 17%
where the time goes in v15:
time: 315 us; the launch traced here: 314 us
  waiting for transfers between devices  131 us (42%)
  Pallas kernels  70.7 us (22%)
  blocking collectives  31.5 us (10%)
  local copies, waits for them, and re-layouts  25.1 us (8%)
  matrix products  25.1 us (8%)
  between operations  13.6 us (4%)
  starting transfers between devices  10.5 us (3%)
  other arithmetic  6.82 us (2%)
    all_gather x1, waiting for transfers between devices, gather_occ_rows(): blocks = lax.all_gather(piece, ('row', 'col'), axis=0, tiled=False)  75 us
    pallas_call x1, Pallas kernels, exchange(): pl.pallas_call(functools.partial(exchange_kernel, mesh_axis, split_axis,...  54.8 us
    all_to_all x1, waiting for transfers between devices, shards(): lax.all_to_all(by_dest, ('row', 'col'), split_axis=0, concat_axis=0, tile...  51.4 us
    all_to_all x1, blocking collectives, shards(): lax.all_to_all(shaped, 'col', split_axis=2, concat_axis=4, tiled=True)  31.5 us
    pallas_call x1, Pallas kernels, doubling_sum(): pl.pallas_call(two_round_kernel, out_shape=jax.ShapeDtypeStruct(partial.s...  15.8 us
    all_to_all x1, starting transfers between devices, shards(): lax.all_to_all(by_dest, ('row', 'col'), split_axis=0, concat_axis=0, tile...  10.1 us
  transfers between devices with their start and end apart: 6, of which 4 were waited for; matrix products, arithmetic and copies ran while one was open for 14% of the time, Pallas kernels for 17%

profile of v15, /device:TPU:24, one launch (start us, length us, event | category | flops | bytes accessed | tf_op | source)
XLA Modules:
  0.0 314.5 jit_solution(14093606641546073631)
XLA Ops:
  6.5 0.0 copy-start
  6.5 0.0 all-gather.6.cloned.1.call-start
  6.5 1.4 dynamic_slice.17
  8.0 0.0 all-gather.6.cloned.1.call-update
  8.0 0.0 all-gather.4.cloned.1.call-start
  8.1 0.0 copy-done
  8.1 0.8 constant_dynamic-slice_fusion.2
  8.9 0.0 all-gather.4.cloned.1.call-update
  8.9 0.9 fusion.29
  9.8 0.1 broadcast_bitcast_fusion
  9.9 3.2 %broadcast_multiply_fusion.x_ref = bf16[32,256,128]{2,1,0:T(8,128)(2,1)} fusion(bf16[32,256,128]{2,1,0:T(8,128)(2,1)} %param.4, bf16[256]{0:T(256)(128)(2,1)S(1)} %broadcast_bitcast_fusion), kind=kLoop, calls=%fused_computation.20 | loop fusion | flops 1048576 | bytes 4194816 | tf_op jit(solution)/shard_map/mul | solution.py:235
  13.1 54.8 %shard_map.46 = bf16[4,2048,128]{2,1,0:T(8,128)(2,1)} custom-call(bf16[32,256,128]{2,1,0:T(8,128)(2,1)} %broadcast_multiply_fusion.x_ref), custom_call_target="tpu_custom_call" | custom-call | bytes 4194304 | tf_op jit(solution)/shard_map/pallas_call | solution.py:182
  67.9 75.0 %all-gather.6.cloned.1.call-done = bf16[16384,128]{1,0:T(8,128)(2,1)} async-done(((bf16[128,128]{1,0:T(8,128)(2,1)}), bf16[16384,128]{1,0:T(8,128)(2,1)}) %all-gather.6.cloned.1.call-update) | async-done | bytes 4194320 | tf_op jit(solution)/shard_map/all_gather | solution.py:206
  142.9 4.9 %copy.28 = bf16[8,16,128,128]{3,1,2,0:T(8,128)(2,1)S(1)} copy(bf16[8,16,128,128]{3,2,1,0:T(8,128)(2,1)} %bitcast.71) | data formatting | bytes 8388608 | tf_op jit(solution)/shard_map/reshape | solution.py:207
  147.8 0.0 copy-start.2
  147.8 4.1 %copy.53 = bf16[128,8,16,128]{3,1,2,0:T(8,128)(2,1)} copy(bf16[128,8,16,128]{3,2,1,0:T(8,128)(2,1)S(1)} %bitcast.63) | data formatting | bytes 8388608
  151.9 0.0 collective-permute-start
  151.9 0.0 copy-done.2
  151.9 0.1 constant_dynamic-slice_fusion
  152.0 4.7 %fusion.6 = f32[4,128,2048]{2,1,0:T(8,128)S(1)} fusion(bf16[4,1024,128]{2,1,0:T(8,128)(2,1)S(1)} %bitcast.70, bf16[1024,2048]{1,0:T(8,128)(2,1)} %bitcast.62), kind=kOutput, calls=%fused_computation.7 | convolution fusion | flops 2147483648 | bytes 9437184 | tf_op jit(solution)/shard_map/ml,pmn->pln/dot_general | solution.py:245
  156.8 2.6 collective-permute-done
  159.4 6.0 %fusion.10 = bf16[4,2048,128]{1,2,0:T(8,128)(2,1)} fusion(f32[4,128,2048]{2,1,0:T(8,128)S(1)} %fusion.6, bf16[4,1024,128]{2,1,0:T(8,128)(2,1)S(1)} %bitcast.72, bf16[1024,2048]{1,0:T(8,128)(2,1)} %collective-permute-done), kind=kOutput, calls=%fused_computation.10 | convolution fusion | flops 2149580800 | bytes 11534336 | tf_op jit(solution)/shard_map/ml,pmn->pln/dot_general | solution.py:246
  165.4 3.1 copy.31
  168.4 0.6 copy.32
  169.0 31.5 %all_to_all.20 = bf16[4,8,16,16,128]{4,3,1,0,2:T(8,128)(2,1)S(1)} all-to-all(bf16[4,8,16,16,128]{4,3,1,0,2:T(8,128)(2,1)S(1)} %copy.32), channel_id=1, replica_groups=mesh['aux'=2,'row'=8,'col'=16] {'col'}, dimensions={2} | all-to-all | bytes 4194304 | tf_op jit(solution)/shard_map/all_to_all | solution.py:250
  200.5 2.4 copy.33
  202.9 2.3 reshape.65
  205.3 0.0 all-gather.4.cloned.1.call-done
  205.3 0.0 collective-permute-start.1
  205.3 0.0 copy-start.4
  205.3 5.3 %fusion.17 = bf16[4,128,1024]{2,1,0:T(8,128)(2,1)S(1)} fusion(bf16[4,128,2048]{2,1,0:T(8,128)(2,1)} %reshape.65, bf16[2048,1024]{1,0:T(8,128)(2,1)} %all-gather.4.cloned.1.call-done), kind=kOutput, calls=%fused_computation.16 | convolution fusion | flops 2148007936 | bytes 7340032 | tf_op jit(solution)/shard_map/pln,ns->pls/dot_general | solution.py:254
  210.6 2.2 collective-permute-done.1
  212.8 0.0 copy-done.4
  212.8 4.5 %fusion.20 = bf16[4,128,1024]{2,1,0:T(8,128)(2,1)S(1)} fusion(bf16[4,128,2048]{2,1,0:T(8,128)(2,1)S(1)} %copy-done.4, bf16[2048,1024]{1,0:T(8,128)(2,1)} %collective-permute-done.1), kind=kOutput, calls=%fused_computation.17 | convolution fusion | flops 2148007936 | bytes 7340032 | tf_op jit(solution)/shard_map/pln,ns->pls/dot_general | solution.py:255
  217.3 0.8 maximum_select_fusion
  218.1 0.6 copy.41
  218.7 1.9 copy.34
  220.6 0.0 copy-start.3
  220.6 10.1 %all-to-all-start.1 = ((bf16[128,4,16,128]{3,2,1,0:T(8,128)(2,1)}), bf16[128,4,16,128]{3,2,1,0:T(8,128)(2,1)}, u32[]{:S(2)}, u32[]{:S(2)}) async-start(bf16[128,4,16,128]{3,2,1,0:T(8,128)(2,1)} %bitcast.65), calls=%async_computation.1 | async-start | bytes 4194304 | tf_op jit(solution)/shard_map/all_to_all | solution.py:266
  230.8 0.0 copy-done.3
  230.8 0.3 collective-permute-start.2
  231.1 51.4 %all-to-all-done.1 = bf16[128,4,16,128]{3,2,1,0:T(8,128)(2,1)} async-done(((bf16[128,4,16,128]{3,2,1,0:T(8,128)(2,1)}), bf16[128,4,16,128]{3,2,1,0:T(8,128)(2,1)}, u32[]{:S(2)}, u32[]{:S(2)}) %all-to-all-start.1) | async-done | bytes 2097184 | tf_op jit(solution)/shard_map/all_to_all | solution.py:266
  282.5 2.6 copy.35
  285.1 0.0 copy-start.1
  285.1 1.5 fusion.23
  286.6 0.0 collective-permute-done.2
  286.6 3.1 broadcast_select_fusion.1
  289.8 0.7 pad_maximum_fusion.x_ref
  290.4 15.8 %shard_map.47 = f32[32,64]{1,0:T(8,128)} custom-call(f32[32,64]{1,0:T(8,128)} %pad_maximum_fusion.x_ref), custom_call_target="tpu_custom_call" | custom-call | tf_op jit(solution)/shard_map/pallas_call | solution.py:79
  306.3 1.3 broadcast_multiply_fusion.1
  307.6 0.0 copy-done.1
Async XLA Ops:
  6.5 1.5 copy-start
  6.5 136.3 %all-gather.6.cloned.1.call-start = ((), (), s32[]{:S(2)}) async-start(), calls=%async_computation.3 | async-start | bytes 4227072 | tf_op jit(solution)/shard_map/all_gather | solution.py:206
  8.0 197.3 %all-gather.4.cloned.1.call-start = ((), (), s32[]{:S(2)}) async-start(), calls=%async_computation.2 | async-start | bytes 4718592 | tf_op jit(solution)/shard_map/all_gather | solution.py:99
  147.8 4.1 %copy-start.2 = (bf16[4,2048,128]{2,1,0:T(8,128)(2,1)S(1)}, bf16[4,2048,128]{2,1,0:T(8,128)(2,1)}, u32[]{:S(2)}) copy-start(bf16[4,2048,128]{2,1,0:T(8,128)(2,1)} %shard_map.46) | copy-start | bytes 6291460
  151.9 7.5 %collective-permute-start = (bf16[1024,2048]{1,0:T(8,128)(2,1)}, bf16[1024,2048]{1,0:T(8,128)(2,1)}, u32[]{:S(2)}, u32[]{:S(2)}) collective-permute-start(bf16[1024,2048]{1,0:T(8,128)(2,1)} %bitcast.62), channel_id=1, source_target_pairs={{0,128},{128,0},{1,129},{129,1},{2,130},{130,2},{3,131},{131,3},{4... | collective-permute-start | bytes 12582920 | tf_op jit(solution)/shard_map/ppermute | solution.py:112
  205.3 7.5 %collective-permute-start.1 = (bf16[2048,1024]{1,0:T(8,128)(2,1)}, bf16[2048,1024]{1,0:T(8,128)(2,1)}, u32[]{:S(2)}, u32[]{:S(2)}) collective-permute-start(bf16[2048,1024]{1,0:T(8,128)(2,1)} %all-gather.4.cloned.1.call-done), channel_id=1, source_target_pairs={{0,128},{128,0},{1,129},{129,1},{2,130},{130,2},{3,131},{131,3},{4... | collective-permute-start | bytes 12582920 | tf_op jit(solution)/shard_map/ppermute | solution.py:112
  205.3 7.5 %copy-start.4 = (bf16[4,128,2048]{2,1,0:T(8,128)(2,1)S(1)}, bf16[4,128,2048]{2,1,0:T(8,128)(2,1)}, u32[]{:S(2)}) copy-start(bf16[4,128,2048]{2,1,0:T(8,128)(2,1)} %reshape.65) | copy-start | bytes 6291460
  220.6 10.2 %copy-start.3 = (bf16[32,256,128]{2,1,0:T(8,128)(2,1)S(1)}, bf16[32,256,128]{2,1,0:T(8,128)(2,1)}, u32[]{:S(2)}) copy-start(bf16[32,256,128]{2,1,0:T(8,128)(2,1)} %broadcast_multiply_fusion.x_ref) | copy-start | bytes 6291460
  220.6 61.9 %all-to-all-start.1 = ((bf16[128,4,16,128]{3,2,1,0:T(8,128)(2,1)}), bf16[128,4,16,128]{3,2,1,0:T(8,128)(2,1)}, u32[]{:S(2)}, u32[]{:S(2)}) async-start(bf16[128,4,16,128]{3,2,1,0:T(8,128)(2,1)} %bitcast.65), calls=%async_computation.1 | async-start | bytes 4194304 | tf_op jit(solution)/shard_map/all_to_all | solution.py:266
  230.8 55.9 %collective-permute-start.2 = (bf16[32,256,128]{2,1,0:T(8,128)(2,1)S(1)}, bf16[32,256,128]{2,1,0:T(8,128)(2,1)}, u32[]{:S(2)}, u32[]{:S(2)}) collective-permute-start(bf16[32,256,128]{2,1,0:T(8,128)(2,1)S(1)} %copy-done.3), channel_id=1, source_target_pairs={{0,128},{128,0},{1,129},{129,1},{2,130},{130,2},{3,131},{131,3},{4... | collective-permute-start | bytes 6291464 | tf_op jit(solution)/shard_map/ppermute | solution.py:17
  285.1 22.5 %copy-start.1 = (bf16[256,2048]{1,0:T(8,128)(2,1)S(1)}, bf16[256,2048]{1,0:T(8,128)(2,1)}, u32[]{:S(2)}) copy-start(bf16[256,2048]{1,0:T(8,128)(2,1)} %param.6) | copy-start | bytes 3145732
Sparse Core Ops, SparseCore 0:
  11.0 131.8 all-gather.5
  144.6 51.4 all-gather.3

commit v16 on v14

--- a/solution.py
+++ b/solution.py
@@ -263,11 +263,16 @@
         .reshape(rows * cols, pieces, jpart, ncol)
     )
     got = lax.all_to_all(by_dest, ("row", "col"), split_axis=0, concat_axis=0, tiled=True)
-    returned = got.reshape(rows, cols, pieces, jpart, ncol).transpose(0, 2, 1, 3, 4)
-    aligned = returned.reshape(pdev, mrow, ncol)
+    returned = got.reshape(rows, cols, pieces, jpart, ncol)
     theirs = swapped(screened, "aux", 0)
-    with_mine = jnp.einsum("pls,qls->pq", aligned, screened, preferred_element_type=jnp.float32)
-    with_theirs = jnp.einsum("pls,qls->pq", aligned, theirs, preferred_element_type=jnp.float32)
+
+    def against(block):
+        split = block.reshape(pdev, cols, jpart, ncol)
+        return jnp.einsum(
+            "rcpjs,qcjs->rpq", returned, split, preferred_element_type=jnp.float32
+        ).reshape(pdev, pdev)
+
+    with_mine, with_theirs = against(screened), against(theirs)
     first_half = jnp.where(aux_idx == 0, with_mine, with_theirs)
     second_half = jnp.where(aux_idx == 0, with_theirs, with_mine)
     partial_chi = jnp.concatenate([first_half, second_half], axis=1)

time: 253 us -> 253 us (level)
    dot_general x0 -> x1, local copies, waits for them, and re-layouts: none -> 2.62 us  [against(): jnp.einsum('rcpjs,qcjs->rpq', returned, split, preferred_element_type=jnp...]
    transpose x1 -> x0, local copies, waits for them, and re-layouts: 2.62 us -> none  [shards(): got.reshape(rows, cols, pieces, jpart, ncol).transpose(0, 2, 1, 3, 4)]
where the time goes in v16:
time: 253 us; the launch traced here: 252 us
  Pallas kernels  80.5 us (32%)
  waiting for transfers between devices  67.9 us (27%)
  blocking collectives  31.6 us (12%)
  matrix products  22.8 us (9%)
  local copies, waits for them, and re-layouts  18.9 us (7%)
  between operations  13.6 us (5%)
  starting transfers between devices  11.8 us (5%)
  other arithmetic  5.27 us (2%)
    pallas_call x2, Pallas kernels, exchange(): pl.pallas_call(functools.partial(exchange_kernel, mesh_axis, split_axis,...  64.6 us
    all_to_all x1, waiting for transfers between devices, shards(): lax.all_to_all(by_dest, ('row', 'col'), split_axis=0, concat_axis=0, tile...  51.6 us
    all_to_all x1, blocking collectives, shards(): lax.all_to_all(shaped, 'col', split_axis=2, concat_axis=4, tiled=True)  31.6 us
    pallas_call x1, Pallas kernels, doubling_sum(): pl.pallas_call(two_round_kernel, out_shape=jax.ShapeDtypeStruct(partial.s...  15.8 us
    all_to_all x1, starting transfers between devices, shards(): lax.all_to_all(by_dest, ('row', 'col'), split_axis=0, concat_axis=0, tile...  11.6 us
    all_gather x1, waiting for transfers between devices, gather_occ_rows(): return lax.all_gather(column, 'col', axis=1, tiled=True)  8.8 us
    dot_general x1, matrix products, shards(): jnp.einsum('ml,pmn->pln', occ_other, other, preferred_element_type=jnp.fl...  5.91 us
    dot_general x1, matrix products, shards(): jnp.einsum('pln,ns->pls', spread, virt_own, preferred_element_type=jnp.fl...  5.3 us
  transfers between devices with their start and end apart: 6, of which 5 were waited for; matrix products, arithmetic and copies ran while one was open for 12% of the time, Pallas kernels for 20%

profile of v16, /device:TPU:24, one launch (start us, length us, event | category | flops | bytes accessed | tf_op | source)
XLA Modules:
  0.0 252.2 jit_solution(14139809310476102207)
XLA Ops:
  6.5 0.0 copy-start
  6.5 0.0 copy-start.3
  6.5 0.0 all-gather.5.cloned.1.call-start
  6.5 0.9 dynamic_slice.17
  7.5 0.7 tile.4
  8.2 14.7 %shard_map.46 = bf16[1024,128]{1,0:T(8,128)(2,1)} custom-call(bf16[1024,128]{1,0:T(8,128)(2,1)} %bitcast.74), custom_call_target="tpu_custom_call" | custom-call | bytes 524288 | tf_op jit(solution)/shard_map/pallas_call | solution.py:182
  22.9 0.0 all-gather.5.cloned.1.call-update
  22.9 0.0 all-gather.3.cloned.1.call-start
  23.0 0.0 copy-done
  23.0 0.8 constant_dynamic-slice_fusion.2
  23.8 0.0 all-gather.3.cloned.1.call-update
  23.9 0.9 fusion.29
  24.7 0.1 broadcast_bitcast_fusion
  24.8 0.0 copy-done.3
  24.8 1.6 broadcast_multiply_fusion.x_ref
  26.4 49.9 %shard_map.47 = bf16[4,2048,128]{2,1,0:T(8,128)(2,1)} custom-call(bf16[32,256,128]{2,1,0:T(8,128)(2,1)} %broadcast_multiply_fusion.x_ref), custom_call_target="tpu_custom_call" | custom-call | bytes 4194304 | tf_op jit(solution)/shard_map/pallas_call | solution.py:182
  76.3 8.8 %all-gather.5.cloned.1.call-done = bf16[1024,2048]{1,0:T(8,128)(2,1)} async-done(((bf16[1024,128]{1,0:T(8,128)(2,1)}), bf16[1024,2048]{1,0:T(8,128)(2,1)}) %all-gather.5.cloned.1.call-update) | async-done | bytes 4194320 | tf_op jit(solution)/shard_map/all_gather | solution.py:207
  85.1 0.0 collective-permute-start
  85.1 0.0 copy-start.2
  85.1 1.8 constant_dynamic-slice_fusion
  87.0 1.0 copy-done.2
  87.9 2.4 fusion.6
  90.4 2.2 collective-permute-done
  92.6 5.9 %fusion.10 = bf16[4,2048,128]{1,2,0:T(8,128)(2,1)} fusion(f32[4,128,2048]{2,1,0:T(8,128)S(1)} %fusion.6, bf16[4,1024,128]{2,1,0:T(8,128)(2,1)S(1)} %bitcast.71, bf16[1024,2048]{1,0:T(8,128)(2,1)} %collective-permute-done), kind=kOutput, calls=%fused_computation.9 | convolution fusion | flops 2149580800 | bytes 11534336 | tf_op jit(solution)/shard_map/ml,pmn->pln/dot_general | solution.py:245
  98.5 3.0 %copy.27 = bf16[4,2048,128]{2,1,0:T(8,128)(2,1)S(1)} copy(bf16[4,2048,128]{1,2,0:T(8,128)(2,1)} %fusion.10) | data formatting | bytes 4194304 | tf_op jit(solution)/shard_map/convert_element_type | solution.py:246
  101.6 0.6 copy.28
  102.2 31.6 %all_to_all.20 = bf16[4,8,16,16,128]{4,3,1,0,2:T(8,128)(2,1)S(1)} all-to-all(bf16[4,8,16,16,128]{4,3,1,0,2:T(8,128)(2,1)S(1)} %copy.28), channel_id=1, replica_groups=mesh['aux'=2,'row'=8,'col'=16] {'col'}, dimensions={2} | all-to-all | bytes 4194304 | tf_op jit(solution)/shard_map/all_to_all | solution.py:249
  133.8 2.4 copy.29
  136.2 2.3 reshape.68
  138.5 3.0 %all-gather.3.cloned.1.call-done = bf16[2048,1024]{1,0:T(8,128)(2,1)} async-done(((bf16[256,1024]{1,0:T(8,128)(2,1)}), bf16[2048,1024]{1,0:T(8,128)(2,1)}) %all-gather.3.cloned.1.call-update) | async-done | bytes 4194320 | tf_op jit(solution)/shard_map/all_gather | solution.py:99
  141.6 0.0 collective-permute-start.1
  141.6 0.0 copy-start.4
  141.6 5.3 %fusion.17 = bf16[4,128,1024]{2,1,0:T(8,128)(2,1)S(1)} fusion(bf16[4,128,2048]{2,1,0:T(8,128)(2,1)} %reshape.68, bf16[2048,1024]{1,0:T(8,128)(2,1)} %all-gather.3.cloned.1.call-done), kind=kOutput, calls=%fused_computation.15 | convolution fusion | flops 2148007936 | bytes 7340032 | tf_op jit(solution)/shard_map/pln,ns->pls/dot_general | solution.py:253
  146.9 2.2 collective-permute-done.1
  149.1 0.0 copy-done.4
  149.1 4.5 %fusion.20 = bf16[4,128,1024]{2,1,0:T(8,128)(2,1)S(1)} fusion(bf16[4,128,2048]{2,1,0:T(8,128)(2,1)S(1)} %copy-done.4, bf16[2048,1024]{1,0:T(8,128)(2,1)} %collective-permute-done.1), kind=kOutput, calls=%fused_computation.16 | convolution fusion | flops 2148007936 | bytes 7340032 | tf_op jit(solution)/shard_map/pln,ns->pls/dot_general | solution.py:254
  153.6 0.8 maximum_select_fusion
  154.4 0.6 copy.38
  155.0 1.9 copy.30
  156.9 0.0 copy-start.1
  156.9 11.6 %all-to-all-start.1 = ((bf16[128,4,16,128]{3,2,1,0:T(8,128)(2,1)}), bf16[128,4,16,128]{3,2,1,0:T(8,128)(2,1)}, u32[]{:S(2)}, u32[]{:S(2)}) async-start(bf16[128,4,16,128]{3,2,1,0:T(8,128)(2,1)} %bitcast.65), calls=%async_computation.1 | async-start | bytes 4194304 | tf_op jit(solution)/shard_map/all_to_all | solution.py:265
  168.5 0.0 copy-done.1
  168.5 0.1 collective-permute-start.2
  168.6 51.6 %all-to-all-done.1 = bf16[128,4,16,128]{3,2,1,0:T(8,128)(2,1)} async-done(((bf16[128,4,16,128]{3,2,1,0:T(8,128)(2,1)}), bf16[128,4,16,128]{3,2,1,0:T(8,128)(2,1)}, u32[]{:S(2)}, u32[]{:S(2)}) %all-to-all-start.1) | async-done | bytes 2097184 | tf_op jit(solution)/shard_map/all_to_all | solution.py:265
  220.3 2.6 %copy.31 = bf16[8,4,16,16,128]{4,1,0,3,2:T(4,128)(2,1)S(1)} copy(bf16[8,4,16,16,128]{4,3,1,2,0:T(8,128)(2,1)} %bitcast.16) | data formatting | bytes 4194304 | tf_op jit(solution)/shard_map/rcpjs,qcjs->rpq/dot_general | solution.py:271
  222.9 1.5 fusion.23
  224.4 0.0 collective-permute-done.2
  224.4 3.1 %broadcast_select_fusion.1 = (f32[32,32]{1,0:T(8,128)S(1)}, f32[32,32]{1,0:T(8,128)S(1)}) fusion(f32[32,32]{1,0:T(8,128)S(1)} %fusion.23, pred[]{:T(512)S(6)} %eq.2, bf16[32,16,16,128]{3,0,2,1:T(8,128)(2,1)S(1)} %bitcast.73, bf16[32,16,16,128]{3,2,1,0:T(8,128)(2,1)} %bitcast.21), kind=kOutput, calls=%fused_computation.23 | convolution fusion | flops 67110912 | bytes 4206593 | tf_op jit(solution)/shard_map/rcpjs,qcjs->rpq/dot_general | solution.py:271
  227.5 0.7 pad_maximum_fusion.x_ref
  228.2 15.8 %shard_map.48 = f32[32,64]{1,0:T(8,128)} custom-call(f32[32,64]{1,0:T(8,128)} %pad_maximum_fusion.x_ref), custom_call_target="tpu_custom_call" | custom-call | tf_op jit(solution)/shard_map/pallas_call | solution.py:79
  244.1 1.3 broadcast_multiply_fusion.1
Async XLA Ops:
  6.5 16.4 %copy-start = (bf16[256,2048]{1,0:T(8,128)(2,1)S(1)}, bf16[256,2048]{1,0:T(8,128)(2,1)}, u32[]{:S(2)}) copy-start(bf16[256,2048]{1,0:T(8,128)(2,1)} %param.6) | copy-start | bytes 3145732
  6.5 18.3 %copy-start.3 = (bf16[32,256,128]{2,1,0:T(8,128)(2,1)S(1)}, bf16[32,256,128]{2,1,0:T(8,128)(2,1)}, u32[]{:S(2)}) copy-start(bf16[32,256,128]{2,1,0:T(8,128)(2,1)} %param.4) | copy-start | bytes 6291460
  6.5 78.6 %all-gather.5.cloned.1.call-start = ((), (), s32[]{:S(2)}) async-start(), calls=%async_computation.3 | async-start | bytes 4456448 | tf_op jit(solution)/shard_map/all_gather | solution.py:207
  22.9 118.6 %all-gather.3.cloned.1.call-start = ((), (), s32[]{:S(2)}) async-start(), calls=%async_computation.2 | async-start | bytes 4718592 | tf_op jit(solution)/shard_map/all_gather | solution.py:99
  85.1 7.5 %collective-permute-start = (bf16[1024,2048]{1,0:T(8,128)(2,1)}, bf16[1024,2048]{1,0:T(8,128)(2,1)}, u32[]{:S(2)}, u32[]{:S(2)}) collective-permute-start(bf16[1024,2048]{1,0:T(8,128)(2,1)} %all-gather.5.cloned.1.call-done), channel_id=1, source_target_pairs={{0,128},{128,0},{1,129},{129,1},{2,130},{130,2},{3,131},{131,3},{4... | collective-permute-start | bytes 12582920 | tf_op jit(solution)/shard_map/ppermute | solution.py:112
  85.1 2.8 %copy-start.2 = (bf16[1024,2048]{1,0:T(8,128)(2,1)S(1)}, bf16[1024,2048]{1,0:T(8,128)(2,1)}, u32[]{:S(2)}) copy-start(bf16[1024,2048]{1,0:T(8,128)(2,1)} %all-gather.5.cloned.1.call-done) | copy-start | bytes 12582916
  141.6 7.5 %collective-permute-start.1 = (bf16[2048,1024]{1,0:T(8,128)(2,1)}, bf16[2048,1024]{1,0:T(8,128)(2,1)}, u32[]{:S(2)}, u32[]{:S(2)}) collective-permute-start(bf16[2048,1024]{1,0:T(8,128)(2,1)} %all-gather.3.cloned.1.call-done), channel_id=1, source_target_pairs={{0,128},{128,0},{1,129},{129,1},{2,130},{130,2},{3,131},{131,3},{4... | collective-permute-start | bytes 12582920 | tf_op jit(solution)/shard_map/ppermute | solution.py:112
  141.6 7.5 %copy-start.4 = (bf16[4,128,2048]{2,1,0:T(8,128)(2,1)S(1)}, bf16[4,128,2048]{2,1,0:T(8,128)(2,1)}, u32[]{:S(2)}) copy-start(bf16[4,128,2048]{2,1,0:T(8,128)(2,1)} %reshape.68) | copy-start | bytes 6291460
  156.9 11.6 %copy-start.1 = (bf16[32,256,128]{2,1,0:T(8,128)(2,1)S(1)}, bf16[32,256,128]{2,1,0:T(8,128)(2,1)}, u32[]{:S(2)}) copy-start(bf16[32,256,128]{2,1,0:T(8,128)(2,1)} %broadcast_multiply_fusion.x_ref) | copy-start | bytes 6291460
  156.9 63.4 %all-to-all-start.1 = ((bf16[128,4,16,128]{3,2,1,0:T(8,128)(2,1)}), bf16[128,4,16,128]{3,2,1,0:T(8,128)(2,1)}, u32[]{:S(2)}, u32[]{:S(2)}) async-start(bf16[128,4,16,128]{3,2,1,0:T(8,128)(2,1)} %bitcast.65), calls=%async_computation.1 | async-start | bytes 4194304 | tf_op jit(solution)/shard_map/all_to_all | solution.py:265
  168.5 55.8 %collective-permute-start.2 = (bf16[32,256,128]{2,1,0:T(8,128)(2,1)S(1)}, bf16[32,256,128]{2,1,0:T(8,128)(2,1)}, u32[]{:S(2)}, u32[]{:S(2)}) collective-permute-start(bf16[32,256,128]{2,1,0:T(8,128)(2,1)S(1)} %copy-done.1), channel_id=1, source_target_pairs={{0,128},{128,0},{1,129},{129,1},{2,130},{130,2},{3,131},{131,3},{4... | collective-permute-start | bytes 6291464 | tf_op jit(solution)/shard_map/ppermute | solution.py:17
Sparse Core Ops, SparseCore 0:
  23.0 62.0 all-gather.4
  86.9 54.6 all-gather.2

commit v17 on v16

--- a/solution.py
+++ b/solution.py
@@ -241,19 +241,22 @@
     mine = core_rows(moved, aux_idx)
     other = core_rows(moved, 1 - aux_idx)
     half = (
-        jnp.einsum("ml,pmn->pln", occ_rows, mine, preferred_element_type=jnp.float32)
-        + jnp.einsum("ml,pmn->pln", occ_other, other, preferred_element_type=jnp.float32)
+        jnp.einsum("ml,pmn->pnl", occ_rows, mine, preferred_element_type=jnp.float32)
+        + jnp.einsum("ml,pmn->pnl", occ_other, other, preferred_element_type=jnp.float32)
     ).astype(jnp.bfloat16)
     jpart = mrow // cols
-    shaped = half.reshape(pieces, rows, cols, jpart, ncol)
-    spread = lax.all_to_all(shaped, "col", split_axis=2, concat_axis=4, tiled=True)
-    spread = spread.reshape(pieces, rows * jpart, nao)
+    by_col = half.reshape(pieces, ncol, rows, cols, jpart).transpose(3, 0, 1, 2, 4)
+    spread = lax.all_to_all(by_col, "col", split_axis=0, concat_axis=0, tiled=True)
     virt_own, spread = lax.optimization_barrier((virt_own, spread))
     virt_other = swapped_core(virt_own)
-    dressed_own = jnp.einsum("pln,ns->pls", spread, virt_own, preferred_element_type=jnp.float32)
-    dressed_other = jnp.einsum(
-        "pln,ns->pls", spread, virt_other, preferred_element_type=jnp.float32
-    )
+
+    def dress(columns):
+        split = columns.reshape(cols, ncol, columns.shape[1])
+        out = jnp.einsum("cpnrj,cns->prjs", spread, split, preferred_element_type=jnp.float32)
+        return out.reshape(pieces, rows * jpart, columns.shape[1])
+
+    dressed_own = dress(virt_own)
+    dressed_other = dress(virt_other)
     dressed = join_halves(
         dressed_own.astype(jnp.bfloat16), dressed_other.astype(jnp.bfloat16), axis=2
     )

time: 253 us -> 253 us (level)
  blocking collectives: 31.6 us -> 0 us
  waiting for transfers between devices: 67.9 us -> 98 us
  starting transfers between devices: 11.8 us -> 17.5 us
  local copies, waits for them, and re-layouts: 18.9 us -> 15.5 us
    all_to_all x1 -> x0, blocking collectives: 31.6 us -> none  [shards(): lax.all_to_all(shaped, 'col', split_axis=2, concat_axis=4, tiled=True)]
    all_gather x1, waiting for transfers between devices: 3.02 us -> 32.3 us  [gather_half(): return lax.all_gather(part, 'row', axis=0, tiled=True)]
    all_to_all x0 -> x1, starting transfers between devices: none -> 5.72 us  [shards(): lax.all_to_all(by_col, 'col', split_axis=0, concat_axis=0, tiled=True)]
    reshape x2 -> x0, local copies, waits for them, and re-layouts: 2.95 us -> none  [the longest x1 2.35 us: shards(): spread = spread.reshape(pieces, rows * jpart, nao)]
  transfers between devices with their start and end apart: 6 -> 7, of which waited for: 5 -> 5; matrix products, arithmetic and copies ran while one was open for 12% -> 11% of each run, Pallas kernels for 20% -> 20%
where the time goes in v17:
time: 253 us; the launch traced here: 252 us
  waiting for transfers between devices  98 us (39%)
  Pallas kernels  80.5 us (32%)
  matrix products  22 us (9%)
  starting transfers between devices  17.5 us (7%)
  local copies, waits for them, and re-layouts  15.5 us (6%)
  between operations  13.6 us (5%)
  other arithmetic  5.28 us (2%)
    pallas_call x2, Pallas kernels, exchange(): pl.pallas_call(functools.partial(exchange_kernel, mesh_axis, split_axis,...  64.6 us
    all_to_all x1, waiting for transfers between devices, shards(): lax.all_to_all(by_dest, ('row', 'col'), split_axis=0, concat_axis=0, tile...  51.6 us
    all_gather x1, waiting for transfers between devices, gather_half(): return lax.all_gather(part, 'row', axis=0, tiled=True)  32.3 us
    pallas_call x1, Pallas kernels, doubling_sum(): pl.pallas_call(two_round_kernel, out_shape=jax.ShapeDtypeStruct(partial.s...  15.9 us
    all_to_all x1, starting transfers between devices, shards(): lax.all_to_all(by_dest, ('row', 'col'), split_axis=0, concat_axis=0, tile...  11.6 us
    dot_general x2, matrix products, dress(): jnp.einsum('cpnrj,cns->prjs', spread, split, preferred_element_type=jnp.f...  9.03 us
    all_gather x1, waiting for transfers between devices, gather_occ_rows(): return lax.all_gather(column, 'col', axis=1, tiled=True)  8.79 us
    dot_general x1, matrix products, shards(): jnp.einsum('ml,pmn->pnl', occ_other, other, preferred_element_type=jnp.fl...  5.92 us
  transfers between devices with their start and end apart: 7, of which 5 were waited for; matrix products, arithmetic and copies ran while one was open for 11% of the time, Pallas kernels for 20%

profile of v17, /device:TPU:24, one launch (start us, length us, event | category | flops | bytes accessed | tf_op | source)
XLA Modules:
  0.0 252.2 jit_solution(12525935936866411107)
XLA Ops:
  6.5 0.0 copy-start
  6.5 0.0 copy-start.3
  6.5 0.0 all-gather.5.cloned.1.call-start
  6.5 0.9 dynamic_slice.17
  7.5 0.7 tile.4
  8.2 14.7 %shard_map.46 = bf16[1024,128]{1,0:T(8,128)(2,1)} custom-call(bf16[1024,128]{1,0:T(8,128)(2,1)} %bitcast.83), custom_call_target="tpu_custom_call" | custom-call | bytes 524288 | tf_op jit(solution)/shard_map/pallas_call | solution.py:182
  22.9 0.0 all-gather.5.cloned.1.call-update
  22.9 0.0 all-gather.3.cloned.1.call-start
  23.0 0.0 copy-done
  23.0 0.9 constant_dynamic-slice_fusion.2
  23.8 0.0 all-gather.3.cloned.1.call-update
  23.9 0.9 fusion.16
  24.7 0.1 broadcast_bitcast_fusion
  24.8 0.0 copy-done.3
  24.8 1.6 broadcast_multiply_fusion.x_ref
  26.4 49.9 %shard_map.47 = bf16[4,2048,128]{2,1,0:T(8,128)(2,1)} custom-call(bf16[32,256,128]{2,1,0:T(8,128)(2,1)} %broadcast_multiply_fusion.x_ref), custom_call_target="tpu_custom_call" | custom-call | bytes 4194304 | tf_op jit(solution)/shard_map/pallas_call | solution.py:182
  76.3 8.8 %all-gather.5.cloned.1.call-done = bf16[1024,2048]{1,0:T(8,128)(2,1)} async-done(((bf16[1024,128]{1,0:T(8,128)(2,1)}), bf16[1024,2048]{1,0:T(8,128)(2,1)}) %all-gather.5.cloned.1.call-update) | async-done | bytes 4194320 | tf_op jit(solution)/shard_map/all_gather | solution.py:207
  85.1 0.0 collective-permute-start
  85.1 0.0 copy-start.2
  85.1 1.8 constant_dynamic-slice_fusion
  87.0 1.0 copy-done.2
  87.9 2.4 fusion.2
  90.4 2.2 collective-permute-done
  92.6 5.9 %add_convert_fusion = bf16[4,128,2048]{2,1,0:T(8,128)(2,1)} fusion(f32[4,128,2048]{2,1,0:T(8,128)S(1)} %fusion.2, bf16[4,1024,128]{2,1,0:T(8,128)(2,1)S(1)} %bitcast.78, bf16[1024,2048]{1,0:T(8,128)(2,1)} %collective-permute-done), kind=kOutput, calls=%fused_computation.4 | convolution fusion | flops 2149580800 | bytes 11534336 | tf_op jit(solution)/shard_map/ml,pmn->pnl/dot_general | solution.py:245
  98.5 3.0 %copy.29 = bf16[4,128,2048]{1,2,0:T(8,128)(2,1)S(1)} copy(bf16[4,128,2048]{2,1,0:T(8,128)(2,1)} %add_convert_fusion) | data formatting | bytes 4194304 | tf_op jit(solution)/shard_map/convert_element_type | solution.py:246
  101.6 2.0 copy.30
  103.5 5.7 %all-to-all-start = ((bf16[16,4,128,8,16]{2,4,3,1,0:T(8,128)(2,1)}), bf16[16,4,128,8,16]{2,4,3,1,0:T(8,128)(2,1)S(1)}, u32[]{:S(2)}, u32[]{:S(2)}) async-start(bf16[16,4,128,8,16]{2,4,3,1,0:T(8,128)(2,1)} %copy.30), calls=%async_computation | async-start | bytes 4194304 | tf_op jit(solution)/shard_map/all_to_all | solution.py:249
  109.3 32.3 %all-gather.3.cloned.1.call-done = bf16[2048,1024]{1,0:T(8,128)(2,1)} async-done(((bf16[256,1024]{1,0:T(8,128)(2,1)}), bf16[2048,1024]{1,0:T(8,128)(2,1)}) %all-gather.3.cloned.1.call-update) | async-done | bytes 4194320 | tf_op jit(solution)/shard_map/all_gather | solution.py:99
  141.5 0.0 all-to-all-done
  141.6 0.0 collective-permute-start.1
  141.6 4.5 %bitcast_convert_fusion.1 = bf16[4,128,1024]{2,1,0:T(8,128)(2,1)S(1)} fusion(bf16[4,128,16,128]{3,1,0,2:T(8,128)(2,1)S(1)} %bitcast.79, bf16[16,128,1024,1]{2,1,3,0:T(8,128)(2,1)} %bitcast.84), kind=kOutput, calls=%fused_computation.6 | convolution fusion | flops 2148007936 | bytes 7340032 | tf_op jit(solution)/shard_map/cpnrj,cns->prjs/dot_general | solution.py:255
  146.1 3.0 %collective-permute-done.1 = bf16[2048,1024]{1,0:T(8,128)(2,1)} collective-permute-done((bf16[2048,1024]{1,0:T(8,128)(2,1)}, bf16[2048,1024]{1,0:T(8,128)(2,1)}, u32[]{:S(2)}, u32[]{:S(2)}) %collective-permute-start.1) | collective-permute-done | bytes 4194336 | tf_op jit(solution)/shard_map/ppermute | solution.py:112
  149.1 4.5 %bitcast_convert_fusion = bf16[4,128,1024]{2,1,0:T(8,128)(2,1)S(1)} fusion(bf16[4,128,16,128]{3,1,0,2:T(8,128)(2,1)S(1)} %bitcast.80, bf16[16,128,1024,1]{2,1,3,0:T(8,128)(2,1)} %bitcast.42), kind=kOutput, calls=%fused_computation.5 | convolution fusion | flops 2148007936 | bytes 7340032 | tf_op jit(solution)/shard_map/cpnrj,cns->prjs/dot_general | solution.py:255
  153.6 0.8 maximum_select_fusion
  154.4 0.6 copy.46
  155.0 1.9 copy.34
  156.9 0.0 copy-start.1
  156.9 11.6 %all-to-all-start.1 = ((bf16[128,4,16,128]{3,2,1,0:T(8,128)(2,1)}), bf16[128,4,16,128]{3,2,1,0:T(8,128)(2,1)}, u32[]{:S(2)}, u32[]{:S(2)}) async-start(bf16[128,4,16,128]{3,2,1,0:T(8,128)(2,1)} %bitcast.73), calls=%async_computation.1 | async-start | bytes 4194304 | tf_op jit(solution)/shard_map/all_to_all | solution.py:268
  168.5 0.0 copy-done.1
  168.5 0.1 collective-permute-start.2
  168.6 51.6 %all-to-all-done.1 = bf16[128,4,16,128]{3,2,1,0:T(8,128)(2,1)} async-done(((bf16[128,4,16,128]{3,2,1,0:T(8,128)(2,1)}), bf16[128,4,16,128]{3,2,1,0:T(8,128)(2,1)}, u32[]{:S(2)}, u32[]{:S(2)}) %all-to-all-start.1) | async-done | bytes 2097184 | tf_op jit(solution)/shard_map/all_to_all | solution.py:268
  220.3 2.6 %copy.35 = bf16[8,4,16,16,128]{4,1,0,3,2:T(4,128)(2,1)S(1)} copy(bf16[8,4,16,16,128]{4,3,1,2,0:T(8,128)(2,1)} %bitcast.25) | data formatting | bytes 4194304 | tf_op jit(solution)/shard_map/rcpjs,qcjs->rpq/dot_general | solution.py:274
  222.9 1.5 fusion.10
  224.4 0.0 collective-permute-done.2
  224.4 3.1 %broadcast_select_fusion.1 = (f32[32,32]{1,0:T(8,128)S(1)}, f32[32,32]{1,0:T(8,128)S(1)}) fusion(f32[32,32]{1,0:T(8,128)S(1)} %fusion.10, pred[]{:T(512)S(6)} %eq.2, bf16[32,16,16,128]{3,0,2,1:T(8,128)(2,1)S(1)} %bitcast.82, bf16[32,16,16,128]{3,2,1,0:T(8,128)(2,1)} %bitcast.30), kind=kOutput, calls=%fused_computation.18 | convolution fusion | flops 67110912 | bytes 4206593 | tf_op jit(solution)/shard_map/rcpjs,qcjs->rpq/dot_general | solution.py:274
  227.5 0.7 pad_maximum_fusion.x_ref
  228.2 15.9 %shard_map.48 = f32[32,64]{1,0:T(8,128)} custom-call(f32[32,64]{1,0:T(8,128)} %pad_maximum_fusion.x_ref), custom_call_target="tpu_custom_call" | custom-call | tf_op jit(solution)/shard_map/pallas_call | solution.py:79
  244.0 1.3 broadcast_multiply_fusion.1
Async XLA Ops:
  6.5 16.4 %copy-start = (bf16[256,2048]{1,0:T(8,128)(2,1)S(1)}, bf16[256,2048]{1,0:T(8,128)(2,1)}, u32[]{:S(2)}) copy-start(bf16[256,2048]{1,0:T(8,128)(2,1)} %param.6) | copy-start | bytes 3145732
  6.5 18.3 %copy-start.3 = (bf16[32,256,128]{2,1,0:T(8,128)(2,1)S(1)}, bf16[32,256,128]{2,1,0:T(8,128)(2,1)}, u32[]{:S(2)}) copy-start(bf16[32,256,128]{2,1,0:T(8,128)(2,1)} %param.4) | copy-start | bytes 6291460
  6.5 78.6 %all-gather.5.cloned.1.call-start = ((), (), s32[]{:S(2)}) async-start(), calls=%async_computation.3 | async-start | bytes 4456448 | tf_op jit(solution)/shard_map/all_gather | solution.py:207
  22.9 118.6 %all-gather.3.cloned.1.call-start = ((), (), s32[]{:S(2)}) async-start(), calls=%async_computation.2 | async-start | bytes 4718592 | tf_op jit(solution)/shard_map/all_gather | solution.py:99
  85.1 7.5 %collective-permute-start = (bf16[1024,2048]{1,0:T(8,128)(2,1)}, bf16[1024,2048]{1,0:T(8,128)(2,1)}, u32[]{:S(2)}, u32[]{:S(2)}) collective-permute-start(bf16[1024,2048]{1,0:T(8,128)(2,1)} %all-gather.5.cloned.1.call-done), channel_id=1, source_target_pairs={{0,128},{128,0},{1,129},{129,1},{2,130},{130,2},{3,131},{131,3},{4... | collective-permute-start | bytes 12582920 | tf_op jit(solution)/shard_map/ppermute | solution.py:112
  85.1 2.8 %copy-start.2 = (bf16[1024,2048]{1,0:T(8,128)(2,1)S(1)}, bf16[1024,2048]{1,0:T(8,128)(2,1)}, u32[]{:S(2)}) copy-start(bf16[1024,2048]{1,0:T(8,128)(2,1)} %all-gather.5.cloned.1.call-done) | copy-start | bytes 12582916
  103.5 38.0 %all-to-all-start = ((bf16[16,4,128,8,16]{2,4,3,1,0:T(8,128)(2,1)}), bf16[16,4,128,8,16]{2,4,3,1,0:T(8,128)(2,1)S(1)}, u32[]{:S(2)}, u32[]{:S(2)}) async-start(bf16[16,4,128,8,16]{2,4,3,1,0:T(8,128)(2,1)} %copy.30), calls=%async_computation | async-start | bytes 4194304 | tf_op jit(solution)/shard_map/all_to_all | solution.py:249
  141.6 7.5 %collective-permute-start.1 = (bf16[2048,1024]{1,0:T(8,128)(2,1)}, bf16[2048,1024]{1,0:T(8,128)(2,1)}, u32[]{:S(2)}, u32[]{:S(2)}) collective-permute-start(bf16[2048,1024]{1,0:T(8,128)(2,1)} %all-gather.3.cloned.1.call-done), channel_id=1, source_target_pairs={{0,128},{128,0},{1,129},{129,1},{2,130},{130,2},{3,131},{131,3},{4... | collective-permute-start | bytes 12582920 | tf_op jit(solution)/shard_map/ppermute | solution.py:112
  156.9 11.6 %copy-start.1 = (bf16[32,256,128]{2,1,0:T(8,128)(2,1)S(1)}, bf16[32,256,128]{2,1,0:T(8,128)(2,1)}, u32[]{:S(2)}) copy-start(bf16[32,256,128]{2,1,0:T(8,128)(2,1)} %broadcast_multiply_fusion.x_ref) | copy-start | bytes 6291460
  156.9 63.4 %all-to-all-start.1 = ((bf16[128,4,16,128]{3,2,1,0:T(8,128)(2,1)}), bf16[128,4,16,128]{3,2,1,0:T(8,128)(2,1)}, u32[]{:S(2)}, u32[]{:S(2)}) async-start(bf16[128,4,16,128]{3,2,1,0:T(8,128)(2,1)} %bitcast.73), calls=%async_computation.1 | async-start | bytes 4194304 | tf_op jit(solution)/shard_map/all_to_all | solution.py:268
  168.5 55.8 %collective-permute-start.2 = (bf16[32,256,128]{2,1,0:T(8,128)(2,1)S(1)}, bf16[32,256,128]{2,1,0:T(8,128)(2,1)}, u32[]{:S(2)}, u32[]{:S(2)}) collective-permute-start(bf16[32,256,128]{2,1,0:T(8,128)(2,1)S(1)} %copy-done.1), channel_id=1, source_target_pairs={{0,128},{128,0},{1,129},{129,1},{2,130},{130,2},{3,131},{131,3},{4... | collective-permute-start | bytes 6291464 | tf_op jit(solution)/shard_map/ppermute | solution.py:17
Sparse Core Ops, SparseCore 0:
  23.0 62.0 all-gather.4
  86.9 54.6 all-gather.2

commit v18 on v17

--- a/solution.py
+++ b/solution.py
@@ -215,6 +215,29 @@
     return picked.reshape(pieces, nao // 2, ncol)
 
 
+def ring_half(local, after):
+    width = local.shape[1] // 2
+    part = lax.dynamic_slice_in_dim(local, lax.axis_index("aux") * width, width, axis=1)
+    part, after = lax.optimization_barrier((part, after))
+    n, me = lax.axis_size("row"), lax.axis_index("row")
+    ahead, back = part[:, : width // 2], part[:, width // 2:]
+    got_ahead, got_back = [ahead], [back]
+    for _ in range(1, n):
+        ahead = lax.ppermute(ahead, "row", [(i, (i + 1) % n) for i in range(n)])
+        back = lax.ppermute(back, "row", [(i, (i - 1) % n) for i in range(n)])
+        got_ahead.append(ahead)
+        got_back.append(back)
+    by_offset_ahead = jnp.stack([got_ahead[(n - j) % n] for j in range(n)])
+    by_offset_back = jnp.stack(got_back)
+
+    def placed(by_offset):
+        twice = jnp.concatenate([by_offset, by_offset])
+        return lax.dynamic_slice_in_dim(twice, (n - me) % n, n, axis=0)
+
+    joined = jnp.concatenate([placed(by_offset_ahead), placed(by_offset_back)], axis=2)
+    return joined.reshape(n * local.shape[0], width)
+
+
 def shards(coulomb, occupied, virtual, tile_mask):
     rows = lax.axis_size("row")
     cols = lax.axis_size("col")
@@ -233,8 +256,8 @@
     )
     screened = coulomb * local_mask[None]
     occ_rows = gather_occ_rows(occupied)
-    virt_own = gather_half(virtual)
     moved = exchange(screened, "row", 0, 1, 1)
+    virt_own = ring_half(virtual, moved)
     occ_rows, moved = lax.optimization_barrier((occ_rows, moved))
     pieces = moved.shape[0]
     occ_other = swapped_core(occ_rows)

time: 253 us -> 309 us (1.22)
  starting transfers between devices: 17.5 us -> 41.9 us
  local copies, waits for them, and re-layouts: 15.5 us -> 34.1 us
  waiting for transfers between devices: 98 us -> 109 us
  other arithmetic: 5.28 us -> 9.33 us
    all_gather x1 -> x0, waiting for transfers between devices: 32.3 us -> none  [gather_half(): return lax.all_gather(part, 'row', axis=0, tiled=True)]
    ppermute x0 -> x14, waiting for transfers between devices: none -> 31.4 us  [the longest x7 31.4 us: ring_half(): ahead = lax.ppermute(ahead, 'row', [(i, (i + 1) % n) for i in range(n)])]
    ppermute x0 -> x14, starting transfers between devices: none -> 23.4 us  [the longest x7 22.7 us: ring_half(): back = lax.ppermute(back, 'row', [(i, (i - 1) % n) for i in range(n)])]
    all_to_all x1, waiting for transfers between devices: 0.01 us -> 23.4 us  [shards(): lax.all_to_all(by_col, 'col', split_axis=0, concat_axis=0, tiled=True)]
    unnamed x9 -> x72, local copies, waits for them, and re-layouts: 1.61 us -> 20 us
    all_gather x1, waiting for transfers between devices: 8.79 us -> 0.01 us  [gather_occ_rows(): return lax.all_gather(column, 'col', axis=1, tiled=True)]
  transfers between devices with their start and end apart: 7 -> 20, of which waited for: 5 -> 10; matrix products, arithmetic and copies ran while one was open for 11% -> 12% of each run, Pallas kernels for 20% -> 16%
where the time goes in v18:
time: 309 us
  waiting for transfers between devices  109 us (35%)
  Pallas kernels  80.5 us (26%)
  starting transfers between devices  41.9 us (14%)
  local copies, waits for them, and re-layouts  34.1 us (11%)
  matrix products  19.8 us (6%)
  between operations  13.8 us (4%)
  other arithmetic  9.33 us (3%)
    pallas_call x2, Pallas kernels, exchange(): pl.pallas_call(functools.partial(exchange_kernel, mesh_axis, split_axis,...  64.6 us
    all_to_all x1, waiting for transfers between devices, shards(): lax.all_to_all(by_dest, ('row', 'col'), split_axis=0, concat_axis=0, tile...  51.6 us
    ppermute x7, waiting for transfers between devices, ring_half(): ahead = lax.ppermute(ahead, 'row', [(i, (i + 1) % n) for i in range(n)])  31.4 us
    all_to_all x1, waiting for transfers between devices, shards(): lax.all_to_all(by_col, 'col', split_axis=0, concat_axis=0, tiled=True)  23.4 us
    ppermute x7, starting transfers between devices, ring_half(): back = lax.ppermute(back, 'row', [(i, (i - 1) % n) for i in range(n)])  22.7 us
    unnamed x72, local copies, waits for them, and re-layouts  20 us
    pallas_call x1, Pallas kernels, doubling_sum(): pl.pallas_call(two_round_kernel, out_shape=jax.ShapeDtypeStruct(partial.s...  15.8 us
    all_to_all x1, starting transfers between devices, shards(): lax.all_to_all(by_dest, ('row', 'col'), split_axis=0, concat_axis=0, tile...  10.9 us
  transfers between devices with their start and end apart: 20, of which 10 were waited for; matrix products, arithmetic and copies ran while one was open for 12% of the time, Pallas kernels for 16%

profile of v18, /device:TPU:24, one launch (start us, length us, event | category | flops | bytes accessed | tf_op | source)
XLA Modules:
  0.0 308.8 jit_solution(4367952405586217245)
XLA Ops:
  6.5 0.8 dynamic_slice.26
  7.4 0.7 tile.4
  8.1 14.7 %shard_map.47 = bf16[1024,128]{1,0:T(8,128)(2,1)} custom-call(bf16[1024,128]{1,0:T(8,128)(2,1)} %bitcast.134), custom_call_target="tpu_custom_call" | custom-call | bytes 524288 | tf_op jit(solution)/shard_map/pallas_call | solution.py:182
  22.9 0.9 fusion.16
  23.8 3.1 %broadcast_multiply_fusion.x_ref = bf16[32,256,128]{2,1,0:T(8,128)(2,1)} fusion(bf16[32,256,128]{2,1,0:T(8,128)(2,1)} %param.4, bf16[256]{0:T(256)(128)(2,1)S(1)} %broadcast_bitcast_fusion), kind=kLoop, calls=%fused_computation.15 | loop fusion | flops 1048576 | bytes 4194816 | tf_op jit(solution)/shard_map/mul | solution.py:257
  26.9 49.9 %shard_map.46 = bf16[4,2048,128]{2,1,0:T(8,128)(2,1)} custom-call(bf16[32,256,128]{2,1,0:T(8,128)(2,1)} %broadcast_multiply_fusion.x_ref), custom_call_target="tpu_custom_call" | custom-call | bytes 4194304 | tf_op jit(solution)/shard_map/pallas_call | solution.py:182
  77.0 0.7 collective-permute-start
  77.7 2.6 collective-permute-start.7
  80.3 5.9 %collective-permute-done = bf16[256,512]{1,0:T(8,128)(2,1)S(1)} collective-permute-done((bf16[256,512]{1,0:T(8,128)(2,1)S(1)}, bf16[256,512]{1,0:T(8,128)(2,1)S(1)}, u32[]{:S(2)}, u32[]{:S(2)}) %collective-permute-start) | collective-permute-done | bytes 262176 | tf_op jit(solution)/shard_map/ppermute | solution.py:226
  86.2 3.2 %collective-permute-start.8 = (bf16[256,512]{1,0:T(8,128)(2,1)S(1)}, bf16[256,512]{1,0:T(8,128)(2,1)S(1)}, u32[]{:S(2)}, u32[]{:S(2)}) collective-permute-start(bf16[256,512]{1,0:T(8,128)(2,1)S(1)} %collective-permute-done.7), channel_id=1, source_target_pairs={{0,112},{16,0},{32,16},{48,32},{64,48},{80,64},{96,80},{112,96},{1... | collective-permute-start | bytes 786440 | tf_op jit(solution)/shard_map/ppermute | solution.py:227
  89.4 5.1 %collective-permute-done.1 = bf16[256,512]{1,0:T(8,128)(2,1)S(1)} collective-permute-done((bf16[256,512]{1,0:T(8,128)(2,1)S(1)}, bf16[256,512]{1,0:T(8,128)(2,1)S(1)}, u32[]{:S(2)}, u32[]{:S(2)}) %collective-permute-start.1) | collective-permute-done | bytes 262176 | tf_op jit(solution)/shard_map/ppermute | solution.py:226
  94.5 3.2 %collective-permute-start.9 = (bf16[256,512]{1,0:T(8,128)(2,1)S(1)}, bf16[256,512]{1,0:T(8,128)(2,1)S(1)}, u32[]{:S(2)}, u32[]{:S(2)}) collective-permute-start(bf16[256,512]{1,0:T(8,128)(2,1)S(1)} %collective-permute-done.8), channel_id=1, source_target_pairs={{0,112},{16,0},{32,16},{48,32},{64,48},{80,64},{96,80},{112,96},{1... | collective-permute-start | bytes 786440 | tf_op jit(solution)/shard_map/ppermute | solution.py:227
  97.7 4.3 %collective-permute-done.2 = bf16[256,512]{1,0:T(8,128)(2,1)S(1)} collective-permute-done((bf16[256,512]{1,0:T(8,128)(2,1)S(1)}, bf16[256,512]{1,0:T(8,128)(2,1)S(1)}, u32[]{:S(2)}, u32[]{:S(2)}) %collective-permute-start.2) | collective-permute-done | bytes 262176 | tf_op jit(solution)/shard_map/ppermute | solution.py:226
  102.1 3.2 %collective-permute-start.10 = (bf16[256,512]{1,0:T(8,128)(2,1)S(1)}, bf16[256,512]{1,0:T(8,128)(2,1)S(1)}, u32[]{:S(2)}, u32[]{:S(2)}) collective-permute-start(bf16[256,512]{1,0:T(8,128)(2,1)S(1)} %collective-permute-done.9), channel_id=1, source_target_pairs={{0,112},{16,0},{32,16},{48,32},{64,48},{80,64},{96,80},{112,96},{1... | collective-permute-start | bytes 786440 | tf_op jit(solution)/shard_map/ppermute | solution.py:227
  105.3 0.9 bitcast_dynamic-update-slice_fusion.30
  106.2 3.9 %collective-permute-done.3 = bf16[256,512]{1,0:T(8,128)(2,1)S(1)} collective-permute-done((bf16[256,512]{1,0:T(8,128)(2,1)S(1)}, bf16[256,512]{1,0:T(8,128)(2,1)S(1)}, u32[]{:S(2)}, u32[]{:S(2)}) %collective-permute-start.3) | collective-permute-done | bytes 262176 | tf_op jit(solution)/shard_map/ppermute | solution.py:226
  110.1 0.7 bitcast_dynamic-update-slice_fusion.12
  110.8 3.3 %collective-permute-start.11 = (bf16[256,512]{1,0:T(8,128)(2,1)S(1)}, bf16[256,512]{1,0:T(8,128)(2,1)S(1)}, u32[]{:S(2)}, u32[]{:S(2)}) collective-permute-start(bf16[256,512]{1,0:T(8,128)(2,1)S(1)} %collective-permute-done.10), channel_id=1, source_target_pairs={{0,112},{16,0},{32,16},{48,32},{64,48},{80,64},{96,80},{112,96},{1... | collective-permute-start | bytes 786440 | tf_op jit(solution)/shard_map/ppermute | solution.py:227
  114.1 0.7 bitcast_dynamic-update-slice_fusion.10
  114.9 4.4 %collective-permute-done.4 = bf16[256,512]{1,0:T(8,128)(2,1)S(1)} collective-permute-done((bf16[256,512]{1,0:T(8,128)(2,1)S(1)}, bf16[256,512]{1,0:T(8,128)(2,1)S(1)}, u32[]{:S(2)}, u32[]{:S(2)}) %collective-permute-start.4) | collective-permute-done | bytes 262176 | tf_op jit(solution)/shard_map/ppermute | solution.py:226
  119.3 0.7 bitcast_dynamic-update-slice_fusion.8
  120.0 3.7 %collective-permute-start.12 = (bf16[256,512]{1,0:T(8,128)(2,1)S(1)}, bf16[256,512]{1,0:T(8,128)(2,1)S(1)}, u32[]{:S(2)}, u32[]{:S(2)}) collective-permute-start(bf16[256,512]{1,0:T(8,128)(2,1)S(1)} %collective-permute-done.11), channel_id=1, source_target_pairs={{0,112},{16,0},{32,16},{48,32},{64,48},{80,64},{96,80},{112,96},{1... | collective-permute-start | bytes 786440 | tf_op jit(solution)/shard_map/ppermute | solution.py:227
  123.7 0.7 bitcast_dynamic-update-slice_fusion.6
  124.4 5.2 %collective-permute-done.5 = bf16[256,512]{1,0:T(8,128)(2,1)S(1)} collective-permute-done((bf16[256,512]{1,0:T(8,128)(2,1)S(1)}, bf16[256,512]{1,0:T(8,128)(2,1)S(1)}, u32[]{:S(2)}, u32[]{:S(2)}) %collective-permute-start.5) | collective-permute-done | bytes 262176 | tf_op jit(solution)/shard_map/ppermute | solution.py:226
  129.6 0.8 bitcast_dynamic-update-slice_fusion.4
  130.4 3.4 %collective-permute-start.13 = (bf16[256,512]{1,0:T(8,128)(2,1)S(1)}, bf16[256,512]{1,0:T(8,128)(2,1)S(1)}, u32[]{:S(2)}, u32[]{:S(2)}) collective-permute-start(bf16[256,512]{1,0:T(8,128)(2,1)S(1)} %collective-permute-done.12), channel_id=1, source_target_pairs={{0,112},{16,0},{32,16},{48,32},{64,48},{80,64},{96,80},{112,96},{1... | collective-permute-start | bytes 786440 | tf_op jit(solution)/shard_map/ppermute | solution.py:227
  133.8 0.7 bitcast_dynamic-update-slice_fusion.2
  134.5 2.6 collective-permute-done.6
  137.2 0.7 copy-done.20
  137.9 0.7 bitcast_dynamic-update-slice_fusion.28
  138.7 1.7 bitcast_dynamic-update-slice_fusion.26
  140.5 0.7 bitcast_dynamic-update-slice_fusion.24
  141.2 0.7 bitcast_dynamic-update-slice_fusion.22
  141.9 0.7 bitcast_dynamic-update-slice_fusion.20
  142.7 0.7 bitcast_dynamic-update-slice_fusion.18
  143.4 0.7 bitcast_dynamic-update-slice_fusion.16
  144.1 0.8 bitcast_dynamic-update-slice_fusion
  144.9 0.9 bitcast_dynamic-update-slice_fusion.31
  145.8 0.8 bitcast_dynamic-update-slice_fusion.13
  147.3 0.7 bitcast_dynamic-update-slice_fusion.25
  148.0 0.7 bitcast_dynamic-update-slice_fusion.23
  148.8 0.7 bitcast_dynamic-update-slice_fusion.21
  150.2 0.7 bitcast_dynamic-update-slice_fusion.17
  151.1 2.5 fusion.2
  153.6 3.7 %add_convert_fusion = bf16[4,128,2048]{2,1,0:T(8,128)(2,1)} fusion(f32[4,128,2048]{2,1,0:T(8,128)S(1)} %fusion.2, bf16[4,1024,128]{2,1,0:T(8,128)(2,1)S(1)} %bitcast.129, bf16[1024,2048]{1,0:T(8,128)(2,1)S(1)} %collective-permute-done.14), kind=kOutput, calls=%fused_computation.5 | convolution fusion | flops 2149580800 | bytes 11534336 | tf_op jit(solution)/shard_map/ml,pmn->pnl/dot_general | solution.py:268
  157.3 3.0 copy.29
  160.4 1.9 copy.30
  162.3 7.5 %all-to-all-start = ((bf16[16,4,128,8,16]{2,4,3,1,0:T(8,128)(2,1)}), bf16[16,4,128,8,16]{2,4,3,1,0:T(8,128)(2,1)S(1)}, u32[]{:S(2)}, u32[]{:S(2)}) async-start(bf16[16,4,128,8,16]{2,4,3,1,0:T(8,128)(2,1)} %copy.30), calls=%async_computation | async-start | bytes 4194304 | tf_op jit(solution)/shard_map/all_to_all | solution.py:272
  169.8 1.9 constant_dynamic-slice_fusion.3
  171.7 0.9 copy-done.5
  173.0 2.5 pad_maximum_fusion
  175.5 23.4 %all-to-all-done = bf16[16,4,128,8,16]{2,4,3,1,0:T(8,128)(2,1)S(1)} async-done(((bf16[16,4,128,8,16]{2,4,3,1,0:T(8,128)(2,1)}), bf16[16,4,128,8,16]{2,4,3,1,0:T(8,128)(2,1)S(1)}, u32[]{:S(2)}, u32[]{:S(2)}) %all-to-all-start) | async-done | bytes 2097184 | tf_op jit(solution)/shard_map/all_to_all | solution.py:272
  198.9 4.5 %bitcast_convert_fusion.1 = bf16[4,128,1024]{2,1,0:T(8,128)(2,1)S(1)} fusion(bf16[4,128,16,128]{3,1,0,2:T(8,128)(2,1)S(1)} %bitcast.130, bf16[16,128,1024,1]{2,1,3,0:T(8,128)(2,1)} %bitcast.128), kind=kOutput, calls=%fused_computation.7 | convolution fusion | flops 2148007936 | bytes 7340032 | tf_op jit(solution)/shard_map/cpnrj,cns->prjs/dot_general | solution.py:278
  203.4 3.0 collective-permute-done.15
  206.4 4.5 %bitcast_convert_fusion = bf16[4,128,1024]{2,1,0:T(8,128)(2,1)S(1)} fusion(bf16[4,128,16,128]{3,1,0,2:T(8,128)(2,1)S(1)} %bitcast.131, bf16[16,128,1024,1]{2,1,3,0:T(8,128)(2,1)} %bitcast.59), kind=kOutput, calls=%fused_computation.6 | convolution fusion | flops 2148007936 | bytes 7340032 | tf_op jit(solution)/shard_map/cpnrj,cns->prjs/dot_general | solution.py:278
  210.9 0.8 maximum_select_fusion
  212.4 1.9 copy.34
  214.2 10.9 %all-to-all-start.1 = ((bf16[128,4,16,128]{3,2,1,0:T(8,128)(2,1)}), bf16[128,4,16,128]{3,2,1,0:T(8,128)(2,1)}, u32[]{:S(2)}, u32[]{:S(2)}) async-start(bf16[128,4,16,128]{3,2,1,0:T(8,128)(2,1)} %bitcast.122), calls=%async_computation.1 | async-start | bytes 4194304 | tf_op jit(solution)/shard_map/all_to_all | solution.py:291
  225.2 51.6 %all-to-all-done.1 = bf16[128,4,16,128]{3,2,1,0:T(8,128)(2,1)} async-done(((bf16[128,4,16,128]{3,2,1,0:T(8,128)(2,1)}), bf16[128,4,16,128]{3,2,1,0:T(8,128)(2,1)}, u32[]{:S(2)}, u32[]{:S(2)}) %all-to-all-start.1) | async-done | bytes 2097184 | tf_op jit(solution)/shard_map/all_to_all | solution.py:291
  276.9 2.6 copy.35
  279.5 1.5 fusion.10
  281.0 3.1 %broadcast_select_fusion.1 = (f32[32,32]{1,0:T(8,128)S(1)}, f32[32,32]{1,0:T(8,128)S(1)}) fusion(f32[32,32]{1,0:T(8,128)S(1)} %fusion.10, pred[]{:T(512)S(6)} %eq.8, bf16[32,16,16,128]{3,0,2,1:T(8,128)(2,1)S(1)} %bitcast.133, bf16[32,16,16,128]{3,2,1,0:T(8,128)(2,1)} %bitcast.47), kind=kOutput, calls=%fused_computation.51 | convolution fusion | flops 67110912 | bytes 4206593 | tf_op jit(solution)/shard_map/rcpjs,qcjs->rpq/dot_general | solution.py:297
  284.8 15.8 %shard_map.48 = f32[32,64]{1,0:T(8,128)} custom-call(f32[32,64]{1,0:T(8,128)} %pad_maximum_fusion.1.x_ref), custom_call_target="tpu_custom_call" | custom-call | tf_op jit(solution)/shard_map/pallas_call | solution.py:79
  300.7 1.3 broadcast_multiply_fusion.1
  (78 shorter events, 3.7 us)
Async XLA Ops:
  6.5 70.3 %copy-start = (bf16[256,2048]{1,0:T(8,128)(2,1)S(1)}, bf16[256,2048]{1,0:T(8,128)(2,1)}, u32[]{:S(2)}) copy-start(bf16[256,2048]{1,0:T(8,128)(2,1)} %param.6) | copy-start | bytes 3145732
  6.5 132.1 %all-gather.2.cloned.1.call-start = ((), (), s32[]{:S(2)}) async-start(), calls=%async_computation.2 | async-start | bytes 4456448 | tf_op jit(solution)/shard_map/all_gather | solution.py:207
  77.0 9.2 %collective-permute-start = (bf16[256,512]{1,0:T(8,128)(2,1)S(1)}, bf16[256,512]{1,0:T(8,128)(2,1)S(1)}, u32[]{:S(2)}, u32[]{:S(2)}) collective-permute-start(bf16[256,512]{1,0:T(8,128)(2,1)S(1)} %get-tuple-element.19), channel_id=1, source_target_pairs={{0,16},{16,32},{32,48},{48,64},{64,80},{80,96},{96,112},{112,0},{1... | collective-permute-start | bytes 786440 | tf_op jit(solution)/shard_map/ppermute | solution.py:226
  77.7 8.5 %collective-permute-start.7 = (bf16[256,512]{1,0:T(8,128)(2,1)S(1)}, bf16[256,512]{1,0:T(8,128)(2,1)S(1)}, u32[]{:S(2)}, u32[]{:S(2)}) collective-permute-start(bf16[256,512]{1,0:T(8,128)(2,1)S(1)} %get-tuple-element.20), channel_id=1, source_target_pairs={{0,112},{16,0},{32,16},{48,32},{64,48},{80,64},{96,80},{112,96},{1... | collective-permute-start | bytes 786440 | tf_op jit(solution)/shard_map/ppermute | solution.py:227
  86.2 8.3 %collective-permute-start.1 = (bf16[256,512]{1,0:T(8,128)(2,1)S(1)}, bf16[256,512]{1,0:T(8,128)(2,1)S(1)}, u32[]{:S(2)}, u32[]{:S(2)}) collective-permute-start(bf16[256,512]{1,0:T(8,128)(2,1)S(1)} %collective-permute-done), channel_id=1, source_target_pairs={{0,16},{16,32},{32,48},{48,64},{64,80},{80,96},{96,112},{112,0},{1... | collective-permute-start | bytes 786440 | tf_op jit(solution)/shard_map/ppermute | solution.py:226
  86.2 24.7 %copy-start.18 = (bf16[256,512]{1,0:T(8,128)(2,1)}, bf16[256,512]{1,0:T(8,128)(2,1)S(1)}, u32[]{:S(2)}) copy-start(bf16[256,512]{1,0:T(8,128)(2,1)S(1)} %collective-permute-done.7) | copy-start | bytes 786436
  86.2 8.3 %collective-permute-start.8 = (bf16[256,512]{1,0:T(8,128)(2,1)S(1)}, bf16[256,512]{1,0:T(8,128)(2,1)S(1)}, u32[]{:S(2)}, u32[]{:S(2)}) collective-permute-start(bf16[256,512]{1,0:T(8,128)(2,1)S(1)} %collective-permute-done.7), channel_id=1, source_target_pairs={{0,112},{16,0},{32,16},{48,32},{64,48},{80,64},{96,80},{112,96},{1... | collective-permute-start | bytes 786440 | tf_op jit(solution)/shard_map/ppermute | solution.py:227
  94.5 7.6 %collective-permute-start.2 = (bf16[256,512]{1,0:T(8,128)(2,1)S(1)}, bf16[256,512]{1,0:T(8,128)(2,1)S(1)}, u32[]{:S(2)}, u32[]{:S(2)}) collective-permute-start(bf16[256,512]{1,0:T(8,128)(2,1)S(1)} %collective-permute-done.1), channel_id=1, source_target_pairs={{0,16},{16,32},{32,48},{48,64},{64,80},{80,96},{96,112},{112,0},{1... | collective-permute-start | bytes 786440 | tf_op jit(solution)/shard_map/ppermute | solution.py:226
  94.5 7.6 %collective-permute-start.9 = (bf16[256,512]{1,0:T(8,128)(2,1)S(1)}, bf16[256,512]{1,0:T(8,128)(2,1)S(1)}, u32[]{:S(2)}, u32[]{:S(2)}) collective-permute-start(bf16[256,512]{1,0:T(8,128)(2,1)S(1)} %collective-permute-done.8), channel_id=1, source_target_pairs={{0,112},{16,0},{32,16},{48,32},{64,48},{80,64},{96,80},{112,96},{1... | collective-permute-start | bytes 786440 | tf_op jit(solution)/shard_map/ppermute | solution.py:227
  102.1 8.0 %collective-permute-start.3 = (bf16[256,512]{1,0:T(8,128)(2,1)S(1)}, bf16[256,512]{1,0:T(8,128)(2,1)S(1)}, u32[]{:S(2)}, u32[]{:S(2)}) collective-permute-start(bf16[256,512]{1,0:T(8,128)(2,1)S(1)} %collective-permute-done.2), channel_id=1, source_target_pairs={{0,16},{16,32},{32,48},{48,64},{64,80},{80,96},{96,112},{112,0},{1... | collective-permute-start | bytes 786440 | tf_op jit(solution)/shard_map/ppermute | solution.py:226
  102.1 42.8 %copy-start.6 = (bf16[256,512]{1,0:T(8,128)(2,1)}, bf16[256,512]{1,0:T(8,128)(2,1)S(1)}, u32[]{:S(2)}) copy-start(bf16[256,512]{1,0:T(8,128)(2,1)S(1)} %collective-permute-done.9) | copy-start | bytes 786436
  102.1 8.8 %collective-permute-start.10 = (bf16[256,512]{1,0:T(8,128)(2,1)S(1)}, bf16[256,512]{1,0:T(8,128)(2,1)S(1)}, u32[]{:S(2)}, u32[]{:S(2)}) collective-permute-start(bf16[256,512]{1,0:T(8,128)(2,1)S(1)} %collective-permute-done.9), channel_id=1, source_target_pairs={{0,112},{16,0},{32,16},{48,32},{64,48},{80,64},{96,80},{112,96},{1... | collective-permute-start | bytes 786440 | tf_op jit(solution)/shard_map/ppermute | solution.py:227
  110.1 9.2 %collective-permute-start.4 = (bf16[256,512]{1,0:T(8,128)(2,1)S(1)}, bf16[256,512]{1,0:T(8,128)(2,1)S(1)}, u32[]{:S(2)}, u32[]{:S(2)}) collective-permute-start(bf16[256,512]{1,0:T(8,128)(2,1)S(1)} %collective-permute-done.3), channel_id=1, source_target_pairs={{0,16},{16,32},{32,48},{48,64},{64,80},{80,96},{96,112},{112,0},{1... | collective-permute-start | bytes 786440 | tf_op jit(solution)/shard_map/ppermute | solution.py:226
  110.8 35.8 %copy-start.8 = (bf16[256,512]{1,0:T(8,128)(2,1)}, bf16[256,512]{1,0:T(8,128)(2,1)S(1)}, u32[]{:S(2)}) copy-start(bf16[256,512]{1,0:T(8,128)(2,1)S(1)} %collective-permute-done.10) | copy-start | bytes 786436
  110.8 9.2 %collective-permute-start.11 = (bf16[256,512]{1,0:T(8,128)(2,1)S(1)}, bf16[256,512]{1,0:T(8,128)(2,1)S(1)}, u32[]{:S(2)}, u32[]{:S(2)}) collective-permute-start(bf16[256,512]{1,0:T(8,128)(2,1)S(1)} %collective-permute-done.10), channel_id=1, source_target_pairs={{0,112},{16,0},{32,16},{48,32},{64,48},{80,64},{96,80},{112,96},{1... | collective-permute-start | bytes 786440 | tf_op jit(solution)/shard_map/ppermute | solution.py:227
  119.3 10.3 %collective-permute-start.5 = (bf16[256,512]{1,0:T(8,128)(2,1)S(1)}, bf16[256,512]{1,0:T(8,128)(2,1)S(1)}, u32[]{:S(2)}, u32[]{:S(2)}) collective-permute-start(bf16[256,512]{1,0:T(8,128)(2,1)S(1)} %collective-permute-done.4), channel_id=1, source_target_pairs={{0,16},{16,32},{32,48},{48,64},{64,80},{80,96},{96,112},{112,0},{1... | collective-permute-start | bytes 786440 | tf_op jit(solution)/shard_map/ppermute | solution.py:226
  120.0 27.3 %copy-start.10 = (bf16[256,512]{1,0:T(8,128)(2,1)}, bf16[256,512]{1,0:T(8,128)(2,1)S(1)}, u32[]{:S(2)}) copy-start(bf16[256,512]{1,0:T(8,128)(2,1)S(1)} %collective-permute-done.11) | copy-start | bytes 786436
  120.0 10.4 %collective-permute-start.12 = (bf16[256,512]{1,0:T(8,128)(2,1)S(1)}, bf16[256,512]{1,0:T(8,128)(2,1)S(1)}, u32[]{:S(2)}, u32[]{:S(2)}) collective-permute-start(bf16[256,512]{1,0:T(8,128)(2,1)S(1)} %collective-permute-done.11), channel_id=1, source_target_pairs={{0,112},{16,0},{32,16},{48,32},{64,48},{80,64},{96,80},{112,96},{1... | collective-permute-start | bytes 786440 | tf_op jit(solution)/shard_map/ppermute | solution.py:227
  129.6 0.8 copy-start.16
  129.6 7.6 %collective-permute-start.6 = (bf16[256,512]{1,0:T(8,128)(2,1)S(1)}, bf16[256,512]{1,0:T(8,128)(2,1)S(1)}, u32[]{:S(2)}, u32[]{:S(2)}) collective-permute-start(bf16[256,512]{1,0:T(8,128)(2,1)S(1)} %collective-permute-done.5), channel_id=1, source_target_pairs={{0,16},{16,32},{32,48},{48,64},{64,80},{80,96},{96,112},{112,0},{1... | collective-permute-start | bytes 786440 | tf_op jit(solution)/shard_map/ppermute | solution.py:226
  130.4 18.4 %copy-start.12 = (bf16[256,512]{1,0:T(8,128)(2,1)}, bf16[256,512]{1,0:T(8,128)(2,1)S(1)}, u32[]{:S(2)}) copy-start(bf16[256,512]{1,0:T(8,128)(2,1)S(1)} %collective-permute-done.12) | copy-start | bytes 786436
  130.4 13.7 %collective-permute-start.13 = (bf16[256,512]{1,0:T(8,128)(2,1)S(1)}, bf16[256,512]{1,0:T(8,128)(2,1)S(1)}, u32[]{:S(2)}, u32[]{:S(2)}) collective-permute-start(bf16[256,512]{1,0:T(8,128)(2,1)S(1)} %collective-permute-done.12), channel_id=1, source_target_pairs={{0,112},{16,0},{32,16},{48,32},{64,48},{80,64},{96,80},{112,96},{1... | collective-permute-start | bytes 786440 | tf_op jit(solution)/shard_map/ppermute | solution.py:227
  137.2 0.7 copy-start.20
  138.6 7.2 %copy-start.19 = (bf16[256,512]{1,0:T(8,128)(2,1)S(1)}, bf16[256,512]{1,0:T(8,128)(2,1)}, u32[]{:S(2)}) copy-start(bf16[256,512]{1,0:T(8,128)(2,1)} %copy-done.18) | copy-start | bytes 786436
  138.6 7.2 %copy-start.21 = (bf16[256,512]{1,0:T(8,128)(2,1)S(1)}, bf16[256,512]{1,0:T(8,128)(2,1)}, u32[]{:S(2)}) copy-start(bf16[256,512]{1,0:T(8,128)(2,1)} %copy-done.20) | copy-start | bytes 786436
  138.6 8.0 %copy-start.17 = (bf16[256,512]{1,0:T(8,128)(2,1)S(1)}, bf16[256,512]{1,0:T(8,128)(2,1)}, u32[]{:S(2)}) copy-start(bf16[256,512]{1,0:T(8,128)(2,1)} %copy-done.16) | copy-start | bytes 786436
  138.6 15.0 %collective-permute-start.14 = (bf16[1024,2048]{1,0:T(8,128)(2,1)}, bf16[1024,2048]{1,0:T(8,128)(2,1)S(1)}, u32[]{:S(2)}, u32[]{:S(2)}) collective-permute-start(bf16[1024,2048]{1,0:T(8,128)(2,1)} %all-gather.2.cloned.1.call-done), channel_id=1, source_target_pairs={{0,128},{128,0},{1,129},{129,1},{2,130},{130,2},{3,131},{131,3},{4... | collective-permute-start | bytes 12582920 | tf_op jit(solution)/shard_map/ppermute | solution.py:112
  140.5 10.5 %copy-start.2 = (bf16[4,2048,128]{2,1,0:T(8,128)(2,1)S(1)}, bf16[4,2048,128]{2,1,0:T(8,128)(2,1)}, u32[]{:S(2)}) copy-start(bf16[4,2048,128]{2,1,0:T(8,128)(2,1)} %shard_map.46) | copy-start | bytes 6291460
  144.1 7.0 %copy-start.14 = (bf16[256,512]{1,0:T(8,128)(2,1)}, bf16[256,512]{1,0:T(8,128)(2,1)S(1)}, u32[]{:S(2)}) copy-start(bf16[256,512]{1,0:T(8,128)(2,1)S(1)} %collective-permute-done.13) | copy-start | bytes 786436
  145.8 5.4 %copy-start.4 = (bf16[1024,2048]{1,0:T(8,128)(2,1)S(1)}, bf16[1024,2048]{1,0:T(8,128)(2,1)}, u32[]{:S(2)}) copy-start(bf16[1024,2048]{1,0:T(8,128)(2,1)} %all-gather.2.cloned.1.call-done) | copy-start | bytes 12582916
  162.3 10.3 %copy-start.7 = (bf16[256,512]{1,0:T(8,128)(2,1)S(1)}, bf16[256,512]{1,0:T(8,128)(2,1)}, u32[]{:S(2)}) copy-start(bf16[256,512]{1,0:T(8,128)(2,1)} %copy-done.6) | copy-start | bytes 786436
  162.3 10.3 %copy-start.9 = (bf16[256,512]{1,0:T(8,128)(2,1)S(1)}, bf16[256,512]{1,0:T(8,128)(2,1)}, u32[]{:S(2)}) copy-start(bf16[256,512]{1,0:T(8,128)(2,1)} %copy-done.8) | copy-start | bytes 786436
  162.3 10.4 %copy-start.11 = (bf16[256,512]{1,0:T(8,128)(2,1)S(1)}, bf16[256,512]{1,0:T(8,128)(2,1)}, u32[]{:S(2)}) copy-start(bf16[256,512]{1,0:T(8,128)(2,1)} %copy-done.10) | copy-start | bytes 786436
  162.3 36.6 %all-to-all-start = ((bf16[16,4,128,8,16]{2,4,3,1,0:T(8,128)(2,1)}), bf16[16,4,128,8,16]{2,4,3,1,0:T(8,128)(2,1)S(1)}, u32[]{:S(2)}, u32[]{:S(2)}) async-start(bf16[16,4,128,8,16]{2,4,3,1,0:T(8,128)(2,1)} %copy.30), calls=%async_computation | async-start | bytes 4194304 | tf_op jit(solution)/shard_map/all_to_all | solution.py:272
  169.7 2.8 copy-start.5
  169.7 2.9 copy-start.13
  169.7 3.0 copy-start.15
  198.9 7.5 %collective-permute-start.15 = (bf16[2048,1024]{1,0:T(8,128)(2,1)}, bf16[2048,1024]{1,0:T(8,128)(2,1)}, u32[]{:S(2)}, u32[]{:S(2)}) collective-permute-start(bf16[2048,1024]{1,0:T(8,128)(2,1)} %bitcast.127), channel_id=1, source_target_pairs={{0,128},{128,0},{1,129},{129,1},{2,130},{130,2},{3,131},{131,3},{4... | collective-permute-start | bytes 12582920 | tf_op jit(solution)/shard_map/ppermute | solution.py:112
  212.3 12.8 %copy-start.3 = (bf16[32,256,128]{2,1,0:T(8,128)(2,1)S(1)}, bf16[32,256,128]{2,1,0:T(8,128)(2,1)}, u32[]{:S(2)}) copy-start(bf16[32,256,128]{2,1,0:T(8,128)(2,1)} %broadcast_multiply_fusion.x_ref) | copy-start | bytes 6291460
  214.2 62.6 %all-to-all-start.1 = ((bf16[128,4,16,128]{3,2,1,0:T(8,128)(2,1)}), bf16[128,4,16,128]{3,2,1,0:T(8,128)(2,1)}, u32[]{:S(2)}, u32[]{:S(2)}) async-start(bf16[128,4,16,128]{3,2,1,0:T(8,128)(2,1)} %bitcast.122), calls=%async_computation.1 | async-start | bytes 4194304 | tf_op jit(solution)/shard_map/all_to_all | solution.py:291
  225.1 55.9 %collective-permute-start.16 = (bf16[32,256,128]{2,1,0:T(8,128)(2,1)S(1)}, bf16[32,256,128]{2,1,0:T(8,128)(2,1)}, u32[]{:S(2)}, u32[]{:S(2)}) collective-permute-start(bf16[32,256,128]{2,1,0:T(8,128)(2,1)S(1)} %copy-done.3), channel_id=1, source_target_pairs={{0,128},{128,0},{1,129},{129,1},{2,130},{130,2},{3,131},{131,3},{4... | collective-permute-start | bytes 6291464 | tf_op jit(solution)/shard_map/ppermute | solution.py:17
  279.5 22.5 %copy-start.1 = (bf16[256,2048]{1,0:T(8,128)(2,1)S(1)}, bf16[256,2048]{1,0:T(8,128)(2,1)}, u32[]{:S(2)}) copy-start(bf16[256,2048]{1,0:T(8,128)(2,1)} %param.6) | copy-start | bytes 3145732
Sparse Core Ops, SparseCore 0:
  23.0 62.0 all-gather.1

commit v19 on v16

--- a/solution.py
+++ b/solution.py
@@ -204,7 +204,12 @@
         local, (lax.axis_index("aux") * height, lax.axis_index("col") * width), (height, width)
     )
     column = exchange(jnp.tile(piece, (rows, 1)), "row", 0, 0, 5)
-    return lax.all_gather(column, "col", axis=1, tiled=True)
+    top, bottom = column[: height * rows // 2], column[height * rows // 2:]
+    by_gather = lax.all_gather(top, "col", axis=1, tiled=True)
+    copies = jnp.broadcast_to(bottom[None], (cols,) + bottom.shape)
+    by_swap = lax.all_to_all(copies, "col", split_axis=0, concat_axis=0, tiled=True)
+    by_swap = by_swap.transpose(1, 0, 2).reshape(bottom.shape[0], cols * width)
+    return jnp.concatenate([by_gather, by_swap], axis=0)
 
 
 def core_rows(moved, core):

time: 253 us -> 262 us (1.036)
  waiting for transfers between devices: 67.9 us -> 57.6 us
  starting transfers between devices: 11.8 us -> 20.2 us
  other arithmetic: 5.27 us -> 11.7 us
    all_gather x1, waiting for transfers between devices: 8.8 us -> 1.26 us  [gather_occ_rows(): by_gather = lax.all_gather(top, 'col', axis=1, tiled=True)]
    all_to_all x0 -> x1, starting transfers between devices: none -> 7.17 us  [gather_occ_rows(): lax.all_to_all(copies, 'col', split_axis=0, concat_axis=0, tiled=True)]
    concatenate x0 -> x1, other arithmetic: none -> 4.79 us  [gather_occ_rows(): return jnp.concatenate([by_gather, by_swap], axis=0)]
    all_gather x1, waiting for transfers between devices: 3.02 us -> 0.01 us  [gather_half(): return lax.all_gather(part, 'row', axis=0, tiled=True)]
  transfers between devices with their start and end apart: 6 -> 7, of which waited for: 5 -> 4; matrix products, arithmetic and copies ran while one was open for 12% -> 16% of each run, Pallas kernels for 20% -> 19%
where the time goes in v19:
time: 262 us; the launch traced here: 261 us
  Pallas kernels  79.9 us (30%)
  waiting for transfers between devices  57.6 us (22%)
  blocking collectives  31.9 us (12%)
  matrix products  25.2 us (10%)
  local copies, waits for them, and re-layouts  21.3 us (8%)
  starting transfers between devices  20.2 us (8%)
  between operations  13.6 us (5%)
  other arithmetic  11.7 us (4%)
    pallas_call x2, Pallas kernels, exchange(): pl.pallas_call(functools.partial(exchange_kernel, mesh_axis, split_axis,...  64 us
    all_to_all x1, waiting for transfers between devices, shards(): lax.all_to_all(by_dest, ('row', 'col'), split_axis=0, concat_axis=0, tile...  51.4 us
    all_to_all x1, blocking collectives, shards(): lax.all_to_all(shaped, 'col', split_axis=2, concat_axis=4, tiled=True)  31.9 us
    pallas_call x1, Pallas kernels, doubling_sum(): pl.pallas_call(two_round_kernel, out_shape=jax.ShapeDtypeStruct(partial.s...  15.8 us
    all_to_all x1, starting transfers between devices, shards(): lax.all_to_all(by_dest, ('row', 'col'), split_axis=0, concat_axis=0, tile...  12.7 us
    all_to_all x1, starting transfers between devices, gather_occ_rows(): lax.all_to_all(copies, 'col', split_axis=0, concat_axis=0, tiled=True)  7.17 us
    dot_general x1, matrix products, shards(): jnp.einsum('ml,pmn->pln', occ_other, other, preferred_element_type=jnp.fl...  6.08 us
    dot_general x1, matrix products, shards(): jnp.einsum('pln,ns->pls', spread, virt_own, preferred_element_type=jnp.fl...  5.3 us
  transfers between devices with their start and end apart: 7, of which 4 were waited for; matrix products, arithmetic and copies ran while one was open for 16% of the time, Pallas kernels for 19%

profile of v19, /device:TPU:24, one launch (start us, length us, event | category | flops | bytes accessed | tf_op | source)
XLA Modules:
  0.0 261.3 jit_solution(18027119807779177010)
XLA Ops:
  6.5 0.0 copy-start
  6.5 0.0 all-gather.5.cloned.1.call-start
  6.5 0.8 dynamic_slice.17
  7.4 0.7 tile.4
  8.1 14.7 %shard_map.46 = bf16[1024,128]{1,0:T(8,128)(2,1)} custom-call(bf16[1024,128]{1,0:T(8,128)(2,1)} %bitcast.80), custom_call_target="tpu_custom_call" | custom-call | bytes 524288 | tf_op jit(solution)/shard_map/pallas_call | solution.py:182
  22.8 1.6 fusion.30
  24.5 0.0 all-gather.5.cloned.1.call-update
  24.5 1.7 broadcast_in_dim.4
  26.2 7.2 %all-to-all-start = ((bf16[16,512,128]{2,1,0:T(8,128)(2,1)}), bf16[16,512,128]{2,1,0:T(8,128)(2,1)S(1)}, u32[]{:S(2)}, u32[]{:S(2)}) async-start(bf16[16,512,128]{2,1,0:T(8,128)(2,1)} %broadcast_in_dim.4), calls=%async_computation | async-start | bytes 4194304 | tf_op jit(solution)/shard_map/all_to_all | solution.py:210
  33.4 0.0 all-gather.3.cloned.1.call-start
  33.4 0.0 copy-done
  33.5 0.9 constant_dynamic-slice_fusion.2
  34.3 0.0 all-gather.3.cloned.1.call-update
  34.3 0.9 fusion.29
  35.2 0.1 broadcast_bitcast_fusion
  35.3 3.2 %broadcast_multiply_fusion.x_ref = bf16[32,256,128]{2,1,0:T(8,128)(2,1)} fusion(bf16[32,256,128]{2,1,0:T(8,128)(2,1)} %param.4, bf16[256]{0:T(256)(128)(2,1)S(1)} %broadcast_bitcast_fusion), kind=kLoop, calls=%fused_computation.21 | loop fusion | flops 1048576 | bytes 4194816 | tf_op jit(solution)/shard_map/mul | solution.py:239
  38.5 49.3 %shard_map.47 = bf16[4,2048,128]{2,1,0:T(8,128)(2,1)} custom-call(bf16[32,256,128]{2,1,0:T(8,128)(2,1)} %broadcast_multiply_fusion.x_ref), custom_call_target="tpu_custom_call" | custom-call | bytes 4194304 | tf_op jit(solution)/shard_map/pallas_call | solution.py:182
  87.8 0.0 all-to-all-done
  87.8 1.6 copy_bitcast_fusion
  89.5 0.0 copy-start.2
  89.5 1.3 all-gather.5.cloned.1.call-done
  90.7 4.8 %pad_maximum_fusion = bf16[1024,2048]{1,0:T(8,128)(2,1)} fusion(bf16[512,2048]{1,0:T(8,128)(2,1)} %copy_bitcast_fusion, bf16[512,2048]{1,0:T(8,128)(2,1)} %all-gather.5.cloned.1.call-done), kind=kLoop, calls=%fused_computation | loop fusion | flops 8388608 | bytes 8388608 | tf_op jit(solution)/shard_map/concatenate | solution.py:212
  95.5 0.0 collective-permute-start
  95.5 0.0 copy-done.2
  95.5 0.2 constant_dynamic-slice_fusion
  95.7 4.6 %fusion.6 = f32[4,128,2048]{2,1,0:T(8,128)S(1)} fusion(bf16[4,1024,128]{2,1,0:T(8,128)(2,1)S(1)} %bitcast.76, bf16[1024,2048]{1,0:T(8,128)(2,1)} %pad_maximum_fusion), kind=kOutput, calls=%fused_computation.7 | convolution fusion | flops 2147483648 | bytes 9437184 | tf_op jit(solution)/shard_map/ml,pmn->pln/dot_general | solution.py:249
  100.3 2.7 %collective-permute-done = bf16[1024,2048]{1,0:T(8,128)(2,1)} collective-permute-done((bf16[1024,2048]{1,0:T(8,128)(2,1)}, bf16[1024,2048]{1,0:T(8,128)(2,1)}, u32[]{:S(2)}, u32[]{:S(2)}) %collective-permute-start) | collective-permute-done | bytes 4194336 | tf_op jit(solution)/shard_map/ppermute | solution.py:112
  103.0 6.1 %fusion.10 = bf16[4,2048,128]{1,2,0:T(8,128)(2,1)} fusion(f32[4,128,2048]{2,1,0:T(8,128)S(1)} %fusion.6, bf16[4,1024,128]{2,1,0:T(8,128)(2,1)S(1)} %bitcast.77, bf16[1024,2048]{1,0:T(8,128)(2,1)} %collective-permute-done), kind=kOutput, calls=%fused_computation.10 | convolution fusion | flops 2149580800 | bytes 11534336 | tf_op jit(solution)/shard_map/ml,pmn->pln/dot_general | solution.py:250
  109.1 3.0 %copy.28 = bf16[4,2048,128]{2,1,0:T(8,128)(2,1)S(1)} copy(bf16[4,2048,128]{1,2,0:T(8,128)(2,1)} %fusion.10) | data formatting | bytes 4194304 | tf_op jit(solution)/shard_map/convert_element_type | solution.py:251
  112.2 0.6 copy.29
  112.8 31.9 %all_to_all.25 = bf16[4,8,16,16,128]{4,3,1,0,2:T(8,128)(2,1)S(1)} all-to-all(bf16[4,8,16,16,128]{4,3,1,0,2:T(8,128)(2,1)S(1)} %copy.29), channel_id=1, replica_groups=mesh['aux'=2,'row'=8,'col'=16] {'col'}, dimensions={2} | all-to-all | bytes 4194304 | tf_op jit(solution)/shard_map/all_to_all | solution.py:254
  144.7 2.4 copy.30
  147.1 2.4 reshape.73
  149.5 0.0 all-gather.3.cloned.1.call-done
  149.5 0.0 collective-permute-start.1
  149.5 0.0 copy-start.4
  149.5 5.3 %fusion.17 = bf16[4,128,1024]{2,1,0:T(8,128)(2,1)S(1)} fusion(bf16[4,128,2048]{2,1,0:T(8,128)(2,1)} %reshape.73, bf16[2048,1024]{1,0:T(8,128)(2,1)} %all-gather.3.cloned.1.call-done), kind=kOutput, calls=%fused_computation.17 | convolution fusion | flops 2148007936 | bytes 7340032 | tf_op jit(solution)/shard_map/pln,ns->pls/dot_general | solution.py:258
  154.8 2.2 collective-permute-done.1
  157.0 0.0 copy-done.4
  157.0 4.5 %fusion.20 = bf16[4,128,1024]{2,1,0:T(8,128)(2,1)S(1)} fusion(bf16[4,128,2048]{2,1,0:T(8,128)(2,1)S(1)} %copy-done.4, bf16[2048,1024]{1,0:T(8,128)(2,1)} %collective-permute-done.1), kind=kOutput, calls=%fused_computation.18 | convolution fusion | flops 2148007936 | bytes 7340032 | tf_op jit(solution)/shard_map/pln,ns->pls/dot_general | solution.py:259
  161.5 0.8 maximum_select_fusion
  162.3 0.6 copy.40
  162.9 1.9 copy.31
  164.8 0.0 copy-start.3
  164.8 12.7 %all-to-all-start.2 = ((bf16[128,4,16,128]{3,2,1,0:T(8,128)(2,1)}), bf16[128,4,16,128]{3,2,1,0:T(8,128)(2,1)}, u32[]{:S(2)}, u32[]{:S(2)}) async-start(bf16[128,4,16,128]{3,2,1,0:T(8,128)(2,1)} %bitcast.71), calls=%async_computation.2 | async-start | bytes 4194304 | tf_op jit(solution)/shard_map/all_to_all | solution.py:270
  177.5 0.0 copy-done.3
  177.5 0.3 collective-permute-start.2
  177.8 51.4 %all-to-all-done.2 = bf16[128,4,16,128]{3,2,1,0:T(8,128)(2,1)} async-done(((bf16[128,4,16,128]{3,2,1,0:T(8,128)(2,1)}), bf16[128,4,16,128]{3,2,1,0:T(8,128)(2,1)}, u32[]{:S(2)}, u32[]{:S(2)}) %all-to-all-start.2) | async-done | bytes 2097184 | tf_op jit(solution)/shard_map/all_to_all | solution.py:270
  229.2 2.6 %copy.32 = bf16[8,4,16,16,128]{4,1,0,3,2:T(4,128)(2,1)S(1)} copy(bf16[8,4,16,16,128]{4,3,1,2,0:T(8,128)(2,1)} %bitcast.17) | data formatting | bytes 4194304 | tf_op jit(solution)/shard_map/rcpjs,qcjs->rpq/dot_general | solution.py:276
  231.8 1.5 fusion.23
  233.3 0.0 collective-permute-done.2
  233.3 0.0 copy-start.1
  233.3 3.2 %broadcast_select_fusion.1 = (f32[32,32]{1,0:T(8,128)S(1)}, f32[32,32]{1,0:T(8,128)S(1)}) fusion(f32[32,32]{1,0:T(8,128)S(1)} %fusion.23, pred[]{:T(512)S(6)} %eq.2, bf16[32,16,16,128]{3,0,2,1:T(8,128)(2,1)S(1)} %bitcast.79, bf16[32,16,16,128]{3,2,1,0:T(8,128)(2,1)} %bitcast.22), kind=kOutput, calls=%fused_computation.25 | convolution fusion | flops 67110912 | bytes 4206593 | tf_op jit(solution)/shard_map/rcpjs,qcjs->rpq/dot_general | solution.py:276
  236.6 0.7 pad_maximum_fusion.1.x_ref
  237.2 15.8 %shard_map.48 = f32[32,64]{1,0:T(8,128)} custom-call(f32[32,64]{1,0:T(8,128)} %pad_maximum_fusion.1.x_ref), custom_call_target="tpu_custom_call" | custom-call | tf_op jit(solution)/shard_map/pallas_call | solution.py:79
  253.1 1.3 broadcast_multiply_fusion.1
  254.4 0.0 copy-done.1
Async XLA Ops:
  6.5 26.9 %copy-start = (bf16[256,2048]{1,0:T(8,128)(2,1)S(1)}, bf16[256,2048]{1,0:T(8,128)(2,1)}, u32[]{:S(2)}) copy-start(bf16[256,2048]{1,0:T(8,128)(2,1)} %param.6) | copy-start | bytes 3145732
  6.5 84.2 %all-gather.5.cloned.1.call-start = ((), (), s32[]{:S(2)}) async-start(), calls=%async_computation.4 | async-start | bytes 2228224 | tf_op jit(solution)/shard_map/all_gather | solution.py:208
  26.2 61.6 %all-to-all-start = ((bf16[16,512,128]{2,1,0:T(8,128)(2,1)}), bf16[16,512,128]{2,1,0:T(8,128)(2,1)S(1)}, u32[]{:S(2)}, u32[]{:S(2)}) async-start(bf16[16,512,128]{2,1,0:T(8,128)(2,1)} %broadcast_in_dim.4), calls=%async_computation | async-start | bytes 4194304 | tf_op jit(solution)/shard_map/all_to_all | solution.py:210
  33.4 116.1 %all-gather.3.cloned.1.call-start = ((), (), s32[]{:S(2)}) async-start(), calls=%async_computation.3 | async-start | bytes 4718592 | tf_op jit(solution)/shard_map/all_gather | solution.py:99
  89.5 6.1 %copy-start.2 = (bf16[4,2048,128]{2,1,0:T(8,128)(2,1)S(1)}, bf16[4,2048,128]{2,1,0:T(8,128)(2,1)}, u32[]{:S(2)}) copy-start(bf16[4,2048,128]{2,1,0:T(8,128)(2,1)} %shard_map.47) | copy-start | bytes 6291460
  95.5 7.5 %collective-permute-start = (bf16[1024,2048]{1,0:T(8,128)(2,1)}, bf16[1024,2048]{1,0:T(8,128)(2,1)}, u32[]{:S(2)}, u32[]{:S(2)}) collective-permute-start(bf16[1024,2048]{1,0:T(8,128)(2,1)} %pad_maximum_fusion), channel_id=1, source_target_pairs={{0,128},{128,0},{1,129},{129,1},{2,130},{130,2},{3,131},{131,3},{4... | collective-permute-start | bytes 12582920 | tf_op jit(solution)/shard_map/ppermute | solution.py:112
  149.5 7.5 %collective-permute-start.1 = (bf16[2048,1024]{1,0:T(8,128)(2,1)}, bf16[2048,1024]{1,0:T(8,128)(2,1)}, u32[]{:S(2)}, u32[]{:S(2)}) collective-permute-start(bf16[2048,1024]{1,0:T(8,128)(2,1)} %all-gather.3.cloned.1.call-done), channel_id=1, source_target_pairs={{0,128},{128,0},{1,129},{129,1},{2,130},{130,2},{3,131},{131,3},{4... | collective-permute-start | bytes 12582920 | tf_op jit(solution)/shard_map/ppermute | solution.py:112
  149.5 7.5 %copy-start.4 = (bf16[4,128,2048]{2,1,0:T(8,128)(2,1)S(1)}, bf16[4,128,2048]{2,1,0:T(8,128)(2,1)}, u32[]{:S(2)}) copy-start(bf16[4,128,2048]{2,1,0:T(8,128)(2,1)} %reshape.73) | copy-start | bytes 6291460
  164.8 12.7 %copy-start.3 = (bf16[32,256,128]{2,1,0:T(8,128)(2,1)S(1)}, bf16[32,256,128]{2,1,0:T(8,128)(2,1)}, u32[]{:S(2)}) copy-start(bf16[32,256,128]{2,1,0:T(8,128)(2,1)} %broadcast_multiply_fusion.x_ref) | copy-start | bytes 6291460
  164.8 64.4 %all-to-all-start.2 = ((bf16[128,4,16,128]{3,2,1,0:T(8,128)(2,1)}), bf16[128,4,16,128]{3,2,1,0:T(8,128)(2,1)}, u32[]{:S(2)}, u32[]{:S(2)}) async-start(bf16[128,4,16,128]{3,2,1,0:T(8,128)(2,1)} %bitcast.71), calls=%async_computation.2 | async-start | bytes 4194304 | tf_op jit(solution)/shard_map/all_to_all | solution.py:270
  177.5 55.8 %collective-permute-start.2 = (bf16[32,256,128]{2,1,0:T(8,128)(2,1)S(1)}, bf16[32,256,128]{2,1,0:T(8,128)(2,1)}, u32[]{:S(2)}, u32[]{:S(2)}) collective-permute-start(bf16[32,256,128]{2,1,0:T(8,128)(2,1)S(1)} %copy-done.3), channel_id=1, source_target_pairs={{0,128},{128,0},{1,129},{129,1},{2,130},{130,2},{3,131},{131,3},{4... | collective-permute-start | bytes 6291464 | tf_op jit(solution)/shard_map/ppermute | solution.py:17
  233.3 21.1 %copy-start.1 = (bf16[256,2048]{1,0:T(8,128)(2,1)S(1)}, bf16[256,2048]{1,0:T(8,128)(2,1)}, u32[]{:S(2)}) copy-start(bf16[256,2048]{1,0:T(8,128)(2,1)} %param.6) | copy-start | bytes 3145732
Sparse Core Ops, SparseCore 0:
  24.6 66.0 all-gather.4
  92.5 54.6 all-gather.2

commit v20 on v16

--- a/solution.py
+++ b/solution.py
@@ -71,7 +71,8 @@
         pl.semaphore_signal(barrier, inc=1, device_id=peer, device_id_type=pl.DeviceIdType.MESH)
     pl.semaphore_wait(barrier, len(peers))
     by_col = gather_round("col", here, x_ref[...], col_slots, send_a, recv_a)
-    o_ref[...] = gather_round("row", here, by_col, row_slots, send_b, recv_b)
+    total = gather_round("row", here, by_col, row_slots, send_b, recv_b)
+    o_ref[...] = total * (1.0 / NAO)
 
 
 def doubling_sum(partial):
@@ -276,8 +277,7 @@
     first_half = jnp.where(aux_idx == 0, with_mine, with_theirs)
     second_half = jnp.where(aux_idx == 0, with_theirs, with_mine)
     partial_chi = jnp.concatenate([first_half, second_half], axis=1)
-    total_chi = doubling_sum(partial_chi)
-    return total_chi / NAO
+    return doubling_sum(partial_chi)
 
 
 def solution(mesh):

time: 253 us -> 253 us (level)
  no operation moved by 1% of the time
where the time goes in v20:
time: 253 us; the launch traced here: 252 us
  Pallas kernels  80.5 us (32%)
  waiting for transfers between devices  67.9 us (27%)
  blocking collectives  31.6 us (12%)
  matrix products  22.8 us (9%)
  local copies, waits for them, and re-layouts  20.2 us (8%)
  between operations  13.6 us (5%)
  starting transfers between devices  11.8 us (5%)
  other arithmetic  3.94 us (2%)
    pallas_call x2, Pallas kernels, exchange(): pl.pallas_call(functools.partial(exchange_kernel, mesh_axis, split_axis,...  64.6 us
    all_to_all x1, waiting for transfers between devices, shards(): lax.all_to_all(by_dest, ('row', 'col'), split_axis=0, concat_axis=0, tile...  51.6 us
    all_to_all x1, blocking collectives, shards(): lax.all_to_all(shaped, 'col', split_axis=2, concat_axis=4, tiled=True)  31.6 us
    pallas_call x1, Pallas kernels, doubling_sum(): pl.pallas_call(two_round_kernel, out_shape=jax.ShapeDtypeStruct(partial.s...  15.8 us
    all_to_all x1, starting transfers between devices, shards(): lax.all_to_all(by_dest, ('row', 'col'), split_axis=0, concat_axis=0, tile...  11.6 us
    all_gather x1, waiting for transfers between devices, gather_occ_rows(): return lax.all_gather(column, 'col', axis=1, tiled=True)  8.8 us
    dot_general x1, matrix products, shards(): jnp.einsum('ml,pmn->pln', occ_other, other, preferred_element_type=jnp.fl...  5.91 us
    dot_general x1, matrix products, shards(): jnp.einsum('pln,ns->pls', spread, virt_own, preferred_element_type=jnp.fl...  5.3 us
  transfers between devices with their start and end apart: 6, of which 5 were waited for; matrix products, arithmetic and copies ran while one was open for 12% of the time, Pallas kernels for 20%

profile of v20, /device:TPU:24, one launch (start us, length us, event | category | flops | bytes accessed | tf_op | source)
XLA Modules:
  0.0 252.2 jit_solution(2331854488452792854)
XLA Ops:
  6.5 0.0 copy-start
  6.5 0.0 copy-start.3
  6.5 0.0 all-gather.5.cloned.1.call-start
  6.5 0.9 dynamic_slice.17
  7.5 0.7 tile.4
  8.2 14.7 %shard_map.46 = bf16[1024,128]{1,0:T(8,128)(2,1)} custom-call(bf16[1024,128]{1,0:T(8,128)(2,1)} %bitcast.74), custom_call_target="tpu_custom_call" | custom-call | bytes 524288 | tf_op jit(solution)/shard_map/pallas_call | solution.py:183
  22.9 0.0 all-gather.5.cloned.1.call-update
  22.9 0.0 all-gather.3.cloned.1.call-start
  23.0 0.0 copy-done
  23.0 0.8 constant_dynamic-slice_fusion.2
  23.8 0.0 all-gather.3.cloned.1.call-update
  23.9 0.9 fusion.29
  24.7 0.1 broadcast_bitcast_fusion
  24.8 0.0 copy-done.3
  24.8 1.6 broadcast_multiply_fusion.x_ref
  26.4 49.9 %shard_map.47 = bf16[4,2048,128]{2,1,0:T(8,128)(2,1)} custom-call(bf16[32,256,128]{2,1,0:T(8,128)(2,1)} %broadcast_multiply_fusion.x_ref), custom_call_target="tpu_custom_call" | custom-call | bytes 4194304 | tf_op jit(solution)/shard_map/pallas_call | solution.py:183
  76.3 8.8 %all-gather.5.cloned.1.call-done = bf16[1024,2048]{1,0:T(8,128)(2,1)} async-done(((bf16[1024,128]{1,0:T(8,128)(2,1)}), bf16[1024,2048]{1,0:T(8,128)(2,1)}) %all-gather.5.cloned.1.call-update) | async-done | bytes 4194320 | tf_op jit(solution)/shard_map/all_gather | solution.py:208
  85.1 0.0 collective-permute-start
  85.1 0.0 copy-start.2
  85.1 1.8 constant_dynamic-slice_fusion
  87.0 1.0 copy-done.2
  87.9 2.4 fusion.6
  90.4 2.2 collective-permute-done
  92.6 5.9 %fusion.10 = bf16[4,2048,128]{1,2,0:T(8,128)(2,1)} fusion(f32[4,128,2048]{2,1,0:T(8,128)S(1)} %fusion.6, bf16[4,1024,128]{2,1,0:T(8,128)(2,1)S(1)} %bitcast.71, bf16[1024,2048]{1,0:T(8,128)(2,1)} %collective-permute-done), kind=kOutput, calls=%fused_computation.9 | convolution fusion | flops 2149580800 | bytes 11534336 | tf_op jit(solution)/shard_map/ml,pmn->pln/dot_general | solution.py:246
  98.5 3.0 %copy.27 = bf16[4,2048,128]{2,1,0:T(8,128)(2,1)S(1)} copy(bf16[4,2048,128]{1,2,0:T(8,128)(2,1)} %fusion.10) | data formatting | bytes 4194304 | tf_op jit(solution)/shard_map/convert_element_type | solution.py:247
  101.6 0.6 copy.28
  102.2 31.6 %all_to_all.20 = bf16[4,8,16,16,128]{4,3,1,0,2:T(8,128)(2,1)S(1)} all-to-all(bf16[4,8,16,16,128]{4,3,1,0,2:T(8,128)(2,1)S(1)} %copy.28), channel_id=1, replica_groups=mesh['aux'=2,'row'=8,'col'=16] {'col'}, dimensions={2} | all-to-all | bytes 4194304 | tf_op jit(solution)/shard_map/all_to_all | solution.py:250
  133.8 2.4 copy.29
  136.2 2.3 reshape.68
  138.5 3.0 %all-gather.3.cloned.1.call-done = bf16[2048,1024]{1,0:T(8,128)(2,1)} async-done(((bf16[256,1024]{1,0:T(8,128)(2,1)}), bf16[2048,1024]{1,0:T(8,128)(2,1)}) %all-gather.3.cloned.1.call-update) | async-done | bytes 4194320 | tf_op jit(solution)/shard_map/all_gather | solution.py:100
  141.6 0.0 collective-permute-start.1
  141.6 0.0 copy-start.4
  141.6 5.3 %fusion.17 = bf16[4,128,1024]{2,1,0:T(8,128)(2,1)S(1)} fusion(bf16[4,128,2048]{2,1,0:T(8,128)(2,1)} %reshape.68, bf16[2048,1024]{1,0:T(8,128)(2,1)} %all-gather.3.cloned.1.call-done), kind=kOutput, calls=%fused_computation.15 | convolution fusion | flops 2148007936 | bytes 7340032 | tf_op jit(solution)/shard_map/pln,ns->pls/dot_general | solution.py:254
  146.9 2.2 collective-permute-done.1
  149.1 0.0 copy-done.4
  149.1 4.5 %fusion.20 = bf16[4,128,1024]{2,1,0:T(8,128)(2,1)S(1)} fusion(bf16[4,128,2048]{2,1,0:T(8,128)(2,1)S(1)} %copy-done.4, bf16[2048,1024]{1,0:T(8,128)(2,1)} %collective-permute-done.1), kind=kOutput, calls=%fused_computation.16 | convolution fusion | flops 2148007936 | bytes 7340032 | tf_op jit(solution)/shard_map/pln,ns->pls/dot_general | solution.py:255
  153.6 0.8 maximum_select_fusion
  154.4 0.6 copy.38
  155.0 1.9 copy.30
  156.9 0.0 copy-start.1
  156.9 11.6 %all-to-all-start.1 = ((bf16[128,4,16,128]{3,2,1,0:T(8,128)(2,1)}), bf16[128,4,16,128]{3,2,1,0:T(8,128)(2,1)}, u32[]{:S(2)}, u32[]{:S(2)}) async-start(bf16[128,4,16,128]{3,2,1,0:T(8,128)(2,1)} %bitcast.65), calls=%async_computation.1 | async-start | bytes 4194304 | tf_op jit(solution)/shard_map/all_to_all | solution.py:266
  168.5 0.0 copy-done.1
  168.5 0.1 collective-permute-start.2
  168.6 51.6 %all-to-all-done.1 = bf16[128,4,16,128]{3,2,1,0:T(8,128)(2,1)} async-done(((bf16[128,4,16,128]{3,2,1,0:T(8,128)(2,1)}), bf16[128,4,16,128]{3,2,1,0:T(8,128)(2,1)}, u32[]{:S(2)}, u32[]{:S(2)}) %all-to-all-start.1) | async-done | bytes 2097184 | tf_op jit(solution)/shard_map/all_to_all | solution.py:266
  220.3 2.6 %copy.31 = bf16[8,4,16,16,128]{4,1,0,3,2:T(4,128)(2,1)S(1)} copy(bf16[8,4,16,16,128]{4,3,1,2,0:T(8,128)(2,1)} %bitcast.16) | data formatting | bytes 4194304 | tf_op jit(solution)/shard_map/rcpjs,qcjs->rpq/dot_general | solution.py:272
  222.9 1.5 fusion.23
  224.4 0.0 collective-permute-done.2
  224.4 3.1 %broadcast_select_fusion.1 = (f32[32,32]{1,0:T(8,128)S(1)}, f32[32,32]{1,0:T(8,128)S(1)}) fusion(f32[32,32]{1,0:T(8,128)S(1)} %fusion.23, pred[]{:T(512)S(6)} %eq.2, bf16[32,16,16,128]{3,0,2,1:T(8,128)(2,1)S(1)} %bitcast.73, bf16[32,16,16,128]{3,2,1,0:T(8,128)(2,1)} %bitcast.21), kind=kOutput, calls=%fused_computation.22 | convolution fusion | flops 67110912 | bytes 4206593 | tf_op jit(solution)/shard_map/rcpjs,qcjs->rpq/dot_general | solution.py:272
  227.5 0.7 pad_maximum_fusion.x_ref
  228.2 15.8 %shard_map.48 = f32[32,64]{1,0:T(8,128)} custom-call(f32[32,64]{1,0:T(8,128)} %pad_maximum_fusion.x_ref), custom_call_target="tpu_custom_call" | custom-call | tf_op jit(solution)/shard_map/pallas_call | solution.py:80
  244.1 1.3 copy.50
Async XLA Ops:
  6.5 16.4 %copy-start = (bf16[256,2048]{1,0:T(8,128)(2,1)S(1)}, bf16[256,2048]{1,0:T(8,128)(2,1)}, u32[]{:S(2)}) copy-start(bf16[256,2048]{1,0:T(8,128)(2,1)} %param.6) | copy-start | bytes 3145732
  6.5 18.3 %copy-start.3 = (bf16[32,256,128]{2,1,0:T(8,128)(2,1)S(1)}, bf16[32,256,128]{2,1,0:T(8,128)(2,1)}, u32[]{:S(2)}) copy-start(bf16[32,256,128]{2,1,0:T(8,128)(2,1)} %param.4) | copy-start | bytes 6291460
  6.5 78.6 %all-gather.5.cloned.1.call-start = ((), (), s32[]{:S(2)}) async-start(), calls=%async_computation.3 | async-start | bytes 4456448 | tf_op jit(solution)/shard_map/all_gather | solution.py:208
  22.9 118.6 %all-gather.3.cloned.1.call-start = ((), (), s32[]{:S(2)}) async-start(), calls=%async_computation.2 | async-start | bytes 4718592 | tf_op jit(solution)/shard_map/all_gather | solution.py:100
  85.1 7.5 %collective-permute-start = (bf16[1024,2048]{1,0:T(8,128)(2,1)}, bf16[1024,2048]{1,0:T(8,128)(2,1)}, u32[]{:S(2)}, u32[]{:S(2)}) collective-permute-start(bf16[1024,2048]{1,0:T(8,128)(2,1)} %all-gather.5.cloned.1.call-done), channel_id=1, source_target_pairs={{0,128},{128,0},{1,129},{129,1},{2,130},{130,2},{3,131},{131,3},{4... | collective-permute-start | bytes 12582920 | tf_op jit(solution)/shard_map/ppermute | solution.py:113
  85.1 2.8 %copy-start.2 = (bf16[1024,2048]{1,0:T(8,128)(2,1)S(1)}, bf16[1024,2048]{1,0:T(8,128)(2,1)}, u32[]{:S(2)}) copy-start(bf16[1024,2048]{1,0:T(8,128)(2,1)} %all-gather.5.cloned.1.call-done) | copy-start | bytes 12582916
  141.6 7.5 %collective-permute-start.1 = (bf16[2048,1024]{1,0:T(8,128)(2,1)}, bf16[2048,1024]{1,0:T(8,128)(2,1)}, u32[]{:S(2)}, u32[]{:S(2)}) collective-permute-start(bf16[2048,1024]{1,0:T(8,128)(2,1)} %all-gather.3.cloned.1.call-done), channel_id=1, source_target_pairs={{0,128},{128,0},{1,129},{129,1},{2,130},{130,2},{3,131},{131,3},{4... | collective-permute-start | bytes 12582920 | tf_op jit(solution)/shard_map/ppermute | solution.py:113
  141.6 7.5 %copy-start.4 = (bf16[4,128,2048]{2,1,0:T(8,128)(2,1)S(1)}, bf16[4,128,2048]{2,1,0:T(8,128)(2,1)}, u32[]{:S(2)}) copy-start(bf16[4,128,2048]{2,1,0:T(8,128)(2,1)} %reshape.68) | copy-start | bytes 6291460
  156.9 11.6 %copy-start.1 = (bf16[32,256,128]{2,1,0:T(8,128)(2,1)S(1)}, bf16[32,256,128]{2,1,0:T(8,128)(2,1)}, u32[]{:S(2)}) copy-start(bf16[32,256,128]{2,1,0:T(8,128)(2,1)} %broadcast_multiply_fusion.x_ref) | copy-start | bytes 6291460
  156.9 63.4 %all-to-all-start.1 = ((bf16[128,4,16,128]{3,2,1,0:T(8,128)(2,1)}), bf16[128,4,16,128]{3,2,1,0:T(8,128)(2,1)}, u32[]{:S(2)}, u32[]{:S(2)}) async-start(bf16[128,4,16,128]{3,2,1,0:T(8,128)(2,1)} %bitcast.65), calls=%async_computation.1 | async-start | bytes 4194304 | tf_op jit(solution)/shard_map/all_to_all | solution.py:266
  168.5 55.8 %collective-permute-start.2 = (bf16[32,256,128]{2,1,0:T(8,128)(2,1)S(1)}, bf16[32,256,128]{2,1,0:T(8,128)(2,1)}, u32[]{:S(2)}, u32[]{:S(2)}) collective-permute-start(bf16[32,256,128]{2,1,0:T(8,128)(2,1)S(1)} %copy-done.1), channel_id=1, source_target_pairs={{0,128},{128,0},{1,129},{129,1},{2,130},{130,2},{3,131},{131,3},{4... | collective-permute-start | bytes 6291464 | tf_op jit(solution)/shard_map/ppermute | solution.py:17
Sparse Core Ops, SparseCore 0:
  23.0 62.0 all-gather.4
  86.9 54.6 all-gather.2

commit v21 on v16

--- a/solution.py
+++ b/solution.py
@@ -118,11 +118,13 @@
     return ref.at[tuple(index)]
 
 
-def exchange_kernel(mesh_axis, split_axis, concat_axis, x_ref, o_ref, send_sem, recv_sem, local_sem):
+def exchange_kernel(mesh_axis, split_axis, concat_axis, window, x_ref, o_ref, send_sem, recv_sem, local_sem):
     here = {name: lax.axis_index(name) for name in ("aux", "row", "col")}
     me, n = here[mesh_axis], lax.axis_size(mesh_axis)
     depth = x_ref.shape[split_axis] // n
     height = o_ref.shape[concat_axis] // n
+    if window is not None:
+        depth = window[0]
 
     def device(index):
         place = dict(here)
@@ -130,6 +132,11 @@
         return (place["aux"], place["row"], place["col"])
 
     def piece(index):
+        if window is not None:
+            height, width = window
+            return x_ref.at[
+                pl.ds(here["aux"] * height, height), pl.ds(here["col"] * width, width)
+            ]
         return sliced(x_ref, split_axis, index * depth, depth)
 
     def slot(index):
@@ -173,14 +180,17 @@
     local.wait()
 
 
-def exchange(x, mesh_axis, split_axis, concat_axis, collective_id):
+def exchange(x, mesh_axis, split_axis, concat_axis, collective_id, window=None):
     n = lax.axis_size(mesh_axis)
     shape = list(x.shape)
-    shape[split_axis] //= n
-    shape[concat_axis] *= n
+    if window is not None:
+        shape = [window[0] * n, window[1]]
+    else:
+        shape[split_axis] //= n
+        shape[concat_axis] *= n
     nbytes = x.size * x.dtype.itemsize
     return pl.pallas_call(
-        functools.partial(exchange_kernel, mesh_axis, split_axis, concat_axis),
+        functools.partial(exchange_kernel, mesh_axis, split_axis, concat_axis, window),
         out_shape=jax.ShapeDtypeStruct(tuple(shape), x.dtype),
         in_specs=[pl.BlockSpec(memory_space=pl.ANY)],
         out_specs=pl.BlockSpec(memory_space=pl.ANY),
@@ -200,10 +210,7 @@
     rows, cols = lax.axis_size("row"), lax.axis_size("col")
     width = local.shape[1] // cols
     height = local.shape[0] // 2
-    piece = lax.dynamic_slice(
-        local, (lax.axis_index("aux") * height, lax.axis_index("col") * width), (height, width)
-    )
-    column = exchange(jnp.tile(piece, (rows, 1)), "row", 0, 0, 5)
+    column = exchange(local, "row", 0, 0, 5, window=(height, width))
     return lax.all_gather(column, "col", axis=1, tiled=True)
 
 

time: 253 us -> 252 us (level)
  no operation moved by 1% of the time
where the time goes in v21:
time: 252 us; the launch traced here: 251 us
  Pallas kernels  80.5 us (32%)
  waiting for transfers between devices  68.5 us (27%)
  blocking collectives  31.6 us (13%)
  matrix products  22.8 us (9%)
  local copies, waits for them, and re-layouts  17.3 us (7%)
  between operations  13.6 us (5%)
  starting transfers between devices  11.8 us (5%)
  other arithmetic  5.27 us (2%)
    pallas_call x2, Pallas kernels, exchange(): pl.pallas_call(functools.partial(exchange_kernel, mesh_axis, split_axis,...  64.6 us
    all_to_all x1, waiting for transfers between devices, shards(): lax.all_to_all(by_dest, ('row', 'col'), split_axis=0, concat_axis=0, tile...  51.6 us
    all_to_all x1, blocking collectives, shards(): lax.all_to_all(shaped, 'col', split_axis=2, concat_axis=4, tiled=True)  31.6 us
    pallas_call x1, Pallas kernels, doubling_sum(): pl.pallas_call(two_round_kernel, out_shape=jax.ShapeDtypeStruct(partial.s...  15.8 us
    all_to_all x1, starting transfers between devices, shards(): lax.all_to_all(by_dest, ('row', 'col'), split_axis=0, concat_axis=0, tile...  11.6 us
    all_gather x1, waiting for transfers between devices, gather_occ_rows(): return lax.all_gather(column, 'col', axis=1, tiled=True)  9.41 us
    dot_general x1, matrix products, shards(): jnp.einsum('ml,pmn->pln', occ_other, other, preferred_element_type=jnp.fl...  5.91 us
    dot_general x1, matrix products, shards(): jnp.einsum('pln,ns->pls', spread, virt_own, preferred_element_type=jnp.fl...  5.3 us
  transfers between devices with their start and end apart: 6, of which 5 were waited for; matrix products, arithmetic and copies ran while one was open for 12% of the time, Pallas kernels for 20%

profile of v21, /device:TPU:24, one launch (start us, length us, event | category | flops | bytes accessed | tf_op | source)
XLA Modules:
  0.0 251.2 jit_solution(7099692290019751329)
XLA Ops:
  6.5 0.0 copy-start
  6.5 0.0 copy-start.3
  6.5 0.0 all-gather.5.cloned.1.call-start
  6.5 14.8 %shard_map.46 = bf16[1024,128]{1,0:T(8,128)(2,1)} custom-call(bf16[256,2048]{1,0:T(8,128)(2,1)} %x_ref.1), custom_call_target="tpu_custom_call" | custom-call | bytes 2097152 | tf_op jit(solution)/shard_map/pallas_call | solution.py:192
  21.4 0.0 all-gather.5.cloned.1.call-update
  21.4 0.0 all-gather.3.cloned.1.call-start
  21.4 0.0 copy-done
  21.5 0.8 constant_dynamic-slice_fusion.2
  22.3 0.0 all-gather.3.cloned.1.call-update
  22.3 0.9 fusion.29
  23.2 0.1 broadcast_bitcast_fusion
  23.3 0.0 copy-done.3
  23.3 1.6 broadcast_multiply_fusion.x_ref
  24.9 49.8 %shard_map.47 = bf16[4,2048,128]{2,1,0:T(8,128)(2,1)} custom-call(bf16[32,256,128]{2,1,0:T(8,128)(2,1)} %broadcast_multiply_fusion.x_ref), custom_call_target="tpu_custom_call" | custom-call | bytes 4194304 | tf_op jit(solution)/shard_map/pallas_call | solution.py:192
  74.7 9.4 %all-gather.5.cloned.1.call-done = bf16[1024,2048]{1,0:T(8,128)(2,1)} async-done(((bf16[1024,128]{1,0:T(8,128)(2,1)}), bf16[1024,2048]{1,0:T(8,128)(2,1)}) %all-gather.5.cloned.1.call-update) | async-done | bytes 4194320 | tf_op jit(solution)/shard_map/all_gather | solution.py:214
  84.1 0.0 collective-permute-start
  84.1 0.0 copy-start.2
  84.1 1.8 constant_dynamic-slice_fusion
  85.9 1.0 copy-done.2
  86.9 2.4 fusion.6
  89.3 2.2 collective-permute-done
  91.6 5.9 %fusion.10 = bf16[4,2048,128]{1,2,0:T(8,128)(2,1)} fusion(f32[4,128,2048]{2,1,0:T(8,128)S(1)} %fusion.6, bf16[4,1024,128]{2,1,0:T(8,128)(2,1)S(1)} %bitcast.70, bf16[1024,2048]{1,0:T(8,128)(2,1)} %collective-permute-done), kind=kOutput, calls=%fused_computation.9 | convolution fusion | flops 2149580800 | bytes 11534336 | tf_op jit(solution)/shard_map/ml,pmn->pln/dot_general | solution.py:252
  97.5 3.0 %copy.27 = bf16[4,2048,128]{2,1,0:T(8,128)(2,1)S(1)} copy(bf16[4,2048,128]{1,2,0:T(8,128)(2,1)} %fusion.10) | data formatting | bytes 4194304 | tf_op jit(solution)/shard_map/convert_element_type | solution.py:253
  100.5 0.6 copy.28
  101.1 31.6 %all_to_all.20 = bf16[4,8,16,16,128]{4,3,1,0,2:T(8,128)(2,1)S(1)} all-to-all(bf16[4,8,16,16,128]{4,3,1,0,2:T(8,128)(2,1)S(1)} %copy.28), channel_id=1, replica_groups=mesh['aux'=2,'row'=8,'col'=16] {'col'}, dimensions={2} | all-to-all | bytes 4194304 | tf_op jit(solution)/shard_map/all_to_all | solution.py:256
  132.7 2.4 copy.29
  135.2 2.3 reshape.64
  137.5 3.0 %all-gather.3.cloned.1.call-done = bf16[2048,1024]{1,0:T(8,128)(2,1)} async-done(((bf16[256,1024]{1,0:T(8,128)(2,1)}), bf16[2048,1024]{1,0:T(8,128)(2,1)}) %all-gather.3.cloned.1.call-update) | async-done | bytes 4194320 | tf_op jit(solution)/shard_map/all_gather | solution.py:99
  140.5 0.0 collective-permute-start.1
  140.5 0.0 copy-start.4
  140.5 5.3 %fusion.17 = bf16[4,128,1024]{2,1,0:T(8,128)(2,1)S(1)} fusion(bf16[4,128,2048]{2,1,0:T(8,128)(2,1)} %reshape.64, bf16[2048,1024]{1,0:T(8,128)(2,1)} %all-gather.3.cloned.1.call-done), kind=kOutput, calls=%fused_computation.15 | convolution fusion | flops 2148007936 | bytes 7340032 | tf_op jit(solution)/shard_map/pln,ns->pls/dot_general | solution.py:260
  145.8 2.2 collective-permute-done.1
  148.0 0.0 copy-done.4
  148.0 4.5 %fusion.20 = bf16[4,128,1024]{2,1,0:T(8,128)(2,1)S(1)} fusion(bf16[4,128,2048]{2,1,0:T(8,128)(2,1)S(1)} %copy-done.4, bf16[2048,1024]{1,0:T(8,128)(2,1)} %collective-permute-done.1), kind=kOutput, calls=%fused_computation.16 | convolution fusion | flops 2148007936 | bytes 7340032 | tf_op jit(solution)/shard_map/pln,ns->pls/dot_general | solution.py:261
  152.6 0.8 maximum_select_fusion
  153.4 0.6 copy.38
  154.0 1.9 copy.30
  155.9 0.0 copy-start.1
  155.9 11.6 %all-to-all-start.1 = ((bf16[128,4,16,128]{3,2,1,0:T(8,128)(2,1)}), bf16[128,4,16,128]{3,2,1,0:T(8,128)(2,1)}, u32[]{:S(2)}, u32[]{:S(2)}) async-start(bf16[128,4,16,128]{3,2,1,0:T(8,128)(2,1)} %bitcast.64), calls=%async_computation.1 | async-start | bytes 4194304 | tf_op jit(solution)/shard_map/all_to_all | solution.py:272
  167.5 0.0 copy-done.1
  167.5 0.1 collective-permute-start.2
  167.6 51.6 %all-to-all-done.1 = bf16[128,4,16,128]{3,2,1,0:T(8,128)(2,1)} async-done(((bf16[128,4,16,128]{3,2,1,0:T(8,128)(2,1)}), bf16[128,4,16,128]{3,2,1,0:T(8,128)(2,1)}, u32[]{:S(2)}, u32[]{:S(2)}) %all-to-all-start.1) | async-done | bytes 2097184 | tf_op jit(solution)/shard_map/all_to_all | solution.py:272
  219.2 2.6 %copy.31 = bf16[8,4,16,16,128]{4,1,0,3,2:T(4,128)(2,1)S(1)} copy(bf16[8,4,16,16,128]{4,3,1,2,0:T(8,128)(2,1)} %bitcast.15) | data formatting | bytes 4194304 | tf_op jit(solution)/shard_map/rcpjs,qcjs->rpq/dot_general | solution.py:278
  221.9 1.5 fusion.23
  223.3 0.0 collective-permute-done.2
  223.4 3.1 %broadcast_select_fusion.1 = (f32[32,32]{1,0:T(8,128)S(1)}, f32[32,32]{1,0:T(8,128)S(1)}) fusion(f32[32,32]{1,0:T(8,128)S(1)} %fusion.23, pred[]{:T(512)S(6)} %eq.2, bf16[32,16,16,128]{3,0,2,1:T(8,128)(2,1)S(1)} %bitcast.72, bf16[32,16,16,128]{3,2,1,0:T(8,128)(2,1)} %bitcast.20), kind=kOutput, calls=%fused_computation.23 | convolution fusion | flops 67110912 | bytes 4206593 | tf_op jit(solution)/shard_map/rcpjs,qcjs->rpq/dot_general | solution.py:278
  226.5 0.7 pad_maximum_fusion.x_ref
  227.2 15.8 %shard_map.48 = f32[32,64]{1,0:T(8,128)} custom-call(f32[32,64]{1,0:T(8,128)} %pad_maximum_fusion.x_ref), custom_call_target="tpu_custom_call" | custom-call | tf_op jit(solution)/shard_map/pallas_call | solution.py:79
  243.0 1.3 broadcast_multiply_fusion.1
Async XLA Ops:
  6.5 14.9 %copy-start = (bf16[256,2048]{1,0:T(8,128)(2,1)S(1)}, bf16[256,2048]{1,0:T(8,128)(2,1)}, u32[]{:S(2)}) copy-start(bf16[256,2048]{1,0:T(8,128)(2,1)} %param.6) | copy-start | bytes 3145732
  6.5 16.7 %copy-start.3 = (bf16[32,256,128]{2,1,0:T(8,128)(2,1)S(1)}, bf16[32,256,128]{2,1,0:T(8,128)(2,1)}, u32[]{:S(2)}) copy-start(bf16[32,256,128]{2,1,0:T(8,128)(2,1)} %param.4) | copy-start | bytes 6291460
  6.5 77.5 %all-gather.5.cloned.1.call-start = ((), (), s32[]{:S(2)}) async-start(), calls=%async_computation.3 | async-start | bytes 4456448 | tf_op jit(solution)/shard_map/all_gather | solution.py:214
  21.4 119.1 %all-gather.3.cloned.1.call-start = ((), (), s32[]{:S(2)}) async-start(), calls=%async_computation.2 | async-start | bytes 4718592 | tf_op jit(solution)/shard_map/all_gather | solution.py:99
  84.1 7.5 %collective-permute-start = (bf16[1024,2048]{1,0:T(8,128)(2,1)}, bf16[1024,2048]{1,0:T(8,128)(2,1)}, u32[]{:S(2)}, u32[]{:S(2)}) collective-permute-start(bf16[1024,2048]{1,0:T(8,128)(2,1)} %all-gather.5.cloned.1.call-done), channel_id=1, source_target_pairs={{0,128},{128,0},{1,129},{129,1},{2,130},{130,2},{3,131},{131,3},{4... | collective-permute-start | bytes 12582920 | tf_op jit(solution)/shard_map/ppermute | solution.py:112
  84.1 2.8 %copy-start.2 = (bf16[1024,2048]{1,0:T(8,128)(2,1)S(1)}, bf16[1024,2048]{1,0:T(8,128)(2,1)}, u32[]{:S(2)}) copy-start(bf16[1024,2048]{1,0:T(8,128)(2,1)} %all-gather.5.cloned.1.call-done) | copy-start | bytes 12582916
  140.5 7.5 %collective-permute-start.1 = (bf16[2048,1024]{1,0:T(8,128)(2,1)}, bf16[2048,1024]{1,0:T(8,128)(2,1)}, u32[]{:S(2)}, u32[]{:S(2)}) collective-permute-start(bf16[2048,1024]{1,0:T(8,128)(2,1)} %all-gather.3.cloned.1.call-done), channel_id=1, source_target_pairs={{0,128},{128,0},{1,129},{129,1},{2,130},{130,2},{3,131},{131,3},{4... | collective-permute-start | bytes 12582920 | tf_op jit(solution)/shard_map/ppermute | solution.py:112
  140.5 7.5 %copy-start.4 = (bf16[4,128,2048]{2,1,0:T(8,128)(2,1)S(1)}, bf16[4,128,2048]{2,1,0:T(8,128)(2,1)}, u32[]{:S(2)}) copy-start(bf16[4,128,2048]{2,1,0:T(8,128)(2,1)} %reshape.64) | copy-start | bytes 6291460
  155.9 11.6 %copy-start.1 = (bf16[32,256,128]{2,1,0:T(8,128)(2,1)S(1)}, bf16[32,256,128]{2,1,0:T(8,128)(2,1)}, u32[]{:S(2)}) copy-start(bf16[32,256,128]{2,1,0:T(8,128)(2,1)} %broadcast_multiply_fusion.x_ref) | copy-start | bytes 6291460
  155.9 63.4 %all-to-all-start.1 = ((bf16[128,4,16,128]{3,2,1,0:T(8,128)(2,1)}), bf16[128,4,16,128]{3,2,1,0:T(8,128)(2,1)}, u32[]{:S(2)}, u32[]{:S(2)}) async-start(bf16[128,4,16,128]{3,2,1,0:T(8,128)(2,1)} %bitcast.64), calls=%async_computation.1 | async-start | bytes 4194304 | tf_op jit(solution)/shard_map/all_to_all | solution.py:272
  167.5 55.8 %collective-permute-start.2 = (bf16[32,256,128]{2,1,0:T(8,128)(2,1)S(1)}, bf16[32,256,128]{2,1,0:T(8,128)(2,1)}, u32[]{:S(2)}, u32[]{:S(2)}) collective-permute-start(bf16[32,256,128]{2,1,0:T(8,128)(2,1)S(1)} %copy-done.1), channel_id=1, source_target_pairs={{0,128},{128,0},{1,129},{129,1},{2,130},{130,2},{3,131},{131,3},{4... | collective-permute-start | bytes 6291464 | tf_op jit(solution)/shard_map/ppermute | solution.py:17
Sparse Core Ops, SparseCore 0:
  21.5 62.5 all-gather.4
  85.9 54.6 all-gather.2

commit v22 on v21

--- a/solution.py
+++ b/solution.py
@@ -242,11 +242,11 @@
     occ_rows = gather_occ_rows(occupied)
     virt_own = gather_half(virtual)
     moved = exchange(screened, "row", 0, 1, 1)
-    occ_rows, moved = lax.optimization_barrier((occ_rows, moved))
     pieces = moved.shape[0]
-    occ_other = swapped_core(occ_rows)
     mine = core_rows(moved, aux_idx)
     other = core_rows(moved, 1 - aux_idx)
+    occ_rows, mine, other = lax.optimization_barrier((occ_rows, mine, other))
+    occ_other = swapped_core(occ_rows)
     half = (
         jnp.einsum("ml,pmn->pln", occ_rows, mine, preferred_element_type=jnp.float32)
         + jnp.einsum("ml,pmn->pln", occ_other, other, preferred_element_type=jnp.float32)

time: 252 us -> 252 us (level)
    all_gather x1, waiting for transfers between devices: 9.41 us -> 5.77 us  [gather_occ_rows(): return lax.all_gather(column, 'col', axis=1, tiled=True)]
  transfers between devices with their start and end apart: 6 -> 6, of which waited for: 5 -> 5; matrix products, arithmetic and copies ran while one was open for 12% -> 13% of each run, Pallas kernels for 20% -> 20%
where the time goes in v22:
time: 252 us; the launch traced here: 251 us
  Pallas kernels  80.5 us (32%)
  waiting for transfers between devices  67.6 us (27%)
  blocking collectives  31.5 us (12%)
  matrix products  22.9 us (9%)
  local copies, waits for them, and re-layouts  18 us (7%)
  between operations  13.6 us (5%)
  starting transfers between devices  11.8 us (5%)
  other arithmetic  5.3 us (2%)
    pallas_call x2, Pallas kernels, exchange(): pl.pallas_call(functools.partial(exchange_kernel, mesh_axis, split_axis,...  64.6 us
    all_to_all x1, waiting for transfers between devices, shards(): lax.all_to_all(by_dest, ('row', 'col'), split_axis=0, concat_axis=0, tile...  51.6 us
    all_to_all x1, blocking collectives, shards(): lax.all_to_all(shaped, 'col', split_axis=2, concat_axis=4, tiled=True)  31.5 us
    pallas_call x1, Pallas kernels, doubling_sum(): pl.pallas_call(two_round_kernel, out_shape=jax.ShapeDtypeStruct(partial.s...  15.8 us
    all_to_all x1, starting transfers between devices, shards(): lax.all_to_all(by_dest, ('row', 'col'), split_axis=0, concat_axis=0, tile...  11.6 us
    all_gather x1, waiting for transfers between devices, gather_occ_rows(): return lax.all_gather(column, 'col', axis=1, tiled=True)  5.77 us
    all_gather x1, waiting for transfers between devices, gather_half(): return lax.all_gather(part, 'row', axis=0, tiled=True)  5.44 us
    dot_general x1, matrix products, shards(): jnp.einsum('pln,ns->pls', spread, virt_own, preferred_element_type=jnp.fl...  5.3 us
  transfers between devices with their start and end apart: 6, of which 5 were waited for; matrix products, arithmetic and copies ran while one was open for 13% of the time, Pallas kernels for 20%

profile of v22, /device:TPU:24, one launch (start us, length us, event | category | flops | bytes accessed | tf_op | source)
XLA Modules:
  0.0 251.2 jit_solution(12986123967028554015)
XLA Ops:
  6.5 0.0 copy-start
  6.5 0.0 copy-start.2
  6.5 0.0 all-gather.5.cloned.1.call-start
  6.5 14.8 %shard_map.46 = bf16[1024,128]{1,0:T(8,128)(2,1)} custom-call(bf16[256,2048]{1,0:T(8,128)(2,1)} %x_ref.1), custom_call_target="tpu_custom_call" | custom-call | bytes 2097152 | tf_op jit(solution)/shard_map/pallas_call | solution.py:192
  21.4 0.0 all-gather.5.cloned.1.call-update
  21.4 0.0 all-gather.3.cloned.1.call-start
  21.4 0.0 copy-done
  21.5 0.9 constant_dynamic-slice_fusion.2
  22.3 0.0 all-gather.3.cloned.1.call-update
  22.4 0.9 fusion.29
  23.2 0.1 broadcast_bitcast_fusion
  23.3 0.0 copy-done.2
  23.3 1.6 broadcast_multiply_fusion.x_ref
  24.9 49.8 %shard_map.47 = bf16[4,2048,128]{2,1,0:T(8,128)(2,1)} custom-call(bf16[32,256,128]{2,1,0:T(8,128)(2,1)} %broadcast_multiply_fusion.x_ref), custom_call_target="tpu_custom_call" | custom-call | bytes 4194304 | tf_op jit(solution)/shard_map/pallas_call | solution.py:192
  74.7 1.7 constant_dynamic-slice_fusion
  76.5 1.3 copy.36
  77.8 0.5 copy.37
  78.3 5.8 %all-gather.5.cloned.1.call-done = bf16[1024,2048]{1,0:T(8,128)(2,1)} async-done(((bf16[1024,128]{1,0:T(8,128)(2,1)}), bf16[1024,2048]{1,0:T(8,128)(2,1)}) %all-gather.5.cloned.1.call-update) | async-done | bytes 4194320 | tf_op jit(solution)/shard_map/all_gather | solution.py:214
  84.1 0.0 collective-permute-start
  84.1 4.8 %fusion.6 = f32[4,128,2048]{2,1,0:T(8,128)S(1)} fusion(bf16[4,1024,128]{1,2,0:T(8,128)(2,1)} %copy.36, bf16[1024,2048]{1,0:T(8,128)(2,1)} %all-gather.5.cloned.1.call-done), kind=kOutput, calls=%fused_computation.6 | convolution fusion | flops 2147483648 | bytes 9437184 | tf_op jit(solution)/shard_map/ml,pmn->pln/dot_general | solution.py:251
  88.9 2.5 %collective-permute-done = bf16[1024,2048]{1,0:T(8,128)(2,1)S(1)} collective-permute-done((bf16[1024,2048]{1,0:T(8,128)(2,1)}, bf16[1024,2048]{1,0:T(8,128)(2,1)S(1)}, u32[]{:S(2)}, u32[]{:S(2)}) %collective-permute-start) | collective-permute-done | bytes 4194336 | tf_op jit(solution)/shard_map/ppermute | solution.py:112
  91.4 3.7 %fusion.10 = bf16[4,2048,128]{1,2,0:T(8,128)(2,1)} fusion(f32[4,128,2048]{2,1,0:T(8,128)S(1)} %fusion.6, bf16[4,1024,128]{1,2,0:T(8,128)(2,1)S(1)} %copy.37, bf16[1024,2048]{1,0:T(8,128)(2,1)S(1)} %collective-permute-done), kind=kOutput, calls=%fused_computation.9 | convolution fusion | flops 2149580800 | bytes 11534336 | tf_op jit(solution)/shard_map/ml,pmn->pln/dot_general | solution.py:252
  95.1 3.1 %copy.27 = bf16[4,2048,128]{2,1,0:T(8,128)(2,1)S(1)} copy(bf16[4,2048,128]{1,2,0:T(8,128)(2,1)} %fusion.10) | data formatting | bytes 4194304 | tf_op jit(solution)/shard_map/convert_element_type | solution.py:253
  98.2 0.6 copy.28
  98.8 31.5 %all_to_all.20 = bf16[4,8,16,16,128]{4,3,1,0,2:T(8,128)(2,1)S(1)} all-to-all(bf16[4,8,16,16,128]{4,3,1,0,2:T(8,128)(2,1)S(1)} %copy.28), channel_id=1, replica_groups=mesh['aux'=2,'row'=8,'col'=16] {'col'}, dimensions={2} | all-to-all | bytes 4194304 | tf_op jit(solution)/shard_map/all_to_all | solution.py:256
  130.4 2.4 copy.29
  132.8 2.3 reshape.64
  135.1 5.4 %all-gather.3.cloned.1.call-done = bf16[2048,1024]{1,0:T(8,128)(2,1)} async-done(((bf16[256,1024]{1,0:T(8,128)(2,1)}), bf16[2048,1024]{1,0:T(8,128)(2,1)}) %all-gather.3.cloned.1.call-update) | async-done | bytes 4194320 | tf_op jit(solution)/shard_map/all_gather | solution.py:99
  140.5 0.0 collective-permute-start.1
  140.5 0.0 copy-start.3
  140.5 5.3 %fusion.17 = bf16[4,128,1024]{2,1,0:T(8,128)(2,1)S(1)} fusion(bf16[4,128,2048]{2,1,0:T(8,128)(2,1)} %reshape.64, bf16[2048,1024]{1,0:T(8,128)(2,1)} %all-gather.3.cloned.1.call-done), kind=kOutput, calls=%fused_computation.15 | convolution fusion | flops 2148007936 | bytes 7340032 | tf_op jit(solution)/shard_map/pln,ns->pls/dot_general | solution.py:260
  145.8 2.2 collective-permute-done.1
  148.0 0.0 copy-done.3
  148.0 4.5 %fusion.20 = bf16[4,128,1024]{2,1,0:T(8,128)(2,1)S(1)} fusion(bf16[4,128,2048]{2,1,0:T(8,128)(2,1)S(1)} %copy-done.3, bf16[2048,1024]{1,0:T(8,128)(2,1)} %collective-permute-done.1), kind=kOutput, calls=%fused_computation.16 | convolution fusion | flops 2148007936 | bytes 7340032 | tf_op jit(solution)/shard_map/pln,ns->pls/dot_general | solution.py:261
  152.6 0.8 maximum_select_fusion
  153.4 0.6 copy.38
  154.0 1.9 copy.30
  155.9 0.0 copy-start.1
  155.9 11.6 %all-to-all-start.1 = ((bf16[128,4,16,128]{3,2,1,0:T(8,128)(2,1)}), bf16[128,4,16,128]{3,2,1,0:T(8,128)(2,1)}, u32[]{:S(2)}, u32[]{:S(2)}) async-start(bf16[128,4,16,128]{3,2,1,0:T(8,128)(2,1)} %bitcast.64), calls=%async_computation.1 | async-start | bytes 4194304 | tf_op jit(solution)/shard_map/all_to_all | solution.py:272
  167.5 0.0 copy-done.1
  167.5 0.1 collective-permute-start.2
  167.6 51.6 %all-to-all-done.1 = bf16[128,4,16,128]{3,2,1,0:T(8,128)(2,1)} async-done(((bf16[128,4,16,128]{3,2,1,0:T(8,128)(2,1)}), bf16[128,4,16,128]{3,2,1,0:T(8,128)(2,1)}, u32[]{:S(2)}, u32[]{:S(2)}) %all-to-all-start.1) | async-done | bytes 2097184 | tf_op jit(solution)/shard_map/all_to_all | solution.py:272
  219.2 2.6 %copy.31 = bf16[8,4,16,16,128]{4,1,0,3,2:T(4,128)(2,1)S(1)} copy(bf16[8,4,16,16,128]{4,3,1,2,0:T(8,128)(2,1)} %bitcast.15) | data formatting | bytes 4194304 | tf_op jit(solution)/shard_map/rcpjs,qcjs->rpq/dot_general | solution.py:278
  221.9 1.5 fusion.23
  223.3 0.0 collective-permute-done.2
  223.4 3.1 %broadcast_select_fusion.1 = (f32[32,32]{1,0:T(8,128)S(1)}, f32[32,32]{1,0:T(8,128)S(1)}) fusion(f32[32,32]{1,0:T(8,128)S(1)} %fusion.23, pred[]{:T(512)S(6)} %eq.2, bf16[32,16,16,128]{3,0,2,1:T(8,128)(2,1)S(1)} %bitcast.72, bf16[32,16,16,128]{3,2,1,0:T(8,128)(2,1)} %bitcast.20), kind=kOutput, calls=%fused_computation.23 | convolution fusion | flops 67110912 | bytes 4206593 | tf_op jit(solution)/shard_map/rcpjs,qcjs->rpq/dot_general | solution.py:278
  226.5 0.7 pad_maximum_fusion.x_ref
  227.2 15.8 %shard_map.48 = f32[32,64]{1,0:T(8,128)} custom-call(f32[32,64]{1,0:T(8,128)} %pad_maximum_fusion.x_ref), custom_call_target="tpu_custom_call" | custom-call | tf_op jit(solution)/shard_map/pallas_call | solution.py:79
  243.0 1.3 broadcast_multiply_fusion.1
Async XLA Ops:
  6.5 14.9 %copy-start = (bf16[256,2048]{1,0:T(8,128)(2,1)S(1)}, bf16[256,2048]{1,0:T(8,128)(2,1)}, u32[]{:S(2)}) copy-start(bf16[256,2048]{1,0:T(8,128)(2,1)} %param.6) | copy-start | bytes 3145732
  6.5 16.8 %copy-start.2 = (bf16[32,256,128]{2,1,0:T(8,128)(2,1)S(1)}, bf16[32,256,128]{2,1,0:T(8,128)(2,1)}, u32[]{:S(2)}) copy-start(bf16[32,256,128]{2,1,0:T(8,128)(2,1)} %param.4) | copy-start | bytes 6291460
  6.5 77.5 %all-gather.5.cloned.1.call-start = ((), (), s32[]{:S(2)}) async-start(), calls=%async_computation.3 | async-start | bytes 4456448 | tf_op jit(solution)/shard_map/all_gather | solution.py:214
  21.4 119.1 %all-gather.3.cloned.1.call-start = ((), (), s32[]{:S(2)}) async-start(), calls=%async_computation.2 | async-start | bytes 4718592 | tf_op jit(solution)/shard_map/all_gather | solution.py:99
  84.1 7.4 %collective-permute-start = (bf16[1024,2048]{1,0:T(8,128)(2,1)}, bf16[1024,2048]{1,0:T(8,128)(2,1)S(1)}, u32[]{:S(2)}, u32[]{:S(2)}) collective-permute-start(bf16[1024,2048]{1,0:T(8,128)(2,1)} %all-gather.5.cloned.1.call-done), channel_id=1, source_target_pairs={{0,128},{128,0},{1,129},{129,1},{2,130},{130,2},{3,131},{131,3},{4... | collective-permute-start | bytes 12582920 | tf_op jit(solution)/shard_map/ppermute | solution.py:112
  140.5 7.5 %collective-permute-start.1 = (bf16[2048,1024]{1,0:T(8,128)(2,1)}, bf16[2048,1024]{1,0:T(8,128)(2,1)}, u32[]{:S(2)}, u32[]{:S(2)}) collective-permute-start(bf16[2048,1024]{1,0:T(8,128)(2,1)} %all-gather.3.cloned.1.call-done), channel_id=1, source_target_pairs={{0,128},{128,0},{1,129},{129,1},{2,130},{130,2},{3,131},{131,3},{4... | collective-permute-start | bytes 12582920 | tf_op jit(solution)/shard_map/ppermute | solution.py:112
  140.5 7.5 %copy-start.3 = (bf16[4,128,2048]{2,1,0:T(8,128)(2,1)S(1)}, bf16[4,128,2048]{2,1,0:T(8,128)(2,1)}, u32[]{:S(2)}) copy-start(bf16[4,128,2048]{2,1,0:T(8,128)(2,1)} %reshape.64) | copy-start | bytes 6291460
  155.9 11.6 %copy-start.1 = (bf16[32,256,128]{2,1,0:T(8,128)(2,1)S(1)}, bf16[32,256,128]{2,1,0:T(8,128)(2,1)}, u32[]{:S(2)}) copy-start(bf16[32,256,128]{2,1,0:T(8,128)(2,1)} %broadcast_multiply_fusion.x_ref) | copy-start | bytes 6291460
  155.9 63.4 %all-to-all-start.1 = ((bf16[128,4,16,128]{3,2,1,0:T(8,128)(2,1)}), bf16[128,4,16,128]{3,2,1,0:T(8,128)(2,1)}, u32[]{:S(2)}, u32[]{:S(2)}) async-start(bf16[128,4,16,128]{3,2,1,0:T(8,128)(2,1)} %bitcast.64), calls=%async_computation.1 | async-start | bytes 4194304 | tf_op jit(solution)/shard_map/all_to_all | solution.py:272
  167.5 55.8 %collective-permute-start.2 = (bf16[32,256,128]{2,1,0:T(8,128)(2,1)S(1)}, bf16[32,256,128]{2,1,0:T(8,128)(2,1)}, u32[]{:S(2)}, u32[]{:S(2)}) collective-permute-start(bf16[32,256,128]{2,1,0:T(8,128)(2,1)S(1)} %copy-done.1), channel_id=1, source_target_pairs={{0,128},{128,0},{1,129},{129,1},{2,130},{130,2},{3,131},{131,3},{4... | collective-permute-start | bytes 6291464 | tf_op jit(solution)/shard_map/ppermute | solution.py:17
Sparse Core Ops, SparseCore 0:
  21.5 62.5 all-gather.4
  85.9 54.6 all-gather.2
